TPU v7x, 32 devices: a whole 2x2x4 slice. The times are simulated.
32 devices in a mesh: grp: 2 (over y), user: 4 (over z), tm: 4 (over x, core).
Axes of the slice: x: 2, y: 2, z: 4, core: 2. Of those that a mesh axis runs over, the one named last changes fastest.
Arguments:
- history: bfloat16 [8, 1024, 512], P(('grp', 'user'), 'tm'), parts along dimension 0, may hold values from -6 to 6
- z_weight: bfloat16 [512, 1024], replicated, may hold values from -0.25 to 0.25
- xbc_weight: bfloat16 [512, 1280], replicated, may hold values from -0.25 to 0.25
- dt_weight: bfloat16 [512, 16], replicated, may hold values from -0.125 to 0.125
- dt_bias: float32 [16], replicated, may hold values from -1 to 0.5
- a_log: float32 [16], replicated
- conv_weight: float32 [4, 1280], replicated, may hold values from -3 to 3
- conv_bias: float32 [1280], replicated, may hold values from -3 to 3
- d_skip: float32 [16], replicated, may hold values from 0.5 to 1.5
- norm_gain: float32 [1024], replicated, may hold values from 0.1 to 1.9
- out_weight: bfloat16 [1024, 512], replicated, may hold values from -0.1875 to 0.1875
- label_pos: int32 [8, 2048], P(('grp', 'user'), 'tm'), parts along dimension 0, may hold values from 0 to 1023, as said below
- label_count: int32 [8, 4], P(('grp', 'user'), 'tm'), parts along dimension 0, may hold values from 1 to 511, as said below
- label_value: int32 [8, 2048], P(('grp', 'user'), 'tm'), parts along dimension 0, may hold values 0 or 1
- item_feat: bfloat16 [8, 2048, 512], P(('grp', 'user'), 'tm'), parts along dimension 0, may hold values from -6 to 6
- first_weight: bfloat16 [1024, 1024], replicated, may hold values from -0.1875 to 0.1875
- second_weight: bfloat16 [1024], replicated, may hold values from -0.1875 to 0.1875
Outputs:
- encoded: bfloat16 [8, 1024, 512], P(('grp', 'user'), 'tm'), parts along dimension 0
- row_logit: float32 [8, 2048], P(('grp', 'user'), 'tm'), parts along dimension 0
- grad_first: float32 [2048, 1024], P('grp'), parts along dimension 0
- grad_second: float32 [2048], P('grp'), parts along dimension 0
There are 2 independent parts, one for each index of `grp`. A program takes and returns all parts, laid end to end along the dimension named above; an argument that names none is the same for every part. Nothing has to cross between parts.
Inputs may be any that keep to these rules, and one draw needn't show every extreme that they name: `label_pos`: positions in slots k * 512 to (k + 1) * 512 - 1 of a user lie in events k * 256 to (k + 1) * 256 - 1. label_count[u, k] slots are used in block k of user u's slots, and they are the block's first ones; the counts of blocks 2 * k and 2 * k + 1 of a user sum to 512.
All inputs are finite; a program needn't handle non-finite values. No bound on the sum of `label_value` on one device may be relied on, other than what follows from the above.
Results may differ from a plain program's by a relative error of at most 0.015.
Values may be sent and summed in bfloat16 or wider, within the bound.
No kernel may reach another device: no remote copies, remote signals or barrier semaphores. Data moves between devices by JAX's collectives and lax.ppermute only.
A program may use at most 64 MiB of HBM per device.

v0:
```python
import jax
import jax.numpy as jnp
from jax import lax
from jax.sharding import PartitionSpec as P

BLOCK = 256


def passed_along(shard, axis, by):
    peers = lax.axis_size(axis)
    pairs = [(i, i + by) for i in range(peers) if 0 <= i + by < peers]
    return lax.ppermute(shard, axis, pairs)


def silu_grad(values):
    sig = jax.nn.sigmoid(values)
    return sig * (1.0 + values * (1.0 - sig))


def ranker(rank_rows, target, live_mask, first_weight, second_weight):
    pre_act = jnp.dot(rank_rows, first_weight, preferred_element_type=jnp.float32)
    hidden = jax.nn.silu(pre_act).astype(jnp.bfloat16)
    logit_vec = jnp.dot(hidden, second_weight, preferred_element_type=jnp.float32)
    dlogit = live_mask * (jax.nn.sigmoid(logit_vec) - target)
    grad_two = jnp.dot(dlogit, hidden.astype(jnp.float32), precision=lax.Precision.HIGHEST)
    grad_pre = (
        dlogit[:, None] * second_weight.astype(jnp.float32)[None, :] * silu_grad(pre_act)
    ).astype(jnp.bfloat16)
    grad_one = jnp.dot(rank_rows.T, grad_pre, preferred_element_type=jnp.float32)
    return (live_mask * logit_vec, grad_one, grad_two)


def body(
    history,
    z_weight,
    xbc_weight,
    dt_weight,
    dt_bias,
    a_log,
    conv_weight,
    conv_bias,
    d_skip,
    norm_gain,
    out_weight,
    label_pos,
    label_count,
    label_value,
    item_feat,
    first_weight,
    second_weight,
):
    user_count, length, model_width = history.shape
    inner_width = z_weight.shape[1]
    head_count = a_log.shape[0]
    head_size = inner_width // head_count
    state_dim = (xbc_weight.shape[1] - inner_width) // 2
    tap_count = conv_weight.shape[0]
    flat_rows = history.reshape(user_count * length, model_width)
    z_gate = (
        jnp.dot(flat_rows, z_weight, preferred_element_type=jnp.float32)
        .astype(jnp.bfloat16)
        .reshape(user_count, length, inner_width)
    )
    xbc_raw = (
        jnp.dot(flat_rows, xbc_weight, preferred_element_type=jnp.float32)
        .astype(jnp.bfloat16)
        .reshape(user_count, length, -1)
    )
    step_size = jax.nn.softplus(
        jnp.dot(flat_rows, dt_weight, preferred_element_type=jnp.float32) + dt_bias
    ).reshape(user_count, length, head_count)
    rim_rows = passed_along(xbc_raw[:, length - (tap_count - 1) :, :], "tm", 1)
    padded = jnp.concatenate([rim_rows, xbc_raw], axis=1)
    conv_sum = jnp.zeros(xbc_raw.shape, jnp.float32) + conv_bias
    for tap in range(tap_count):
        conv_sum = conv_sum + conv_weight[tap] * padded[:, tap : tap + length, :].astype(
            jnp.float32
        )
    xbc = jax.nn.silu(conv_sum).astype(jnp.bfloat16)
    block_count = length // BLOCK
    x_part = xbc[..., :inner_width].reshape(user_count, block_count, BLOCK, head_count, head_size)
    b_part = xbc[..., inner_width : inner_width + state_dim].reshape(
        user_count, block_count, BLOCK, state_dim
    )
    c_part = xbc[..., inner_width + state_dim :].reshape(user_count, block_count, BLOCK, state_dim)
    log_decay = (-jnp.exp(a_log) * step_size).reshape(user_count, block_count, BLOCK, head_count)
    cumulated = jnp.cumsum(log_decay, axis=2)
    step_blocks = step_size.reshape(user_count, block_count, BLOCK, head_count)
    rows_idx = lax.broadcasted_iota(jnp.int32, (BLOCK, BLOCK), 0)
    cols_idx = lax.broadcasted_iota(jnp.int32, (BLOCK, BLOCK), 1)
    causal = (cols_idx <= rows_idx)[None, None]

    def block_step(carry_state, inputs):
        x_block, b_block, c_block, cum_block, step_block = inputs
        scores = jnp.einsum("utn,usn->uts", c_block, b_block, preferred_element_type=jnp.float32)
        cum_heads = jnp.swapaxes(cum_block, 1, 2)
        gaps = cum_heads[:, :, :, None] - cum_heads[:, :, None, :]
        decays = jnp.where(causal, jnp.exp(jnp.where(causal, gaps, 0.0)), 0.0)
        weights = (decays * jnp.swapaxes(step_block, 1, 2)[:, :, None, :] * scores[:, None]).astype(
            jnp.bfloat16
        )
        within = jnp.einsum("uhts,ushp->uthp", weights, x_block, preferred_element_type=jnp.float32)
        last_cum = cum_block[:, -1, :]
        carried = (
            (jnp.exp(last_cum[:, None, :] - cum_block) * step_block)[..., None]
            * x_block.astype(jnp.float32)
        ).astype(jnp.bfloat16)
        new_state = jnp.exp(last_cum)[:, :, None, None] * carry_state + jnp.einsum(
            "ushp,usn->uhpn", carried, b_block, preferred_element_type=jnp.float32
        )
        result = within + d_skip[None, None, :, None] * x_block.astype(jnp.float32)
        return (new_state, (result, carry_state))

    zero_state = jnp.zeros((user_count, head_count, head_size, state_dim), jnp.float32)
    scan_inputs = (
        jnp.moveaxis(x_part, 1, 0),
        jnp.moveaxis(b_part, 1, 0),
        jnp.moveaxis(c_part, 1, 0),
        jnp.moveaxis(cumulated, 1, 0),
        jnp.moveaxis(step_blocks, 1, 0),
    )
    local_end, (partial_value, entering_local) = lax.scan(block_step, zero_state, scan_inputs)
    block_last = cumulated[:, :, -1, :]
    before_log = jnp.cumsum(block_last, axis=1) - block_last
    chain_gain = jnp.exp(jnp.sum(block_last, axis=1))
    incoming = jnp.zeros_like(local_end)
    for relay_step in range(lax.axis_size("tm") - 1):
        outgoing = chain_gain[:, :, None, None] * incoming + local_end
        incoming = passed_along(outgoing, "tm", 1)
    entering = (
        jnp.moveaxis(entering_local, 0, 1)
        + jnp.exp(before_log)[..., None, None] * incoming[:, None]
    )
    entering_high = entering.astype(jnp.bfloat16)
    entering_low = (entering - entering_high.astype(jnp.float32)).astype(jnp.bfloat16)
    state_read = jnp.einsum(
        "ubtn,ubhpn->ubthp", c_part, entering_high, preferred_element_type=jnp.float32
    )
    state_read = state_read + jnp.einsum(
        "ubtn,ubhpn->ubthp", c_part, entering_low, preferred_element_type=jnp.float32
    )
    across = jnp.exp(cumulated)[..., None] * state_read
    ssd_out = (jnp.moveaxis(partial_value, 0, 1) + across).reshape(user_count, length, inner_width)
    gated_out = ssd_out * jax.nn.silu(z_gate.astype(jnp.float32))
    normed = (
        gated_out
        * lax.rsqrt(jnp.mean(gated_out * gated_out, axis=-1, keepdims=True) + 1e-05)
        * norm_gain
    ).astype(jnp.bfloat16)
    encoded = (
        jnp.dot(normed.reshape(-1, inner_width), out_weight, preferred_element_type=jnp.float32)
        .astype(jnp.bfloat16)
        .reshape(user_count, length, model_width)
    )
    slot_count = label_pos.shape[1]
    tm_index = lax.axis_index("tm")
    local_pos = label_pos - tm_index * length
    enc_rows = jax.vmap(lambda table, indices: table[indices])(encoded, local_pos)
    rank_rows = jnp.concatenate([enc_rows, item_feat], axis=-1)
    slot_iota = lax.broadcasted_iota(jnp.int32, (user_count, slot_count), 1)
    live_mask = (slot_iota < label_count).astype(jnp.float32)
    target = label_value.astype(jnp.float32)
    logit_vec, grad_one, grad_two = ranker(
        rank_rows.reshape(-1, 2 * model_width),
        target.reshape(-1),
        live_mask.reshape(-1),
        first_weight,
        second_weight,
    )
    row_logit = logit_vec.reshape(user_count, slot_count)
    share_first, share_second = (
        lax.psum_scatter(
            grad_one.astype(jnp.bfloat16), "tm", scatter_dimension=0, tiled=True
        ).astype(jnp.float32),
        lax.psum_scatter(
            grad_two.astype(jnp.bfloat16), "tm", scatter_dimension=0, tiled=True
        ).astype(jnp.float32),
    )
    summed_first, summed_second = (
        lax.psum(share_first.astype(jnp.bfloat16), "user").astype(jnp.float32),
        lax.psum(share_second.astype(jnp.bfloat16), "user").astype(jnp.float32),
    )
    grad_first, grad_second = (
        lax.all_gather(summed_first.astype(jnp.bfloat16), "tm", axis=0, tiled=True).astype(
            summed_first.dtype
        ),
        lax.all_gather(summed_second.astype(jnp.bfloat16), "tm", axis=0, tiled=True).astype(
            summed_second.dtype
        ),
    )
    return (encoded, row_logit, grad_first, grad_second)


def solution(mesh):
    in_specs = (
        P(("grp", "user"), "tm", None),
        P(),
        P(),
        P(),
        P(),
        P(),
        P(),
        P(),
        P(),
        P(),
        P(),
        P(("grp", "user"), "tm"),
        P(("grp", "user"), "tm"),
        P(("grp", "user"), "tm"),
        P(("grp", "user"), "tm", None),
        P(),
        P(),
    )
    out_specs = (P(("grp", "user"), "tm", None), P(("grp", "user"), "tm"), P("grp", None), P("grp"))
    return jax.shard_map(body, mesh=mesh, in_specs=in_specs, out_specs=out_specs, check_vma=False)
```

profile of v0, /device:TPU:0, one launch (start us, length us, event | category | flops | bytes accessed | tf_op | source)
XLA Modules:
  0.0 186.1 jit_solution(1924651855535223238)
XLA Ops:
  7.3 2.0 %convolution_convert_fusion = bf16[256,1280]{1,0:T(8,128)(2,1)S(1)} fusion(bf16[512,1280]{1,0:T(8,128)(2,1)} %param.19, bf16[1,256,512]{2,1,0:T(8,128)(2,1)} %param.17), kind=kOutput, calls=%fused_computation.2 | convolution fusion | flops 335872000 | bytes 2228224 | tf_op jit(solution)/shard_map/dot_general | solution.py:65
  9.4 2.4 %collective-permute-start = (bf16[1,3,1280]{2,1,0:T(4,128)(2,1)S(1)}, bf16[1,3,1280]{2,1,0:T(4,128)(2,1)S(1)}, u32[]{:S(2)}, u32[]{:S(2)}) collective-permute-start(bf16[1,3,1280]{2,1,0:T(4,128)(2,1)S(1)} %slice.63), channel_id=1, source_target_pairs={{0,1},{1,2},{2,3},{4,5},{5,6},{6,7},{8,9},{9,10},{10,11},{12,13},{... | collective-permute-start | bytes 23048 | tf_op jit(solution)/shard_map/ppermute | solution.py:12
  14.7 2.5 %copy.42 = f32[1,256,1024]{2,1,0:T(8,128)} copy(f32[1,256,1024]{1,2,0:T(8,128)} %bitcast.132) | data formatting | bytes 2097152 | tf_op jit(solution)/shard_map/while/body/eval_jaxpr/mul | solution.py:105
  19.6 1.4 convolution_add_fusion.1
  21.9 5.3 %collective-permute-start.1 = (f32[1,16,64,128]{3,2,1,0:T(8,128)}, f32[1,16,64,128]{3,2,1,0:T(8,128)}, u32[]{:S(2)}, u32[]{:S(2)}) collective-permute-start(f32[1,16,64,128]{3,2,1,0:T(8,128)} %add_bitcast_fusion), channel_id=1, source_target_pairs={{0,1},{1,2},{2,3},{4,5},{5,6},{6,7},{8,9},{9,10},{10,11},{12,13},{... | collective-permute-start | bytes 1572872 | tf_op jit(solution)/shard_map/ppermute | solution.py:12
  28.3 2.0 %bitcast_add_fusion.2 = f32[1,16,64,128]{3,2,1,0:T(8,128)} fusion(f32[16,64,128]{2,1,0:T(8,128)S(1)} %convolution_add_fusion.1, f32[1,16,64,128]{3,2,1,0:T(8,128)} %collective-permute-done.1, f32[16]{0:T(128)S(1)} %get-tuple-element.31), kind=kLoop, calls=%fused_computation.47 | loop fusion | flops 262144 | bytes 1572928 | tf_op jit(solution)/shard_map/add | solution.py:128
  30.3 7.3 %collective-permute-start.2 = (f32[1,16,64,128]{3,2,1,0:T(8,128)}, f32[1,16,64,128]{3,2,1,0:T(8,128)}, u32[]{:S(2)}, u32[]{:S(2)}) collective-permute-start(f32[1,16,64,128]{3,2,1,0:T(8,128)} %bitcast_add_fusion.2), channel_id=1, source_target_pairs={{0,1},{1,2},{2,3},{4,5},{5,6},{6,7},{8,9},{9,10},{10,11},{12,13},{... | collective-permute-start | bytes 1572872 | tf_op jit(solution)/shard_map/ppermute | solution.py:12
  38.3 1.3 slice_convert_fusion
  39.6 2.6 %copy.41 = f32[1,256,1024]{1,2,0:T(8,128)} copy(f32[1,256,1024]{2,1,0:T(8,128)} %get-tuple-element.45) | data formatting | bytes 2097152 | tf_op jit(solution)/shard_map/while/body/eval_jaxpr/convert_element_type | solution.py:106
  42.1 2.0 %copy.37 = bf16[1,256,1024]{1,2,0:T(8,128)(2,1)} copy(bf16[1,256,1024]{2,1,0:T(8,128)(2,1)} %get-tuple-element.46) | data formatting | bytes 1048576 | tf_op jit(solution)/shard_map/slice | solution.py:81
  45.4 3.6 %collective-permute-start.3 = (f32[1,16,64,128]{3,2,1,0:T(8,128)S(1)}, f32[1,16,64,128]{3,2,1,0:T(8,128)S(1)}, u32[]{:S(2)}, u32[]{:S(2)}) collective-permute-start(f32[1,16,64,128]{3,2,1,0:T(8,128)S(1)} %bitcast_add_fusion.1), channel_id=1, source_target_pairs={{0,1},{1,2},{2,3},{4,5},{5,6},{6,7},{8,9},{9,10},{10,11},{12,13},{... | collective-permute-start | bytes 1572872 | tf_op jit(solution)/shard_map/ppermute | solution.py:12
  49.2 2.8 %fusion.11 = f32[256,16,64]{0,2,1:T(8,128)S(1)} fusion(bf16[256,16,64]{0,2,1:T(8,128)(2,1)} %bitcast.138, f32[256,256]{1,0:T(8,128)S(1)} %fusion.38, f32[16,256]{1,0:T(8,128)S(1)} %bitcast.139, f32[16,256]{1,0:T(8,128)S(1)} %bitcast.142, pred[256,256]{1,0:T(8,128)(4,1)S(1)} %iota_compare_fusion, f32[1,256,16,64]{1,3,2,0:T(8,128)} %bitcast.135, ...), kind=kOutput, calls=%fused_computation.19 | convolution fusion | flops 141033472 | bytes 2981952 | tf_op jit(solution)/shard_map/while/body/eval_jaxpr/uhts,ushp->uthp/dot_general | solution.py:102
  52.4 1.4 fusion.9
  53.8 2.5 %copy.44 = f32[256,1024]{1,0:T(8,128)} copy(f32[256,1024]{0,1:T(8,128)} %bitcast.133) | data formatting | bytes 2097152 | tf_op jit(solution)/shard_map/reshape | solution.py:143
  56.4 2.3 %multiply_reduce_fusion = (f32[256]{0:T(256)S(1)}, f32[256,1024]{1,0:T(8,128)S(1)}) fusion(f32[256,1024]{1,0:T(8,128)} %copy.44, bf16[512,1024]{1,0:T(8,128)(2,1)} %param.18, bf16[1,256,512]{2,1,0:T(8,128)(2,1)S(1)} %copy-done.4), kind=kOutput, calls=%fused_computation.38 | convolution fusion | flops 270794496 | bytes 3408896 | tf_op jit(solution)/shard_map/dot_general | solution.py:60
  59.2 5.8 %gather_fusion = bf16[512,512]{1,0:T(8,128)(2,1)} fusion(bf16[1,256,512]{2,1,0:T(8,128)(2,1)S(1)} %fusion.12, s32[512]{0:T(512)S(1)} %bitcast.129), kind=kCustom, calls=%fused_computation | custom fusion | bytes 1052672 | tf_op jit(solution)/shard_map/vmap()/gather | solution.py:158
  65.0 2.8 %multiply_convert_fusion.3 = (bf16[512,1024]{1,0:T(8,128)(2,1)S(1)}, f32[512,1024]{1,0:T(8,128)S(1)}) fusion(bf16[1024,1024]{1,0:T(8,128)(2,1)S(1)} %copy-done, bf16[1,512,512]{2,1,0:T(8,128)(2,1)} %param.31, bf16[1,512,512]{2,1,0:T(8,128)(2,1)} %bitcast.136), kind=kOutput, calls=%fused_computation.5 | convolution fusion | flops 1078460416 | bytes 6291456 | tf_op jit(solution)/shard_map/dot_general | solution.py:21
  68.8 3.0 %convolution_convert_fusion.1 = bf16[1024,1024]{1,0:T(8,128)(2,1)} fusion(f32[512,1024]{1,0:T(8,128)S(1)} %get-tuple-element.52, f32[1024]{0:T(1024)S(1)} %convert_element_type.159, f32[512]{0:T(512)S(1)} %get-tuple-element.47, bf16[1,512,512]{2,1,0:T(8,128)(2,1)S(1)} %copy-done.15, bf16[1,512,512]{2,1,0:T(8,128)(2,1)S(1)} %bitcast.137), kind=kOutput, calls=%fused_computation.13 | convolution fusion | flops 1082130432 | bytes 5249024 | tf_op jit(solution)/shard_map/dot_general | solution.py:29
  71.9 38.7 %reduce-scatter.2.cloned.1.call-done = bf16[256,1024]{1,0:T(8,128)(2,1)} async-done(((bf16[1024,1024]{1,0:T(8,128)(2,1)}), bf16[256,1024]{1,0:T(8,128)(2,1)}) %reduce-scatter.2.cloned.1.call-update) | async-done | bytes 524304 | tf_op jit(solution)/shard_map/reduce_scatter | solution.py:172
  110.7 40.8 %all-reduce.3.cloned.1.call-done = bf16[256,1024]{1,0:T(8,128)(2,1)} async-done(((bf16[256,1024]{1,0:T(8,128)(2,1)}), bf16[256,1024]{1,0:T(8,128)(2,1)}) %all-reduce.3.cloned.1.call-update) | async-done | bytes 524304 | tf_op jit(solution)/shard_map/psum | solution.py:180
  153.3 5.6 %all-reduce = bf16[1024]{0:T(1024)(128)(2,1)S(1)} all-reduce(bf16[1024]{0:T(1024)(128)(2,1)S(1)} %convert_element_type.163), channel_id=3, replica_groups=mesh['grp'=2,'user'=4,'tm'=4] {'tm'}, use_global_device_ids=true, to_apply=%region_5.6.clone | all-reduce | flops 1024 | bytes 4096
  159.0 10.6 %psum.15 = bf16[256]{0:T(256)(128)(2,1)S(1)} all-reduce(bf16[256]{0:T(256)(128)(2,1)S(1)} %dynamic-slice.4), channel_id=1, replica_groups=mesh['grp'=2,'user'=4,'tm'=4] {'user'}, use_global_device_ids=true, to_apply=%region_6.7 | all-reduce | flops 256 | bytes 1024 | tf_op jit(solution)/shard_map/psum | solution.py:181
  169.6 5.1 %all-gather = bf16[4,1,256]{2,1,0:T(2,128)(2,1)S(1)} all-gather(bf16[1,1,256]{2,1,0:T(2,128)(2,1)S(1)} %reshape.326), channel_id=1, replica_groups=mesh['grp'=2,'user'=4,'tm'=4] {'tm'}, dimensions={0}, use_global_device_ids=true | all-gather | bytes 2560 | tf_op jit(solution)/shard_map/all_gather | solution.py:187
  175.5 4.1 %convert_element_type.162 = f32[1024,1024]{1,0:T(8,128)} convert(bf16[1024,1024]{1,0:T(8,128)(2,1)} %all-gather.3.cloned.1.call-done) | non-fusion elementwise | flops 1048576 | bytes 6291456 | tf_op jit(solution)/shard_map/convert_element_type | solution.py:184
  (92 shorter events, 12.5 us)
Async XLA Ops:
  7.2 57.8 %copy-start = (bf16[1024,1024]{1,0:T(8,128)(2,1)S(1)}, bf16[1024,1024]{1,0:T(8,128)(2,1)}, u32[]{:S(2)}) copy-start(bf16[1024,1024]{1,0:T(8,128)(2,1)} %param.32) | copy-start | bytes 6291460
  7.2 4.6 %copy-start.3 = (bf16[1,256,512]{2,1,0:T(8,128)(2,1)S(1)}, bf16[1,256,512]{2,1,0:T(8,128)(2,1)}, u32[]{:S(2)}) copy-start(bf16[1,256,512]{2,1,0:T(8,128)(2,1)} %param.17) | copy-start | bytes 786436
  7.2 4.6 %copy-start.16 = (f32[16]{0:T(128)S(1)}, f32[16]{0:T(128)}, u32[]{:S(2)}) copy-start(f32[16]{0:T(128)} %param.22) | copy-start | bytes 196
  7.2 4.6 %copy-start.14 = (f32[16]{0:T(128)S(1)}, f32[16]{0:T(128)}, u32[]{:S(2)}) copy-start(f32[16]{0:T(128)} %param.21) | copy-start | bytes 196
  7.2 4.6 %copy-start.8 = (bf16[512,16]{0,1:T(8,128)(2,1)S(1)}, bf16[512,16]{0,1:T(8,128)(2,1)}, u32[]{:S(2)}) copy-start(bf16[512,16]{0,1:T(8,128)(2,1)} %param.20) | copy-start | bytes 49156
  7.2 6.4 %copy-start.7 = (f32[4,1280]{1,0:T(4,128)S(1)}, f32[4,1280]{1,0:T(4,128)}, u32[]{:S(2)}) copy-start(f32[4,1280]{1,0:T(4,128)} %param.23) | copy-start | bytes 61444
  7.2 103.4 %reduce-scatter.2.cloned.1.call-start = ((), (), s32[]{:S(2)}) async-start(), calls=%async_computation.1 | async-start | bytes 2621440 | tf_op jit(solution)/shard_map/reduce_scatter | solution.py:172
  9.3 7.9 %copy-start.9 = (f32[1280]{0:T(1024)S(1)}, f32[1280]{0:T(1024)}, u32[]{:S(2)}) copy-start(f32[1280]{0:T(1024)} %param.24) | copy-start | bytes 15364
  9.4 7.9 %collective-permute-start = (bf16[1,3,1280]{2,1,0:T(4,128)(2,1)S(1)}, bf16[1,3,1280]{2,1,0:T(4,128)(2,1)S(1)}, u32[]{:S(2)}, u32[]{:S(2)}) collective-permute-start(bf16[1,3,1280]{2,1,0:T(4,128)(2,1)S(1)} %slice.63), channel_id=1, source_target_pairs={{0,1},{1,2},{2,3},{4,5},{5,6},{6,7},{8,9},{9,10},{10,11},{12,13},{... | collective-permute-start | bytes 23048 | tf_op jit(solution)/shard_map/ppermute | solution.py:12
  18.6 8.6 %copy-start.12 = (s32[1,512]{1,0:T(1,128)S(1)}, s32[1,512]{1,0:T(1,128)}, u32[]{:S(2)}) copy-start(s32[1,512]{1,0:T(1,128)} %param.28) | copy-start | bytes 6148
  19.6 17.9 %copy-start.10 = (bf16[1024]{0:T(1024)(128)(2,1)S(1)}, bf16[1024]{0:T(1024)(128)(2,1)}, u32[]{:S(2)}) copy-start(bf16[1024]{0:T(1024)(128)(2,1)} %param.33) | copy-start | bytes 6148
  19.6 18.6 %copy-start.13 = (s32[1,512]{1,0:T(1,128)S(1)}, s32[1,512]{1,0:T(1,128)}, u32[]{:S(2)}) copy-start(s32[1,512]{1,0:T(1,128)} %param.30) | copy-start | bytes 6148
  21.9 6.3 %collective-permute-start.1 = (f32[1,16,64,128]{3,2,1,0:T(8,128)}, f32[1,16,64,128]{3,2,1,0:T(8,128)}, u32[]{:S(2)}, u32[]{:S(2)}) collective-permute-start(f32[1,16,64,128]{3,2,1,0:T(8,128)} %add_bitcast_fusion), channel_id=1, source_target_pairs={{0,1},{1,2},{2,3},{4,5},{5,6},{6,7},{8,9},{9,10},{10,11},{12,13},{... | collective-permute-start | bytes 1572872 | tf_op jit(solution)/shard_map/ppermute | solution.py:12
  30.3 13.9 %collective-permute-start.2 = (f32[1,16,64,128]{3,2,1,0:T(8,128)}, f32[1,16,64,128]{3,2,1,0:T(8,128)}, u32[]{:S(2)}, u32[]{:S(2)}) collective-permute-start(f32[1,16,64,128]{3,2,1,0:T(8,128)} %bitcast_add_fusion.2), channel_id=1, source_target_pairs={{0,1},{1,2},{2,3},{4,5},{5,6},{6,7},{8,9},{9,10},{10,11},{12,13},{... | collective-permute-start | bytes 1572872 | tf_op jit(solution)/shard_map/ppermute | solution.py:12
  39.6 9.6 %copy-start.17 = (f32[16]{0:T(128)S(1)}, f32[16]{0:T(128)}, u32[]{:S(2)}) copy-start(f32[16]{0:T(128)} %param.25) | copy-start | bytes 196
  45.4 6.7 %collective-permute-start.3 = (f32[1,16,64,128]{3,2,1,0:T(8,128)S(1)}, f32[1,16,64,128]{3,2,1,0:T(8,128)S(1)}, u32[]{:S(2)}, u32[]{:S(2)}) collective-permute-start(f32[1,16,64,128]{3,2,1,0:T(8,128)S(1)} %bitcast_add_fusion.1), channel_id=1, source_target_pairs={{0,1},{1,2},{2,3},{4,5},{5,6},{6,7},{8,9},{9,10},{10,11},{12,13},{... | collective-permute-start | bytes 1572872 | tf_op jit(solution)/shard_map/ppermute | solution.py:12
  52.4 4.0 %copy-start.4 = (bf16[1,256,512]{2,1,0:T(8,128)(2,1)S(1)}, bf16[1,256,512]{2,1,0:T(8,128)(2,1)}, u32[]{:S(2)}) copy-start(bf16[1,256,512]{2,1,0:T(8,128)(2,1)} %param.17) | copy-start | bytes 786436
  56.4 2.3 %copy-start.11 = (f32[1024]{0:T(1024)S(1)}, f32[1024]{0:T(1024)}, u32[]{:S(2)}) copy-start(f32[1024]{0:T(1024)} %param.26) | copy-start | bytes 12292
  59.2 5.8 %copy-start.1 = (bf16[1,256,512]{2,1,0:T(8,128)(2,1)}, bf16[1,256,512]{2,1,0:T(8,128)(2,1)S(1)}, u32[]{:S(2)}) copy-start(bf16[1,256,512]{2,1,0:T(8,128)(2,1)S(1)} %fusion.12) | copy-start | bytes 786436
  65.0 3.8 %copy-start.6 = (bf16[512,512]{1,0:T(8,128)(2,1)S(1)}, bf16[512,512]{1,0:T(8,128)(2,1)}, u32[]{:S(2)}) copy-start(bf16[512,512]{1,0:T(8,128)(2,1)} %gather_fusion) | copy-start | bytes 1572868
  65.0 3.8 %copy-start.15 = (bf16[1,512,512]{2,1,0:T(8,128)(2,1)S(1)}, bf16[1,512,512]{2,1,0:T(8,128)(2,1)}, u32[]{:S(2)}) copy-start(bf16[1,512,512]{2,1,0:T(8,128)(2,1)} %param.31) | copy-start | bytes 1572868
  71.8 79.7 %copy-start.18 = (u32[32]{0:T(128)S(1)}, u32[32]{0:T(128)}, u32[]{:S(2)}) copy-start(u32[32]{0:T(128)} %constant.78) | copy-start | bytes 388
  71.8 79.6 %all-reduce.3.cloned.1.call-start = ((), (), s32[]{:S(2)}) async-start(), calls=%async_computation.2 | async-start | bytes 1048576 | tf_op jit(solution)/shard_map/psum | solution.py:180
  110.6 64.9 %all-gather.3.cloned.1.call-start = ((), (), s32[]{:S(2)}) async-start(), calls=%async_computation.3 | async-start | bytes 2621440 | tf_op jit(solution)/shard_map/all_gather | solution.py:184
  (2 other events, 3.5 us)
Sparse Core Ops, SparseCore 0:
  72.0 38.5 reduce-scatter.1
  112.9 38.4 all-reduce.2
  153.0 22.3 all-gather.2
where the time goes:
time: 187 us; the launch traced here: 186 us
  waiting for transfers between devices  80.8 us (43%)
  blocking collectives  21.3 us (11%)
  local copies, waits for them, and re-layouts  19.2 us (10%)
  starting transfers between devices  18.7 us (10%)
  matrix products  17.8 us (10%)
  between operations  15.4 us (8%)
  other arithmetic  12.8 us (7%)
    psum x1, waiting for transfers between devices, body(): lax.psum(share_first.astype(jnp.bfloat16), 'user').astype(jnp.float32)  40.8 us
    reduce_scatter x1, waiting for transfers between devices, body(): lax.psum_scatter(grad_one.astype(jnp.bfloat16), 'tm', scatter_dimension=0...  38.7 us
    ppermute x4, starting transfers between devices, passed_along(): return lax.ppermute(shard, axis, pairs)  18.6 us
    psum x1, blocking collectives, body(): lax.psum(share_second.astype(jnp.bfloat16), 'user').astype(jnp.float32)  10.6 us
    gather x2, local copies, waits for them, and re-layouts, body(): table[indices]  5.84 us
    unnamed x1, blocking collectives  5.65 us
    all_gather x1, blocking collectives, body(): lax.all_gather(summed_second.astype(jnp.bfloat16), 'tm', axis=0, tiled=True)  5.13 us
    convert_element_type x1, other arithmetic, body(): lax.all_gather(summed_first.astype(jnp.bfloat16), 'tm', axis=0, tiled=True)  4.07 us
  transfers between devices with their start and end apart: 7, of which 4 were waited for; matrix products, arithmetic and copies ran while one was open for 9% of the time, Pallas kernels for 0%

commit v1 on v0

v1 whole, which is shorter than its diff:
```python
import functools

import jax
import jax.numpy as jnp
from jax import lax
from jax.experimental import pallas as pl
from jax.experimental.pallas import tpu as pltpu
from jax.sharding import PartitionSpec as P

F32 = jnp.float32
BF16 = jnp.bfloat16
LANES = 128
ALIGN = 16
VMEM = pl.BlockSpec(memory_space=pltpu.VMEM)
SMEM = pl.BlockSpec(memory_space=pltpu.SMEM)
LIMIT = 56 * 1024 * 1024


def dot(a, b):
    return jnp.dot(a, b, preferred_element_type=F32)


def dot_nt(a, b):
    return lax.dot_general(a, b, (((1,), (1,)), ((), ())), preferred_element_type=F32)


def dot_tn(a, b):
    return lax.dot_general(a, b, (((0,), (0,)), ((), ())), preferred_element_type=F32)


def split3(v):
    high = v.astype(BF16)
    rest = v - high.astype(F32)
    mid = rest.astype(BF16)
    low = (rest - mid.astype(F32)).astype(BF16)
    return high, mid, low


def spread(cols, first_head, head_size, rows):
    lane = lax.broadcasted_iota(jnp.int32, (rows, LANES), 1)
    out = jnp.broadcast_to(cols[:, first_head : first_head + 1], (rows, LANES))
    for k in range(1, LANES // head_size):
        nxt = cols[:, first_head + k : first_head + k + 1]
        out = jnp.where(lane >= k * head_size, nxt, out)
    return out


def scan_kernel(
    heads, halo, hist, w, dtw, dtb, alog, cw, cb, xbc, dt_o, cum_o, dt_t, cum_t, pay, raw, carried
):
    length = hist.shape[0]
    edge = halo.shape[0]
    taps = cw.shape[0]
    width = xbc.shape[1]
    inner = carried.shape[1]
    state = (width - inner) // 2
    head_size = inner // heads
    per = LANES // head_size
    rows = jnp.concatenate([halo[...], hist[...]], axis=0)

    v = dot_nt(hist[...], dtw[...]) + dtb[...]
    dt = jnp.maximum(v, 0.0) + jnp.log1p(jnp.exp(-jnp.abs(v)))
    decay = -jnp.exp(alog[...]) * dt
    ri = lax.broadcasted_iota(jnp.int32, (length, length), 0)
    ci = lax.broadcasted_iota(jnp.int32, (length, length), 1)
    tri = jnp.where(ci <= ri, 1.0, 0.0).astype(BF16)
    parts = split3(decay)
    cum = dot(tri, parts[0]) + (dot(tri, parts[1]) + dot(tri, parts[2]))
    dt_o[...] = dt
    cum_o[...] = cum
    dt_t[...] = dt.T
    cum_t[...] = cum.T
    last = cum[length - 1 : length, :]
    weight = jnp.exp(last - cum) * dt

    step = 2 * LANES
    for start in list(range(inner, width, step)) + list(range(0, inner, step)):
        cols = slice(start, start + step)
        piece = dot(rows, w[:, cols]).astype(BF16).astype(F32)
        raw[:, cols] = piece
        acc = jnp.broadcast_to(cb[:, cols], (length, step))
        for k in range(taps):
            acc = acc + cw[k : k + 1, cols] * raw[pl.ds(edge - (taps - 1) + k, length), cols]
        xbc[:, cols] = (acc / (1.0 + jnp.exp(-acc))).astype(BF16)
    for start in range(0, inner, LANES):
        cols = slice(start, start + LANES)
        x = xbc[:, cols].astype(F32)
        carried[:, cols] = (
            spread(weight, start // LANES * per, head_size, length) * x
        ).astype(BF16)
    b = xbc[:, inner : inner + state]
    pay[:state, :] = dot_tn(b, carried[...]).astype(BF16)
    gain = jnp.broadcast_to(jnp.exp(last), (ALIGN, heads))
    pick = lax.broadcasted_iota(jnp.int32, (ALIGN, LANES), 0)
    for start in range(0, inner, LANES):
        g = spread(gain, start // LANES * per, head_size, ALIGN)
        high = g.astype(BF16).astype(F32)
        pay[state:, start : start + LANES] = jnp.where(
            pick == 0, high, jnp.where(pick == 1, g - high, 0.0)
        ).astype(BF16)


def gain_row(pay, state):
    tail = pay[state:, :].astype(F32)
    return tail[0:1, :] + tail[1:2, :]


def chip_kernel(where_am_i, mine, other, out, gain_out):
    state = out.shape[0]
    odd = where_am_i[0] == 1
    m = mine[:state, :].astype(F32)
    o = other[:state, :].astype(F32)
    gm = gain_row(mine, state)
    go = gain_row(other, state)
    out[...] = jnp.where(odd, o * gm + m, m * go + o).astype(BF16)
    gain_out[...] = jnp.broadcast_to(gm * go, gain_out.shape)


def within_kernel(heads, d_skip, hist, zw, xbc, cum, dt_t, cum_t, item, first_low, part, gate, pre):
    length = hist.shape[0]
    inner = zw.shape[1]
    state = (xbc.shape[1] - inner) // 2
    head_size = inner // heads
    per = LANES // head_size
    b = xbc[:, inner : inner + state]
    c = xbc[:, inner + state :]
    scores = dot_nt(c, b)
    half = length // 2
    tops = lax.broadcasted_iota(jnp.int32, (half, half), 0)
    lefts = lax.broadcasted_iota(jnp.int32, (half, half), 1)
    low_tri = lefts <= tops
    lane = lax.broadcasted_iota(jnp.int32, (length, LANES), 1)
    for start in range(0, inner, LANES):
        cols = slice(start, start + LANES)
        x = xbc[:, cols]
        out = None
        for k in range(per):
            h = start // LANES * per + k
            row = cum_t[h : h + 1, :]
            col = cum[:, h : h + 1]
            dts = dt_t[h : h + 1, :]

            def block(r, s, masked):
                gap = col[r : r + half] - row[:, s : s + half]
                if masked:
                    gap = jnp.where(low_tri, gap, 0.0)
                d = jnp.exp(gap)
                if masked:
                    d = jnp.where(low_tri, d, 0.0)
                return (d * dts[:, s : s + half] * scores[r : r + half, s : s + half]).astype(BF16)

            upper = dot(block(0, 0, True), x[:half])
            lower = dot(block(half, 0, False), x[:half]) + dot(block(half, half, True), x[half:])
            got = jnp.concatenate([upper, lower], axis=0)
            skip = d_skip[h]
            got = got + skip * x.astype(F32)
            out = got if out is None else jnp.where(lane >= k * head_size, got, out)
        part[:, cols] = out
    step = 2 * LANES
    for start in range(0, inner, step):
        cols = slice(start, start + step)
        z = dot(hist[...], zw[:, cols]).astype(BF16).astype(F32)
        gate[:, cols] = z / (1.0 + jnp.exp(-z))
    for start in range(0, pre.shape[1], step):
        cols = slice(start, start + step)
        pre[:, cols] = dot(item[...], first_low[:, cols])


def rank_kernel(
    heads,
    where_am_i,
    count,
    incoming,
    other,
    xbc,
    cum,
    part,
    gate,
    gain,
    ow,
    pos,
    value,
    item,
    pre,
    first_high,
    second,
    enc_o,
    logit_o,
    send_o,
    keep_o,
    gated_s,
    rank_s,
    slope_s,
    hid_s,
    gp_s,
):
    length, inner = part.shape
    state = incoming.shape[0]
    head_size = inner // heads
    per = LANES // head_size
    slots = pos.shape[1]
    odd = where_am_i[0] == 1
    base = where_am_i[1]
    arrived = incoming[...].astype(F32)
    enter = jnp.where(
        odd, arrived * gain_row(other, state) + other[:state, :].astype(F32), arrived
    )
    high = enter.astype(BF16)
    low = (enter - high.astype(F32)).astype(BF16)
    c = xbc[:, inner + state :]
    grow = jnp.exp(cum[...])
    total = jnp.zeros((length, LANES), F32)
    for start in range(0, inner, LANES):
        cols = slice(start, start + LANES)
        read = dot(c, high[:, cols]) + dot(c, low[:, cols])
        y = part[:, cols] + spread(grow, start // LANES * per, head_size, length) * read
        y = y * gate[:, cols]
        gated_s[:, cols] = y
        total = total + y * y
    mean = jnp.sum(total, axis=1, keepdims=True) * (1.0 / inner)
    scale = lax.rsqrt(mean + 1e-05)
    normed = (gated_s[...] * scale * gain[...]).astype(BF16)
    enc = dot(normed, ow[...]).astype(BF16)
    enc_o[...] = enc
    width = enc.shape[1]
    place = pos[...] - base
    hot = (lax.broadcasted_iota(jnp.int32, (length, slots), 0) == place).astype(F32).astype(BF16)
    rank_s[...] = dot_tn(hot, enc).astype(BF16)

    hidden_width = pre.shape[1]
    step = 2 * LANES
    logit = jnp.zeros((slots, LANES), F32)
    for start in range(0, hidden_width, step):
        cols = slice(start, start + step)
        v = pre[:, cols] + dot(rank_s[...], first_high[:, cols])
        sig = 1.0 / (1.0 + jnp.exp(-v))
        hid = (v * sig).astype(BF16)
        hid_s[:, cols] = hid
        w2 = second[:, cols].astype(F32)
        prod = hid.astype(F32) * w2
        for k in range(0, step, LANES):
            logit = logit + prod[:, k : k + LANES]
        slope_s[:, cols] = w2 * (sig * (1.0 + v * (1.0 - sig)))
    ones = jnp.ones((8, LANES), BF16)
    p = split3(logit)
    logit8 = dot_nt(ones, p[0]) + (dot_nt(ones, p[1]) + dot_nt(ones, p[2]))
    slot = lax.broadcasted_iota(jnp.int32, (8, slots), 1)
    live = jnp.where(slot < count[0, 0], 1.0, 0.0)
    logit_o[...] = (live * logit8)[0:1, :]
    target = value[...].astype(F32)
    dl = live * (1.0 / (1.0 + jnp.exp(-logit8)) - target)
    d0, d1, d2 = split3(dl)
    which = lax.broadcasted_iota(jnp.int32, (8, slots), 0)
    dl3 = jnp.where(
        which == 0,
        d0.astype(F32),
        jnp.where(which == 1, d1.astype(F32), jnp.where(which == 2, d2.astype(F32), 0.0)),
    ).astype(BF16)
    grad2 = jnp.sum(dot(dl3, hid_s[...]), axis=0, keepdims=True)
    dcol = dot_tn(dl3, jnp.ones((8, LANES), BF16))
    for start in range(0, hidden_width, LANES):
        cols = slice(start, start + LANES)
        gp_s[:, cols] = (dcol * slope_s[:, cols]).astype(BF16)
    rows = width
    pick = lax.broadcasted_iota(jnp.int32, (8, hidden_width), 0)
    extra = jnp.where(pick == 0, grad2, 0.0).astype(BF16)
    away = jnp.where(odd, rank_s[...], item[...])
    home = jnp.where(odd, item[...], rank_s[...])
    send_o[:rows, :] = dot_tn(away, gp_s[...]).astype(BF16)
    send_o[rows:, :] = extra
    keep_o[:rows, :] = dot_tn(home, gp_s[...]).astype(BF16)
    keep_o[rows:, :] = extra


def call(kernel, out_shape, in_specs, scratch, args, flops, moved):
    return pl.pallas_call(
        kernel,
        out_shape=out_shape,
        in_specs=in_specs,
        out_specs=jax.tree.map(lambda _: VMEM, out_shape),
        scratch_shapes=scratch,
        compiler_params=pltpu.CompilerParams(vmem_limit_bytes=LIMIT),
        cost_estimate=pl.CostEstimate(flops=flops, bytes_accessed=moved, transcendentals=0),
    )(*args)


def shape(dims, dtype):
    return jax.ShapeDtypeStruct(dims, dtype)


def bits_of(n):
    return max(n.bit_length() - 1, 0)


def body(
    history,
    z_weight,
    xbc_weight,
    dt_weight,
    dt_bias,
    a_log,
    conv_weight,
    conv_bias,
    d_skip,
    norm_gain,
    out_weight,
    label_pos,
    label_count,
    label_value,
    item_feat,
    first_weight,
    second_weight,
):
    hist = history[0]
    item = item_feat[0]
    length, width = hist.shape
    inner = z_weight.shape[1]
    heads = a_log.shape[0]
    channels = xbc_weight.shape[1]
    state = (channels - inner) // 2
    slots = label_pos.shape[1]
    hidden = first_weight.shape[1]
    n_tm = lax.axis_size("tm")
    n_user = lax.axis_size("user")
    chips = n_tm // 2
    tm = lax.axis_index("tm")
    user = lax.axis_index("user")
    odd = tm % 2
    where_am_i = jnp.stack([odd, tm * length]).astype(jnp.int32)

    halo = lax.ppermute(hist[length - ALIGN :], "tm", [(i, i + 1) for i in range(n_tm - 1)])
    xbc, dt, cum, dt_t, cum_t, pay = call(
        functools.partial(scan_kernel, heads),
        (
            shape((length, channels), BF16),
            shape((length, heads), F32),
            shape((length, heads), F32),
            shape((heads, length), F32),
            shape((heads, length), F32),
            shape((state + ALIGN, inner), BF16),
        ),
        [VMEM] * 8,
        [pltpu.VMEM((length + ALIGN, channels), F32), pltpu.VMEM((length, inner), BF16)],
        (
            halo,
            hist,
            xbc_weight,
            dt_weight.T,
            dt_bias.reshape(1, heads),
            a_log.reshape(1, heads),
            conv_weight,
            conv_bias.reshape(1, channels),
        ),
        2 * length * width * channels,
        4 * width * channels,
    )
    other = lax.ppermute(pay, "tm", [(i, i ^ 1) for i in range(n_tm)])
    chip_state, chip_gain = call(
        chip_kernel,
        (shape((state, inner), BF16), shape((8, inner), F32)),
        [SMEM, VMEM, VMEM],
        [],
        (where_am_i, pay, other),
        state * inner,
        6 * state * inner,
    )
    onward = [(i, i + 2) for i in range(n_tm - 2)]
    incoming = lax.ppermute(chip_state, "tm", onward)
    for _ in range(chips - 2):
        passed = chip_gain[0:1] * incoming.astype(F32) + chip_state.astype(F32)
        incoming = lax.ppermute(passed.astype(BF16), "tm", onward)
    part, gate, pre = call(
        functools.partial(within_kernel, heads),
        (
            shape((length, inner), F32),
            shape((length, inner), F32),
            shape((slots, hidden), F32),
        ),
        [SMEM] + [VMEM] * 8,
        [],
        (d_skip, hist, z_weight, xbc, cum, dt_t, cum_t, item, first_weight[width:]),
        2 * length * width * inner + 2 * slots * width * hidden + 4 * length * length * inner,
        16 * length * inner * 4,
    )
    enc, row_logit, send, keep = call(
        functools.partial(rank_kernel, heads),
        (
            shape((length, width), BF16),
            shape((1, slots), F32),
            shape((width + 8, hidden), BF16),
            shape((width + 8, hidden), BF16),
        ),
        [SMEM, SMEM] + [VMEM] * 14,
        [
            pltpu.VMEM((length, inner), F32),
            pltpu.VMEM((slots, width), BF16),
            pltpu.VMEM((slots, hidden), F32),
            pltpu.VMEM((slots, hidden), BF16),
            pltpu.VMEM((slots, hidden), BF16),
        ],
        (
            where_am_i,
            label_count,
            incoming,
            other,
            xbc,
            cum,
            part,
            gate,
            norm_gain.reshape(1, inner),
            out_weight,
            label_pos,
            label_value,
            item,
            pre,
            first_weight[:width],
            second_weight.reshape(1, hidden),
        ),
        4 * slots * width * hidden,
        8 * slots * hidden,
    )
    grad_first, grad_second = total_sum(send, keep, n_user, n_tm, user, tm)
    return (enc[None], row_logit, grad_first, grad_second)


def total_sum(send, keep, n_user, n_tm, user, tm):
    rows = keep.shape[0] - 8
    odd = tm % 2
    axes = ("user", "tm")
    every = [(u, t) for u in range(n_user) for t in range(n_tm)]

    def swap(value, partner):
        pairs = [(u * n_tm + t, partner(u, t)) for u, t in every]
        return lax.ppermute(value, axes, pairs)

    chip_bits = [("tm", k) for k in range(bits_of(n_tm // 2))]
    user_bits = [("user", k) for k in range(bits_of(n_user))]
    order_even = chip_bits + user_bits
    order_odd = user_bits + chip_bits

    def partner_of(level):
        def partner(u, t):
            axis, k = (order_even if t % 2 == 0 else order_odd)[level]
            if axis == "tm":
                return u * n_tm + (t ^ (2 << k))
            return (u ^ (1 << k)) * n_tm + t

        return partner

    def bit_of(level):
        def one(entry):
            axis, k = entry
            return (tm >> (k + 1)) & 1 if axis == "tm" else (user >> k) & 1

        return jnp.where(odd == 0, one(order_even[level]), one(order_odd[level])) == 1

    got = swap(send, lambda u, t: u * n_tm + (t ^ 1))
    levels = len(order_even)
    size = rows
    extra_a, extra_b = keep[rows:].astype(F32), got[rows:].astype(F32)
    main_a, main_b = keep[:rows], got[:rows]
    extra = (extra_a + extra_b).astype(BF16)
    for level in range(levels):
        size //= 2
        bit = bit_of(level)
        low = main_a[:size].astype(F32) + main_b[:size].astype(F32)
        high = main_a[size:].astype(F32) + main_b[size:].astype(F32)
        leave = jnp.where(bit, low, high).astype(BF16)
        main_a = jnp.where(bit, high, low).astype(BF16)
        got = swap(jnp.concatenate([leave, extra], axis=0), partner_of(level))
        main_b = got[:size]
        extra = (extra.astype(F32) + got[size:].astype(F32)).astype(BF16)
    whole = (main_a.astype(F32) + main_b.astype(F32)).astype(BF16)
    for level in reversed(range(levels)):
        got = swap(whole, partner_of(level))
        bit = bit_of(level)
        whole = jnp.concatenate([jnp.where(bit, got, whole), jnp.where(bit, whole, got)], axis=0)
    got = swap(jnp.concatenate([whole, extra], axis=0), lambda u, t: u * n_tm + (t ^ 1))
    bit = odd == 1
    grad_second = jnp.where(bit, got[rows:], extra)[0].astype(F32)
    got = got[:rows]
    grad_first = jnp.concatenate(
        [jnp.where(bit, got, whole), jnp.where(bit, whole, got)], axis=0
    ).astype(F32)
    return grad_first, grad_second


def solution(mesh):
    in_specs = (
        P(("grp", "user"), "tm", None),
        P(),
        P(),
        P(),
        P(),
        P(),
        P(),
        P(),
        P(),
        P(),
        P(),
        P(("grp", "user"), "tm"),
        P(("grp", "user"), "tm"),
        P(("grp", "user"), "tm"),
        P(("grp", "user"), "tm", None),
        P(),
        P(),
    )
    out_specs = (P(("grp", "user"), "tm", None), P(("grp", "user"), "tm"), P("grp", None), P("grp"))
    return jax.shard_map(body, mesh=mesh, in_specs=in_specs, out_specs=out_specs, check_vma=False)
```

time: 187 us -> 105 us (0.56)
  waiting for transfers between devices: 80.8 us -> 39.8 us
  Pallas kernels: 0 us -> 21.6 us
  blocking collectives: 21.3 us -> 0 us
  matrix products: 17.8 us -> 0 us
  between operations: 15.4 us -> 1.45 us
  local copies, waits for them, and re-layouts: 19.2 us -> 6.99 us
  starting transfers between devices: 18.7 us -> 26.5 us
  other arithmetic: 12.8 us -> 7.55 us
    psum x1 -> x0, waiting for transfers between devices: 40.8 us -> none  [body(): lax.psum(share_first.astype(jnp.bfloat16), 'user').astype(jnp.float32)]
    ppermute x4 -> x11, waiting for transfers between devices: 1.02 us -> 39.8 us  [the longest x8 39.8 us: swap(): return lax.ppermute(value, axes, pairs)]
    reduce_scatter x1 -> x0, waiting for transfers between devices: 38.7 us -> none  [body(): lax.psum_scatter(grad_one.astype(jnp.bfloat16), 'tm', scatter_dimension=0...]
    pallas_call x0 -> x4, Pallas kernels: none -> 21.6 us  [call(): pl.pallas_call(kernel, out_shape=out_shape, in_specs=in_specs, out_specs=...]
    dot_general x13 -> x0, matrix products: 17.8 us -> none  [the longest x1 3.01 us: ranker(): jnp.dot(rank_rows.T, grad_pre, preferred_element_type=jnp.float32)]
    psum x1 -> x0, blocking collectives: 10.6 us -> none  [body(): lax.psum(share_second.astype(jnp.bfloat16), 'user').astype(jnp.float32)]
    ppermute x4 -> x11, starting transfers between devices: 18.6 us -> 26.5 us  [the longest x8 17.7 us: swap(): return lax.ppermute(value, axes, pairs)]
    gather x2 -> x0, local copies, waits for them, and re-layouts: 5.84 us -> none  [body(): table[indices]]
  transfers between devices with their start and end apart: 7 -> 11, of which waited for: 4 -> 8; matrix products, arithmetic and copies ran while one was open for 9% -> 5% of each run, Pallas kernels for 0% -> 5%
where the time goes in v1:
time: 105 us; the launch traced here: 104 us
  waiting for transfers between devices  39.8 us (38%)
  starting transfers between devices  26.5 us (25%)
  Pallas kernels  21.6 us (21%)
  other arithmetic  7.55 us (7%)
  local copies, waits for them, and re-layouts  6.99 us (7%)
  between operations  1.45 us (1%)
    ppermute x8, waiting for transfers between devices, swap(): return lax.ppermute(value, axes, pairs)  39.8 us
    pallas_call x4, Pallas kernels, call(): pl.pallas_call(kernel, out_shape=out_shape, in_specs=in_specs, out_specs=...  21.6 us
    ppermute x8, starting transfers between devices, swap(): return lax.ppermute(value, axes, pairs)  17.7 us
    ppermute x1, starting transfers between devices, body(): incoming = lax.ppermute(chip_state, 'tm', onward)  3.82 us
    ppermute x1, starting transfers between devices, body(): other = lax.ppermute(pay, 'tm', [(i, i ^ 1) for i in range(n_tm)])  2.59 us
    convert_element_type x1, other arithmetic, total_sum(): grad_first = jnp.concatenate([jnp.where(bit, got, whole), jnp.where(bit,...  2.45 us
    ppermute x1, starting transfers between devices, body(): lax.ppermute(hist[length - ALIGN:], 'tm', [(i, i + 1) for i in range(n_tm...  2.39 us
  transfers between devices with their start and end apart: 11, of which 8 were waited for; matrix products, arithmetic and copies ran while one was open for 5% of the time, Pallas kernels for 5%

profile of v1, /device:TPU:0, one launch (start us, length us, event | category | flops | bytes accessed | tf_op | source)
XLA Modules:
  0.0 103.9 jit_solution(13128045221864672690)
XLA Ops:
  1.5 2.4 %collective-permute-start = (bf16[16,512]{1,0:T(8,128)(2,1)S(1)}, bf16[16,512]{1,0:T(8,128)(2,1)S(1)}, u32[]{:S(2)}, u32[]{:S(2)}) collective-permute-start(bf16[16,512]{1,0:T(8,128)(2,1)S(1)} %slice_bitcast_fusion), channel_id=1, source_target_pairs={{0,1},{1,2},{2,3},{4,5},{5,6},{6,7},{8,9},{9,10},{10,11},{12,13},{... | collective-permute-start | bytes 49160 | tf_op jit(solution)/shard_map/ppermute | solution.py:331
  5.8 4.7 %shard_map.192 = (bf16[256,1280]{1,0:T(8,128)(2,1)}, f32[256,16]{1,0:T(8,128)}, f32[256,16]{1,0:T(8,128)}, f32[16,256]{1,0:T(8,128)}, f32[16,256]{1,0:T(8,128)}, /*index=5*/bf16[144,1024]{1,0:T(8,128)(2,1)}) custom-call(bf16[16,512]{1,0:T(8,128)(2,1)} %copy-done.3, bf16[256,512]{1,0:T(8,128)(2,1)} %bitcast.14, bf16[512,1280]{1,0:T(8,128)(2,1)} %w.1, ...), custom_call_target="tpu_custom_call" | custom-call | flops 335544320 | bytes 2621440 | tf_op jit(solution)/shard_map/pallas_call | solution.py:276
  10.5 2.6 %collective-permute-start.1 = (bf16[144,1024]{1,0:T(8,128)(2,1)}, bf16[144,1024]{1,0:T(8,128)(2,1)S(1)}, u32[]{:S(2)}, u32[]{:S(2)}) collective-permute-start(bf16[144,1024]{1,0:T(8,128)(2,1)} %get-tuple-element.17.mine), channel_id=1, source_target_pairs={{0,1},{1,0},{2,3},{3,2},{4,5},{5,4},{6,7},{7,6},{8,9},{9,8},{10,11... | collective-permute-start | bytes 884744 | tf_op jit(solution)/shard_map/ppermute | solution.py:357
  16.4 1.9 %shard_map.193 = (bf16[128,1024]{1,0:T(8,128)(2,1)}, f32[8,1024]{1,0:T(8,128)}) custom-call(s32[2]{0:T(128)} %pad_add_fusion.where_am_i, bf16[144,1024]{1,0:T(8,128)(2,1)} %get-tuple-element.17.mine, bf16[144,1024]{1,0:T(8,128)(2,1)} %copy-done.1), custom_call_target="tpu_custom_call" | custom-call | flops 131072 | bytes 786432 | tf_op jit(solution)/shard_map/pallas_call | solution.py:276
  18.3 3.8 %collective-permute-start.2 = (bf16[128,1024]{1,0:T(8,128)(2,1)}, bf16[128,1024]{1,0:T(8,128)(2,1)S(1)}, u32[]{:S(2)}, u32[]{:S(2)}) collective-permute-start(bf16[128,1024]{1,0:T(8,128)(2,1)} %get-tuple-element.18), channel_id=1, source_target_pairs={{0,2},{1,3},{4,6},{5,7},{8,10},{9,11},{12,14},{13,15},{16,18},{17,... | collective-permute-start | bytes 786440 | tf_op jit(solution)/shard_map/ppermute | solution.py:368
  22.2 1.5 %fusion.1 = (bf16[512,1024]{1,0:T(8,128)(2,1)}, bf16[512,1024]{1,0:T(8,128)(2,1)}) fusion(bf16[1024,1024]{1,0:T(8,128)(2,1)S(1)} %copy-done), kind=kLoop, calls=%fused_computation.37 | loop fusion | bytes 4194304 | tf_op jit(solution)/shard_map/slice | solution.py:416
  23.7 5.5 %shard_map.194 = (f32[256,1024]{1,0:T(8,128)}, f32[256,1024]{1,0:T(8,128)}, f32[512,1024]{1,0:T(8,128)}) custom-call(f32[16]{0:T(128)} %d_skip.1, bf16[256,512]{1,0:T(8,128)(2,1)} %bitcast.15, bf16[512,1024]{1,0:T(8,128)(2,1)} %zw.1, bf16[256,1280]{1,0:T(8,128)(2,1)} %get-tuple-element.19.xbc, f32[256,16]{1,0:T(8,128)} %get-tuple-element.20.cum, ...), custom_call_target="tpu_custom_call" | custom-call | flops 1073741824 | bytes 16777216 | tf_op jit(solution)/shard_map/pallas_call | solution.py:276
  29.9 9.5 %shard_map.195 = (bf16[256,512]{1,0:T(8,128)(2,1)}, f32[1,512]{1,0:T(1,128)}, bf16[520,1024]{1,0:T(8,128)(2,1)}, bf16[520,1024]{1,0:T(8,128)(2,1)}) custom-call(s32[2]{0:T(128)} %pad_add_fusion.where_am_i, s32[1,1]{1,0:T(1,128)S(6)} %copy.21.count, bf16[128,1024]{1,0:T(8,128)(2,1)} %copy-done.2, bf16[144,1024]{1,0:T(8,128)(2,1)} %copy-done.1, ...), custom_call_target="tpu_custom_call" | custom-call | flops 1073741824 | bytes 4194304 | tf_op jit(solution)/shard_map/pallas_call | solution.py:276
  39.6 2.7 %collective-permute-done.3 = bf16[520,1024]{1,0:T(8,128)(2,1)S(1)} collective-permute-done((bf16[520,1024]{1,0:T(8,128)(2,1)}, bf16[520,1024]{1,0:T(8,128)(2,1)S(1)}, u32[]{:S(2)}, u32[]{:S(2)}) %collective-permute-start.3) | collective-permute-done | bytes 1064992 | tf_op jit(solution)/shard_map/ppermute | solution.py:434
  43.0 1.6 %select_convert_fusion.1 = (bf16[256,1024]{1,0:T(8,128)(2,1)S(1)}, bf16[256,1024]{1,0:T(8,128)(2,1)S(1)}) fusion(pred[]{:T(512)S(6)} %eq.28, bf16[520,1024]{1,0:T(8,128)(2,1)S(1)} %collective-permute-done.3, bf16[520,1024]{1,0:T(8,128)(2,1)} %get-tuple-element.28), kind=kLoop, calls=%fused_computation.4 | loop fusion | flops 2621440 | bytes 3145729 | tf_op jit(solution)/shard_map/convert_element_type | solution.py:469
  44.7 1.8 %collective-permute-start.4 = (bf16[264,1024]{1,0:T(8,128)(2,1)S(1)}, bf16[264,1024]{1,0:T(8,128)(2,1)S(1)}, u32[]{:S(2)}, u32[]{:S(2)}) collective-permute-start(bf16[264,1024]{1,0:T(8,128)(2,1)S(1)} %pad_maximum_fusion.2), channel_id=1, source_target_pairs={{0,2},{1,5},{2,0},{3,7},{4,6},{5,1},{6,4},{7,3},{8,10},{9,13},{10,... | collective-permute-start | bytes 1622024 | tf_op jit(solution)/shard_map/ppermute | solution.py:434
  46.5 7.6 %collective-permute-done.4 = bf16[264,1024]{1,0:T(8,128)(2,1)S(1)} collective-permute-done((bf16[264,1024]{1,0:T(8,128)(2,1)S(1)}, bf16[264,1024]{1,0:T(8,128)(2,1)S(1)}, u32[]{:S(2)}, u32[]{:S(2)}) %collective-permute-start.4) | collective-permute-done | bytes 540704 | tf_op jit(solution)/shard_map/ppermute | solution.py:434
  54.3 1.6 %collective-permute-start.5 = (bf16[136,1024]{1,0:T(8,128)(2,1)S(1)}, bf16[136,1024]{1,0:T(8,128)(2,1)S(1)}, u32[]{:S(2)}, u32[]{:S(2)}) collective-permute-start(bf16[136,1024]{1,0:T(8,128)(2,1)S(1)} %pad_maximum_fusion.4), channel_id=1, source_target_pairs={{0,4},{1,9},{2,6},{3,11},{4,0},{5,13},{6,2},{7,15},{8,12},{9,1},{1... | collective-permute-start | bytes 835592 | tf_op jit(solution)/shard_map/ppermute | solution.py:434
  56.0 6.6 %collective-permute-done.5 = bf16[136,1024]{1,0:T(8,128)(2,1)S(1)} collective-permute-done((bf16[136,1024]{1,0:T(8,128)(2,1)S(1)}, bf16[136,1024]{1,0:T(8,128)(2,1)S(1)}, u32[]{:S(2)}, u32[]{:S(2)}) %collective-permute-start.5) | collective-permute-done | bytes 278560 | tf_op jit(solution)/shard_map/ppermute | solution.py:434
  62.7 3.0 %collective-permute-start.6 = (bf16[72,1024]{1,0:T(8,128)(2,1)S(1)}, bf16[72,1024]{1,0:T(8,128)(2,1)S(1)}, u32[]{:S(2)}, u32[]{:S(2)}) collective-permute-start(bf16[72,1024]{1,0:T(8,128)(2,1)S(1)} %pad_maximum_fusion.6), channel_id=1, source_target_pairs={{0,8},{1,3},{2,10},{3,1},{4,12},{5,7},{6,14},{7,5},{8,0},{9,11},{1... | collective-permute-start | bytes 442376 | tf_op jit(solution)/shard_map/ppermute | solution.py:434
  65.7 3.1 %collective-permute-done.6 = bf16[72,1024]{1,0:T(8,128)(2,1)S(1)} collective-permute-done((bf16[72,1024]{1,0:T(8,128)(2,1)S(1)}, bf16[72,1024]{1,0:T(8,128)(2,1)S(1)}, u32[]{:S(2)}, u32[]{:S(2)}) %collective-permute-start.6) | collective-permute-done | bytes 147488 | tf_op jit(solution)/shard_map/ppermute | solution.py:434
  68.9 3.0 %collective-permute-start.7 = (bf16[64,1024]{1,0:T(8,128)(2,1)S(1)}, bf16[64,1024]{1,0:T(8,128)(2,1)S(1)}, u32[]{:S(2)}, u32[]{:S(2)}) collective-permute-start(bf16[64,1024]{1,0:T(8,128)(2,1)S(1)} %add_convert_fusion), channel_id=1, source_target_pairs={{0,8},{1,3},{2,10},{3,1},{4,12},{5,7},{6,14},{7,5},{8,0},{9,11},{1... | collective-permute-start | bytes 393224 | tf_op jit(solution)/shard_map/ppermute | solution.py:434
  72.0 3.5 %collective-permute-done.7 = bf16[64,1024]{1,0:T(8,128)(2,1)S(1)} collective-permute-done((bf16[64,1024]{1,0:T(8,128)(2,1)S(1)}, bf16[64,1024]{1,0:T(8,128)(2,1)S(1)}, u32[]{:S(2)}, u32[]{:S(2)}) %collective-permute-start.7) | collective-permute-done | bytes 131104 | tf_op jit(solution)/shard_map/ppermute | solution.py:434
  75.6 6.2 %collective-permute-start.8 = (bf16[128,1024]{1,0:T(8,128)(2,1)S(1)}, bf16[128,1024]{1,0:T(8,128)(2,1)S(1)}, u32[]{:S(2)}, u32[]{:S(2)}) collective-permute-start(bf16[128,1024]{1,0:T(8,128)(2,1)S(1)} %pad_maximum_fusion.5), channel_id=1, source_target_pairs={{0,4},{1,9},{2,6},{3,11},{4,0},{5,13},{6,2},{7,15},{8,12},{9,1},{1... | collective-permute-start | bytes 786440 | tf_op jit(solution)/shard_map/ppermute | solution.py:434
  81.7 6.1 %collective-permute-done.8 = bf16[128,1024]{1,0:T(8,128)(2,1)S(1)} collective-permute-done((bf16[128,1024]{1,0:T(8,128)(2,1)S(1)}, bf16[128,1024]{1,0:T(8,128)(2,1)S(1)}, u32[]{:S(2)}, u32[]{:S(2)}) %collective-permute-start.8) | collective-permute-done | bytes 262176 | tf_op jit(solution)/shard_map/ppermute | solution.py:434
  87.9 1.8 %collective-permute-start.9 = (bf16[256,1024]{1,0:T(8,128)(2,1)S(1)}, bf16[256,1024]{1,0:T(8,128)(2,1)S(1)}, u32[]{:S(2)}, u32[]{:S(2)}) collective-permute-start(bf16[256,1024]{1,0:T(8,128)(2,1)S(1)} %pad_maximum_fusion.3), channel_id=1, source_target_pairs={{0,2},{1,5},{2,0},{3,7},{4,6},{5,1},{6,4},{7,3},{8,10},{9,13},{10,... | collective-permute-start | bytes 1572872 | tf_op jit(solution)/shard_map/ppermute | solution.py:434
  89.7 7.5 %collective-permute-done.9 = bf16[256,1024]{1,0:T(8,128)(2,1)S(1)} collective-permute-done((bf16[256,1024]{1,0:T(8,128)(2,1)S(1)}, bf16[256,1024]{1,0:T(8,128)(2,1)S(1)}, u32[]{:S(2)}, u32[]{:S(2)}) %collective-permute-start.9) | collective-permute-done | bytes 524320 | tf_op jit(solution)/shard_map/ppermute | solution.py:434
  97.6 2.7 %collective-permute-done.10 = bf16[520,1024]{1,0:T(8,128)(2,1)S(1)} collective-permute-done((bf16[520,1024]{1,0:T(8,128)(2,1)S(1)}, bf16[520,1024]{1,0:T(8,128)(2,1)S(1)}, u32[]{:S(2)}, u32[]{:S(2)}) %collective-permute-start.10) | collective-permute-done | bytes 1064992 | tf_op jit(solution)/shard_map/ppermute | solution.py:434
  101.4 2.4 %maximum_convert_fusion = f32[1024,1024]{1,0:T(8,128)} fusion(bf16[512,1024]{1,0:T(8,128)(2,1)S(1)} %get-tuple-element.33, bf16[512,1024]{1,0:T(8,128)(2,1)S(1)} %get-tuple-element.32), kind=kLoop, calls=%fused_computation | loop fusion | flops 4194304 | bytes 6291456 | tf_op jit(solution)/shard_map/convert_element_type | solution.py:484
  (36 shorter events, 9.3 us)
Async XLA Ops:
  0.6 21.5 %copy-start = (bf16[1024,1024]{1,0:T(8,128)(2,1)S(1)}, bf16[1024,1024]{1,0:T(8,128)(2,1)}, u32[]{:S(2)}) copy-start(bf16[1024,1024]{1,0:T(8,128)(2,1)} %param.32) | copy-start | bytes 6291460
  1.5 3.7 %collective-permute-start = (bf16[16,512]{1,0:T(8,128)(2,1)S(1)}, bf16[16,512]{1,0:T(8,128)(2,1)S(1)}, u32[]{:S(2)}, u32[]{:S(2)}) collective-permute-start(bf16[16,512]{1,0:T(8,128)(2,1)S(1)} %slice_bitcast_fusion), channel_id=1, source_target_pairs={{0,1},{1,2},{2,3},{4,5},{5,6},{6,7},{8,9},{9,10},{10,11},{12,13},{... | collective-permute-start | bytes 49160 | tf_op jit(solution)/shard_map/ppermute | solution.py:331
  5.2 0.6 copy-start.3
  10.5 5.2 %collective-permute-start.1 = (bf16[144,1024]{1,0:T(8,128)(2,1)}, bf16[144,1024]{1,0:T(8,128)(2,1)S(1)}, u32[]{:S(2)}, u32[]{:S(2)}) collective-permute-start(bf16[144,1024]{1,0:T(8,128)(2,1)} %get-tuple-element.17.mine), channel_id=1, source_target_pairs={{0,1},{1,0},{2,3},{3,2},{4,5},{5,4},{6,7},{7,6},{8,9},{9,8},{10,11... | collective-permute-start | bytes 884744 | tf_op jit(solution)/shard_map/ppermute | solution.py:357
  15.7 0.7 copy-start.1
  18.3 10.8 %collective-permute-start.2 = (bf16[128,1024]{1,0:T(8,128)(2,1)}, bf16[128,1024]{1,0:T(8,128)(2,1)S(1)}, u32[]{:S(2)}, u32[]{:S(2)}) collective-permute-start(bf16[128,1024]{1,0:T(8,128)(2,1)} %get-tuple-element.18), channel_id=1, source_target_pairs={{0,2},{1,3},{4,6},{5,7},{8,10},{9,11},{12,14},{13,15},{16,18},{17,... | collective-permute-start | bytes 786440 | tf_op jit(solution)/shard_map/ppermute | solution.py:368
  29.1 0.7 copy-start.2
  39.4 2.9 %collective-permute-start.3 = (bf16[520,1024]{1,0:T(8,128)(2,1)}, bf16[520,1024]{1,0:T(8,128)(2,1)S(1)}, u32[]{:S(2)}, u32[]{:S(2)}) collective-permute-start(bf16[520,1024]{1,0:T(8,128)(2,1)} %get-tuple-element.29), channel_id=1, source_target_pairs={{0,1},{1,0},{2,3},{3,2},{4,5},{5,4},{6,7},{7,6},{8,9},{9,8},{10,11... | collective-permute-start | bytes 3194888 | tf_op jit(solution)/shard_map/ppermute | solution.py:434
  44.7 9.4 %collective-permute-start.4 = (bf16[264,1024]{1,0:T(8,128)(2,1)S(1)}, bf16[264,1024]{1,0:T(8,128)(2,1)S(1)}, u32[]{:S(2)}, u32[]{:S(2)}) collective-permute-start(bf16[264,1024]{1,0:T(8,128)(2,1)S(1)} %pad_maximum_fusion.2), channel_id=1, source_target_pairs={{0,2},{1,5},{2,0},{3,7},{4,6},{5,1},{6,4},{7,3},{8,10},{9,13},{10,... | collective-permute-start | bytes 1622024 | tf_op jit(solution)/shard_map/ppermute | solution.py:434
  54.3 8.3 %collective-permute-start.5 = (bf16[136,1024]{1,0:T(8,128)(2,1)S(1)}, bf16[136,1024]{1,0:T(8,128)(2,1)S(1)}, u32[]{:S(2)}, u32[]{:S(2)}) collective-permute-start(bf16[136,1024]{1,0:T(8,128)(2,1)S(1)} %pad_maximum_fusion.4), channel_id=1, source_target_pairs={{0,4},{1,9},{2,6},{3,11},{4,0},{5,13},{6,2},{7,15},{8,12},{9,1},{1... | collective-permute-start | bytes 835592 | tf_op jit(solution)/shard_map/ppermute | solution.py:434
  62.7 6.1 %collective-permute-start.6 = (bf16[72,1024]{1,0:T(8,128)(2,1)S(1)}, bf16[72,1024]{1,0:T(8,128)(2,1)S(1)}, u32[]{:S(2)}, u32[]{:S(2)}) collective-permute-start(bf16[72,1024]{1,0:T(8,128)(2,1)S(1)} %pad_maximum_fusion.6), channel_id=1, source_target_pairs={{0,8},{1,3},{2,10},{3,1},{4,12},{5,7},{6,14},{7,5},{8,0},{9,11},{1... | collective-permute-start | bytes 442376 | tf_op jit(solution)/shard_map/ppermute | solution.py:434
  68.9 6.6 %collective-permute-start.7 = (bf16[64,1024]{1,0:T(8,128)(2,1)S(1)}, bf16[64,1024]{1,0:T(8,128)(2,1)S(1)}, u32[]{:S(2)}, u32[]{:S(2)}) collective-permute-start(bf16[64,1024]{1,0:T(8,128)(2,1)S(1)} %add_convert_fusion), channel_id=1, source_target_pairs={{0,8},{1,3},{2,10},{3,1},{4,12},{5,7},{6,14},{7,5},{8,0},{9,11},{1... | collective-permute-start | bytes 393224 | tf_op jit(solution)/shard_map/ppermute | solution.py:434
  75.6 12.2 %collective-permute-start.8 = (bf16[128,1024]{1,0:T(8,128)(2,1)S(1)}, bf16[128,1024]{1,0:T(8,128)(2,1)S(1)}, u32[]{:S(2)}, u32[]{:S(2)}) collective-permute-start(bf16[128,1024]{1,0:T(8,128)(2,1)S(1)} %pad_maximum_fusion.5), channel_id=1, source_target_pairs={{0,4},{1,9},{2,6},{3,11},{4,0},{5,13},{6,2},{7,15},{8,12},{9,1},{1... | collective-permute-start | bytes 786440 | tf_op jit(solution)/shard_map/ppermute | solution.py:434
  87.9 9.2 %collective-permute-start.9 = (bf16[256,1024]{1,0:T(8,128)(2,1)S(1)}, bf16[256,1024]{1,0:T(8,128)(2,1)S(1)}, u32[]{:S(2)}, u32[]{:S(2)}) collective-permute-start(bf16[256,1024]{1,0:T(8,128)(2,1)S(1)} %pad_maximum_fusion.3), channel_id=1, source_target_pairs={{0,2},{1,5},{2,0},{3,7},{4,6},{5,1},{6,4},{7,3},{8,10},{9,13},{10,... | collective-permute-start | bytes 1572872 | tf_op jit(solution)/shard_map/ppermute | solution.py:434
  97.5 2.7 %collective-permute-start.10 = (bf16[520,1024]{1,0:T(8,128)(2,1)S(1)}, bf16[520,1024]{1,0:T(8,128)(2,1)S(1)}, u32[]{:S(2)}, u32[]{:S(2)}) collective-permute-start(bf16[520,1024]{1,0:T(8,128)(2,1)S(1)} %pad_maximum_fusion), channel_id=1, source_target_pairs={{0,1},{1,0},{2,3},{3,2},{4,5},{5,4},{6,7},{7,6},{8,9},{9,8},{10,11... | collective-permute-start | bytes 3194888 | tf_op jit(solution)/shard_map/ppermute | solution.py:434

commit v2 on v1

--- a/solution.py
+++ b/solution.py
@@ -13,7 +13,7 @@
 ALIGN = 16
 VMEM = pl.BlockSpec(memory_space=pltpu.VMEM)
 SMEM = pl.BlockSpec(memory_space=pltpu.SMEM)
-LIMIT = 56 * 1024 * 1024
+HBM = pl.BlockSpec(memory_space=pltpu.HBM)
 
 
 def dot(a, b):
@@ -46,8 +46,10 @@
 
 
 def scan_kernel(
-    heads, halo, hist, w, dtw, dtb, alog, cw, cb, xbc, dt_o, cum_o, dt_t, cum_t, pay, raw, carried
+    heads, take, halo, xbc, cum_o, dt_t, cum_t, pay, raw, carried
 ):
+    hist = take(0)
+    dtw, dtb, alog, cw, cb = take(1), take(2), take(3), take(4), take(5)
     length = hist.shape[0]
     edge = halo.shape[0]
     taps = cw.shape[0]
@@ -66,7 +68,6 @@
     tri = jnp.where(ci <= ri, 1.0, 0.0).astype(BF16)
     parts = split3(decay)
     cum = dot(tri, parts[0]) + (dot(tri, parts[1]) + dot(tri, parts[2]))
-    dt_o[...] = dt
     cum_o[...] = cum
     dt_t[...] = dt.T
     cum_t[...] = cum.T
@@ -74,11 +75,15 @@
     weight = jnp.exp(last - cum) * dt
 
     step = 2 * LANES
+    w = take(6)
     for start in list(range(inner, width, step)) + list(range(0, inner, step)):
         cols = slice(start, start + step)
         piece = dot(rows, w[:, cols]).astype(BF16).astype(F32)
         raw[:, cols] = piece
-        acc = jnp.broadcast_to(cb[:, cols], (length, step))
+        first = start // LANES
+        acc = jnp.concatenate(
+            [jnp.broadcast_to(cb[k : k + 1, :], (length, LANES)) for k in (first, first + 1)], axis=1
+        )
         for k in range(taps):
             acc = acc + cw[k : k + 1, cols] * raw[pl.ds(edge - (taps - 1) + k, length), cols]
         xbc[:, cols] = (acc / (1.0 + jnp.exp(-acc))).astype(BF16)
@@ -105,9 +110,9 @@
     return tail[0:1, :] + tail[1:2, :]
 
 
-def chip_kernel(where_am_i, mine, other, out, gain_out):
+def chip_kernel(take, mine, other, out, gain_out):
     state = out.shape[0]
-    odd = where_am_i[0] == 1
+    odd = lax.rem(lax.axis_index("tm"), 2) == 1
     m = mine[:state, :].astype(F32)
     o = other[:state, :].astype(F32)
     gm = gain_row(mine, state)
@@ -116,9 +121,8 @@
     gain_out[...] = jnp.broadcast_to(gm * go, gain_out.shape)
 
 
-def within_kernel(heads, d_skip, hist, zw, xbc, cum, dt_t, cum_t, item, first_low, part, gate, pre):
-    length = hist.shape[0]
-    inner = zw.shape[1]
+def within_kernel(heads, take, d_skip, xbc, cum, dt_t, cum_t, part, gate, pre):
+    length, inner = part.shape
     state = (xbc.shape[1] - inner) // 2
     head_size = inner // heads
     per = LANES // head_size
@@ -157,18 +161,20 @@
             out = got if out is None else jnp.where(lane >= k * head_size, got, out)
         part[:, cols] = out
     step = 2 * LANES
+    hist, zw = take(0), take(1)
     for start in range(0, inner, step):
         cols = slice(start, start + step)
         z = dot(hist[...], zw[:, cols]).astype(BF16).astype(F32)
         gate[:, cols] = z / (1.0 + jnp.exp(-z))
+    item, first = take(2), take(3)
     for start in range(0, pre.shape[1], step):
         cols = slice(start, start + step)
-        pre[:, cols] = dot(item[...], first_low[:, cols])
+        pre[:, cols] = dot(item[...], first[:, cols])
 
 
 def rank_kernel(
     heads,
-    where_am_i,
+    take,
     count,
     incoming,
     other,
@@ -176,14 +182,7 @@
     cum,
     part,
     gate,
-    gain,
-    ow,
-    pos,
-    value,
-    item,
     pre,
-    first_high,
-    second,
     enc_o,
     logit_o,
     send_o,
@@ -198,9 +197,10 @@
     state = incoming.shape[0]
     head_size = inner // heads
     per = LANES // head_size
-    slots = pos.shape[1]
-    odd = where_am_i[0] == 1
-    base = where_am_i[1]
+    slots = pre.shape[0]
+    tm = lax.axis_index("tm")
+    odd = lax.rem(tm, 2) == 1
+    base = tm * length
     arrived = incoming[...].astype(F32)
     enter = jnp.where(
         odd, arrived * gain_row(other, state) + other[:state, :].astype(F32), arrived
@@ -219,10 +219,12 @@
         total = total + y * y
     mean = jnp.sum(total, axis=1, keepdims=True) * (1.0 / inner)
     scale = lax.rsqrt(mean + 1e-05)
+    gain, ow = take(0), take(1)
     normed = (gated_s[...] * scale * gain[...]).astype(BF16)
     enc = dot(normed, ow[...]).astype(BF16)
     enc_o[...] = enc
     width = enc.shape[1]
+    pos = take(2)
     place = pos[...] - base
     hot = (lax.broadcasted_iota(jnp.int32, (length, slots), 0) == place).astype(F32).astype(BF16)
     rank_s[...] = dot_tn(hot, enc).astype(BF16)
@@ -230,13 +232,16 @@
     hidden_width = pre.shape[1]
     step = 2 * LANES
     logit = jnp.zeros((slots, LANES), F32)
+    first, second = take(3), take(4)
+    weights2 = second[...].astype(F32)
     for start in range(0, hidden_width, step):
         cols = slice(start, start + step)
-        v = pre[:, cols] + dot(rank_s[...], first_high[:, cols])
+        v = pre[:, cols] + dot(rank_s[...], first[:, cols])
         sig = 1.0 / (1.0 + jnp.exp(-v))
         hid = (v * sig).astype(BF16)
         hid_s[:, cols] = hid
-        w2 = second[:, cols].astype(F32)
+        k = start // LANES
+        w2 = jnp.concatenate([weights2[k : k + 1], weights2[k + 1 : k + 2]], axis=1)
         prod = hid.astype(F32) * w2
         for k in range(0, step, LANES):
             logit = logit + prod[:, k : k + LANES]
@@ -247,6 +252,7 @@
     slot = lax.broadcasted_iota(jnp.int32, (8, slots), 1)
     live = jnp.where(slot < count[0, 0], 1.0, 0.0)
     logit_o[...] = (live * logit8)[0:1, :]
+    value = take(5)
     target = value[...].astype(F32)
     dl = live * (1.0 / (1.0 + jnp.exp(-logit8)) - target)
     d0, d1, d2 = split3(dl)
@@ -262,6 +268,7 @@
         cols = slice(start, start + LANES)
         gp_s[:, cols] = (dcol * slope_s[:, cols]).astype(BF16)
     rows = width
+    item = take(6)
     pick = lax.broadcasted_iota(jnp.int32, (8, hidden_width), 0)
     extra = jnp.where(pick == 0, grad2, 0.0).astype(BF16)
     away = jnp.where(odd, rank_s[...], item[...])
@@ -272,16 +279,43 @@
     keep_o[rows:, :] = extra
 
 
-def call(kernel, out_shape, in_specs, scratch, args, flops, moved):
+def loading(kernel, n_loaded, n_given, n_out, windows):
+    def wrapped(*refs):
+        sources = refs[:n_loaded]
+        given = refs[n_loaded : n_loaded + n_given + n_out]
+        rest = refs[n_loaded + n_given + n_out :]
+        places, sems, scratch = rest[:n_loaded], rest[n_loaded], rest[n_loaded + 1 :]
+        copies = []
+        for i, source in enumerate(sources):
+            window = windows.get(i)
+            view = source if window is None else source.at[pl.ds(*window)]
+            copies.append(pltpu.make_async_copy(view, places[i], sems.at[i]))
+            copies[i].start()
+
+        def take(i):
+            copies[i].wait()
+            return places[i]
+
+        kernel(take, *given, *scratch)
+
+    return wrapped
+
+
+def call(kernel, loaded, given, out_shape, scratch, flops, moved, mib, windows=None, smem=0):
+    windows = windows or {}
+    places = []
+    for i, value in enumerate(loaded):
+        dims = value.shape if i not in windows else (windows[i][1],) + value.shape[1:]
+        places.append(pltpu.VMEM(dims, value.dtype))
     return pl.pallas_call(
-        kernel,
+        loading(kernel, len(loaded), len(given), len(out_shape), windows),
         out_shape=out_shape,
-        in_specs=in_specs,
-        out_specs=jax.tree.map(lambda _: VMEM, out_shape),
-        scratch_shapes=scratch,
-        compiler_params=pltpu.CompilerParams(vmem_limit_bytes=LIMIT),
+        in_specs=[HBM] * len(loaded) + [SMEM] * smem + [VMEM] * (len(given) - smem),
+        out_specs=[VMEM] * len(out_shape),
+        scratch_shapes=places + [pltpu.SemaphoreType.DMA((max(len(loaded), 1),))] + scratch,
+        compiler_params=pltpu.CompilerParams(vmem_limit_bytes=mib * 1024 * 1024),
         cost_estimate=pl.CostEstimate(flops=flops, bytes_accessed=moved, transcendentals=0),
-    )(*args)
+    )(*[pltpu.with_memory_space_constraint(value, pltpu.HBM) for value in loaded], *given)
 
 
 def shape(dims, dtype):
@@ -325,44 +359,42 @@
     chips = n_tm // 2
     tm = lax.axis_index("tm")
     user = lax.axis_index("user")
-    odd = tm % 2
-    where_am_i = jnp.stack([odd, tm * length]).astype(jnp.int32)
 
     halo = lax.ppermute(hist[length - ALIGN :], "tm", [(i, i + 1) for i in range(n_tm - 1)])
-    xbc, dt, cum, dt_t, cum_t, pay = call(
+    xbc, cum, dt_t, cum_t, pay = call(
         functools.partial(scan_kernel, heads),
         (
+            hist,
+            dt_weight.T,
+            dt_bias.reshape(1, heads),
+            a_log.reshape(1, heads),
+            conv_weight,
+            conv_bias.reshape(channels // LANES, LANES),
+            xbc_weight,
+        ),
+        (halo,),
+        (
             shape((length, channels), BF16),
-            shape((length, heads), F32),
             shape((length, heads), F32),
             shape((heads, length), F32),
             shape((heads, length), F32),
             shape((state + ALIGN, inner), BF16),
         ),
-        [VMEM] * 8,
         [pltpu.VMEM((length + ALIGN, channels), F32), pltpu.VMEM((length, inner), BF16)],
-        (
-            halo,
-            hist,
-            xbc_weight,
-            dt_weight.T,
-            dt_bias.reshape(1, heads),
-            a_log.reshape(1, heads),
-            conv_weight,
-            conv_bias.reshape(1, channels),
-        ),
         2 * length * width * channels,
         4 * width * channels,
+        16,
     )
     other = lax.ppermute(pay, "tm", [(i, i ^ 1) for i in range(n_tm)])
     chip_state, chip_gain = call(
         chip_kernel,
+        (),
+        (pay, other),
         (shape((state, inner), BF16), shape((8, inner), F32)),
-        [SMEM, VMEM, VMEM],
         [],
-        (where_am_i, pay, other),
         state * inner,
         6 * state * inner,
+        6,
     )
     onward = [(i, i + 2) for i in range(n_tm - 2)]
     incoming = lax.ppermute(chip_state, "tm", onward)
@@ -371,26 +403,38 @@
         incoming = lax.ppermute(passed.astype(BF16), "tm", onward)
     part, gate, pre = call(
         functools.partial(within_kernel, heads),
+        (hist, z_weight, item, first_weight),
+        (d_skip, xbc, cum, dt_t, cum_t),
         (
             shape((length, inner), F32),
             shape((length, inner), F32),
             shape((slots, hidden), F32),
         ),
-        [SMEM] + [VMEM] * 8,
         [],
-        (d_skip, hist, z_weight, xbc, cum, dt_t, cum_t, item, first_weight[width:]),
         2 * length * width * inner + 2 * slots * width * hidden + 4 * length * length * inner,
         16 * length * inner * 4,
+        20,
+        {3: (width, width)},
+        1,
     )
     enc, row_logit, send, keep = call(
         functools.partial(rank_kernel, heads),
+        (
+            norm_gain.reshape(1, inner),
+            out_weight,
+            label_pos,
+            first_weight,
+            second_weight.reshape(hidden // LANES, LANES),
+            label_value,
+            item,
+        ),
+        (label_count, incoming, other, xbc, cum, part, gate, pre),
         (
             shape((length, width), BF16),
             shape((1, slots), F32),
             shape((width + 8, hidden), BF16),
             shape((width + 8, hidden), BF16),
         ),
-        [SMEM, SMEM] + [VMEM] * 14,
         [
             pltpu.VMEM((length, inner), F32),
             pltpu.VMEM((slots, width), BF16),
@@ -398,26 +442,11 @@
             pltpu.VMEM((slots, hidden), BF16),
             pltpu.VMEM((slots, hidden), BF16),
         ],
-        (
-            where_am_i,
-            label_count,
-            incoming,
-            other,
-            xbc,
-            cum,
-            part,
-            gate,
-            norm_gain.reshape(1, inner),
-            out_weight,
-            label_pos,
-            label_value,
-            item,
-            pre,
-            first_weight[:width],
-            second_weight.reshape(1, hidden),
-        ),
         4 * slots * width * hidden,
         8 * slots * hidden,
+        24,
+        {3: (0, width)},
+        1,
     )
     grad_first, grad_second = total_sum(send, keep, n_user, n_tm, user, tm)
     return (enc[None], row_logit, grad_first, grad_second)

time: 105 us -> 93.7 us (0.89)
  Pallas kernels: 21.6 us -> 14.2 us
  local copies, waits for them, and re-layouts: 6.99 us -> 0.73 us
  waiting for transfers between devices: 39.8 us -> 42.8 us
  other arithmetic: 7.55 us -> 4.97 us
  starting transfers between devices: 26.5 us -> 27.9 us
    pallas_call x4, Pallas kernels: 21.6 us -> 14.2 us  [call(): pl.pallas_call(loading(kernel, len(loaded), len(given), len(out_shape), w...]
    reshape x2 -> x0, local copies, waits for them, and re-layouts: 2.57 us -> none  [the longest x1 1.29 us: body(): conv_bias.reshape(1, channels)]
    unnamed x8 -> x2, local copies, waits for them, and re-layouts: 2.04 us -> 0.01 us
    slice x1 -> x0, local copies, waits for them, and re-layouts: 1.5 us -> none  [body(): first_weight[:width]]
    ppermute x1, waiting for transfers between devices: 0.01 us -> 1.21 us  [body(): other = lax.ppermute(pay, 'tm', [(i, i ^ 1) for i in range(n_tm)])]
    convert_element_type x2, other arithmetic: 1.8 us -> 0.6 us  [total_sum(): main_a = jnp.where(bit, high, low).astype(BF16)]
    ppermute x1, waiting for transfers between devices: 0.01 us -> 1.18 us  [body(): incoming = lax.ppermute(chip_state, 'tm', onward)]
  transfers between devices with their start and end apart: 11 -> 11, of which waited for: 8 -> 11; matrix products, arithmetic and copies ran while one was open for 5% -> 0% of each run, Pallas kernels for 5% -> 4%
where the time goes in v2:
time: 93.7 us; the launch traced here: 92 us
  waiting for transfers between devices  42.8 us (46%)
  starting transfers between devices  27.9 us (30%)
  Pallas kernels  14.2 us (15%)
  other arithmetic  4.97 us (5%)
  between operations  1.49 us (2%)
    ppermute x8, waiting for transfers between devices, swap(): return lax.ppermute(value, axes, pairs)  39.6 us
    ppermute x8, starting transfers between devices, swap(): return lax.ppermute(value, axes, pairs)  18.1 us
    pallas_call x4, Pallas kernels, call(): pl.pallas_call(loading(kernel, len(loaded), len(given), len(out_shape), w...  14.2 us
    ppermute x1, starting transfers between devices, body(): incoming = lax.ppermute(chip_state, 'tm', onward)  4.67 us
    ppermute x1, starting transfers between devices, body(): other = lax.ppermute(pay, 'tm', [(i, i ^ 1) for i in range(n_tm)])  2.69 us
    convert_element_type x1, other arithmetic, total_sum(): grad_first = jnp.concatenate([jnp.where(bit, got, whole), jnp.where(bit,...  2.45 us
    ppermute x1, starting transfers between devices, body(): lax.ppermute(hist[length - ALIGN:], 'tm', [(i, i + 1) for i in range(n_tm...  2.39 us
  transfers between devices with their start and end apart: 11, of which 11 were waited for; matrix products, arithmetic and copies ran while one was open for 0% of the time, Pallas kernels for 4%

profile of v2, /device:TPU:0, one launch (start us, length us, event | category | flops | bytes accessed | tf_op | source)
XLA Modules:
  0.0 92.0 jit_solution(10162268175652222467)
XLA Ops:
  1.4 2.4 %collective-permute-start = (bf16[16,512]{1,0:T(8,128)(2,1)S(1)}, bf16[16,512]{1,0:T(8,128)(2,1)S(1)}, u32[]{:S(2)}, u32[]{:S(2)}) collective-permute-start(bf16[16,512]{1,0:T(8,128)(2,1)S(1)} %slice_bitcast_fusion), channel_id=1, source_target_pairs={{0,1},{1,2},{2,3},{4,5},{5,6},{6,7},{8,9},{9,10},{10,11},{12,13},{... | collective-permute-start | bytes 49160 | tf_op jit(solution)/shard_map/ppermute | solution.py:363
  3.8 0.8 collective-permute-done.refs_7_
  4.6 3.4 %shard_map.192 = (bf16[256,1280]{1,0:T(8,128)(2,1)S(1)}, f32[256,16]{1,0:T(8,128)S(1)}, f32[16,256]{1,0:T(8,128)S(1)}, f32[16,256]{1,0:T(8,128)S(1)}, bf16[144,1024]{1,0:T(8,128)(2,1)S(1)}) custom-call(bf16[256,512]{1,0:T(8,128)(2,1)} %bitcast.14, bf16[16,512]{1,0:T(8,128)(2,1)} %bitcast.16, f32[1,16]{1,0:T(1,128)} %bitcast.21, f32[1,16]{1,0:T(1,128)} %bitcast.22, ...), custom_call_target="tpu_custom_call" | custom-call | flops 335544320 | bytes 2621440 | tf_op jit(solution)/shard_map/pallas_call | solution.py:310
  8.0 2.7 %collective-permute-start.1 = (bf16[144,1024]{1,0:T(8,128)(2,1)S(1)}, bf16[144,1024]{1,0:T(8,128)(2,1)S(1)}, u32[]{:S(2)}, u32[]{:S(2)}) collective-permute-start(bf16[144,1024]{1,0:T(8,128)(2,1)S(1)} %get-tuple-element.17.refs_0_), channel_id=1, source_target_pairs={{0,1},{1,0},{2,3},{3,2},{4,5},{5,4},{6,7},{7,6},{8,9},{9,8},{10,11... | collective-permute-start | bytes 884744 | tf_op jit(solution)/shard_map/ppermute | solution.py:388
  10.7 1.2 %collective-permute-done.1.refs_1_.refs_9_ = bf16[144,1024]{1,0:T(8,128)(2,1)S(1)} collective-permute-done((bf16[144,1024]{1,0:T(8,128)(2,1)S(1)}, bf16[144,1024]{1,0:T(8,128)(2,1)S(1)}, u32[]{:S(2)}, u32[]{:S(2)}) %collective-permute-start.1) | collective-permute-done | bytes 294944 | tf_op jit(solution)/shard_map/ppermute | solution.py:388
  12.6 4.7 %collective-permute-start.2 = (bf16[128,1024]{1,0:T(8,128)(2,1)S(1)}, bf16[128,1024]{1,0:T(8,128)(2,1)S(1)}, u32[]{:S(2)}, u32[]{:S(2)}) collective-permute-start(bf16[128,1024]{1,0:T(8,128)(2,1)S(1)} %get-tuple-element.18), channel_id=1, source_target_pairs={{0,2},{1,3},{4,6},{5,7},{8,10},{9,11},{12,14},{13,15},{16,18},{17,... | collective-permute-start | bytes 786440 | tf_op jit(solution)/shard_map/ppermute | solution.py:400
  17.9 3.8 %shard_map.194 = (f32[256,1024]{1,0:T(8,128)S(1)}, f32[256,1024]{1,0:T(8,128)S(1)}, f32[512,1024]{1,0:T(8,128)S(1)}) custom-call(bf16[256,512]{1,0:T(8,128)(2,1)} %bitcast.15, bf16[512,1024]{1,0:T(8,128)(2,1)} %refs_1_.2, bf16[512,512]{1,0:T(8,128)(2,1)} %bitcast.12, bf16[1024,1024]{1,0:T(8,128)(2,1)} %refs_3_.3, f32[16]{0:T(128)S(1)} %copy-done, ...), custom_call_target="tpu_custom_call" | custom-call | flops 1073741824 | bytes 16777216 | tf_op jit(solution)/shard_map/pallas_call | solution.py:310
  21.7 1.2 %collective-permute-done.2.refs_8_ = bf16[128,1024]{1,0:T(8,128)(2,1)S(1)} collective-permute-done((bf16[128,1024]{1,0:T(8,128)(2,1)S(1)}, bf16[128,1024]{1,0:T(8,128)(2,1)S(1)}, u32[]{:S(2)}, u32[]{:S(2)}) %collective-permute-start.2) | collective-permute-done | bytes 262176 | tf_op jit(solution)/shard_map/ppermute | solution.py:400
  22.9 6.3 %shard_map.195 = (bf16[256,512]{1,0:T(8,128)(2,1)}, f32[1,512]{1,0:T(1,128)}, bf16[520,1024]{1,0:T(8,128)(2,1)S(1)}, bf16[520,1024]{1,0:T(8,128)(2,1)S(1)}) custom-call(f32[1,1024]{1,0:T(1,128)} %bitcast.18, bf16[1024,512]{1,0:T(8,128)(2,1)} %refs_1_.3, s32[1,512]{1,0:T(1,128)} %refs_2_.1, bf16[1024,1024]{1,0:T(8,128)(2,1)} %refs_3_.3, ...), custom_call_target="tpu_custom_call" | custom-call | flops 1073741824 | bytes 4194304 | tf_op jit(solution)/shard_map/pallas_call | solution.py:310
  29.3 2.6 %collective-permute-done.3 = bf16[520,1024]{1,0:T(8,128)(2,1)S(1)} collective-permute-done((bf16[520,1024]{1,0:T(8,128)(2,1)S(1)}, bf16[520,1024]{1,0:T(8,128)(2,1)S(1)}, u32[]{:S(2)}, u32[]{:S(2)}) %collective-permute-start.3) | collective-permute-done | bytes 1064992 | tf_op jit(solution)/shard_map/ppermute | solution.py:463
  32.4 2.6 %collective-permute-start.4 = (bf16[264,1024]{1,0:T(8,128)(2,1)S(1)}, bf16[264,1024]{1,0:T(8,128)(2,1)S(1)}, u32[]{:S(2)}, u32[]{:S(2)}) collective-permute-start(bf16[264,1024]{1,0:T(8,128)(2,1)S(1)} %pad_maximum_fusion.2), channel_id=1, source_target_pairs={{0,2},{1,5},{2,0},{3,7},{4,6},{5,1},{6,4},{7,3},{8,10},{9,13},{10,... | collective-permute-start | bytes 1622024 | tf_op jit(solution)/shard_map/ppermute | solution.py:463
  35.0 7.3 %collective-permute-done.4 = bf16[264,1024]{1,0:T(8,128)(2,1)S(1)} collective-permute-done((bf16[264,1024]{1,0:T(8,128)(2,1)S(1)}, bf16[264,1024]{1,0:T(8,128)(2,1)S(1)}, u32[]{:S(2)}, u32[]{:S(2)}) %collective-permute-start.4) | collective-permute-done | bytes 540704 | tf_op jit(solution)/shard_map/ppermute | solution.py:463
  42.6 1.6 %collective-permute-start.5 = (bf16[136,1024]{1,0:T(8,128)(2,1)S(1)}, bf16[136,1024]{1,0:T(8,128)(2,1)S(1)}, u32[]{:S(2)}, u32[]{:S(2)}) collective-permute-start(bf16[136,1024]{1,0:T(8,128)(2,1)S(1)} %pad_maximum_fusion.4), channel_id=1, source_target_pairs={{0,4},{1,9},{2,6},{3,11},{4,0},{5,13},{6,2},{7,15},{8,12},{9,1},{1... | collective-permute-start | bytes 835592 | tf_op jit(solution)/shard_map/ppermute | solution.py:463
  44.2 6.9 %collective-permute-done.5 = bf16[136,1024]{1,0:T(8,128)(2,1)S(1)} collective-permute-done((bf16[136,1024]{1,0:T(8,128)(2,1)S(1)}, bf16[136,1024]{1,0:T(8,128)(2,1)S(1)}, u32[]{:S(2)}, u32[]{:S(2)}) %collective-permute-start.5) | collective-permute-done | bytes 278560 | tf_op jit(solution)/shard_map/ppermute | solution.py:463
  51.2 2.7 %collective-permute-start.6 = (bf16[72,1024]{1,0:T(8,128)(2,1)S(1)}, bf16[72,1024]{1,0:T(8,128)(2,1)S(1)}, u32[]{:S(2)}, u32[]{:S(2)}) collective-permute-start(bf16[72,1024]{1,0:T(8,128)(2,1)S(1)} %pad_maximum_fusion.6), channel_id=1, source_target_pairs={{0,8},{1,3},{2,10},{3,1},{4,12},{5,7},{6,14},{7,5},{8,0},{9,11},{1... | collective-permute-start | bytes 442376 | tf_op jit(solution)/shard_map/ppermute | solution.py:463
  53.8 3.4 %collective-permute-done.6 = bf16[72,1024]{1,0:T(8,128)(2,1)S(1)} collective-permute-done((bf16[72,1024]{1,0:T(8,128)(2,1)S(1)}, bf16[72,1024]{1,0:T(8,128)(2,1)S(1)}, u32[]{:S(2)}, u32[]{:S(2)}) %collective-permute-start.6) | collective-permute-done | bytes 147488 | tf_op jit(solution)/shard_map/ppermute | solution.py:463
  57.4 2.7 %collective-permute-start.7 = (bf16[64,1024]{1,0:T(8,128)(2,1)S(1)}, bf16[64,1024]{1,0:T(8,128)(2,1)S(1)}, u32[]{:S(2)}, u32[]{:S(2)}) collective-permute-start(bf16[64,1024]{1,0:T(8,128)(2,1)S(1)} %add_convert_fusion), channel_id=1, source_target_pairs={{0,8},{1,3},{2,10},{3,1},{4,12},{5,7},{6,14},{7,5},{8,0},{9,11},{1... | collective-permute-start | bytes 393224 | tf_op jit(solution)/shard_map/ppermute | solution.py:463
  60.1 3.4 %collective-permute-done.7 = bf16[64,1024]{1,0:T(8,128)(2,1)S(1)} collective-permute-done((bf16[64,1024]{1,0:T(8,128)(2,1)S(1)}, bf16[64,1024]{1,0:T(8,128)(2,1)S(1)}, u32[]{:S(2)}, u32[]{:S(2)}) %collective-permute-start.7) | collective-permute-done | bytes 131104 | tf_op jit(solution)/shard_map/ppermute | solution.py:463
  63.5 6.3 %collective-permute-start.8 = (bf16[128,1024]{1,0:T(8,128)(2,1)S(1)}, bf16[128,1024]{1,0:T(8,128)(2,1)S(1)}, u32[]{:S(2)}, u32[]{:S(2)}) collective-permute-start(bf16[128,1024]{1,0:T(8,128)(2,1)S(1)} %pad_maximum_fusion.5), channel_id=1, source_target_pairs={{0,4},{1,9},{2,6},{3,11},{4,0},{5,13},{6,2},{7,15},{8,12},{9,1},{1... | collective-permute-start | bytes 786440 | tf_op jit(solution)/shard_map/ppermute | solution.py:463
  69.8 6.1 %collective-permute-done.8 = bf16[128,1024]{1,0:T(8,128)(2,1)S(1)} collective-permute-done((bf16[128,1024]{1,0:T(8,128)(2,1)S(1)}, bf16[128,1024]{1,0:T(8,128)(2,1)S(1)}, u32[]{:S(2)}, u32[]{:S(2)}) %collective-permute-start.8) | collective-permute-done | bytes 262176 | tf_op jit(solution)/shard_map/ppermute | solution.py:463
  76.0 2.1 %collective-permute-start.9 = (bf16[256,1024]{1,0:T(8,128)(2,1)S(1)}, bf16[256,1024]{1,0:T(8,128)(2,1)S(1)}, u32[]{:S(2)}, u32[]{:S(2)}) collective-permute-start(bf16[256,1024]{1,0:T(8,128)(2,1)S(1)} %pad_maximum_fusion.3), channel_id=1, source_target_pairs={{0,2},{1,5},{2,0},{3,7},{4,6},{5,1},{6,4},{7,3},{8,10},{9,13},{10,... | collective-permute-start | bytes 1572872 | tf_op jit(solution)/shard_map/ppermute | solution.py:463
  78.2 7.2 %collective-permute-done.9 = bf16[256,1024]{1,0:T(8,128)(2,1)S(1)} collective-permute-done((bf16[256,1024]{1,0:T(8,128)(2,1)S(1)}, bf16[256,1024]{1,0:T(8,128)(2,1)S(1)}, u32[]{:S(2)}, u32[]{:S(2)}) %collective-permute-start.9) | collective-permute-done | bytes 524320 | tf_op jit(solution)/shard_map/ppermute | solution.py:463
  85.8 2.7 %collective-permute-done.10 = bf16[520,1024]{1,0:T(8,128)(2,1)S(1)} collective-permute-done((bf16[520,1024]{1,0:T(8,128)(2,1)S(1)}, bf16[520,1024]{1,0:T(8,128)(2,1)S(1)}, u32[]{:S(2)}, u32[]{:S(2)}) %collective-permute-start.10) | collective-permute-done | bytes 1064992 | tf_op jit(solution)/shard_map/ppermute | solution.py:463
  89.6 2.4 %maximum_convert_fusion = f32[1024,1024]{1,0:T(8,128)} fusion(bf16[512,1024]{1,0:T(8,128)(2,1)S(1)} %get-tuple-element.33, bf16[512,1024]{1,0:T(8,128)(2,1)S(1)} %get-tuple-element.32), kind=kLoop, calls=%fused_computation | loop fusion | flops 4194304 | bytes 6291456 | tf_op jit(solution)/shard_map/convert_element_type | solution.py:513
  (26 shorter events, 4.0 us)
Async XLA Ops:
  0.6 17.3 %copy-start = (f32[16]{0:T(128)S(1)}, f32[16]{0:T(128)}, u32[]{:S(2)}) copy-start(f32[16]{0:T(128)} %refs_4_.3) | copy-start | bytes 196
  1.4 3.2 %collective-permute-start = (bf16[16,512]{1,0:T(8,128)(2,1)S(1)}, bf16[16,512]{1,0:T(8,128)(2,1)S(1)}, u32[]{:S(2)}, u32[]{:S(2)}) collective-permute-start(bf16[16,512]{1,0:T(8,128)(2,1)S(1)} %slice_bitcast_fusion), channel_id=1, source_target_pairs={{0,1},{1,2},{2,3},{4,5},{5,6},{6,7},{8,9},{9,10},{10,11},{12,13},{... | collective-permute-start | bytes 49160 | tf_op jit(solution)/shard_map/ppermute | solution.py:363
  8.0 3.9 %collective-permute-start.1 = (bf16[144,1024]{1,0:T(8,128)(2,1)S(1)}, bf16[144,1024]{1,0:T(8,128)(2,1)S(1)}, u32[]{:S(2)}, u32[]{:S(2)}) collective-permute-start(bf16[144,1024]{1,0:T(8,128)(2,1)S(1)} %get-tuple-element.17.refs_0_), channel_id=1, source_target_pairs={{0,1},{1,0},{2,3},{3,2},{4,5},{5,4},{6,7},{7,6},{8,9},{9,8},{10,11... | collective-permute-start | bytes 884744 | tf_op jit(solution)/shard_map/ppermute | solution.py:388
  12.6 10.3 %collective-permute-start.2 = (bf16[128,1024]{1,0:T(8,128)(2,1)S(1)}, bf16[128,1024]{1,0:T(8,128)(2,1)S(1)}, u32[]{:S(2)}, u32[]{:S(2)}) collective-permute-start(bf16[128,1024]{1,0:T(8,128)(2,1)S(1)} %get-tuple-element.18), channel_id=1, source_target_pairs={{0,2},{1,3},{4,6},{5,7},{8,10},{9,11},{12,14},{13,15},{16,18},{17,... | collective-permute-start | bytes 786440 | tf_op jit(solution)/shard_map/ppermute | solution.py:400
  29.2 2.7 %collective-permute-start.3 = (bf16[520,1024]{1,0:T(8,128)(2,1)S(1)}, bf16[520,1024]{1,0:T(8,128)(2,1)S(1)}, u32[]{:S(2)}, u32[]{:S(2)}) collective-permute-start(bf16[520,1024]{1,0:T(8,128)(2,1)S(1)} %get-tuple-element.29), channel_id=1, source_target_pairs={{0,1},{1,0},{2,3},{3,2},{4,5},{5,4},{6,7},{7,6},{8,9},{9,8},{10,11... | collective-permute-start | bytes 3194888 | tf_op jit(solution)/shard_map/ppermute | solution.py:463
  32.4 9.9 %collective-permute-start.4 = (bf16[264,1024]{1,0:T(8,128)(2,1)S(1)}, bf16[264,1024]{1,0:T(8,128)(2,1)S(1)}, u32[]{:S(2)}, u32[]{:S(2)}) collective-permute-start(bf16[264,1024]{1,0:T(8,128)(2,1)S(1)} %pad_maximum_fusion.2), channel_id=1, source_target_pairs={{0,2},{1,5},{2,0},{3,7},{4,6},{5,1},{6,4},{7,3},{8,10},{9,13},{10,... | collective-permute-start | bytes 1622024 | tf_op jit(solution)/shard_map/ppermute | solution.py:463
  42.6 8.5 %collective-permute-start.5 = (bf16[136,1024]{1,0:T(8,128)(2,1)S(1)}, bf16[136,1024]{1,0:T(8,128)(2,1)S(1)}, u32[]{:S(2)}, u32[]{:S(2)}) collective-permute-start(bf16[136,1024]{1,0:T(8,128)(2,1)S(1)} %pad_maximum_fusion.4), channel_id=1, source_target_pairs={{0,4},{1,9},{2,6},{3,11},{4,0},{5,13},{6,2},{7,15},{8,12},{9,1},{1... | collective-permute-start | bytes 835592 | tf_op jit(solution)/shard_map/ppermute | solution.py:463
  51.2 6.1 %collective-permute-start.6 = (bf16[72,1024]{1,0:T(8,128)(2,1)S(1)}, bf16[72,1024]{1,0:T(8,128)(2,1)S(1)}, u32[]{:S(2)}, u32[]{:S(2)}) collective-permute-start(bf16[72,1024]{1,0:T(8,128)(2,1)S(1)} %pad_maximum_fusion.6), channel_id=1, source_target_pairs={{0,8},{1,3},{2,10},{3,1},{4,12},{5,7},{6,14},{7,5},{8,0},{9,11},{1... | collective-permute-start | bytes 442376 | tf_op jit(solution)/shard_map/ppermute | solution.py:463
  57.4 6.1 %collective-permute-start.7 = (bf16[64,1024]{1,0:T(8,128)(2,1)S(1)}, bf16[64,1024]{1,0:T(8,128)(2,1)S(1)}, u32[]{:S(2)}, u32[]{:S(2)}) collective-permute-start(bf16[64,1024]{1,0:T(8,128)(2,1)S(1)} %add_convert_fusion), channel_id=1, source_target_pairs={{0,8},{1,3},{2,10},{3,1},{4,12},{5,7},{6,14},{7,5},{8,0},{9,11},{1... | collective-permute-start | bytes 393224 | tf_op jit(solution)/shard_map/ppermute | solution.py:463
  63.5 12.3 %collective-permute-start.8 = (bf16[128,1024]{1,0:T(8,128)(2,1)S(1)}, bf16[128,1024]{1,0:T(8,128)(2,1)S(1)}, u32[]{:S(2)}, u32[]{:S(2)}) collective-permute-start(bf16[128,1024]{1,0:T(8,128)(2,1)S(1)} %pad_maximum_fusion.5), channel_id=1, source_target_pairs={{0,4},{1,9},{2,6},{3,11},{4,0},{5,13},{6,2},{7,15},{8,12},{9,1},{1... | collective-permute-start | bytes 786440 | tf_op jit(solution)/shard_map/ppermute | solution.py:463
  76.0 9.3 %collective-permute-start.9 = (bf16[256,1024]{1,0:T(8,128)(2,1)S(1)}, bf16[256,1024]{1,0:T(8,128)(2,1)S(1)}, u32[]{:S(2)}, u32[]{:S(2)}) collective-permute-start(bf16[256,1024]{1,0:T(8,128)(2,1)S(1)} %pad_maximum_fusion.3), channel_id=1, source_target_pairs={{0,2},{1,5},{2,0},{3,7},{4,6},{5,1},{6,4},{7,3},{8,10},{9,13},{10,... | collective-permute-start | bytes 1572872 | tf_op jit(solution)/shard_map/ppermute | solution.py:463
  85.7 2.7 %collective-permute-start.10 = (bf16[520,1024]{1,0:T(8,128)(2,1)S(1)}, bf16[520,1024]{1,0:T(8,128)(2,1)S(1)}, u32[]{:S(2)}, u32[]{:S(2)}) collective-permute-start(bf16[520,1024]{1,0:T(8,128)(2,1)S(1)} %pad_maximum_fusion), channel_id=1, source_target_pairs={{0,1},{1,0},{2,3},{3,2},{4,5},{5,4},{6,7},{7,6},{8,9},{9,8},{10,11... | collective-permute-start | bytes 3194888 | tf_op jit(solution)/shard_map/ppermute | solution.py:463

commit v3 on v2

--- a/solution.py
+++ b/solution.py
@@ -457,10 +457,14 @@
     odd = tm % 2
     axes = ("user", "tm")
     every = [(u, t) for u in range(n_user) for t in range(n_tm)]
+    chunks = 2
 
     def swap(value, partner):
         pairs = [(u * n_tm + t, partner(u, t)) for u, t in every]
         return lax.ppermute(value, axes, pairs)
+
+    def across(u, t):
+        return u * n_tm + (t ^ 1)
 
     chip_bits = [("tm", k) for k in range(bits_of(n_tm // 2))]
     user_bits = [("user", k) for k in range(bits_of(n_user))]
@@ -483,35 +487,59 @@
 
         return jnp.where(odd == 0, one(order_even[level]), one(order_odd[level])) == 1
 
-    got = swap(send, lambda u, t: u * n_tm + (t ^ 1))
     levels = len(order_even)
-    size = rows
-    extra_a, extra_b = keep[rows:].astype(F32), got[rows:].astype(F32)
-    main_a, main_b = keep[:rows], got[:rows]
-    extra = (extra_a + extra_b).astype(BF16)
+    bits = [bit_of(level) for level in range(levels)]
+    bit = odd == 1
+    edges = [rows * k // chunks for k in range(chunks + 1)]
+    pieces = []
+    for k in range(chunks):
+        last = k == chunks - 1
+        stop = edges[k + 1] + (8 if last else 0)
+        pieces.append((send[edges[k] : stop], keep[edges[k] : stop], last))
+    size = rows // chunks
+    state = []
+    for leave, stay, has_extra in pieces:
+        got = swap(leave, across)
+        extra = None
+        if has_extra:
+            extra = (stay[size:].astype(F32) + got[size:].astype(F32)).astype(BF16)
+        state.append((stay[:size], got[:size], extra))
     for level in range(levels):
         size //= 2
-        bit = bit_of(level)
-        low = main_a[:size].astype(F32) + main_b[:size].astype(F32)
-        high = main_a[size:].astype(F32) + main_b[size:].astype(F32)
-        leave = jnp.where(bit, low, high).astype(BF16)
-        main_a = jnp.where(bit, high, low).astype(BF16)
-        got = swap(jnp.concatenate([leave, extra], axis=0), partner_of(level))
-        main_b = got[:size]
-        extra = (extra.astype(F32) + got[size:].astype(F32)).astype(BF16)
-    whole = (main_a.astype(F32) + main_b.astype(F32)).astype(BF16)
+        after = []
+        for a, b, extra in state:
+            low = a[:size].astype(F32) + b[:size].astype(F32)
+            high = a[size:].astype(F32) + b[size:].astype(F32)
+            leave = jnp.where(bits[level], low, high).astype(BF16)
+            stay = jnp.where(bits[level], high, low).astype(BF16)
+            if extra is not None:
+                leave = jnp.concatenate([leave, extra], axis=0)
+            got = swap(leave, partner_of(level))
+            if extra is not None:
+                extra = (extra.astype(F32) + got[size:].astype(F32)).astype(BF16)
+            after.append((stay, got[:size], extra))
+        state = after
+    wholes = [((a.astype(F32) + b.astype(F32)).astype(BF16), extra) for a, b, extra in state]
     for level in reversed(range(levels)):
-        got = swap(whole, partner_of(level))
-        bit = bit_of(level)
-        whole = jnp.concatenate([jnp.where(bit, got, whole), jnp.where(bit, whole, got)], axis=0)
-    got = swap(jnp.concatenate([whole, extra], axis=0), lambda u, t: u * n_tm + (t ^ 1))
-    bit = odd == 1
-    grad_second = jnp.where(bit, got[rows:], extra)[0].astype(F32)
-    got = got[:rows]
-    grad_first = jnp.concatenate(
-        [jnp.where(bit, got, whole), jnp.where(bit, whole, got)], axis=0
-    ).astype(F32)
-    return grad_first, grad_second
+        after = []
+        for whole, extra in wholes:
+            got = swap(whole, partner_of(level))
+            first = jnp.where(bits[level], got, whole)
+            second = jnp.where(bits[level], whole, got)
+            after.append((jnp.concatenate([first, second], axis=0), extra))
+        wholes = after
+    tops, bottoms = [], []
+    for whole, extra in wholes:
+        n = whole.shape[0]
+        if extra is None:
+            got = swap(whole, across)
+        else:
+            got = swap(jnp.concatenate([whole, extra], axis=0), across)
+            grad_second = jnp.where(bit, got[n:], extra)[0].astype(F32)
+            got = got[:n]
+        tops.append(jnp.where(bit, got, whole).astype(F32))
+        bottoms.append(jnp.where(bit, whole, got).astype(F32))
+    return jnp.concatenate(tops + bottoms, axis=0), grad_second
 
 
 def solution(mesh):

time: 93.7 us -> 82 us (0.88); the launches traced: 92 us -> 81.6 us
  waiting for transfers between devices: 42.8 us -> 25.1 us
  starting transfers between devices: 27.9 us -> 35 us
    ppermute x8 -> x16, waiting for transfers between devices: 39.6 us -> 21.9 us  [swap(): return lax.ppermute(value, axes, pairs)]
    ppermute x8 -> x16, starting transfers between devices: 18.1 us -> 25.3 us  [swap(): return lax.ppermute(value, axes, pairs)]
    concatenate x6 -> x10, other arithmetic: 0.2 us -> 2.69 us  [the longest x1 2.52 us: total_sum(): return (jnp.concatenate(tops + bottoms, axis=0), grad_second)]
    convert_element_type x7 -> x9, other arithmetic: 3.82 us -> 1.34 us  [the longest x1 0.6 us: total_sum(): grad_second = jnp.where(bit, got[n:], extra)[0].astype(F32)]
  transfers between devices with their start and end apart: 11 -> 19, of which waited for: 11 -> 14; matrix products, arithmetic and copies ran while one was open for 0% -> 1% of each run, Pallas kernels for 4% -> 5%
where the time goes in v3:
time: 82 us; the launch traced here: 81.6 us
  starting transfers between devices  35 us (43%)
  waiting for transfers between devices  25.1 us (31%)
  Pallas kernels  14.2 us (17%)
  other arithmetic  4.92 us (6%)
  between operations  1.59 us (2%)
    ppermute x16, starting transfers between devices, swap(): return lax.ppermute(value, axes, pairs)  25.3 us
    ppermute x16, waiting for transfers between devices, swap(): return lax.ppermute(value, axes, pairs)  21.9 us
    pallas_call x4, Pallas kernels, call(): pl.pallas_call(loading(kernel, len(loaded), len(given), len(out_shape), w...  14.2 us
    ppermute x1, starting transfers between devices, body(): incoming = lax.ppermute(chip_state, 'tm', onward)  4.67 us
    ppermute x1, starting transfers between devices, body(): other = lax.ppermute(pay, 'tm', [(i, i ^ 1) for i in range(n_tm)])  2.69 us
    concatenate x1, other arithmetic, total_sum(): return (jnp.concatenate(tops + bottoms, axis=0), grad_second)  2.52 us
    ppermute x1, starting transfers between devices, body(): lax.ppermute(hist[length - ALIGN:], 'tm', [(i, i + 1) for i in range(n_tm...  2.39 us
  transfers between devices with their start and end apart: 19, of which 14 were waited for; matrix products, arithmetic and copies ran while one was open for 1% of the time, Pallas kernels for 5%

profile of v3, /device:TPU:0, one launch (start us, length us, event | category | flops | bytes accessed | tf_op | source)
XLA Modules:
  0.0 81.6 jit_solution(7656616876970515064)
XLA Ops:
  1.4 2.4 %collective-permute-start = (bf16[16,512]{1,0:T(8,128)(2,1)S(1)}, bf16[16,512]{1,0:T(8,128)(2,1)S(1)}, u32[]{:S(2)}, u32[]{:S(2)}) collective-permute-start(bf16[16,512]{1,0:T(8,128)(2,1)S(1)} %slice_bitcast_fusion), channel_id=1, source_target_pairs={{0,1},{1,2},{2,3},{4,5},{5,6},{6,7},{8,9},{9,10},{10,11},{12,13},{... | collective-permute-start | bytes 49160 | tf_op jit(solution)/shard_map/ppermute | solution.py:363
  4.6 3.4 %shard_map.192 = (bf16[256,1280]{1,0:T(8,128)(2,1)S(1)}, f32[256,16]{1,0:T(8,128)S(1)}, f32[16,256]{1,0:T(8,128)S(1)}, f32[16,256]{1,0:T(8,128)S(1)}, bf16[144,1024]{1,0:T(8,128)(2,1)S(1)}) custom-call(bf16[256,512]{1,0:T(8,128)(2,1)} %bitcast.14, bf16[16,512]{1,0:T(8,128)(2,1)} %bitcast.16, f32[1,16]{1,0:T(1,128)} %bitcast.21, f32[1,16]{1,0:T(1,128)} %bitcast.22, ...), custom_call_target="tpu_custom_call" | custom-call | flops 335544320 | bytes 2621440 | tf_op jit(solution)/shard_map/pallas_call | solution.py:310
  8.0 2.7 %collective-permute-start.1 = (bf16[144,1024]{1,0:T(8,128)(2,1)S(1)}, bf16[144,1024]{1,0:T(8,128)(2,1)S(1)}, u32[]{:S(2)}, u32[]{:S(2)}) collective-permute-start(bf16[144,1024]{1,0:T(8,128)(2,1)S(1)} %get-tuple-element.17.refs_0_), channel_id=1, source_target_pairs={{0,1},{1,0},{2,3},{3,2},{4,5},{5,4},{6,7},{7,6},{8,9},{9,8},{10,11... | collective-permute-start | bytes 884744 | tf_op jit(solution)/shard_map/ppermute | solution.py:388
  12.6 4.7 %collective-permute-start.2 = (bf16[128,1024]{1,0:T(8,128)(2,1)S(1)}, bf16[128,1024]{1,0:T(8,128)(2,1)S(1)}, u32[]{:S(2)}, u32[]{:S(2)}) collective-permute-start(bf16[128,1024]{1,0:T(8,128)(2,1)S(1)} %get-tuple-element.18), channel_id=1, source_target_pairs={{0,2},{1,3},{4,6},{5,7},{8,10},{9,11},{12,14},{13,15},{16,18},{17,... | collective-permute-start | bytes 786440 | tf_op jit(solution)/shard_map/ppermute | solution.py:400
  17.9 3.8 %shard_map.194 = (f32[256,1024]{1,0:T(8,128)S(1)}, f32[256,1024]{1,0:T(8,128)S(1)}, f32[512,1024]{1,0:T(8,128)S(1)}) custom-call(bf16[256,512]{1,0:T(8,128)(2,1)} %bitcast.15, bf16[512,1024]{1,0:T(8,128)(2,1)} %refs_1_.2, bf16[512,512]{1,0:T(8,128)(2,1)} %bitcast.12, bf16[1024,1024]{1,0:T(8,128)(2,1)} %refs_3_.3, f32[16]{0:T(128)S(1)} %copy-done, ...), custom_call_target="tpu_custom_call" | custom-call | flops 1073741824 | bytes 16777216 | tf_op jit(solution)/shard_map/pallas_call | solution.py:310
  22.9 6.3 %shard_map.195 = (bf16[256,512]{1,0:T(8,128)(2,1)}, f32[1,512]{1,0:T(1,128)}, bf16[520,1024]{1,0:T(8,128)(2,1)S(1)}, bf16[520,1024]{1,0:T(8,128)(2,1)S(1)}) custom-call(f32[1,1024]{1,0:T(1,128)} %bitcast.18, bf16[1024,512]{1,0:T(8,128)(2,1)} %refs_1_.3, s32[1,512]{1,0:T(1,128)} %refs_2_.1, bf16[1024,1024]{1,0:T(8,128)(2,1)} %refs_3_.3, ...), custom_call_target="tpu_custom_call" | custom-call | flops 1073741824 | bytes 4194304 | tf_op jit(solution)/shard_map/pallas_call | solution.py:310
  29.9 2.1 %collective-permute-done.3 = bf16[256,1024]{1,0:T(8,128)(2,1)S(1)} collective-permute-done((bf16[256,1024]{1,0:T(8,128)(2,1)S(1)}, bf16[256,1024]{1,0:T(8,128)(2,1)S(1)}, u32[]{:S(2)}, u32[]{:S(2)}) %collective-permute-start.3) | collective-permute-done | bytes 524320 | tf_op jit(solution)/shard_map/ppermute | solution.py:464
  32.4 2.6 %collective-permute-start.4 = (bf16[128,1024]{1,0:T(8,128)(2,1)S(1)}, bf16[128,1024]{1,0:T(8,128)(2,1)S(1)}, u32[]{:S(2)}, u32[]{:S(2)}) collective-permute-start(bf16[128,1024]{1,0:T(8,128)(2,1)S(1)} %get-tuple-element.33), channel_id=1, source_target_pairs={{0,2},{1,5},{2,0},{3,7},{4,6},{5,1},{6,4},{7,3},{8,10},{9,13},{10,... | collective-permute-start | bytes 786440 | tf_op jit(solution)/shard_map/ppermute | solution.py:464
  35.1 4.2 %collective-permute-done.4 = bf16[128,1024]{1,0:T(8,128)(2,1)S(1)} collective-permute-done((bf16[128,1024]{1,0:T(8,128)(2,1)S(1)}, bf16[128,1024]{1,0:T(8,128)(2,1)S(1)}, u32[]{:S(2)}, u32[]{:S(2)}) %collective-permute-start.4) | collective-permute-done | bytes 262176 | tf_op jit(solution)/shard_map/ppermute | solution.py:464
  39.4 1.6 %collective-permute-start.5 = (bf16[64,1024]{1,0:T(8,128)(2,1)S(1)}, bf16[64,1024]{1,0:T(8,128)(2,1)S(1)}, u32[]{:S(2)}, u32[]{:S(2)}) collective-permute-start(bf16[64,1024]{1,0:T(8,128)(2,1)S(1)} %get-tuple-element.45), channel_id=1, source_target_pairs={{0,4},{1,9},{2,6},{3,11},{4,0},{5,13},{6,2},{7,15},{8,12},{9,1},{1... | collective-permute-start | bytes 393224 | tf_op jit(solution)/shard_map/ppermute | solution.py:464
  41.0 1.3 %collective-permute-done.12 = bf16[136,1024]{1,0:T(8,128)(2,1)S(1)} collective-permute-done((bf16[136,1024]{1,0:T(8,128)(2,1)S(1)}, bf16[136,1024]{1,0:T(8,128)(2,1)S(1)}, u32[]{:S(2)}, u32[]{:S(2)}) %collective-permute-start.12) | collective-permute-done | bytes 278560 | tf_op jit(solution)/shard_map/ppermute | solution.py:464
  42.4 1.6 %collective-permute-start.13 = (bf16[72,1024]{1,0:T(8,128)(2,1)S(1)}, bf16[72,1024]{1,0:T(8,128)(2,1)S(1)}, u32[]{:S(2)}, u32[]{:S(2)}) collective-permute-start(bf16[72,1024]{1,0:T(8,128)(2,1)S(1)} %pad_maximum_fusion.6), channel_id=1, source_target_pairs={{0,4},{1,9},{2,6},{3,11},{4,0},{5,13},{6,2},{7,15},{8,12},{9,1},{1... | collective-permute-start | bytes 442376 | tf_op jit(solution)/shard_map/ppermute | solution.py:464
  44.6 3.1 %collective-permute-start.6 = (bf16[32,1024]{1,0:T(8,128)(2,1)S(1)}, bf16[32,1024]{1,0:T(8,128)(2,1)S(1)}, u32[]{:S(2)}, u32[]{:S(2)}) collective-permute-start(bf16[32,1024]{1,0:T(8,128)(2,1)S(1)} %select_convert_fusion.10), channel_id=1, source_target_pairs={{0,8},{1,3},{2,10},{3,1},{4,12},{5,7},{6,14},{7,5},{8,0},{9,11},{1... | collective-permute-start | bytes 196616 | tf_op jit(solution)/shard_map/ppermute | solution.py:464
  48.2 2.7 %collective-permute-start.14 = (bf16[40,1024]{1,0:T(8,128)(2,1)S(1)}, bf16[40,1024]{1,0:T(8,128)(2,1)S(1)}, u32[]{:S(2)}, u32[]{:S(2)}) collective-permute-start(bf16[40,1024]{1,0:T(8,128)(2,1)S(1)} %pad_maximum_fusion.9), channel_id=1, source_target_pairs={{0,8},{1,3},{2,10},{3,1},{4,12},{5,7},{6,14},{7,5},{8,0},{9,11},{1... | collective-permute-start | bytes 245768 | tf_op jit(solution)/shard_map/ppermute | solution.py:464
  50.9 2.1 %collective-permute-start.7 = (bf16[32,1024]{1,0:T(8,128)(2,1)S(1)}, bf16[32,1024]{1,0:T(8,128)(2,1)S(1)}, u32[]{:S(2)}, u32[]{:S(2)}) collective-permute-start(bf16[32,1024]{1,0:T(8,128)(2,1)S(1)} %add_convert_fusion.1), channel_id=1, source_target_pairs={{0,8},{1,3},{2,10},{3,1},{4,12},{5,7},{6,14},{7,5},{8,0},{9,11},{1... | collective-permute-start | bytes 196616 | tf_op jit(solution)/shard_map/ppermute | solution.py:464
  53.6 2.7 %collective-permute-start.15 = (bf16[32,1024]{1,0:T(8,128)(2,1)S(1)}, bf16[32,1024]{1,0:T(8,128)(2,1)S(1)}, u32[]{:S(2)}, u32[]{:S(2)}) collective-permute-start(bf16[32,1024]{1,0:T(8,128)(2,1)S(1)} %add_convert_fusion), channel_id=1, source_target_pairs={{0,8},{1,3},{2,10},{3,1},{4,12},{5,7},{6,14},{7,5},{8,0},{9,11},{1... | collective-permute-start | bytes 196616 | tf_op jit(solution)/shard_map/ppermute | solution.py:464
  56.4 2.6 %collective-permute-start.8 = (bf16[64,1024]{1,0:T(8,128)(2,1)S(1)}, bf16[64,1024]{1,0:T(8,128)(2,1)S(1)}, u32[]{:S(2)}, u32[]{:S(2)}) collective-permute-start(bf16[64,1024]{1,0:T(8,128)(2,1)S(1)} %pad_maximum_fusion.7), channel_id=1, source_target_pairs={{0,4},{1,9},{2,6},{3,11},{4,0},{5,13},{6,2},{7,15},{8,12},{9,1},{1... | collective-permute-start | bytes 393224 | tf_op jit(solution)/shard_map/ppermute | solution.py:464
  59.0 4.1 %collective-permute-done.15 = bf16[32,1024]{1,0:T(8,128)(2,1)S(1)} collective-permute-done((bf16[32,1024]{1,0:T(8,128)(2,1)S(1)}, bf16[32,1024]{1,0:T(8,128)(2,1)S(1)}, u32[]{:S(2)}, u32[]{:S(2)}) %collective-permute-start.15) | collective-permute-done | bytes 65568 | tf_op jit(solution)/shard_map/ppermute | solution.py:464
  63.3 3.8 %collective-permute-start.9 = (bf16[128,1024]{1,0:T(8,128)(2,1)S(1)}, bf16[128,1024]{1,0:T(8,128)(2,1)S(1)}, u32[]{:S(2)}, u32[]{:S(2)}) collective-permute-start(bf16[128,1024]{1,0:T(8,128)(2,1)S(1)} %pad_maximum_fusion.4), channel_id=1, source_target_pairs={{0,2},{1,5},{2,0},{3,7},{4,6},{5,1},{6,4},{7,3},{8,10},{9,13},{10,... | collective-permute-start | bytes 786440 | tf_op jit(solution)/shard_map/ppermute | solution.py:464
  67.1 2.5 %collective-permute-done.16 = bf16[64,1024]{1,0:T(8,128)(2,1)S(1)} collective-permute-done((bf16[64,1024]{1,0:T(8,128)(2,1)S(1)}, bf16[64,1024]{1,0:T(8,128)(2,1)S(1)}, u32[]{:S(2)}, u32[]{:S(2)}) %collective-permute-start.16) | collective-permute-done | bytes 131104 | tf_op jit(solution)/shard_map/ppermute | solution.py:464
  69.7 1.6 %collective-permute-start.17 = (bf16[128,1024]{1,0:T(8,128)(2,1)S(1)}, bf16[128,1024]{1,0:T(8,128)(2,1)S(1)}, u32[]{:S(2)}, u32[]{:S(2)}) collective-permute-start(bf16[128,1024]{1,0:T(8,128)(2,1)S(1)} %pad_maximum_fusion.5), channel_id=1, source_target_pairs={{0,2},{1,5},{2,0},{3,7},{4,6},{5,1},{6,4},{7,3},{8,10},{9,13},{10,... | collective-permute-start | bytes 786440 | tf_op jit(solution)/shard_map/ppermute | solution.py:464
  71.7 4.4 %collective-permute-done.17 = bf16[128,1024]{1,0:T(8,128)(2,1)S(1)} collective-permute-done((bf16[128,1024]{1,0:T(8,128)(2,1)S(1)}, bf16[128,1024]{1,0:T(8,128)(2,1)S(1)}, u32[]{:S(2)}, u32[]{:S(2)}) %collective-permute-start.17) | collective-permute-done | bytes 262176 | tf_op jit(solution)/shard_map/ppermute | solution.py:464
  76.6 1.6 %collective-permute-done.18 = bf16[264,1024]{1,0:T(8,128)(2,1)S(1)} collective-permute-done((bf16[264,1024]{1,0:T(8,128)(2,1)S(1)}, bf16[264,1024]{1,0:T(8,128)(2,1)S(1)}, u32[]{:S(2)}, u32[]{:S(2)}) %collective-permute-start.18) | collective-permute-done | bytes 540704 | tf_op jit(solution)/shard_map/ppermute | solution.py:464
  79.1 2.5 %maximum_convert_fusion = f32[1024,1024]{1,0:T(8,128)} fusion(bf16[256,1024]{1,0:T(8,128)(2,1)S(1)} %get-tuple-element.35, bf16[256,1024]{1,0:T(8,128)(2,1)S(1)} %get-tuple-element.39, bf16[256,1024]{1,0:T(8,128)(2,1)S(1)} %get-tuple-element.34, bf16[256,1024]{1,0:T(8,128)(2,1)S(1)} %get-tuple-element.38), kind=kLoop, calls=%fused_computation | loop fusion | flops 8388608 | bytes 6291456 | tf_op jit(solution)/shard_map/concatenate | solution.py:542
  (54 shorter events, 9.7 us)
Async XLA Ops:
  0.6 17.3 %copy-start = (f32[16]{0:T(128)S(1)}, f32[16]{0:T(128)}, u32[]{:S(2)}) copy-start(f32[16]{0:T(128)} %refs_4_.3) | copy-start | bytes 196
  1.4 3.2 %collective-permute-start = (bf16[16,512]{1,0:T(8,128)(2,1)S(1)}, bf16[16,512]{1,0:T(8,128)(2,1)S(1)}, u32[]{:S(2)}, u32[]{:S(2)}) collective-permute-start(bf16[16,512]{1,0:T(8,128)(2,1)S(1)} %slice_bitcast_fusion), channel_id=1, source_target_pairs={{0,1},{1,2},{2,3},{4,5},{5,6},{6,7},{8,9},{9,10},{10,11},{12,13},{... | collective-permute-start | bytes 49160 | tf_op jit(solution)/shard_map/ppermute | solution.py:363
  8.0 3.9 %collective-permute-start.1 = (bf16[144,1024]{1,0:T(8,128)(2,1)S(1)}, bf16[144,1024]{1,0:T(8,128)(2,1)S(1)}, u32[]{:S(2)}, u32[]{:S(2)}) collective-permute-start(bf16[144,1024]{1,0:T(8,128)(2,1)S(1)} %get-tuple-element.17.refs_0_), channel_id=1, source_target_pairs={{0,1},{1,0},{2,3},{3,2},{4,5},{5,4},{6,7},{7,6},{8,9},{9,8},{10,11... | collective-permute-start | bytes 884744 | tf_op jit(solution)/shard_map/ppermute | solution.py:388
  12.6 10.3 %collective-permute-start.2 = (bf16[128,1024]{1,0:T(8,128)(2,1)S(1)}, bf16[128,1024]{1,0:T(8,128)(2,1)S(1)}, u32[]{:S(2)}, u32[]{:S(2)}) collective-permute-start(bf16[128,1024]{1,0:T(8,128)(2,1)S(1)} %get-tuple-element.18), channel_id=1, source_target_pairs={{0,2},{1,3},{4,6},{5,7},{8,10},{9,11},{12,14},{13,15},{16,18},{17,... | collective-permute-start | bytes 786440 | tf_op jit(solution)/shard_map/ppermute | solution.py:400
  29.3 2.8 %collective-permute-start.11 = (bf16[264,1024]{1,0:T(8,128)(2,1)S(1)}, bf16[264,1024]{1,0:T(8,128)(2,1)S(1)}, u32[]{:S(2)}, u32[]{:S(2)}) collective-permute-start(bf16[264,1024]{1,0:T(8,128)(2,1)S(1)} %slice.145), channel_id=1, source_target_pairs={{0,1},{1,0},{2,3},{3,2},{4,5},{5,4},{6,7},{7,6},{8,9},{9,8},{10,11... | collective-permute-start | bytes 1622024 | tf_op jit(solution)/shard_map/ppermute | solution.py:464
  29.4 2.6 %collective-permute-start.3 = (bf16[256,1024]{1,0:T(8,128)(2,1)S(1)}, bf16[256,1024]{1,0:T(8,128)(2,1)S(1)}, u32[]{:S(2)}, u32[]{:S(2)}) collective-permute-start(bf16[256,1024]{1,0:T(8,128)(2,1)S(1)} %slice.132), channel_id=1, source_target_pairs={{0,1},{1,0},{2,3},{3,2},{4,5},{5,4},{6,7},{7,6},{8,9},{9,8},{10,11... | collective-permute-start | bytes 1572872 | tf_op jit(solution)/shard_map/ppermute | solution.py:464
  32.4 6.9 %collective-permute-start.4 = (bf16[128,1024]{1,0:T(8,128)(2,1)S(1)}, bf16[128,1024]{1,0:T(8,128)(2,1)S(1)}, u32[]{:S(2)}, u32[]{:S(2)}) collective-permute-start(bf16[128,1024]{1,0:T(8,128)(2,1)S(1)} %get-tuple-element.33), channel_id=1, source_target_pairs={{0,2},{1,5},{2,0},{3,7},{4,6},{5,1},{6,4},{7,3},{8,10},{9,13},{10,... | collective-permute-start | bytes 786440 | tf_op jit(solution)/shard_map/ppermute | solution.py:464
  35.0 7.3 %collective-permute-start.12 = (bf16[136,1024]{1,0:T(8,128)(2,1)S(1)}, bf16[136,1024]{1,0:T(8,128)(2,1)S(1)}, u32[]{:S(2)}, u32[]{:S(2)}) collective-permute-start(bf16[136,1024]{1,0:T(8,128)(2,1)S(1)} %pad_maximum_fusion.3), channel_id=1, source_target_pairs={{0,2},{1,5},{2,0},{3,7},{4,6},{5,1},{6,4},{7,3},{8,10},{9,13},{10,... | collective-permute-start | bytes 835592 | tf_op jit(solution)/shard_map/ppermute | solution.py:464
  39.4 5.1 %collective-permute-start.5 = (bf16[64,1024]{1,0:T(8,128)(2,1)S(1)}, bf16[64,1024]{1,0:T(8,128)(2,1)S(1)}, u32[]{:S(2)}, u32[]{:S(2)}) collective-permute-start(bf16[64,1024]{1,0:T(8,128)(2,1)S(1)} %get-tuple-element.45), channel_id=1, source_target_pairs={{0,4},{1,9},{2,6},{3,11},{4,0},{5,13},{6,2},{7,15},{8,12},{9,1},{1... | collective-permute-start | bytes 393224 | tf_op jit(solution)/shard_map/ppermute | solution.py:464
  42.4 5.7 %collective-permute-start.13 = (bf16[72,1024]{1,0:T(8,128)(2,1)S(1)}, bf16[72,1024]{1,0:T(8,128)(2,1)S(1)}, u32[]{:S(2)}, u32[]{:S(2)}) collective-permute-start(bf16[72,1024]{1,0:T(8,128)(2,1)S(1)} %pad_maximum_fusion.6), channel_id=1, source_target_pairs={{0,4},{1,9},{2,6},{3,11},{4,0},{5,13},{6,2},{7,15},{8,12},{9,1},{1... | collective-permute-start | bytes 442376 | tf_op jit(solution)/shard_map/ppermute | solution.py:464
  44.6 6.3 %collective-permute-start.6 = (bf16[32,1024]{1,0:T(8,128)(2,1)S(1)}, bf16[32,1024]{1,0:T(8,128)(2,1)S(1)}, u32[]{:S(2)}, u32[]{:S(2)}) collective-permute-start(bf16[32,1024]{1,0:T(8,128)(2,1)S(1)} %select_convert_fusion.10), channel_id=1, source_target_pairs={{0,8},{1,3},{2,10},{3,1},{4,12},{5,7},{6,14},{7,5},{8,0},{9,11},{1... | collective-permute-start | bytes 196616 | tf_op jit(solution)/shard_map/ppermute | solution.py:464
  48.2 5.4 %collective-permute-start.14 = (bf16[40,1024]{1,0:T(8,128)(2,1)S(1)}, bf16[40,1024]{1,0:T(8,128)(2,1)S(1)}, u32[]{:S(2)}, u32[]{:S(2)}) collective-permute-start(bf16[40,1024]{1,0:T(8,128)(2,1)S(1)} %pad_maximum_fusion.9), channel_id=1, source_target_pairs={{0,8},{1,3},{2,10},{3,1},{4,12},{5,7},{6,14},{7,5},{8,0},{9,11},{1... | collective-permute-start | bytes 245768 | tf_op jit(solution)/shard_map/ppermute | solution.py:464
  50.9 5.4 %collective-permute-start.7 = (bf16[32,1024]{1,0:T(8,128)(2,1)S(1)}, bf16[32,1024]{1,0:T(8,128)(2,1)S(1)}, u32[]{:S(2)}, u32[]{:S(2)}) collective-permute-start(bf16[32,1024]{1,0:T(8,128)(2,1)S(1)} %add_convert_fusion.1), channel_id=1, source_target_pairs={{0,8},{1,3},{2,10},{3,1},{4,12},{5,7},{6,14},{7,5},{8,0},{9,11},{1... | collective-permute-start | bytes 196616 | tf_op jit(solution)/shard_map/ppermute | solution.py:464
  53.6 9.5 %collective-permute-start.15 = (bf16[32,1024]{1,0:T(8,128)(2,1)S(1)}, bf16[32,1024]{1,0:T(8,128)(2,1)S(1)}, u32[]{:S(2)}, u32[]{:S(2)}) collective-permute-start(bf16[32,1024]{1,0:T(8,128)(2,1)S(1)} %add_convert_fusion), channel_id=1, source_target_pairs={{0,8},{1,3},{2,10},{3,1},{4,12},{5,7},{6,14},{7,5},{8,0},{9,11},{1... | collective-permute-start | bytes 196616 | tf_op jit(solution)/shard_map/ppermute | solution.py:464
  56.4 6.8 %collective-permute-start.8 = (bf16[64,1024]{1,0:T(8,128)(2,1)S(1)}, bf16[64,1024]{1,0:T(8,128)(2,1)S(1)}, u32[]{:S(2)}, u32[]{:S(2)}) collective-permute-start(bf16[64,1024]{1,0:T(8,128)(2,1)S(1)} %pad_maximum_fusion.7), channel_id=1, source_target_pairs={{0,4},{1,9},{2,6},{3,11},{4,0},{5,13},{6,2},{7,15},{8,12},{9,1},{1... | collective-permute-start | bytes 393224 | tf_op jit(solution)/shard_map/ppermute | solution.py:464
  63.1 6.4 %collective-permute-start.16 = (bf16[64,1024]{1,0:T(8,128)(2,1)S(1)}, bf16[64,1024]{1,0:T(8,128)(2,1)S(1)}, u32[]{:S(2)}, u32[]{:S(2)}) collective-permute-start(bf16[64,1024]{1,0:T(8,128)(2,1)S(1)} %pad_maximum_fusion.8), channel_id=1, source_target_pairs={{0,4},{1,9},{2,6},{3,11},{4,0},{5,13},{6,2},{7,15},{8,12},{9,1},{1... | collective-permute-start | bytes 393224 | tf_op jit(solution)/shard_map/ppermute | solution.py:464
  63.3 8.2 %collective-permute-start.9 = (bf16[128,1024]{1,0:T(8,128)(2,1)S(1)}, bf16[128,1024]{1,0:T(8,128)(2,1)S(1)}, u32[]{:S(2)}, u32[]{:S(2)}) collective-permute-start(bf16[128,1024]{1,0:T(8,128)(2,1)S(1)} %pad_maximum_fusion.4), channel_id=1, source_target_pairs={{0,2},{1,5},{2,0},{3,7},{4,6},{5,1},{6,4},{7,3},{8,10},{9,13},{10,... | collective-permute-start | bytes 786440 | tf_op jit(solution)/shard_map/ppermute | solution.py:464
  69.7 6.4 %collective-permute-start.17 = (bf16[128,1024]{1,0:T(8,128)(2,1)S(1)}, bf16[128,1024]{1,0:T(8,128)(2,1)S(1)}, u32[]{:S(2)}, u32[]{:S(2)}) collective-permute-start(bf16[128,1024]{1,0:T(8,128)(2,1)S(1)} %pad_maximum_fusion.5), channel_id=1, source_target_pairs={{0,2},{1,5},{2,0},{3,7},{4,6},{5,1},{6,4},{7,3},{8,10},{9,13},{10,... | collective-permute-start | bytes 786440 | tf_op jit(solution)/shard_map/ppermute | solution.py:464
  71.6 4.7 %collective-permute-start.10 = (bf16[256,1024]{1,0:T(8,128)(2,1)S(1)}, bf16[256,1024]{1,0:T(8,128)(2,1)S(1)}, u32[]{:S(2)}, u32[]{:S(2)}) collective-permute-start(bf16[256,1024]{1,0:T(8,128)(2,1)S(1)} %pad_maximum_fusion.1), channel_id=1, source_target_pairs={{0,1},{1,0},{2,3},{3,2},{4,5},{5,4},{6,7},{7,6},{8,9},{9,8},{10,11... | collective-permute-start | bytes 1572872 | tf_op jit(solution)/shard_map/ppermute | solution.py:464
  76.3 2.0 %collective-permute-start.18 = (bf16[264,1024]{1,0:T(8,128)(2,1)S(1)}, bf16[264,1024]{1,0:T(8,128)(2,1)S(1)}, u32[]{:S(2)}, u32[]{:S(2)}) collective-permute-start(bf16[264,1024]{1,0:T(8,128)(2,1)S(1)} %pad_maximum_fusion), channel_id=1, source_target_pairs={{0,1},{1,0},{2,3},{3,2},{4,5},{5,4},{6,7},{7,6},{8,9},{9,8},{10,11... | collective-permute-start | bytes 1622024 | tf_op jit(solution)/shard_map/ppermute | solution.py:464

commit v4 on v3

--- a/solution.py
+++ b/solution.py
@@ -58,7 +58,8 @@
     state = (width - inner) // 2
     head_size = inner // heads
     per = LANES // head_size
-    rows = jnp.concatenate([halo[...], hist[...]], axis=0)
+    before = jnp.where(lax.axis_index("tm") == 0, 0.0, halo[...].astype(F32)).astype(BF16)
+    rows = jnp.concatenate([before, hist[...]], axis=0)
 
     v = dot_nt(hist[...], dtw[...]) + dtb[...]
     dt = jnp.maximum(v, 0.0) + jnp.log1p(jnp.exp(-jnp.abs(v)))
@@ -201,7 +202,7 @@
     tm = lax.axis_index("tm")
     odd = lax.rem(tm, 2) == 1
     base = tm * length
-    arrived = incoming[...].astype(F32)
+    arrived = jnp.where(tm < 2, 0.0, incoming[...].astype(F32))
     enter = jnp.where(
         odd, arrived * gain_row(other, state) + other[:state, :].astype(F32), arrived
     )
@@ -360,7 +361,7 @@
     tm = lax.axis_index("tm")
     user = lax.axis_index("user")
 
-    halo = lax.ppermute(hist[length - ALIGN :], "tm", [(i, i + 1) for i in range(n_tm - 1)])
+    halo = lax.ppermute(hist[length - ALIGN :], "tm", [(i, (i + 1) % n_tm) for i in range(n_tm)])
     xbc, cum, dt_t, cum_t, pay = call(
         functools.partial(scan_kernel, heads),
         (
@@ -396,10 +397,11 @@
         6 * state * inner,
         6,
     )
-    onward = [(i, i + 2) for i in range(n_tm - 2)]
+    onward = [(i, (i + 2) % n_tm) for i in range(n_tm)]
     incoming = lax.ppermute(chip_state, "tm", onward)
     for _ in range(chips - 2):
-        passed = chip_gain[0:1] * incoming.astype(F32) + chip_state.astype(F32)
+        incoming = jnp.where(tm < 2, 0.0, incoming.astype(F32))
+        passed = chip_gain[0:1] * incoming + chip_state.astype(F32)
         incoming = lax.ppermute(passed.astype(BF16), "tm", onward)
     part, gate, pre = call(
         functools.partial(within_kernel, heads),
@@ -504,7 +506,7 @@
         if has_extra:
             extra = (stay[size:].astype(F32) + got[size:].astype(F32)).astype(BF16)
         state.append((stay[:size], got[:size], extra))
-    for level in range(levels):
+    for level in range(levels - 1):
         size //= 2
         after = []
         for a, b, extra in state:
@@ -519,8 +521,17 @@
                 extra = (extra.astype(F32) + got[size:].astype(F32)).astype(BF16)
             after.append((stay, got[:size], extra))
         state = after
-    wholes = [((a.astype(F32) + b.astype(F32)).astype(BF16), extra) for a, b, extra in state]
-    for level in reversed(range(levels)):
+    wholes = []
+    for a, b, extra in state:
+        whole = (a.astype(F32) + b.astype(F32)).astype(BF16)
+        if levels:
+            leave = whole if extra is None else jnp.concatenate([whole, extra], axis=0)
+            got = swap(leave, partner_of(levels - 1))
+            whole = (whole.astype(F32) + got[:size].astype(F32)).astype(BF16)
+            if extra is not None:
+                extra = (extra.astype(F32) + got[size:].astype(F32)).astype(BF16)
+        wholes.append((whole, extra))
+    for level in reversed(range(levels - 1)):
         after = []
         for whole, extra in wholes:
             got = swap(whole, partner_of(level))

time: 82 us -> 75.5 us (0.921)
  starting transfers between devices: 35 us -> 23.2 us
  waiting for transfers between devices: 25.1 us -> 30.6 us
    ppermute x16 -> x14, starting transfers between devices: 25.3 us -> 20.1 us  [swap(): return lax.ppermute(value, axes, pairs)]
    ppermute x1, waiting for transfers between devices: 0.82 us -> 3.33 us  [body(): lax.ppermute(hist[length - ALIGN:], 'tm', [(i, (i + 1) % n_tm) for i in r...]
    ppermute x1, starting transfers between devices: 2.69 us -> 0.19 us  [body(): other = lax.ppermute(pay, 'tm', [(i, i ^ 1) for i in range(n_tm)])]
    ppermute x1, starting transfers between devices: 4.67 us -> 2.37 us  [body(): incoming = lax.ppermute(chip_state, 'tm', onward)]
    ppermute x1, starting transfers between devices: 2.39 us -> 0.49 us  [body(): lax.ppermute(hist[length - ALIGN:], 'tm', [(i, (i + 1) % n_tm) for i in r...]
    ppermute x16 -> x14, waiting for transfers between devices: 21.9 us -> 23.7 us  [swap(): return lax.ppermute(value, axes, pairs)]
    ppermute x1, waiting for transfers between devices: 1.18 us -> 2.13 us  [body(): incoming = lax.ppermute(chip_state, 'tm', onward)]
  transfers between devices with their start and end apart: 19 -> 17, of which waited for: 14 -> 12; matrix products, arithmetic and copies ran while one was open for 1% -> 2% of each run, Pallas kernels for 5% -> 5%
where the time goes in v4:
time: 75.5 us; the launch traced here: 75.2 us
  waiting for transfers between devices  30.6 us (41%)
  starting transfers between devices  23.2 us (31%)
  Pallas kernels  14.2 us (19%)
  other arithmetic  4.89 us (6%)
  between operations  1.54 us (2%)
  local copies, waits for them, and re-layouts  0.8 us (1%)
    ppermute x14, waiting for transfers between devices, swap(): return lax.ppermute(value, axes, pairs)  23.7 us
    ppermute x14, starting transfers between devices, swap(): return lax.ppermute(value, axes, pairs)  20.1 us
    pallas_call x4, Pallas kernels, call(): pl.pallas_call(loading(kernel, len(loaded), len(given), len(out_shape), w...  14.2 us
    ppermute x1, waiting for transfers between devices, body(): lax.ppermute(hist[length - ALIGN:], 'tm', [(i, (i + 1) % n_tm) for i in r...  3.33 us
    concatenate x1, other arithmetic, total_sum(): return (jnp.concatenate(tops + bottoms, axis=0), grad_second)  2.52 us
    ppermute x1, starting transfers between devices, body(): incoming = lax.ppermute(chip_state, 'tm', onward)  2.37 us
    ppermute x1, waiting for transfers between devices, body(): incoming = lax.ppermute(chip_state, 'tm', onward)  2.13 us
  transfers between devices with their start and end apart: 17, of which 12 were waited for; matrix products, arithmetic and copies ran while one was open for 2% of the time, Pallas kernels for 5%

profile of v4, /device:TPU:0, one launch (start us, length us, event | category | flops | bytes accessed | tf_op | source)
XLA Modules:
  0.0 75.2 jit_solution(8334440873156395734)
XLA Ops:
  1.9 3.3 %collective-permute-done.refs_7_ = bf16[16,512]{1,0:T(8,128)(2,1)S(1)} collective-permute-done((bf16[16,512]{1,0:T(8,128)(2,1)S(1)}, bf16[16,512]{1,0:T(8,128)(2,1)S(1)}, u32[]{:S(2)}, u32[]{:S(2)}) %collective-permute-start) | collective-permute-done | bytes 16416 | tf_op jit(solution)/shard_map/ppermute | solution.py:364
  5.2 3.4 %shard_map.192 = (bf16[256,1280]{1,0:T(8,128)(2,1)S(1)}, f32[256,16]{1,0:T(8,128)S(1)}, f32[16,256]{1,0:T(8,128)S(1)}, f32[16,256]{1,0:T(8,128)S(1)}, bf16[144,1024]{1,0:T(8,128)(2,1)S(1)}) custom-call(bf16[256,512]{1,0:T(8,128)(2,1)} %bitcast.14, bf16[16,512]{1,0:T(8,128)(2,1)} %bitcast.16, f32[1,16]{1,0:T(1,128)} %bitcast.21, f32[1,16]{1,0:T(1,128)} %bitcast.22, ...), custom_call_target="tpu_custom_call" | custom-call | flops 335544320 | bytes 2621440 | tf_op jit(solution)/shard_map/pallas_call | solution.py:311
  8.8 1.5 %collective-permute-done.1.refs_1_.refs_9_ = bf16[144,1024]{1,0:T(8,128)(2,1)S(1)} collective-permute-done((bf16[144,1024]{1,0:T(8,128)(2,1)S(1)}, bf16[144,1024]{1,0:T(8,128)(2,1)S(1)}, u32[]{:S(2)}, u32[]{:S(2)}) %collective-permute-start.1) | collective-permute-done | bytes 294944 | tf_op jit(solution)/shard_map/ppermute | solution.py:389
  10.9 2.4 %collective-permute-start.2 = (bf16[128,1024]{1,0:T(8,128)(2,1)S(1)}, bf16[128,1024]{1,0:T(8,128)(2,1)S(1)}, u32[]{:S(2)}, u32[]{:S(2)}) collective-permute-start(bf16[128,1024]{1,0:T(8,128)(2,1)S(1)} %get-tuple-element.18), channel_id=1, source_target_pairs={{0,2},{1,3},{2,0},{3,1},{4,6},{5,7},{6,4},{7,5},{8,10},{9,11},{10,... | collective-permute-start | bytes 786440 | tf_op jit(solution)/shard_map/ppermute | solution.py:401
  14.0 3.8 %shard_map.194 = (f32[256,1024]{1,0:T(8,128)S(1)}, f32[256,1024]{1,0:T(8,128)S(1)}, f32[512,1024]{1,0:T(8,128)S(1)}) custom-call(bf16[256,512]{1,0:T(8,128)(2,1)} %bitcast.15, bf16[512,1024]{1,0:T(8,128)(2,1)} %refs_1_.2, bf16[512,512]{1,0:T(8,128)(2,1)} %bitcast.12, bf16[1024,1024]{1,0:T(8,128)(2,1)} %refs_3_.3, f32[16]{0:T(128)S(1)} %copy-done, ...), custom_call_target="tpu_custom_call" | custom-call | flops 1073741824 | bytes 16777216 | tf_op jit(solution)/shard_map/pallas_call | solution.py:311
  17.8 2.1 %collective-permute-done.2.refs_8_ = bf16[128,1024]{1,0:T(8,128)(2,1)S(1)} collective-permute-done((bf16[128,1024]{1,0:T(8,128)(2,1)S(1)}, bf16[128,1024]{1,0:T(8,128)(2,1)S(1)}, u32[]{:S(2)}, u32[]{:S(2)}) %collective-permute-start.2) | collective-permute-done | bytes 262176 | tf_op jit(solution)/shard_map/ppermute | solution.py:401
  19.9 6.3 %shard_map.195 = (bf16[256,512]{1,0:T(8,128)(2,1)}, f32[1,512]{1,0:T(1,128)}, bf16[520,1024]{1,0:T(8,128)(2,1)S(1)}, bf16[520,1024]{1,0:T(8,128)(2,1)S(1)}) custom-call(f32[1,1024]{1,0:T(1,128)} %bitcast.18, bf16[1024,512]{1,0:T(8,128)(2,1)} %refs_1_.3, s32[1,512]{1,0:T(1,128)} %refs_2_.1, bf16[1024,1024]{1,0:T(8,128)(2,1)} %refs_3_.3, ...), custom_call_target="tpu_custom_call" | custom-call | flops 1073741824 | bytes 4194304 | tf_op jit(solution)/shard_map/pallas_call | solution.py:311
  27.0 2.1 %collective-permute-done.3 = bf16[256,1024]{1,0:T(8,128)(2,1)S(1)} collective-permute-done((bf16[256,1024]{1,0:T(8,128)(2,1)S(1)}, bf16[256,1024]{1,0:T(8,128)(2,1)S(1)}, u32[]{:S(2)}, u32[]{:S(2)}) %collective-permute-start.3) | collective-permute-done | bytes 524320 | tf_op jit(solution)/shard_map/ppermute | solution.py:466
  29.5 1.8 %collective-permute-start.4 = (bf16[128,1024]{1,0:T(8,128)(2,1)S(1)}, bf16[128,1024]{1,0:T(8,128)(2,1)S(1)}, u32[]{:S(2)}, u32[]{:S(2)}) collective-permute-start(bf16[128,1024]{1,0:T(8,128)(2,1)S(1)} %get-tuple-element.33), channel_id=1, source_target_pairs={{0,2},{1,5},{2,0},{3,7},{4,6},{5,1},{6,4},{7,3},{8,10},{9,13},{10,... | collective-permute-start | bytes 786440 | tf_op jit(solution)/shard_map/ppermute | solution.py:466
  31.6 4.2 %collective-permute-done.4 = bf16[128,1024]{1,0:T(8,128)(2,1)S(1)} collective-permute-done((bf16[128,1024]{1,0:T(8,128)(2,1)S(1)}, bf16[128,1024]{1,0:T(8,128)(2,1)S(1)}, u32[]{:S(2)}, u32[]{:S(2)}) %collective-permute-start.4) | collective-permute-done | bytes 262176 | tf_op jit(solution)/shard_map/ppermute | solution.py:466
  36.0 1.9 %collective-permute-start.5 = (bf16[64,1024]{1,0:T(8,128)(2,1)S(1)}, bf16[64,1024]{1,0:T(8,128)(2,1)S(1)}, u32[]{:S(2)}, u32[]{:S(2)}) collective-permute-start(bf16[64,1024]{1,0:T(8,128)(2,1)S(1)} %select_convert_fusion.6), channel_id=1, source_target_pairs={{0,4},{1,9},{2,6},{3,11},{4,0},{5,13},{6,2},{7,15},{8,12},{9,1},{1... | collective-permute-start | bytes 393224 | tf_op jit(solution)/shard_map/ppermute | solution.py:466
  37.8 1.0 %collective-permute-done.11 = bf16[136,1024]{1,0:T(8,128)(2,1)S(1)} collective-permute-done((bf16[136,1024]{1,0:T(8,128)(2,1)S(1)}, bf16[136,1024]{1,0:T(8,128)(2,1)S(1)}, u32[]{:S(2)}, u32[]{:S(2)}) %collective-permute-start.11) | collective-permute-done | bytes 278560 | tf_op jit(solution)/shard_map/ppermute | solution.py:466
  39.0 1.9 %collective-permute-start.12 = (bf16[72,1024]{1,0:T(8,128)(2,1)S(1)}, bf16[72,1024]{1,0:T(8,128)(2,1)S(1)}, u32[]{:S(2)}, u32[]{:S(2)}) collective-permute-start(bf16[72,1024]{1,0:T(8,128)(2,1)S(1)} %pad_maximum_fusion.6), channel_id=1, source_target_pairs={{0,4},{1,9},{2,6},{3,11},{4,0},{5,13},{6,2},{7,15},{8,12},{9,1},{1... | collective-permute-start | bytes 442376 | tf_op jit(solution)/shard_map/ppermute | solution.py:466
  41.9 2.5 %collective-permute-start.6 = (bf16[64,1024]{1,0:T(8,128)(2,1)S(1)}, bf16[64,1024]{1,0:T(8,128)(2,1)S(1)}, u32[]{:S(2)}, u32[]{:S(2)}) collective-permute-start(bf16[64,1024]{1,0:T(8,128)(2,1)S(1)} %add_convert_fusion.3), channel_id=1, source_target_pairs={{0,8},{1,3},{2,10},{3,1},{4,12},{5,7},{6,14},{7,5},{8,0},{9,11},{1... | collective-permute-start | bytes 393224 | tf_op jit(solution)/shard_map/ppermute | solution.py:466
  45.1 2.7 %collective-permute-start.13 = (bf16[72,1024]{1,0:T(8,128)(2,1)S(1)}, bf16[72,1024]{1,0:T(8,128)(2,1)S(1)}, u32[]{:S(2)}, u32[]{:S(2)}) collective-permute-start(bf16[72,1024]{1,0:T(8,128)(2,1)S(1)} %pad_maximum_fusion.7), channel_id=1, source_target_pairs={{0,8},{1,3},{2,10},{3,1},{4,12},{5,7},{6,14},{7,5},{8,0},{9,11},{1... | collective-permute-start | bytes 442376 | tf_op jit(solution)/shard_map/ppermute | solution.py:466
  47.9 2.5 %collective-permute-start.7 = (bf16[64,1024]{1,0:T(8,128)(2,1)S(1)}, bf16[64,1024]{1,0:T(8,128)(2,1)S(1)}, u32[]{:S(2)}, u32[]{:S(2)}) collective-permute-start(bf16[64,1024]{1,0:T(8,128)(2,1)S(1)} %add_convert_fusion.2), channel_id=1, source_target_pairs={{0,4},{1,9},{2,6},{3,11},{4,0},{5,13},{6,2},{7,15},{8,12},{9,1},{1... | collective-permute-start | bytes 393224 | tf_op jit(solution)/shard_map/ppermute | solution.py:466
  50.4 6.3 %collective-permute-done.13 = bf16[72,1024]{1,0:T(8,128)(2,1)S(1)} collective-permute-done((bf16[72,1024]{1,0:T(8,128)(2,1)S(1)}, bf16[72,1024]{1,0:T(8,128)(2,1)S(1)}, u32[]{:S(2)}, u32[]{:S(2)}) %collective-permute-start.13) | collective-permute-done | bytes 147488 | tf_op jit(solution)/shard_map/ppermute | solution.py:466
  56.7 1.1 %collective-permute-start.14 = (bf16[64,1024]{1,0:T(8,128)(2,1)S(1)}, bf16[64,1024]{1,0:T(8,128)(2,1)S(1)}, u32[]{:S(2)}, u32[]{:S(2)}) collective-permute-start(bf16[64,1024]{1,0:T(8,128)(2,1)S(1)} %add_convert_fusion), channel_id=1, source_target_pairs={{0,4},{1,9},{2,6},{3,11},{4,0},{5,13},{6,2},{7,15},{8,12},{9,1},{1... | collective-permute-start | bytes 393224 | tf_op jit(solution)/shard_map/ppermute | solution.py:466
  57.9 2.5 %collective-permute-start.8 = (bf16[128,1024]{1,0:T(8,128)(2,1)S(1)}, bf16[128,1024]{1,0:T(8,128)(2,1)S(1)}, u32[]{:S(2)}, u32[]{:S(2)}) collective-permute-start(bf16[128,1024]{1,0:T(8,128)(2,1)S(1)} %pad_maximum_fusion.4), channel_id=1, source_target_pairs={{0,2},{1,5},{2,0},{3,7},{4,6},{5,1},{6,4},{7,3},{8,10},{9,13},{10,... | collective-permute-start | bytes 786440 | tf_op jit(solution)/shard_map/ppermute | solution.py:466
  60.4 2.8 %collective-permute-done.14 = bf16[64,1024]{1,0:T(8,128)(2,1)S(1)} collective-permute-done((bf16[64,1024]{1,0:T(8,128)(2,1)S(1)}, bf16[64,1024]{1,0:T(8,128)(2,1)S(1)}, u32[]{:S(2)}, u32[]{:S(2)}) %collective-permute-start.14) | collective-permute-done | bytes 131104 | tf_op jit(solution)/shard_map/ppermute | solution.py:466
  63.2 2.1 %collective-permute-start.15 = (bf16[128,1024]{1,0:T(8,128)(2,1)S(1)}, bf16[128,1024]{1,0:T(8,128)(2,1)S(1)}, u32[]{:S(2)}, u32[]{:S(2)}) collective-permute-start(bf16[128,1024]{1,0:T(8,128)(2,1)S(1)} %pad_maximum_fusion.5), channel_id=1, source_target_pairs={{0,2},{1,5},{2,0},{3,7},{4,6},{5,1},{6,4},{7,3},{8,10},{9,13},{10,... | collective-permute-start | bytes 786440 | tf_op jit(solution)/shard_map/ppermute | solution.py:466
  65.6 4.1 %collective-permute-done.15 = bf16[128,1024]{1,0:T(8,128)(2,1)S(1)} collective-permute-done((bf16[128,1024]{1,0:T(8,128)(2,1)S(1)}, bf16[128,1024]{1,0:T(8,128)(2,1)S(1)}, u32[]{:S(2)}, u32[]{:S(2)}) %collective-permute-start.15) | collective-permute-done | bytes 262176 | tf_op jit(solution)/shard_map/ppermute | solution.py:466
  70.2 1.6 %collective-permute-done.16 = bf16[264,1024]{1,0:T(8,128)(2,1)S(1)} collective-permute-done((bf16[264,1024]{1,0:T(8,128)(2,1)S(1)}, bf16[264,1024]{1,0:T(8,128)(2,1)S(1)}, u32[]{:S(2)}, u32[]{:S(2)}) %collective-permute-start.16) | collective-permute-done | bytes 540704 | tf_op jit(solution)/shard_map/ppermute | solution.py:466
  72.7 2.5 %maximum_convert_fusion = f32[1024,1024]{1,0:T(8,128)} fusion(bf16[256,1024]{1,0:T(8,128)(2,1)S(1)} %get-tuple-element.35, bf16[256,1024]{1,0:T(8,128)(2,1)S(1)} %get-tuple-element.39, bf16[256,1024]{1,0:T(8,128)(2,1)S(1)} %get-tuple-element.34, bf16[256,1024]{1,0:T(8,128)(2,1)S(1)} %get-tuple-element.38), kind=kLoop, calls=%fused_computation | loop fusion | flops 8388608 | bytes 6291456 | tf_op jit(solution)/shard_map/concatenate | solution.py:553
  (46 shorter events, 7.1 us)
Async XLA Ops:
  0.6 13.3 %copy-start = (f32[16]{0:T(128)S(1)}, f32[16]{0:T(128)}, u32[]{:S(2)}) copy-start(f32[16]{0:T(128)} %refs_4_.3) | copy-start | bytes 196
  1.4 3.8 %collective-permute-start = (bf16[16,512]{1,0:T(8,128)(2,1)S(1)}, bf16[16,512]{1,0:T(8,128)(2,1)S(1)}, u32[]{:S(2)}, u32[]{:S(2)}) collective-permute-start(bf16[16,512]{1,0:T(8,128)(2,1)S(1)} %slice_bitcast_fusion), channel_id=1, source_target_pairs={{0,1},{1,2},{2,3},{3,0},{4,5},{5,6},{6,7},{7,4},{8,9},{9,10},{10,1... | collective-permute-start | bytes 49160 | tf_op jit(solution)/shard_map/ppermute | solution.py:364
  8.6 1.6 %collective-permute-start.1 = (bf16[144,1024]{1,0:T(8,128)(2,1)S(1)}, bf16[144,1024]{1,0:T(8,128)(2,1)S(1)}, u32[]{:S(2)}, u32[]{:S(2)}) collective-permute-start(bf16[144,1024]{1,0:T(8,128)(2,1)S(1)} %get-tuple-element.17.refs_0_), channel_id=1, source_target_pairs={{0,1},{1,0},{2,3},{3,2},{4,5},{5,4},{6,7},{7,6},{8,9},{9,8},{10,11... | collective-permute-start | bytes 884744 | tf_op jit(solution)/shard_map/ppermute | solution.py:389
  10.9 9.0 %collective-permute-start.2 = (bf16[128,1024]{1,0:T(8,128)(2,1)S(1)}, bf16[128,1024]{1,0:T(8,128)(2,1)S(1)}, u32[]{:S(2)}, u32[]{:S(2)}) collective-permute-start(bf16[128,1024]{1,0:T(8,128)(2,1)S(1)} %get-tuple-element.18), channel_id=1, source_target_pairs={{0,2},{1,3},{2,0},{3,1},{4,6},{5,7},{6,4},{7,5},{8,10},{9,11},{10,... | collective-permute-start | bytes 786440 | tf_op jit(solution)/shard_map/ppermute | solution.py:401
  26.3 2.8 %collective-permute-start.10 = (bf16[264,1024]{1,0:T(8,128)(2,1)S(1)}, bf16[264,1024]{1,0:T(8,128)(2,1)S(1)}, u32[]{:S(2)}, u32[]{:S(2)}) collective-permute-start(bf16[264,1024]{1,0:T(8,128)(2,1)S(1)} %slice.117), channel_id=1, source_target_pairs={{0,1},{1,0},{2,3},{3,2},{4,5},{5,4},{6,7},{7,6},{8,9},{9,8},{10,11... | collective-permute-start | bytes 1622024 | tf_op jit(solution)/shard_map/ppermute | solution.py:466
  26.4 2.6 %collective-permute-start.3 = (bf16[256,1024]{1,0:T(8,128)(2,1)S(1)}, bf16[256,1024]{1,0:T(8,128)(2,1)S(1)}, u32[]{:S(2)}, u32[]{:S(2)}) collective-permute-start(bf16[256,1024]{1,0:T(8,128)(2,1)S(1)} %slice.108), channel_id=1, source_target_pairs={{0,1},{1,0},{2,3},{3,2},{4,5},{5,4},{6,7},{7,6},{8,9},{9,8},{10,11... | collective-permute-start | bytes 1572872 | tf_op jit(solution)/shard_map/ppermute | solution.py:466
  29.5 6.4 %collective-permute-start.4 = (bf16[128,1024]{1,0:T(8,128)(2,1)S(1)}, bf16[128,1024]{1,0:T(8,128)(2,1)S(1)}, u32[]{:S(2)}, u32[]{:S(2)}) collective-permute-start(bf16[128,1024]{1,0:T(8,128)(2,1)S(1)} %get-tuple-element.33), channel_id=1, source_target_pairs={{0,2},{1,5},{2,0},{3,7},{4,6},{5,1},{6,4},{7,3},{8,10},{9,13},{10,... | collective-permute-start | bytes 786440 | tf_op jit(solution)/shard_map/ppermute | solution.py:466
  31.3 7.6 %collective-permute-start.11 = (bf16[136,1024]{1,0:T(8,128)(2,1)S(1)}, bf16[136,1024]{1,0:T(8,128)(2,1)S(1)}, u32[]{:S(2)}, u32[]{:S(2)}) collective-permute-start(bf16[136,1024]{1,0:T(8,128)(2,1)S(1)} %pad_maximum_fusion.3), channel_id=1, source_target_pairs={{0,2},{1,5},{2,0},{3,7},{4,6},{5,1},{6,4},{7,3},{8,10},{9,13},{10,... | collective-permute-start | bytes 835592 | tf_op jit(solution)/shard_map/ppermute | solution.py:466
  36.0 5.8 %collective-permute-start.5 = (bf16[64,1024]{1,0:T(8,128)(2,1)S(1)}, bf16[64,1024]{1,0:T(8,128)(2,1)S(1)}, u32[]{:S(2)}, u32[]{:S(2)}) collective-permute-start(bf16[64,1024]{1,0:T(8,128)(2,1)S(1)} %select_convert_fusion.6), channel_id=1, source_target_pairs={{0,4},{1,9},{2,6},{3,11},{4,0},{5,13},{6,2},{7,15},{8,12},{9,1},{1... | collective-permute-start | bytes 393224 | tf_op jit(solution)/shard_map/ppermute | solution.py:466
  39.0 6.0 %collective-permute-start.12 = (bf16[72,1024]{1,0:T(8,128)(2,1)S(1)}, bf16[72,1024]{1,0:T(8,128)(2,1)S(1)}, u32[]{:S(2)}, u32[]{:S(2)}) collective-permute-start(bf16[72,1024]{1,0:T(8,128)(2,1)S(1)} %pad_maximum_fusion.6), channel_id=1, source_target_pairs={{0,4},{1,9},{2,6},{3,11},{4,0},{5,13},{6,2},{7,15},{8,12},{9,1},{1... | collective-permute-start | bytes 442376 | tf_op jit(solution)/shard_map/ppermute | solution.py:466
  41.9 5.9 %collective-permute-start.6 = (bf16[64,1024]{1,0:T(8,128)(2,1)S(1)}, bf16[64,1024]{1,0:T(8,128)(2,1)S(1)}, u32[]{:S(2)}, u32[]{:S(2)}) collective-permute-start(bf16[64,1024]{1,0:T(8,128)(2,1)S(1)} %add_convert_fusion.3), channel_id=1, source_target_pairs={{0,8},{1,3},{2,10},{3,1},{4,12},{5,7},{6,14},{7,5},{8,0},{9,11},{1... | collective-permute-start | bytes 393224 | tf_op jit(solution)/shard_map/ppermute | solution.py:466
  45.1 11.6 %collective-permute-start.13 = (bf16[72,1024]{1,0:T(8,128)(2,1)S(1)}, bf16[72,1024]{1,0:T(8,128)(2,1)S(1)}, u32[]{:S(2)}, u32[]{:S(2)}) collective-permute-start(bf16[72,1024]{1,0:T(8,128)(2,1)S(1)} %pad_maximum_fusion.7), channel_id=1, source_target_pairs={{0,8},{1,3},{2,10},{3,1},{4,12},{5,7},{6,14},{7,5},{8,0},{9,11},{1... | collective-permute-start | bytes 442376 | tf_op jit(solution)/shard_map/ppermute | solution.py:466
  47.9 10.0 %collective-permute-start.7 = (bf16[64,1024]{1,0:T(8,128)(2,1)S(1)}, bf16[64,1024]{1,0:T(8,128)(2,1)S(1)}, u32[]{:S(2)}, u32[]{:S(2)}) collective-permute-start(bf16[64,1024]{1,0:T(8,128)(2,1)S(1)} %add_convert_fusion.2), channel_id=1, source_target_pairs={{0,4},{1,9},{2,6},{3,11},{4,0},{5,13},{6,2},{7,15},{8,12},{9,1},{1... | collective-permute-start | bytes 393224 | tf_op jit(solution)/shard_map/ppermute | solution.py:466
  56.7 6.4 %collective-permute-start.14 = (bf16[64,1024]{1,0:T(8,128)(2,1)S(1)}, bf16[64,1024]{1,0:T(8,128)(2,1)S(1)}, u32[]{:S(2)}, u32[]{:S(2)}) collective-permute-start(bf16[64,1024]{1,0:T(8,128)(2,1)S(1)} %add_convert_fusion), channel_id=1, source_target_pairs={{0,4},{1,9},{2,6},{3,11},{4,0},{5,13},{6,2},{7,15},{8,12},{9,1},{1... | collective-permute-start | bytes 393224 | tf_op jit(solution)/shard_map/ppermute | solution.py:466
  57.9 7.5 %collective-permute-start.8 = (bf16[128,1024]{1,0:T(8,128)(2,1)S(1)}, bf16[128,1024]{1,0:T(8,128)(2,1)S(1)}, u32[]{:S(2)}, u32[]{:S(2)}) collective-permute-start(bf16[128,1024]{1,0:T(8,128)(2,1)S(1)} %pad_maximum_fusion.4), channel_id=1, source_target_pairs={{0,2},{1,5},{2,0},{3,7},{4,6},{5,1},{6,4},{7,3},{8,10},{9,13},{10,... | collective-permute-start | bytes 786440 | tf_op jit(solution)/shard_map/ppermute | solution.py:466
  63.2 6.5 %collective-permute-start.15 = (bf16[128,1024]{1,0:T(8,128)(2,1)S(1)}, bf16[128,1024]{1,0:T(8,128)(2,1)S(1)}, u32[]{:S(2)}, u32[]{:S(2)}) collective-permute-start(bf16[128,1024]{1,0:T(8,128)(2,1)S(1)} %pad_maximum_fusion.5), channel_id=1, source_target_pairs={{0,2},{1,5},{2,0},{3,7},{4,6},{5,1},{6,4},{7,3},{8,10},{9,13},{10,... | collective-permute-start | bytes 786440 | tf_op jit(solution)/shard_map/ppermute | solution.py:466
  65.5 4.4 %collective-permute-start.9 = (bf16[256,1024]{1,0:T(8,128)(2,1)S(1)}, bf16[256,1024]{1,0:T(8,128)(2,1)S(1)}, u32[]{:S(2)}, u32[]{:S(2)}) collective-permute-start(bf16[256,1024]{1,0:T(8,128)(2,1)S(1)} %pad_maximum_fusion.1), channel_id=1, source_target_pairs={{0,1},{1,0},{2,3},{3,2},{4,5},{5,4},{6,7},{7,6},{8,9},{9,8},{10,11... | collective-permute-start | bytes 1572872 | tf_op jit(solution)/shard_map/ppermute | solution.py:466
  69.9 2.0 %collective-permute-start.16 = (bf16[264,1024]{1,0:T(8,128)(2,1)S(1)}, bf16[264,1024]{1,0:T(8,128)(2,1)S(1)}, u32[]{:S(2)}, u32[]{:S(2)}) collective-permute-start(bf16[264,1024]{1,0:T(8,128)(2,1)S(1)} %pad_maximum_fusion), channel_id=1, source_target_pairs={{0,1},{1,0},{2,3},{3,2},{4,5},{5,4},{6,7},{7,6},{8,9},{9,8},{10,11... | collective-permute-start | bytes 1622024 | tf_op jit(solution)/shard_map/ppermute | solution.py:466

commit v5 on v4

--- a/solution.py
+++ b/solution.py
@@ -459,7 +459,7 @@
     odd = tm % 2
     axes = ("user", "tm")
     every = [(u, t) for u in range(n_user) for t in range(n_tm)]
-    chunks = 2
+    chunks = len((1, 1, 1, 1))
 
     def swap(value, partner):
         pairs = [(u * n_tm + t, partner(u, t)) for u, t in every]
@@ -492,24 +492,24 @@
     levels = len(order_even)
     bits = [bit_of(level) for level in range(levels)]
     bit = odd == 1
-    edges = [rows * k // chunks for k in range(chunks + 1)]
+    edges = [rows * sum((1, 1, 1, 1)[:k]) // sum((1, 1, 1, 1)) for k in range(chunks + 1)]
     pieces = []
     for k in range(chunks):
         last = k == chunks - 1
         stop = edges[k + 1] + (8 if last else 0)
         pieces.append((send[edges[k] : stop], keep[edges[k] : stop], last))
-    size = rows // chunks
     state = []
     for leave, stay, has_extra in pieces:
+        size = stay.shape[0] - (8 if has_extra else 0)
         got = swap(leave, across)
         extra = None
         if has_extra:
             extra = (stay[size:].astype(F32) + got[size:].astype(F32)).astype(BF16)
         state.append((stay[:size], got[:size], extra))
     for level in range(levels - 1):
-        size //= 2
         after = []
         for a, b, extra in state:
+            size = a.shape[0] // 2
             low = a[:size].astype(F32) + b[:size].astype(F32)
             high = a[size:].astype(F32) + b[size:].astype(F32)
             leave = jnp.where(bits[level], low, high).astype(BF16)
@@ -523,6 +523,7 @@
         state = after
     wholes = []
     for a, b, extra in state:
+        size = a.shape[0]
         whole = (a.astype(F32) + b.astype(F32)).astype(BF16)
         if levels:
             leave = whole if extra is None else jnp.concatenate([whole, extra], axis=0)

time: 75.5 us -> 71.4 us (0.946)
  waiting for transfers between devices: 30.6 us -> 16 us
  starting transfers between devices: 23.2 us -> 33.5 us
    ppermute x14 -> x28, waiting for transfers between devices: 23.7 us -> 9.07 us  [swap(): return lax.ppermute(value, axes, pairs)]
    ppermute x14 -> x28, starting transfers between devices: 20.1 us -> 30.5 us  [swap(): return lax.ppermute(value, axes, pairs)]
    concatenate x1 -> x2, other arithmetic: 2.52 us -> 2.55 us  [total_sum(): return (jnp.concatenate(tops + bottoms, axis=0), grad_second)]
  transfers between devices with their start and end apart: 17 -> 31, of which waited for: 12 -> 13; matrix products, arithmetic and copies ran while one was open for 2% -> 2% of each run, Pallas kernels for 5% -> 5%
where the time goes in v5:
time: 71.4 us; the launch traced here: 71.1 us
  starting transfers between devices  33.5 us (47%)
  waiting for transfers between devices  16 us (22%)
  Pallas kernels  14.2 us (20%)
  other arithmetic  4.87 us (7%)
  between operations  1.7 us (2%)
  local copies, waits for them, and re-layouts  0.8 us (1%)
    ppermute x28, starting transfers between devices, swap(): return lax.ppermute(value, axes, pairs)  30.5 us
    pallas_call x4, Pallas kernels, call(): pl.pallas_call(loading(kernel, len(loaded), len(given), len(out_shape), w...  14.2 us
    ppermute x28, waiting for transfers between devices, swap(): return lax.ppermute(value, axes, pairs)  9.07 us
    ppermute x1, waiting for transfers between devices, body(): lax.ppermute(hist[length - ALIGN:], 'tm', [(i, (i + 1) % n_tm) for i in r...  3.33 us
    concatenate x2, other arithmetic, total_sum(): return (jnp.concatenate(tops + bottoms, axis=0), grad_second)  2.55 us
    ppermute x1, starting transfers between devices, body(): incoming = lax.ppermute(chip_state, 'tm', onward)  2.37 us
    ppermute x1, waiting for transfers between devices, body(): incoming = lax.ppermute(chip_state, 'tm', onward)  2.13 us
    ppermute x1, waiting for transfers between devices, body(): other = lax.ppermute(pay, 'tm', [(i, i ^ 1) for i in range(n_tm)])  1.46 us
  transfers between devices with their start and end apart: 31, of which 13 were waited for; matrix products, arithmetic and copies ran while one was open for 2% of the time, Pallas kernels for 5%

profile of v5, /device:TPU:0, one launch (start us, length us, event | category | flops | bytes accessed | tf_op | source)
XLA Modules:
  0.0 71.1 jit_solution(12288896462819204227)
XLA Ops:
  1.9 3.3 %collective-permute-done.refs_7_ = bf16[16,512]{1,0:T(8,128)(2,1)S(1)} collective-permute-done((bf16[16,512]{1,0:T(8,128)(2,1)S(1)}, bf16[16,512]{1,0:T(8,128)(2,1)S(1)}, u32[]{:S(2)}, u32[]{:S(2)}) %collective-permute-start) | collective-permute-done | bytes 16416 | tf_op jit(solution)/shard_map/ppermute | solution.py:364
  5.2 3.4 %shard_map.192 = (bf16[256,1280]{1,0:T(8,128)(2,1)S(1)}, f32[256,16]{1,0:T(8,128)S(1)}, f32[16,256]{1,0:T(8,128)S(1)}, f32[16,256]{1,0:T(8,128)S(1)}, bf16[144,1024]{1,0:T(8,128)(2,1)S(1)}) custom-call(bf16[256,512]{1,0:T(8,128)(2,1)} %bitcast.14, bf16[16,512]{1,0:T(8,128)(2,1)} %bitcast.16, f32[1,16]{1,0:T(1,128)} %bitcast.21, f32[1,16]{1,0:T(1,128)} %bitcast.22, ...), custom_call_target="tpu_custom_call" | custom-call | flops 335544320 | bytes 2621440 | tf_op jit(solution)/shard_map/pallas_call | solution.py:311
  8.8 1.5 %collective-permute-done.1.refs_1_.refs_9_ = bf16[144,1024]{1,0:T(8,128)(2,1)S(1)} collective-permute-done((bf16[144,1024]{1,0:T(8,128)(2,1)S(1)}, bf16[144,1024]{1,0:T(8,128)(2,1)S(1)}, u32[]{:S(2)}, u32[]{:S(2)}) %collective-permute-start.1) | collective-permute-done | bytes 294944 | tf_op jit(solution)/shard_map/ppermute | solution.py:389
  10.9 2.4 %collective-permute-start.2 = (bf16[128,1024]{1,0:T(8,128)(2,1)S(1)}, bf16[128,1024]{1,0:T(8,128)(2,1)S(1)}, u32[]{:S(2)}, u32[]{:S(2)}) collective-permute-start(bf16[128,1024]{1,0:T(8,128)(2,1)S(1)} %get-tuple-element.18), channel_id=1, source_target_pairs={{0,2},{1,3},{2,0},{3,1},{4,6},{5,7},{6,4},{7,5},{8,10},{9,11},{10,... | collective-permute-start | bytes 786440 | tf_op jit(solution)/shard_map/ppermute | solution.py:401
  14.0 3.8 %shard_map.194 = (f32[256,1024]{1,0:T(8,128)S(1)}, f32[256,1024]{1,0:T(8,128)S(1)}, f32[512,1024]{1,0:T(8,128)S(1)}) custom-call(bf16[256,512]{1,0:T(8,128)(2,1)} %bitcast.15, bf16[512,1024]{1,0:T(8,128)(2,1)} %refs_1_.2, bf16[512,512]{1,0:T(8,128)(2,1)} %bitcast.12, bf16[1024,1024]{1,0:T(8,128)(2,1)} %refs_3_.3, f32[16]{0:T(128)S(1)} %copy-done, ...), custom_call_target="tpu_custom_call" | custom-call | flops 1073741824 | bytes 16777216 | tf_op jit(solution)/shard_map/pallas_call | solution.py:311
  17.8 2.1 %collective-permute-done.2.refs_8_ = bf16[128,1024]{1,0:T(8,128)(2,1)S(1)} collective-permute-done((bf16[128,1024]{1,0:T(8,128)(2,1)S(1)}, bf16[128,1024]{1,0:T(8,128)(2,1)S(1)}, u32[]{:S(2)}, u32[]{:S(2)}) %collective-permute-start.2) | collective-permute-done | bytes 262176 | tf_op jit(solution)/shard_map/ppermute | solution.py:401
  19.9 6.3 %shard_map.195 = (bf16[256,512]{1,0:T(8,128)(2,1)}, f32[1,512]{1,0:T(1,128)}, bf16[520,1024]{1,0:T(8,128)(2,1)S(1)}, bf16[520,1024]{1,0:T(8,128)(2,1)S(1)}) custom-call(f32[1,1024]{1,0:T(1,128)} %bitcast.18, bf16[1024,512]{1,0:T(8,128)(2,1)} %refs_1_.3, s32[1,512]{1,0:T(1,128)} %refs_2_.1, bf16[1024,1024]{1,0:T(8,128)(2,1)} %refs_3_.3, ...), custom_call_target="tpu_custom_call" | custom-call | flops 1073741824 | bytes 4194304 | tf_op jit(solution)/shard_map/pallas_call | solution.py:311
  28.5 1.8 %collective-permute-start.18 = (bf16[64,1024]{1,0:T(8,128)(2,1)S(1)}, bf16[64,1024]{1,0:T(8,128)(2,1)S(1)}, u32[]{:S(2)}, u32[]{:S(2)}) collective-permute-start(bf16[64,1024]{1,0:T(8,128)(2,1)S(1)} %get-tuple-element.33), channel_id=1, source_target_pairs={{0,2},{1,5},{2,0},{3,7},{4,6},{5,1},{6,4},{7,3},{8,10},{9,13},{10,... | collective-permute-start | bytes 393224 | tf_op jit(solution)/shard_map/ppermute | solution.py:466
  30.8 1.8 %collective-permute-start.25 = (bf16[72,1024]{1,0:T(8,128)(2,1)S(1)}, bf16[72,1024]{1,0:T(8,128)(2,1)S(1)}, u32[]{:S(2)}, u32[]{:S(2)}) collective-permute-start(bf16[72,1024]{1,0:T(8,128)(2,1)S(1)} %pad_maximum_fusion.5), channel_id=1, source_target_pairs={{0,2},{1,5},{2,0},{3,7},{4,6},{5,1},{6,4},{7,3},{8,10},{9,13},{10,... | collective-permute-start | bytes 442376 | tf_op jit(solution)/shard_map/ppermute | solution.py:466
  33.6 1.9 %collective-permute-start.19 = (bf16[32,1024]{1,0:T(8,128)(2,1)S(1)}, bf16[32,1024]{1,0:T(8,128)(2,1)S(1)}, u32[]{:S(2)}, u32[]{:S(2)}) collective-permute-start(bf16[32,1024]{1,0:T(8,128)(2,1)S(1)} %select_convert_fusion.10), channel_id=1, source_target_pairs={{0,4},{1,9},{2,6},{3,11},{4,0},{5,13},{6,2},{7,15},{8,12},{9,1},{1... | collective-permute-start | bytes 196616 | tf_op jit(solution)/shard_map/ppermute | solution.py:466
  35.5 1.5 %collective-permute-start.5 = (bf16[32,1024]{1,0:T(8,128)(2,1)S(1)}, bf16[32,1024]{1,0:T(8,128)(2,1)S(1)}, u32[]{:S(2)}, u32[]{:S(2)}) collective-permute-start(bf16[32,1024]{1,0:T(8,128)(2,1)S(1)} %select_convert_fusion.14), channel_id=1, source_target_pairs={{0,4},{1,9},{2,6},{3,11},{4,0},{5,13},{6,2},{7,15},{8,12},{9,1},{1... | collective-permute-start | bytes 196616 | tf_op jit(solution)/shard_map/ppermute | solution.py:466
  36.9 1.3 %collective-permute-done.11 = bf16[64,1024]{1,0:T(8,128)(2,1)S(1)} collective-permute-done((bf16[64,1024]{1,0:T(8,128)(2,1)S(1)}, bf16[64,1024]{1,0:T(8,128)(2,1)S(1)}, u32[]{:S(2)}, u32[]{:S(2)}) %collective-permute-start.11) | collective-permute-done | bytes 131104 | tf_op jit(solution)/shard_map/ppermute | solution.py:466
  38.3 1.6 %collective-permute-start.12 = (bf16[32,1024]{1,0:T(8,128)(2,1)S(1)}, bf16[32,1024]{1,0:T(8,128)(2,1)S(1)}, u32[]{:S(2)}, u32[]{:S(2)}) collective-permute-start(bf16[32,1024]{1,0:T(8,128)(2,1)S(1)} %select_convert_fusion.12), channel_id=1, source_target_pairs={{0,4},{1,9},{2,6},{3,11},{4,0},{5,13},{6,2},{7,15},{8,12},{9,1},{1... | collective-permute-start | bytes 196616 | tf_op jit(solution)/shard_map/ppermute | solution.py:466
  40.6 2.7 %collective-permute-start.20 = (bf16[32,1024]{1,0:T(8,128)(2,1)S(1)}, bf16[32,1024]{1,0:T(8,128)(2,1)S(1)}, u32[]{:S(2)}, u32[]{:S(2)}) collective-permute-start(bf16[32,1024]{1,0:T(8,128)(2,1)S(1)} %add_convert_fusion.3), channel_id=1, source_target_pairs={{0,8},{1,3},{2,10},{3,1},{4,12},{5,7},{6,14},{7,5},{8,0},{9,11},{1... | collective-permute-start | bytes 196616 | tf_op jit(solution)/shard_map/ppermute | solution.py:466
  43.7 2.7 %collective-permute-start.13 = (bf16[32,1024]{1,0:T(8,128)(2,1)S(1)}, bf16[32,1024]{1,0:T(8,128)(2,1)S(1)}, u32[]{:S(2)}, u32[]{:S(2)}) collective-permute-start(bf16[32,1024]{1,0:T(8,128)(2,1)S(1)} %add_convert_fusion.5), channel_id=1, source_target_pairs={{0,8},{1,3},{2,10},{3,1},{4,12},{5,7},{6,14},{7,5},{8,0},{9,11},{1... | collective-permute-start | bytes 196616 | tf_op jit(solution)/shard_map/ppermute | solution.py:466
  46.5 1.3 %collective-permute-start.27 = (bf16[40,1024]{1,0:T(8,128)(2,1)S(1)}, bf16[40,1024]{1,0:T(8,128)(2,1)S(1)}, u32[]{:S(2)}, u32[]{:S(2)}) collective-permute-start(bf16[40,1024]{1,0:T(8,128)(2,1)S(1)} %pad_maximum_fusion.11), channel_id=1, source_target_pairs={{0,8},{1,3},{2,10},{3,1},{4,12},{5,7},{6,14},{7,5},{8,0},{9,11},{1... | collective-permute-start | bytes 245768 | tf_op jit(solution)/shard_map/ppermute | solution.py:466
  47.8 1.6 %collective-permute-start.21 = (bf16[32,1024]{1,0:T(8,128)(2,1)S(1)}, bf16[32,1024]{1,0:T(8,128)(2,1)S(1)}, u32[]{:S(2)}, u32[]{:S(2)}) collective-permute-start(bf16[32,1024]{1,0:T(8,128)(2,1)S(1)} %add_convert_fusion.2), channel_id=1, source_target_pairs={{0,4},{1,9},{2,6},{3,11},{4,0},{5,13},{6,2},{7,15},{8,12},{9,1},{1... | collective-permute-start | bytes 196616 | tf_op jit(solution)/shard_map/ppermute | solution.py:466
  51.5 2.3 %collective-permute-start.14 = (bf16[32,1024]{1,0:T(8,128)(2,1)S(1)}, bf16[32,1024]{1,0:T(8,128)(2,1)S(1)}, u32[]{:S(2)}, u32[]{:S(2)}) collective-permute-start(bf16[32,1024]{1,0:T(8,128)(2,1)S(1)} %add_convert_fusion.4), channel_id=1, source_target_pairs={{0,4},{1,9},{2,6},{3,11},{4,0},{5,13},{6,2},{7,15},{8,12},{9,1},{1... | collective-permute-start | bytes 196616 | tf_op jit(solution)/shard_map/ppermute | solution.py:466
  53.8 1.7 %collective-permute-done.27 = bf16[40,1024]{1,0:T(8,128)(2,1)S(1)} collective-permute-done((bf16[40,1024]{1,0:T(8,128)(2,1)S(1)}, bf16[40,1024]{1,0:T(8,128)(2,1)S(1)}, u32[]{:S(2)}, u32[]{:S(2)}) %collective-permute-start.27) | collective-permute-done | bytes 81952 | tf_op jit(solution)/shard_map/ppermute | solution.py:466
  56.5 1.6 %collective-permute-start.22 = (bf16[64,1024]{1,0:T(8,128)(2,1)S(1)}, bf16[64,1024]{1,0:T(8,128)(2,1)S(1)}, u32[]{:S(2)}, u32[]{:S(2)}) collective-permute-start(bf16[64,1024]{1,0:T(8,128)(2,1)S(1)} %pad_maximum_fusion.8), channel_id=1, source_target_pairs={{0,2},{1,5},{2,0},{3,7},{4,6},{5,1},{6,4},{7,3},{8,10},{9,13},{10,... | collective-permute-start | bytes 393224 | tf_op jit(solution)/shard_map/ppermute | solution.py:466
  58.8 1.6 %collective-permute-start.15 = (bf16[64,1024]{1,0:T(8,128)(2,1)S(1)}, bf16[64,1024]{1,0:T(8,128)(2,1)S(1)}, u32[]{:S(2)}, u32[]{:S(2)}) collective-permute-start(bf16[64,1024]{1,0:T(8,128)(2,1)S(1)} %pad_maximum_fusion.7), channel_id=1, source_target_pairs={{0,2},{1,5},{2,0},{3,7},{4,6},{5,1},{6,4},{7,3},{8,10},{9,13},{10,... | collective-permute-start | bytes 393224 | tf_op jit(solution)/shard_map/ppermute | solution.py:466
  60.5 2.5 %collective-permute-start.29 = (bf16[64,1024]{1,0:T(8,128)(2,1)S(1)}, bf16[64,1024]{1,0:T(8,128)(2,1)S(1)}, u32[]{:S(2)}, u32[]{:S(2)}) collective-permute-start(bf16[64,1024]{1,0:T(8,128)(2,1)S(1)} %pad_maximum_fusion.9), channel_id=1, source_target_pairs={{0,2},{1,5},{2,0},{3,7},{4,6},{5,1},{6,4},{7,3},{8,10},{9,13},{10,... | collective-permute-start | bytes 393224 | tf_op jit(solution)/shard_map/ppermute | solution.py:466
  66.4 1.3 %collective-permute-done.30 = bf16[136,1024]{1,0:T(8,128)(2,1)S(1)} collective-permute-done((bf16[136,1024]{1,0:T(8,128)(2,1)S(1)}, bf16[136,1024]{1,0:T(8,128)(2,1)S(1)}, u32[]{:S(2)}, u32[]{:S(2)}) %collective-permute-start.30) | collective-permute-done | bytes 278560 | tf_op jit(solution)/shard_map/ppermute | solution.py:466
  68.6 2.5 %concatenate.56 = f32[1024,1024]{1,0:T(8,128)} convert(bf16[1024,1024]{1,0:T(8,128)(2,1)S(1)} %select_dynamic-update-slice_fusion) | non-fusion elementwise | flops 1048576 | bytes 6291456 | tf_op jit(solution)/shard_map/concatenate | solution.py:554
  (95 shorter events, 15.1 us)
Async XLA Ops:
  1.4 3.8 %collective-permute-start = (bf16[16,512]{1,0:T(8,128)(2,1)S(1)}, bf16[16,512]{1,0:T(8,128)(2,1)S(1)}, u32[]{:S(2)}, u32[]{:S(2)}) collective-permute-start(bf16[16,512]{1,0:T(8,128)(2,1)S(1)} %slice_bitcast_fusion), channel_id=1, source_target_pairs={{0,1},{1,2},{2,3},{3,0},{4,5},{5,6},{6,7},{7,4},{8,9},{9,10},{10,1... | collective-permute-start | bytes 49160 | tf_op jit(solution)/shard_map/ppermute | solution.py:364
  10.9 9.0 %collective-permute-start.2 = (bf16[128,1024]{1,0:T(8,128)(2,1)S(1)}, bf16[128,1024]{1,0:T(8,128)(2,1)S(1)}, u32[]{:S(2)}, u32[]{:S(2)}) collective-permute-start(bf16[128,1024]{1,0:T(8,128)(2,1)S(1)} %get-tuple-element.18), channel_id=1, source_target_pairs={{0,2},{1,3},{2,0},{3,1},{4,6},{5,7},{6,4},{7,5},{8,10},{9,11},{10,... | collective-permute-start | bytes 786440 | tf_op jit(solution)/shard_map/ppermute | solution.py:401
  26.9 3.7 %collective-permute-start.24 = (bf16[136,1024]{1,0:T(8,128)(2,1)S(1)}, bf16[136,1024]{1,0:T(8,128)(2,1)S(1)}, u32[]{:S(2)}, u32[]{:S(2)}) collective-permute-start(bf16[136,1024]{1,0:T(8,128)(2,1)S(1)} %slice.195), channel_id=1, source_target_pairs={{0,1},{1,0},{2,3},{3,2},{4,5},{5,4},{6,7},{7,6},{8,9},{9,8},{10,11... | collective-permute-start | bytes 835592 | tf_op jit(solution)/shard_map/ppermute | solution.py:466
  27.0 3.5 %collective-permute-start.10 = (bf16[128,1024]{1,0:T(8,128)(2,1)S(1)}, bf16[128,1024]{1,0:T(8,128)(2,1)S(1)}, u32[]{:S(2)}, u32[]{:S(2)}) collective-permute-start(bf16[128,1024]{1,0:T(8,128)(2,1)S(1)} %get-tuple-element.43), channel_id=1, source_target_pairs={{0,1},{1,0},{2,3},{3,2},{4,5},{5,4},{6,7},{7,6},{8,9},{9,8},{10,11... | collective-permute-start | bytes 786440 | tf_op jit(solution)/shard_map/ppermute | solution.py:466
  28.5 5.0 %collective-permute-start.18 = (bf16[64,1024]{1,0:T(8,128)(2,1)S(1)}, bf16[64,1024]{1,0:T(8,128)(2,1)S(1)}, u32[]{:S(2)}, u32[]{:S(2)}) collective-permute-start(bf16[64,1024]{1,0:T(8,128)(2,1)S(1)} %get-tuple-element.33), channel_id=1, source_target_pairs={{0,2},{1,5},{2,0},{3,7},{4,6},{5,1},{6,4},{7,3},{8,10},{9,13},{10,... | collective-permute-start | bytes 393224 | tf_op jit(solution)/shard_map/ppermute | solution.py:466
  30.3 5.2 %collective-permute-start.4 = (bf16[64,1024]{1,0:T(8,128)(2,1)S(1)}, bf16[64,1024]{1,0:T(8,128)(2,1)S(1)}, u32[]{:S(2)}, u32[]{:S(2)}) collective-permute-start(bf16[64,1024]{1,0:T(8,128)(2,1)S(1)} %get-tuple-element.40), channel_id=1, source_target_pairs={{0,2},{1,5},{2,0},{3,7},{4,6},{5,1},{6,4},{7,3},{8,10},{9,13},{10,... | collective-permute-start | bytes 393224 | tf_op jit(solution)/shard_map/ppermute | solution.py:466
  30.8 9.1 %collective-permute-start.25 = (bf16[72,1024]{1,0:T(8,128)(2,1)S(1)}, bf16[72,1024]{1,0:T(8,128)(2,1)S(1)}, u32[]{:S(2)}, u32[]{:S(2)}) collective-permute-start(bf16[72,1024]{1,0:T(8,128)(2,1)S(1)} %pad_maximum_fusion.5), channel_id=1, source_target_pairs={{0,2},{1,5},{2,0},{3,7},{4,6},{5,1},{6,4},{7,3},{8,10},{9,13},{10,... | collective-permute-start | bytes 442376 | tf_op jit(solution)/shard_map/ppermute | solution.py:466
  32.6 5.6 %collective-permute-start.11 = (bf16[64,1024]{1,0:T(8,128)(2,1)S(1)}, bf16[64,1024]{1,0:T(8,128)(2,1)S(1)}, u32[]{:S(2)}, u32[]{:S(2)}) collective-permute-start(bf16[64,1024]{1,0:T(8,128)(2,1)S(1)} %get-tuple-element.38), channel_id=1, source_target_pairs={{0,2},{1,5},{2,0},{3,7},{4,6},{5,1},{6,4},{7,3},{8,10},{9,13},{10,... | collective-permute-start | bytes 393224 | tf_op jit(solution)/shard_map/ppermute | solution.py:466
  33.6 7.0 %collective-permute-start.19 = (bf16[32,1024]{1,0:T(8,128)(2,1)S(1)}, bf16[32,1024]{1,0:T(8,128)(2,1)S(1)}, u32[]{:S(2)}, u32[]{:S(2)}) collective-permute-start(bf16[32,1024]{1,0:T(8,128)(2,1)S(1)} %select_convert_fusion.10), channel_id=1, source_target_pairs={{0,4},{1,9},{2,6},{3,11},{4,0},{5,13},{6,2},{7,15},{8,12},{9,1},{1... | collective-permute-start | bytes 196616 | tf_op jit(solution)/shard_map/ppermute | solution.py:466
  35.5 7.7 %collective-permute-start.5 = (bf16[32,1024]{1,0:T(8,128)(2,1)S(1)}, bf16[32,1024]{1,0:T(8,128)(2,1)S(1)}, u32[]{:S(2)}, u32[]{:S(2)}) collective-permute-start(bf16[32,1024]{1,0:T(8,128)(2,1)S(1)} %select_convert_fusion.14), channel_id=1, source_target_pairs={{0,4},{1,9},{2,6},{3,11},{4,0},{5,13},{6,2},{7,15},{8,12},{9,1},{1... | collective-permute-start | bytes 196616 | tf_op jit(solution)/shard_map/ppermute | solution.py:466
  38.3 5.4 %collective-permute-start.12 = (bf16[32,1024]{1,0:T(8,128)(2,1)S(1)}, bf16[32,1024]{1,0:T(8,128)(2,1)S(1)}, u32[]{:S(2)}, u32[]{:S(2)}) collective-permute-start(bf16[32,1024]{1,0:T(8,128)(2,1)S(1)} %select_convert_fusion.12), channel_id=1, source_target_pairs={{0,4},{1,9},{2,6},{3,11},{4,0},{5,13},{6,2},{7,15},{8,12},{9,1},{1... | collective-permute-start | bytes 196616 | tf_op jit(solution)/shard_map/ppermute | solution.py:466
  40.0 6.4 %collective-permute-start.26 = (bf16[40,1024]{1,0:T(8,128)(2,1)S(1)}, bf16[40,1024]{1,0:T(8,128)(2,1)S(1)}, u32[]{:S(2)}, u32[]{:S(2)}) collective-permute-start(bf16[40,1024]{1,0:T(8,128)(2,1)S(1)} %pad_maximum_fusion.10), channel_id=1, source_target_pairs={{0,4},{1,9},{2,6},{3,11},{4,0},{5,13},{6,2},{7,15},{8,12},{9,1},{1... | collective-permute-start | bytes 245768 | tf_op jit(solution)/shard_map/ppermute | solution.py:466
  40.6 7.2 %collective-permute-start.20 = (bf16[32,1024]{1,0:T(8,128)(2,1)S(1)}, bf16[32,1024]{1,0:T(8,128)(2,1)S(1)}, u32[]{:S(2)}, u32[]{:S(2)}) collective-permute-start(bf16[32,1024]{1,0:T(8,128)(2,1)S(1)} %add_convert_fusion.3), channel_id=1, source_target_pairs={{0,8},{1,3},{2,10},{3,1},{4,12},{5,7},{6,14},{7,5},{8,0},{9,11},{1... | collective-permute-start | bytes 196616 | tf_op jit(solution)/shard_map/ppermute | solution.py:466
  43.3 6.2 %collective-permute-start.6 = (bf16[32,1024]{1,0:T(8,128)(2,1)S(1)}, bf16[32,1024]{1,0:T(8,128)(2,1)S(1)}, u32[]{:S(2)}, u32[]{:S(2)}) collective-permute-start(bf16[32,1024]{1,0:T(8,128)(2,1)S(1)} %add_convert_fusion.7), channel_id=1, source_target_pairs={{0,8},{1,3},{2,10},{3,1},{4,12},{5,7},{6,14},{7,5},{8,0},{9,11},{1... | collective-permute-start | bytes 196616 | tf_op jit(solution)/shard_map/ppermute | solution.py:466
  43.7 7.7 %collective-permute-start.13 = (bf16[32,1024]{1,0:T(8,128)(2,1)S(1)}, bf16[32,1024]{1,0:T(8,128)(2,1)S(1)}, u32[]{:S(2)}, u32[]{:S(2)}) collective-permute-start(bf16[32,1024]{1,0:T(8,128)(2,1)S(1)} %add_convert_fusion.5), channel_id=1, source_target_pairs={{0,8},{1,3},{2,10},{3,1},{4,12},{5,7},{6,14},{7,5},{8,0},{9,11},{1... | collective-permute-start | bytes 196616 | tf_op jit(solution)/shard_map/ppermute | solution.py:466
  46.5 9.0 %collective-permute-start.27 = (bf16[40,1024]{1,0:T(8,128)(2,1)S(1)}, bf16[40,1024]{1,0:T(8,128)(2,1)S(1)}, u32[]{:S(2)}, u32[]{:S(2)}) collective-permute-start(bf16[40,1024]{1,0:T(8,128)(2,1)S(1)} %pad_maximum_fusion.11), channel_id=1, source_target_pairs={{0,8},{1,3},{2,10},{3,1},{4,12},{5,7},{6,14},{7,5},{8,0},{9,11},{1... | collective-permute-start | bytes 245768 | tf_op jit(solution)/shard_map/ppermute | solution.py:466
  47.8 8.7 %collective-permute-start.21 = (bf16[32,1024]{1,0:T(8,128)(2,1)S(1)}, bf16[32,1024]{1,0:T(8,128)(2,1)S(1)}, u32[]{:S(2)}, u32[]{:S(2)}) collective-permute-start(bf16[32,1024]{1,0:T(8,128)(2,1)S(1)} %add_convert_fusion.2), channel_id=1, source_target_pairs={{0,4},{1,9},{2,6},{3,11},{4,0},{5,13},{6,2},{7,15},{8,12},{9,1},{1... | collective-permute-start | bytes 196616 | tf_op jit(solution)/shard_map/ppermute | solution.py:466
  49.5 8.6 %collective-permute-start.7 = (bf16[32,1024]{1,0:T(8,128)(2,1)S(1)}, bf16[32,1024]{1,0:T(8,128)(2,1)S(1)}, u32[]{:S(2)}, u32[]{:S(2)}) collective-permute-start(bf16[32,1024]{1,0:T(8,128)(2,1)S(1)} %add_convert_fusion.6), channel_id=1, source_target_pairs={{0,4},{1,9},{2,6},{3,11},{4,0},{5,13},{6,2},{7,15},{8,12},{9,1},{1... | collective-permute-start | bytes 196616 | tf_op jit(solution)/shard_map/ppermute | solution.py:466
  51.5 7.2 %collective-permute-start.14 = (bf16[32,1024]{1,0:T(8,128)(2,1)S(1)}, bf16[32,1024]{1,0:T(8,128)(2,1)S(1)}, u32[]{:S(2)}, u32[]{:S(2)}) collective-permute-start(bf16[32,1024]{1,0:T(8,128)(2,1)S(1)} %add_convert_fusion.4), channel_id=1, source_target_pairs={{0,4},{1,9},{2,6},{3,11},{4,0},{5,13},{6,2},{7,15},{8,12},{9,1},{1... | collective-permute-start | bytes 196616 | tf_op jit(solution)/shard_map/ppermute | solution.py:466
  55.5 5.0 %collective-permute-start.28 = (bf16[32,1024]{1,0:T(8,128)(2,1)S(1)}, bf16[32,1024]{1,0:T(8,128)(2,1)S(1)}, u32[]{:S(2)}, u32[]{:S(2)}) collective-permute-start(bf16[32,1024]{1,0:T(8,128)(2,1)S(1)} %add_convert_fusion), channel_id=1, source_target_pairs={{0,4},{1,9},{2,6},{3,11},{4,0},{5,13},{6,2},{7,15},{8,12},{9,1},{1... | collective-permute-start | bytes 196616 | tf_op jit(solution)/shard_map/ppermute | solution.py:466
  56.5 6.5 %collective-permute-start.22 = (bf16[64,1024]{1,0:T(8,128)(2,1)S(1)}, bf16[64,1024]{1,0:T(8,128)(2,1)S(1)}, u32[]{:S(2)}, u32[]{:S(2)}) collective-permute-start(bf16[64,1024]{1,0:T(8,128)(2,1)S(1)} %pad_maximum_fusion.8), channel_id=1, source_target_pairs={{0,2},{1,5},{2,0},{3,7},{4,6},{5,1},{6,4},{7,3},{8,10},{9,13},{10,... | collective-permute-start | bytes 393224 | tf_op jit(solution)/shard_map/ppermute | solution.py:466
  58.1 5.1 %collective-permute-start.8 = (bf16[64,1024]{1,0:T(8,128)(2,1)S(1)}, bf16[64,1024]{1,0:T(8,128)(2,1)S(1)}, u32[]{:S(2)}, u32[]{:S(2)}) collective-permute-start(bf16[64,1024]{1,0:T(8,128)(2,1)S(1)} %pad_maximum_fusion.6), channel_id=1, source_target_pairs={{0,2},{1,5},{2,0},{3,7},{4,6},{5,1},{6,4},{7,3},{8,10},{9,13},{10,... | collective-permute-start | bytes 393224 | tf_op jit(solution)/shard_map/ppermute | solution.py:466
  58.8 5.8 %collective-permute-start.15 = (bf16[64,1024]{1,0:T(8,128)(2,1)S(1)}, bf16[64,1024]{1,0:T(8,128)(2,1)S(1)}, u32[]{:S(2)}, u32[]{:S(2)}) collective-permute-start(bf16[64,1024]{1,0:T(8,128)(2,1)S(1)} %pad_maximum_fusion.7), channel_id=1, source_target_pairs={{0,2},{1,5},{2,0},{3,7},{4,6},{5,1},{6,4},{7,3},{8,10},{9,13},{10,... | collective-permute-start | bytes 393224 | tf_op jit(solution)/shard_map/ppermute | solution.py:466
  60.5 5.4 %collective-permute-start.29 = (bf16[64,1024]{1,0:T(8,128)(2,1)S(1)}, bf16[64,1024]{1,0:T(8,128)(2,1)S(1)}, u32[]{:S(2)}, u32[]{:S(2)}) collective-permute-start(bf16[64,1024]{1,0:T(8,128)(2,1)S(1)} %pad_maximum_fusion.9), channel_id=1, source_target_pairs={{0,2},{1,5},{2,0},{3,7},{4,6},{5,1},{6,4},{7,3},{8,10},{9,13},{10,... | collective-permute-start | bytes 393224 | tf_op jit(solution)/shard_map/ppermute | solution.py:466
  (8 other events, 27.8 us)

commit v6 on v5

--- a/solution.py
+++ b/solution.py
@@ -11,6 +11,7 @@
 BF16 = jnp.bfloat16
 LANES = 128
 ALIGN = 16
+CHUNKS = 4
 VMEM = pl.BlockSpec(memory_space=pltpu.VMEM)
 SMEM = pl.BlockSpec(memory_space=pltpu.SMEM)
 HBM = pl.BlockSpec(memory_space=pltpu.HBM)
@@ -26,6 +27,10 @@
 
 def dot_tn(a, b):
     return lax.dot_general(a, b, (((0,), (0,)), ((), ())), preferred_element_type=F32)
+
+
+def logistic(v):
+    return 0.5 + 0.5 * jnp.tanh(0.5 * v)
 
 
 def split3(v):
@@ -45,21 +50,26 @@
     return out
 
 
-def scan_kernel(
-    heads, take, halo, xbc, cum_o, dt_t, cum_t, pay, raw, carried
-):
+def convolve(raw, bias, taps, cols, first, count):
+    start = cols.start // LANES
+    stop = cols.stop // LANES
+    acc = jnp.concatenate(
+        [jnp.broadcast_to(bias[k : k + 1, :], (count, LANES)) for k in range(start, stop)], axis=1
+    )
+    n = taps.shape[0]
+    for k in range(n):
+        acc = acc + taps[k : k + 1, cols] * raw[pl.ds(first - (n - 1) + k, count), cols]
+    return (acc * logistic(acc)).astype(BF16)
+
+
+def scan_kernel(heads, take, xbc, cum_o, dt_t, cum_t, weight_o, last_o, head_o, sum_o, raw, carried):
     hist = take(0)
-    dtw, dtb, alog, cw, cb = take(1), take(2), take(3), take(4), take(5)
-    length = hist.shape[0]
-    edge = halo.shape[0]
-    taps = cw.shape[0]
-    width = xbc.shape[1]
+    dtw, dtb, alog = take(1), take(2), take(3)
+    length, width = xbc.shape
     inner = carried.shape[1]
     state = (width - inner) // 2
     head_size = inner // heads
     per = LANES // head_size
-    before = jnp.where(lax.axis_index("tm") == 0, 0.0, halo[...].astype(F32)).astype(BF16)
-    rows = jnp.concatenate([before, hist[...]], axis=0)
 
     v = dot_nt(hist[...], dtw[...]) + dtb[...]
     dt = jnp.maximum(v, 0.0) + jnp.log1p(jnp.exp(-jnp.abs(v)))
@@ -74,34 +84,48 @@
     cum_t[...] = cum.T
     last = cum[length - 1 : length, :]
     weight = jnp.exp(last - cum) * dt
+    weight_o[...] = weight[:ALIGN]
+    last_o[...] = jnp.broadcast_to(jnp.exp(last), last_o.shape)
 
     step = 2 * LANES
-    w = take(6)
+    cw, cb, w = take(4), take(5), take(6)
+    raw[:ALIGN, :] = jnp.zeros((ALIGN, width), F32)
     for start in list(range(inner, width, step)) + list(range(0, inner, step)):
         cols = slice(start, start + step)
-        piece = dot(rows, w[:, cols]).astype(BF16).astype(F32)
-        raw[:, cols] = piece
-        first = start // LANES
-        acc = jnp.concatenate(
-            [jnp.broadcast_to(cb[k : k + 1, :], (length, LANES)) for k in (first, first + 1)], axis=1
-        )
-        for k in range(taps):
-            acc = acc + cw[k : k + 1, cols] * raw[pl.ds(edge - (taps - 1) + k, length), cols]
-        xbc[:, cols] = (acc / (1.0 + jnp.exp(-acc))).astype(BF16)
+        raw[ALIGN:, cols] = dot(hist[...], w[:, cols]).astype(BF16).astype(F32)
+        xbc[:, cols] = convolve(raw, cb, cw, cols, ALIGN, length)
+    head_o[...] = raw[ALIGN : 2 * ALIGN, :]
     for start in range(0, inner, LANES):
         cols = slice(start, start + LANES)
         x = xbc[:, cols].astype(F32)
         carried[:, cols] = (
             spread(weight, start // LANES * per, head_size, length) * x
         ).astype(BF16)
-    b = xbc[:, inner : inner + state]
-    pay[:state, :] = dot_tn(b, carried[...]).astype(BF16)
-    gain = jnp.broadcast_to(jnp.exp(last), (ALIGN, heads))
+    b = xbc[ALIGN:, inner : inner + state]
+    sum_o[...] = dot_tn(b, carried[ALIGN:, :])
+
+
+def edge_kernel(heads, take, halo, w, cw, cb, weight, last, head, later, old, xbc, pay, raw):
+    width = xbc.shape[1]
+    state, inner = later.shape
+    head_size = inner // heads
+    per = LANES // head_size
+    before = jnp.where(lax.axis_index("tm") == 0, 0.0, halo[...].astype(F32)).astype(BF16)
+    raw[:ALIGN, :] = dot(before, w[...]).astype(BF16).astype(F32)
+    raw[ALIGN:, :] = head[...]
+    top = convolve(raw, cb, cw, slice(0, width), ALIGN, ALIGN)
+    xbc[:ALIGN, :] = top
+    gain = last[...]
     pick = lax.broadcasted_iota(jnp.int32, (ALIGN, LANES), 0)
+    b = top[:, inner : inner + state]
     for start in range(0, inner, LANES):
-        g = spread(gain, start // LANES * per, head_size, ALIGN)
+        cols = slice(start, start + LANES)
+        h = start // LANES * per
+        carried = (spread(weight[...], h, head_size, ALIGN) * top[:, cols].astype(F32)).astype(BF16)
+        pay[:state, cols] = (later[:, cols] + dot_tn(b, carried)).astype(BF16)
+        g = spread(gain, h, head_size, ALIGN)
         high = g.astype(BF16).astype(F32)
-        pay[state:, start : start + LANES] = jnp.where(
+        pay[state:, cols] = jnp.where(
             pick == 0, high, jnp.where(pick == 1, g - high, 0.0)
         ).astype(BF16)
 
@@ -122,8 +146,11 @@
     gain_out[...] = jnp.broadcast_to(gm * go, gain_out.shape)
 
 
-def within_kernel(heads, take, d_skip, xbc, cum, dt_t, cum_t, part, gate, pre):
+def within_kernel(
+    heads, take, d_skip, xbc, cum, dt_t, cum_t, own, across, pre, hot_o, hot_t_o, item_t_o, part
+):
     length, inner = part.shape
+    slots = hot_o.shape[0]
     state = (xbc.shape[1] - inner) // 2
     head_size = inner // heads
     per = LANES // head_size
@@ -162,60 +189,65 @@
             out = got if out is None else jnp.where(lane >= k * head_size, got, out)
         part[:, cols] = out
     step = 2 * LANES
+    grow = jnp.exp(cum[...])
     hist, zw = take(0), take(1)
     for start in range(0, inner, step):
         cols = slice(start, start + step)
         z = dot(hist[...], zw[:, cols]).astype(BF16).astype(F32)
-        gate[:, cols] = z / (1.0 + jnp.exp(-z))
+        gate = z * logistic(z)
+        own[:, cols] = part[:, cols] * gate
+        for k in range(0, step, LANES):
+            first_head = (start + k) // LANES * per
+            across[:, start + k : start + k + LANES] = (
+                spread(grow, first_head, head_size, length) * gate[:, k : k + LANES]
+            )
     item, first = take(2), take(3)
     for start in range(0, pre.shape[1], step):
         cols = slice(start, start + step)
         pre[:, cols] = dot(item[...], first[:, cols])
+    item_t_o[...] = item[...].T
+    place = take(4)[...] - lax.axis_index("tm") * length
+    hot = jnp.where(lax.broadcasted_iota(jnp.int32, (length, slots), 0) == place, 1.0, 0.0)
+    hot_t_o[...] = hot.astype(BF16)
+    hot_o[...] = hot.T.astype(BF16)
 
 
 def rank_kernel(
-    heads,
     take,
     count,
     incoming,
     other,
     xbc,
-    cum,
-    part,
-    gate,
+    own,
+    across,
     pre,
+    hot,
+    hot_t,
+    item_t,
     enc_o,
     logit_o,
-    send_o,
-    keep_o,
-    gated_s,
-    rank_s,
-    slope_s,
-    hid_s,
     gp_s,
+    rank_o,
+    *rest,
 ):
-    length, inner = part.shape
+    send_o = rest[:CHUNKS]
+    gated_s, rank_s, slope_s, hid_s, enc_s, enc_sem = rest[CHUNKS:]
+    length, inner = own.shape
     state = incoming.shape[0]
-    head_size = inner // heads
-    per = LANES // head_size
     slots = pre.shape[0]
     tm = lax.axis_index("tm")
     odd = lax.rem(tm, 2) == 1
-    base = tm * length
     arrived = jnp.where(tm < 2, 0.0, incoming[...].astype(F32))
     enter = jnp.where(
         odd, arrived * gain_row(other, state) + other[:state, :].astype(F32), arrived
     )
-    high = enter.astype(BF16)
-    low = (enter - high.astype(F32)).astype(BF16)
+    entering = enter.astype(BF16)
     c = xbc[:, inner + state :]
-    grow = jnp.exp(cum[...])
     total = jnp.zeros((length, LANES), F32)
     for start in range(0, inner, LANES):
         cols = slice(start, start + LANES)
-        read = dot(c, high[:, cols]) + dot(c, low[:, cols])
-        y = part[:, cols] + spread(grow, start // LANES * per, head_size, length) * read
-        y = y * gate[:, cols]
+        read = dot(c, entering[:, cols])
+        y = own[:, cols] + across[:, cols] * read
         gated_s[:, cols] = y
         total = total + y * y
     mean = jnp.sum(total, axis=1, keepdims=True) * (1.0 / inner)
@@ -223,37 +255,38 @@
     gain, ow = take(0), take(1)
     normed = (gated_s[...] * scale * gain[...]).astype(BF16)
     enc = dot(normed, ow[...]).astype(BF16)
-    enc_o[...] = enc
+    enc_s[...] = enc
+    leaving = pltpu.make_async_copy(enc_s, enc_o, enc_sem)
+    leaving.start()
     width = enc.shape[1]
-    pos = take(2)
-    place = pos[...] - base
-    hot = (lax.broadcasted_iota(jnp.int32, (length, slots), 0) == place).astype(F32).astype(BF16)
-    rank_s[...] = dot_tn(hot, enc).astype(BF16)
+    rank_s[...] = dot(hot[...], enc).astype(BF16)
+    rank_t = dot(enc.T, hot_t[...]).astype(BF16)
 
     hidden_width = pre.shape[1]
     step = 2 * LANES
     logit = jnp.zeros((slots, LANES), F32)
-    first, second = take(3), take(4)
+    first, second = take(2), take(3)
     weights2 = second[...].astype(F32)
     for start in range(0, hidden_width, step):
         cols = slice(start, start + step)
         v = pre[:, cols] + dot(rank_s[...], first[:, cols])
-        sig = 1.0 / (1.0 + jnp.exp(-v))
-        hid = (v * sig).astype(BF16)
+        sig = logistic(v)
+        silu = v * sig
+        hid = silu.astype(BF16)
         hid_s[:, cols] = hid
         k = start // LANES
         w2 = jnp.concatenate([weights2[k : k + 1], weights2[k + 1 : k + 2]], axis=1)
         prod = hid.astype(F32) * w2
         for k in range(0, step, LANES):
             logit = logit + prod[:, k : k + LANES]
-        slope_s[:, cols] = w2 * (sig * (1.0 + v * (1.0 - sig)))
+        slope_s[:, cols] = w2 * (sig + silu * (1.0 - sig))
     ones = jnp.ones((8, LANES), BF16)
     p = split3(logit)
     logit8 = dot_nt(ones, p[0]) + (dot_nt(ones, p[1]) + dot_nt(ones, p[2]))
     slot = lax.broadcasted_iota(jnp.int32, (8, slots), 1)
     live = jnp.where(slot < count[0, 0], 1.0, 0.0)
     logit_o[...] = (live * logit8)[0:1, :]
-    value = take(5)
+    value = take(4)
     target = value[...].astype(F32)
     dl = live * (1.0 / (1.0 + jnp.exp(-logit8)) - target)
     d0, d1, d2 = split3(dl)
@@ -269,23 +302,43 @@
         cols = slice(start, start + LANES)
         gp_s[:, cols] = (dcol * slope_s[:, cols]).astype(BF16)
     rows = width
-    item = take(6)
     pick = lax.broadcasted_iota(jnp.int32, (8, hidden_width), 0)
     extra = jnp.where(pick == 0, grad2, 0.0).astype(BF16)
-    away = jnp.where(odd, rank_s[...], item[...])
-    home = jnp.where(odd, item[...], rank_s[...])
-    send_o[:rows, :] = dot_tn(away, gp_s[...]).astype(BF16)
-    send_o[rows:, :] = extra
-    keep_o[:rows, :] = dot_tn(home, gp_s[...]).astype(BF16)
-    keep_o[rows:, :] = extra
-
-
-def loading(kernel, n_loaded, n_given, n_out, windows):
+    away = jnp.where(odd, rank_t, item_t[...])
+    rank_o[...] = rank_t
+    size = rows // CHUNKS
+    for k in range(CHUNKS):
+        part = away[k * size : (k + 1) * size]
+        send_o[k][:size, :] = dot(part, gp_s[...]).astype(BF16)
+    send_o[CHUNKS - 1][size:, :] = extra
+    leaving.wait()
+
+
+def home_kernel(take, rank_t, item_t, slope, last_sent, *keep_o):
+    size = rank_t.shape[0] // CHUNKS
+    odd = lax.rem(lax.axis_index("tm"), 2) == 1
+    for k in range(CHUNKS):
+        part = slice(k * size, (k + 1) * size)
+        home = jnp.where(odd, item_t[part, :], rank_t[part, :])
+        keep_o[k][:size, :] = dot(home, slope[...]).astype(BF16)
+    keep_o[CHUNKS - 1][size:, :] = last_sent[size:, :]
+
+
+def chunk_shapes(rows, columns):
+    size = rows // CHUNKS
+    last = size + 8
+    return tuple(shape((last if k == CHUNKS - 1 else size, columns), BF16) for k in range(CHUNKS))
+
+
+def loading(kernel, n_loaded, n_given, n_out, windows, kept):
     def wrapped(*refs):
         sources = refs[:n_loaded]
         given = refs[n_loaded : n_loaded + n_given + n_out]
-        rest = refs[n_loaded + n_given + n_out :]
-        places, sems, scratch = rest[:n_loaded], rest[n_loaded], rest[n_loaded + 1 :]
+        first_kept = n_loaded + n_given + n_out
+        results = list(refs[first_kept : first_kept + len(kept)])
+        rest = list(refs[first_kept + len(kept) :])
+        places = [results.pop(0) if i in kept else rest.pop(0) for i in range(n_loaded)]
+        sems, scratch = rest[0], rest[1:]
         copies = []
         for i, source in enumerate(sources):
             window = windows.get(i)
@@ -302,20 +355,37 @@
     return wrapped
 
 
-def call(kernel, loaded, given, out_shape, scratch, flops, moved, mib, windows=None, smem=0):
+def call(
+    kernel,
+    loaded,
+    given,
+    out_shape,
+    scratch,
+    flops,
+    moved,
+    mib,
+    windows=None,
+    smem=0,
+    kept=(),
+    aliases=None,
+    outside=(),
+):
     windows = windows or {}
     places = []
     for i, value in enumerate(loaded):
         dims = value.shape if i not in windows else (windows[i][1],) + value.shape[1:]
-        places.append(pltpu.VMEM(dims, value.dtype))
+        if i not in kept:
+            places.append(pltpu.VMEM(dims, value.dtype))
+    outs = tuple(out_shape) + tuple(shape(loaded[i].shape, loaded[i].dtype) for i in kept)
     return pl.pallas_call(
-        loading(kernel, len(loaded), len(given), len(out_shape), windows),
-        out_shape=out_shape,
+        loading(kernel, len(loaded), len(given), len(out_shape), windows, kept),
+        out_shape=outs,
         in_specs=[HBM] * len(loaded) + [SMEM] * smem + [VMEM] * (len(given) - smem),
-        out_specs=[VMEM] * len(out_shape),
+        out_specs=[HBM if i in outside else VMEM for i in range(len(outs))],
         scratch_shapes=places + [pltpu.SemaphoreType.DMA((max(len(loaded), 1),))] + scratch,
         compiler_params=pltpu.CompilerParams(vmem_limit_bytes=mib * 1024 * 1024),
         cost_estimate=pl.CostEstimate(flops=flops, bytes_accessed=moved, transcendentals=0),
+        input_output_aliases=aliases or {},
     )(*[pltpu.with_memory_space_constraint(value, pltpu.HBM) for value in loaded], *given)
 
 
@@ -362,7 +432,7 @@
     user = lax.axis_index("user")
 
     halo = lax.ppermute(hist[length - ALIGN :], "tm", [(i, (i + 1) % n_tm) for i in range(n_tm)])
-    xbc, cum, dt_t, cum_t, pay = call(
+    early, cum, dt_t, cum_t, weight, last, head, later, taps, bias, w = call(
         functools.partial(scan_kernel, heads),
         (
             hist,
@@ -373,18 +443,33 @@
             conv_bias.reshape(channels // LANES, LANES),
             xbc_weight,
         ),
-        (halo,),
+        (),
         (
             shape((length, channels), BF16),
             shape((length, heads), F32),
             shape((heads, length), F32),
             shape((heads, length), F32),
-            shape((state + ALIGN, inner), BF16),
+            shape((ALIGN, heads), F32),
+            shape((ALIGN, heads), F32),
+            shape((ALIGN, channels), F32),
+            shape((state, inner), F32),
         ),
         [pltpu.VMEM((length + ALIGN, channels), F32), pltpu.VMEM((length, inner), BF16)],
         2 * length * width * channels,
         4 * width * channels,
         16,
+        kept=(4, 5, 6),
+    )
+    xbc, pay = call(
+        functools.partial(edge_kernel, heads),
+        (),
+        (halo, w, taps, bias, weight, last, head, later, early),
+        (shape((length, channels), BF16), shape((state + ALIGN, inner), BF16)),
+        [pltpu.VMEM((2 * ALIGN, channels), F32)],
+        2 * ALIGN * width * channels,
+        2 * width * channels,
+        10,
+        aliases={8: 0},
     )
     other = lax.ppermute(pay, "tm", [(i, i ^ 1) for i in range(n_tm)])
     chip_state, chip_gain = call(
@@ -403,63 +488,77 @@
         incoming = jnp.where(tm < 2, 0.0, incoming.astype(F32))
         passed = chip_gain[0:1] * incoming + chip_state.astype(F32)
         incoming = lax.ppermute(passed.astype(BF16), "tm", onward)
-    part, gate, pre = call(
+    own, across, pre, hot, hot_t, item_t = call(
         functools.partial(within_kernel, heads),
-        (hist, z_weight, item, first_weight),
+        (hist, z_weight, item, first_weight, label_pos),
         (d_skip, xbc, cum, dt_t, cum_t),
         (
             shape((length, inner), F32),
             shape((length, inner), F32),
             shape((slots, hidden), F32),
+            shape((slots, length), BF16),
+            shape((length, slots), BF16),
+            shape((width, slots), BF16),
         ),
-        [],
+        [pltpu.VMEM((length, inner), F32)],
         2 * length * width * inner + 2 * slots * width * hidden + 4 * length * length * inner,
         16 * length * inner * 4,
-        20,
+        24,
         {3: (width, width)},
         1,
     )
-    enc, row_logit, send, keep = call(
-        functools.partial(rank_kernel, heads),
+    enc, row_logit, slope, rank_t, *send = call(
+        rank_kernel,
         (
             norm_gain.reshape(1, inner),
             out_weight,
-            label_pos,
             first_weight,
             second_weight.reshape(hidden // LANES, LANES),
             label_value,
-            item,
         ),
-        (label_count, incoming, other, xbc, cum, part, gate, pre),
+        (label_count, incoming, other, xbc, own, across, pre, hot, hot_t, item_t),
         (
             shape((length, width), BF16),
             shape((1, slots), F32),
-            shape((width + 8, hidden), BF16),
-            shape((width + 8, hidden), BF16),
-        ),
+            shape((slots, hidden), BF16),
+            shape((width, slots), BF16),
+        )
+        + chunk_shapes(width, hidden),
         [
             pltpu.VMEM((length, inner), F32),
             pltpu.VMEM((slots, width), BF16),
             pltpu.VMEM((slots, hidden), F32),
             pltpu.VMEM((slots, hidden), BF16),
-            pltpu.VMEM((slots, hidden), BF16),
+            pltpu.VMEM((length, width), BF16),
+            pltpu.SemaphoreType.DMA,
         ],
         4 * slots * width * hidden,
         8 * slots * hidden,
         24,
-        {3: (0, width)},
+        {2: (0, width)},
         1,
+        outside=(0,),
+    )
+    keep = call(
+        home_kernel,
+        (),
+        (rank_t, item_t, slope, send[-1]),
+        chunk_shapes(width, hidden),
+        [],
+        2 * slots * width * hidden,
+        4 * slots * hidden,
+        8,
     )
     grad_first, grad_second = total_sum(send, keep, n_user, n_tm, user, tm)
     return (enc[None], row_logit, grad_first, grad_second)
 
 
 def total_sum(send, keep, n_user, n_tm, user, tm):
-    rows = keep.shape[0] - 8
+    rows = sum(part.shape[0] for part in keep) - 8
     odd = tm % 2
     axes = ("user", "tm")
     every = [(u, t) for u in range(n_user) for t in range(n_tm)]
-    chunks = len((1, 1, 1, 1))
+    chunks = CHUNKS
 
     def swap(value, partner):
         pairs = [(u * n_tm + t, partner(u, t)) for u, t in every]
@@ -491,19 +590,12 @@
 
     levels = len(order_even)
     bits = [bit_of(level) for level in range(levels)]
-    bit = odd == 1
-    edges = [rows * sum((1, 1, 1, 1)[:k]) // sum((1, 1, 1, 1)) for k in range(chunks + 1)]
-    pieces = []
-    for k in range(chunks):
-        last = k == chunks - 1
-        stop = edges[k + 1] + (8 if last else 0)
-        pieces.append((send[edges[k] : stop], keep[edges[k] : stop], last))
+    size = rows // chunks
     state = []
-    for leave, stay, has_extra in pieces:
-        size = stay.shape[0] - (8 if has_extra else 0)
+    for leave, stay in zip(send, keep):
         got = swap(leave, across)
         extra = None
-        if has_extra:
+        if stay.shape[0] > size:
             extra = (stay[size:].astype(F32) + got[size:].astype(F32)).astype(BF16)
         state.append((stay[:size], got[:size], extra))
     for level in range(levels - 1):
@@ -540,18 +632,74 @@
             second = jnp.where(bits[level], whole, got)
             after.append((jnp.concatenate([first, second], axis=0), extra))
         wholes = after
-    tops, bottoms = [], []
+    arrived = []
     for whole, extra in wholes:
-        n = whole.shape[0]
-        if extra is None:
-            got = swap(whole, across)
-        else:
-            got = swap(jnp.concatenate([whole, extra], axis=0), across)
-            grad_second = jnp.where(bit, got[n:], extra)[0].astype(F32)
-            got = got[:n]
-        tops.append(jnp.where(bit, got, whole).astype(F32))
-        bottoms.append(jnp.where(bit, whole, got).astype(F32))
-    return jnp.concatenate(tops + bottoms, axis=0), grad_second
+        arrived.append(
+            swap(whole if extra is None else jnp.concatenate([whole, extra], axis=0), across)
+        )
+    own_extra = wholes[-1][1]
+    mine = [whole for whole, _ in wholes]
+    total = (2 * rows,) + mine[0].shape[1:]
+    last = chunks - 1
+    own = [(w, 0, k) for k, w in enumerate(mine)]
+    other = [(w, 1, k) for k, w in enumerate(arrived)]
+    grad_first = written(None, own + other[:last], rows, total)
+    grad_first, grad_second = written(grad_first, other[last:], rows, total, own_extra)
+    return grad_first, grad_second.reshape(total[1:])
+
+
+def written(so_far, blocks, half_rows, total, own_extra=None):
+    size = blocks[0][0].shape[0]
+    size -= size % LANES
+    given = [value for value, _, _ in blocks]
+    n = len(given)
+    wide = given[-1].shape[0] > size
+    aliased = so_far is not None
+
+    def kernel(*refs):
+        refs = list(refs)
+        if aliased:
+            refs.pop(0)
+        values = [refs.pop(0) for _ in range(n)]
+        mine = refs.pop(0) if wide else None
+        out = refs.pop(0)
+        second = refs.pop(0) if wide else None
+        buf, sems = refs
+        odd = lax.rem(lax.axis_index("tm"), 2)
+        copies = []
+        for i, (_, other, k) in enumerate(blocks):
+            buf[i] = values[i][:size, :].astype(F32)
+            side = 1 - odd if other else odd
+            at = pl.multiple_of(side * half_rows + k * size, 8)
+            copies.append(pltpu.make_async_copy(buf.at[i], out.at[pl.ds(at, size)], sems.at[i]))
+            copies[i].start()
+        if wide:
+            own = mine[...].astype(F32)[0:1]
+            got = values[-1][size:, :].astype(F32)[0:1]
+            second[...] = jnp.where(odd == 1, got, own)
+        for copy in copies:
+            copy.wait()
+
+    outs = [jax.ShapeDtypeStruct(total, F32)]
+    if wide:
+        outs.append(jax.ShapeDtypeStruct((1, total[1]), F32))
+        given = given + [own_extra]
+    operands = given
+    if aliased:
+        operands = [pltpu.with_memory_space_constraint(so_far, pltpu.HBM)] + given
+    result = pl.pallas_call(
+        kernel,
+        out_shape=tuple(outs),
+        in_specs=[HBM] * aliased + [VMEM] * len(given),
+        out_specs=tuple([HBM] + [VMEM] * wide),
+        scratch_shapes=[pltpu.VMEM((n, size, total[1]), F32), pltpu.SemaphoreType.DMA((n,))],
+        input_output_aliases={0: 0} if aliased else {},
+        compiler_params=pltpu.CompilerParams(vmem_limit_bytes=12 * 1024 * 1024),
+        cost_estimate=pl.CostEstimate(
+            flops=n * size * total[1], bytes_accessed=6 * n * size * total[1], transcendentals=0
+        ),
+    )(*operands)
+    return result if wide else result[0]
 
 
 def solution(mesh):

time: 71.4 us -> 70.2 us (0.983)
  starting transfers between devices: 33.5 us -> 27.5 us
  Pallas kernels: 14.2 us -> 19.2 us
  waiting for transfers between devices: 16 us -> 19.7 us
  other arithmetic: 4.87 us -> 1.18 us
    ppermute x28, starting transfers between devices: 30.5 us -> 24 us  [swap(): return lax.ppermute(value, axes, pairs)]
    ppermute x28, waiting for transfers between devices: 9.07 us -> 15.4 us  [swap(): return lax.ppermute(value, axes, pairs)]
    pallas_call x0 -> x2, Pallas kernels: none -> 3.35 us  [written(): pl.pallas_call(kernel, out_shape=tuple(outs), in_specs=[HBM] * aliased +...]
    ppermute x1, waiting for transfers between devices: 3.33 us -> 0.01 us  [body(): lax.ppermute(hist[length - ALIGN:], 'tm', [(i, (i + 1) % n_tm) for i in r...]
    concatenate x3 -> x1, other arithmetic: 2.57 us -> 0.02 us  [total_sum(): jnp.concatenate([whole, extra], axis=0)]
    ppermute x1, starting transfers between devices: 0.19 us -> 2.66 us  [body(): other = lax.ppermute(pay, 'tm', [(i, i ^ 1) for i in range(n_tm)])]
    ppermute x1, starting transfers between devices: 2.37 us -> 0.33 us  [body(): incoming = lax.ppermute(chip_state, 'tm', onward)]
    pallas_call x4 -> x6, Pallas kernels: 14.2 us -> 15.8 us  [call(): pl.pallas_call(loading(kernel, len(loaded), len(given), len(out_shape), w...]
  transfers between devices with their start and end apart: 31 -> 31, of which waited for: 13 -> 13; matrix products, arithmetic and copies ran while one was open for 2% -> 2% of each run, Pallas kernels for 5% -> 15%
where the time goes in v6:
time: 70.2 us; the launch traced here: 69.9 us
  starting transfers between devices  27.5 us (39%)
  waiting for transfers between devices  19.7 us (28%)
  Pallas kernels  19.2 us (27%)
  between operations  1.69 us (2%)
  other arithmetic  1.18 us (2%)
  local copies, waits for them, and re-layouts  0.73 us (1%)
    ppermute x28, starting transfers between devices, swap(): return lax.ppermute(value, axes, pairs)  24 us
    pallas_call x6, Pallas kernels, call(): pl.pallas_call(loading(kernel, len(loaded), len(given), len(out_shape), w...  15.8 us
    ppermute x28, waiting for transfers between devices, swap(): return lax.ppermute(value, axes, pairs)  15.4 us
    pallas_call x2, Pallas kernels, written(): pl.pallas_call(kernel, out_shape=tuple(outs), in_specs=[HBM] * aliased +...  3.35 us
    ppermute x1, waiting for transfers between devices, body(): incoming = lax.ppermute(chip_state, 'tm', onward)  3.11 us
    ppermute x1, starting transfers between devices, body(): other = lax.ppermute(pay, 'tm', [(i, i ^ 1) for i in range(n_tm)])  2.66 us
  transfers between devices with their start and end apart: 31, of which 13 were waited for; matrix products, arithmetic and copies ran while one was open for 2% of the time, Pallas kernels for 15%

profile of v6, /device:TPU:0, one launch (start us, length us, event | category | flops | bytes accessed | tf_op | source)
XLA Modules:
  0.0 69.9 jit_solution(11364648739009213291)
XLA Ops:
  1.8 3.4 %shard_map.192 = (bf16[256,1280]{1,0:T(8,128)(2,1)S(1)}, f32[256,16]{1,0:T(8,128)S(1)}, f32[16,256]{1,0:T(8,128)S(1)}, f32[16,256]{1,0:T(8,128)S(1)}, f32[16,16]...) custom-call(bf16[256,512]{1,0:T(8,128)(2,1)} %bitcast.12, ...), custom_call_target="tpu_custom_call" | custom-call | flops 335544320 | bytes 2621440 | tf_op jit(solution)/shard_map/pallas_call | solution.py:380
  5.9 2.7 %collective-permute-start.1 = (bf16[144,1024]{1,0:T(8,128)(2,1)S(1)}, bf16[144,1024]{1,0:T(8,128)(2,1)S(1)}, u32[]{:S(2)}, u32[]{:S(2)}) collective-permute-start(bf16[144,1024]{1,0:T(8,128)(2,1)S(1)} %get-tuple-element.46.refs_0_), channel_id=1, source_target_pairs={{0,1},{1,0},{2,3},{3,2},{4,5},{5,4},{6,7},{7,6},{8,9},{9,8},{10,11... | collective-permute-start | bytes 884744 | tf_op jit(solution)/shard_map/ppermute | solution.py:474
  8.6 1.2 %collective-permute-done.1.refs_1_.refs_7_ = bf16[144,1024]{1,0:T(8,128)(2,1)S(1)} collective-permute-done((bf16[144,1024]{1,0:T(8,128)(2,1)S(1)}, bf16[144,1024]{1,0:T(8,128)(2,1)S(1)}, u32[]{:S(2)}, u32[]{:S(2)}) %collective-permute-start.1) | collective-permute-done | bytes 294944 | tf_op jit(solution)/shard_map/ppermute | solution.py:474
  11.4 4.5 %shard_map.195 = (f32[256,1024]{1,0:T(8,128)S(1)}, f32[256,1024]{1,0:T(8,128)S(1)}, f32[512,1024]{1,0:T(8,128)S(1)}, bf16[512,256]{1,0:T(8,128)(2,1)S(1)}, bf16[...) custom-call(bf16[256,512]{1,0:T(8,128)(2,1)} %bitcast.13, bf16[512,1024]{1,0:T(8,128)(2,1)} %refs_1_.2, ...), custom_call_target="tpu_custom_call" | custom-call | flops 1073741824 | bytes 16777216 | tf_op jit(solution)/shard_map/pallas_call | solution.py:380
  16.0 3.1 %collective-permute-done.2.refs_6_ = bf16[128,1024]{1,0:T(8,128)(2,1)S(1)} collective-permute-done((bf16[128,1024]{1,0:T(8,128)(2,1)S(1)}, bf16[128,1024]{1,0:T(8,128)(2,1)S(1)}, u32[]{:S(2)}, u32[]{:S(2)}) %collective-permute-start.2) | collective-permute-done | bytes 262176 | tf_op jit(solution)/shard_map/ppermute | solution.py:486
  19.1 5.9 %shard_map.196 = (bf16[256,512]{1,0:T(8,128)(2,1)}, f32[1,512]{1,0:T(1,128)}, bf16[512,1024]{1,0:T(8,128)(2,1)S(1)}, bf16[512,512]{1,0:T(8,128)(2,1)S(1)}, bf16[...) custom-call(f32[1,1024]{1,0:T(1,128)} %bitcast.17, ...), custom_call_target="tpu_custom_call" | custom-call | flops 1073741824 | bytes 4194304 | tf_op jit(solution)/shard_map/pallas_call | solution.py:380
  27.4 1.7 %collective-permute-start.10 = (bf16[64,1024]{1,0:T(8,128)(2,1)S(1)}, bf16[64,1024]{1,0:T(8,128)(2,1)S(1)}, u32[]{:S(2)}, u32[]{:S(2)}) collective-permute-start(bf16[64,1024]{1,0:T(8,128)(2,1)S(1)} %get-tuple-element.77), channel_id=1, source_target_pairs={{0,2},{1,5},{2,0},{3,7},{4,6},{5,1},{6,4},{7,3},{8,10},{9,13},{10,... | collective-permute-start | bytes 393224 | tf_op jit(solution)/shard_map/ppermute | solution.py:565
  29.8 1.7 %collective-permute-start.22 = (bf16[72,1024]{1,0:T(8,128)(2,1)S(1)}, bf16[72,1024]{1,0:T(8,128)(2,1)S(1)}, u32[]{:S(2)}, u32[]{:S(2)}) collective-permute-start(bf16[72,1024]{1,0:T(8,128)(2,1)S(1)} %pad_maximum_fusion.5), channel_id=1, source_target_pairs={{0,2},{1,5},{2,0},{3,7},{4,6},{5,1},{6,4},{7,3},{8,10},{9,13},{10,... | collective-permute-start | bytes 442376 | tf_op jit(solution)/shard_map/ppermute | solution.py:565
  32.0 1.6 %collective-permute-start.17 = (bf16[32,1024]{1,0:T(8,128)(2,1)S(1)}, bf16[32,1024]{1,0:T(8,128)(2,1)S(1)}, u32[]{:S(2)}, u32[]{:S(2)}) collective-permute-start(bf16[32,1024]{1,0:T(8,128)(2,1)S(1)} %select_convert_fusion.10), channel_id=1, source_target_pairs={{0,4},{1,9},{2,6},{3,11},{4,0},{5,13},{6,2},{7,15},{8,12},{9,1},{1... | collective-permute-start | bytes 196616 | tf_op jit(solution)/shard_map/ppermute | solution.py:565
  33.7 1.4 %collective-permute-start.11 = (bf16[32,1024]{1,0:T(8,128)(2,1)S(1)}, bf16[32,1024]{1,0:T(8,128)(2,1)S(1)}, u32[]{:S(2)}, u32[]{:S(2)}) collective-permute-start(bf16[32,1024]{1,0:T(8,128)(2,1)S(1)} %select_convert_fusion.12), channel_id=1, source_target_pairs={{0,4},{1,9},{2,6},{3,11},{4,0},{5,13},{6,2},{7,15},{8,12},{9,1},{1... | collective-permute-start | bytes 196616 | tf_op jit(solution)/shard_map/ppermute | solution.py:565
  35.1 1.4 %collective-permute-start.5 = (bf16[32,1024]{1,0:T(8,128)(2,1)S(1)}, bf16[32,1024]{1,0:T(8,128)(2,1)S(1)}, u32[]{:S(2)}, u32[]{:S(2)}) collective-permute-start(bf16[32,1024]{1,0:T(8,128)(2,1)S(1)} %select_convert_fusion.14), channel_id=1, source_target_pairs={{0,4},{1,9},{2,6},{3,11},{4,0},{5,13},{6,2},{7,15},{8,12},{9,1},{1... | collective-permute-start | bytes 196616 | tf_op jit(solution)/shard_map/ppermute | solution.py:565
  36.5 1.5 %collective-permute-start.23 = (bf16[40,1024]{1,0:T(8,128)(2,1)S(1)}, bf16[40,1024]{1,0:T(8,128)(2,1)S(1)}, u32[]{:S(2)}, u32[]{:S(2)}) collective-permute-start(bf16[40,1024]{1,0:T(8,128)(2,1)S(1)} %pad_maximum_fusion.10), channel_id=1, source_target_pairs={{0,4},{1,9},{2,6},{3,11},{4,0},{5,13},{6,2},{7,15},{8,12},{9,1},{1... | collective-permute-start | bytes 245768 | tf_op jit(solution)/shard_map/ppermute | solution.py:565
  38.1 2.6 %collective-permute-start.18 = (bf16[32,1024]{1,0:T(8,128)(2,1)S(1)}, bf16[32,1024]{1,0:T(8,128)(2,1)S(1)}, u32[]{:S(2)}, u32[]{:S(2)}) collective-permute-start(bf16[32,1024]{1,0:T(8,128)(2,1)S(1)} %add_convert_fusion.3), channel_id=1, source_target_pairs={{0,8},{1,3},{2,10},{3,1},{4,12},{5,7},{6,14},{7,5},{8,0},{9,11},{1... | collective-permute-start | bytes 196616 | tf_op jit(solution)/shard_map/ppermute | solution.py:565
  41.4 2.5 %collective-permute-start.6 = (bf16[32,1024]{1,0:T(8,128)(2,1)S(1)}, bf16[32,1024]{1,0:T(8,128)(2,1)S(1)}, u32[]{:S(2)}, u32[]{:S(2)}) collective-permute-start(bf16[32,1024]{1,0:T(8,128)(2,1)S(1)} %add_convert_fusion.7), channel_id=1, source_target_pairs={{0,8},{1,3},{2,10},{3,1},{4,12},{5,7},{6,14},{7,5},{8,0},{9,11},{1... | collective-permute-start | bytes 196616 | tf_op jit(solution)/shard_map/ppermute | solution.py:565
  44.6 1.9 %collective-permute-start.19 = (bf16[32,1024]{1,0:T(8,128)(2,1)S(1)}, bf16[32,1024]{1,0:T(8,128)(2,1)S(1)}, u32[]{:S(2)}, u32[]{:S(2)}) collective-permute-start(bf16[32,1024]{1,0:T(8,128)(2,1)S(1)} %add_convert_fusion.2), channel_id=1, source_target_pairs={{0,4},{1,9},{2,6},{3,11},{4,0},{5,13},{6,2},{7,15},{8,12},{9,1},{1... | collective-permute-start | bytes 196616 | tf_op jit(solution)/shard_map/ppermute | solution.py:565
  47.3 5.3 %collective-permute-done.6 = bf16[32,1024]{1,0:T(8,128)(2,1)S(1)} collective-permute-done((bf16[32,1024]{1,0:T(8,128)(2,1)S(1)}, bf16[32,1024]{1,0:T(8,128)(2,1)S(1)}, u32[]{:S(2)}, u32[]{:S(2)}) %collective-permute-start.6) | collective-permute-done | bytes 65568 | tf_op jit(solution)/shard_map/ppermute | solution.py:565
  52.7 1.7 %collective-permute-done.24 = bf16[40,1024]{1,0:T(8,128)(2,1)S(1)} collective-permute-done((bf16[40,1024]{1,0:T(8,128)(2,1)S(1)}, bf16[40,1024]{1,0:T(8,128)(2,1)S(1)}, u32[]{:S(2)}, u32[]{:S(2)}) %collective-permute-start.24) | collective-permute-done | bytes 81952 | tf_op jit(solution)/shard_map/ppermute | solution.py:565
  55.2 1.9 %collective-permute-start.14 = (bf16[64,1024]{1,0:T(8,128)(2,1)S(1)}, bf16[64,1024]{1,0:T(8,128)(2,1)S(1)}, u32[]{:S(2)}, u32[]{:S(2)}) collective-permute-start(bf16[64,1024]{1,0:T(8,128)(2,1)S(1)} %pad_maximum_fusion.7), channel_id=1, source_target_pairs={{0,2},{1,5},{2,0},{3,7},{4,6},{5,1},{6,4},{7,3},{8,10},{9,13},{10,... | collective-permute-start | bytes 393224 | tf_op jit(solution)/shard_map/ppermute | solution.py:565
  57.8 1.6 %collective-permute-done.25 = bf16[32,1024]{1,0:T(8,128)(2,1)S(1)} collective-permute-done((bf16[32,1024]{1,0:T(8,128)(2,1)S(1)}, bf16[32,1024]{1,0:T(8,128)(2,1)S(1)}, u32[]{:S(2)}, u32[]{:S(2)}) %collective-permute-start.25) | collective-permute-done | bytes 65568 | tf_op jit(solution)/shard_map/ppermute | solution.py:565
  61.4 1.3 %collective-permute-done.8 = bf16[64,1024]{1,0:T(8,128)(2,1)S(1)} collective-permute-done((bf16[64,1024]{1,0:T(8,128)(2,1)S(1)}, bf16[64,1024]{1,0:T(8,128)(2,1)S(1)}, u32[]{:S(2)}, u32[]{:S(2)}) %collective-permute-start.8) | collective-permute-done | bytes 131104 | tf_op jit(solution)/shard_map/ppermute | solution.py:565
  62.8 1.7 %collective-permute-done.26 = bf16[64,1024]{1,0:T(8,128)(2,1)S(1)} collective-permute-done((bf16[64,1024]{1,0:T(8,128)(2,1)S(1)}, bf16[64,1024]{1,0:T(8,128)(2,1)S(1)}, u32[]{:S(2)}, u32[]{:S(2)}) %collective-permute-start.26) | collective-permute-done | bytes 131104 | tf_op jit(solution)/shard_map/ppermute | solution.py:565
  65.3 1.3 %collective-permute-done.27.refs_4_ = bf16[128,1024]{1,0:T(8,128)(2,1)S(1)} collective-permute-done((bf16[128,1024]{1,0:T(8,128)(2,1)S(1)}, bf16[128,1024]{1,0:T(8,128)(2,1)S(1)}, u32[]{:S(2)}, u32[]{:S(2)}) %collective-permute-start.27) | collective-permute-done | bytes 262176 | tf_op jit(solution)/shard_map/ppermute | solution.py:565
  66.6 1.9 %shard_map.198.refs_0_ = f32[1024,1024]{1,0:T(8,128)} custom-call(bf16[128,1024]{1,0:T(8,128)(2,1)S(1)} %pad_maximum_fusion.1.refs_0_, bf16[128,1024]{1,0:T(8,128)(2,1)S(1)} %pad_maximum_fusion.2.refs_1_, bf16[128,1024]{1,0:T(8,128)(2,1)S(1)} %pad_maximum_fusion.3.refs_2_, bf16[128,1024]{1,0:T(8,128)(2,1)S(1)} %pad_maximum_fusion.4.refs_3_, ...), custom_call_target="tpu_custom_call" | custom-call | flops 917504 | bytes 5505024 | tf_op jit(solution)/shard_map/pallas_call | solution.py:690
  68.5 1.4 %shard_map.199 = (f32[1024,1024]{1,0:T(8,128)}, f32[1,1024]{1,0:T(1,128)}) custom-call(f32[1024,1024]{1,0:T(8,128)} %shard_map.198.refs_0_, bf16[136,1024]{1,0:T(8,128)(2,1)S(1)} %collective-permute-done.30.refs_1_, bf16[8,1024]{1,0:T(8,128)(2,1)S(1)} %add_convert_fusion.8.refs_2_), custom_call_target="tpu_custom_call", output_to_operand_aliasing={{0}: (0, {})} | custom-call | flops 131072 | bytes 786432 | tf_op jit(solution)/shard_map/pallas_call | solution.py:690
  (89 shorter events, 13.1 us)
Async XLA Ops:
  10.4 8.7 %collective-permute-start.2 = (bf16[128,1024]{1,0:T(8,128)(2,1)S(1)}, bf16[128,1024]{1,0:T(8,128)(2,1)S(1)}, u32[]{:S(2)}, u32[]{:S(2)}) collective-permute-start(bf16[128,1024]{1,0:T(8,128)(2,1)S(1)} %get-tuple-element.47), channel_id=1, source_target_pairs={{0,2},{1,3},{2,0},{3,1},{4,6},{5,7},{6,4},{7,5},{8,10},{9,11},{10,... | collective-permute-start | bytes 786440 | tf_op jit(solution)/shard_map/ppermute | solution.py:486
  25.1 4.6 %collective-permute-start.21 = (bf16[136,1024]{1,0:T(8,128)(2,1)S(1)}, bf16[136,1024]{1,0:T(8,128)(2,1)S(1)}, u32[]{:S(2)}, u32[]{:S(2)}) collective-permute-start(bf16[136,1024]{1,0:T(8,128)(2,1)S(1)} %get-tuple-element.62.refs_3_), channel_id=1, source_target_pairs={{0,1},{1,0},{2,3},{3,2},{4,5},{5,4},{6,7},{7,6},{8,9},{9,8},{10,11... | collective-permute-start | bytes 835592 | tf_op jit(solution)/shard_map/ppermute | solution.py:565
  26.9 5.0 %collective-permute-start.16 = (bf16[64,1024]{1,0:T(8,128)(2,1)S(1)}, bf16[64,1024]{1,0:T(8,128)(2,1)S(1)}, u32[]{:S(2)}, u32[]{:S(2)}) collective-permute-start(bf16[64,1024]{1,0:T(8,128)(2,1)S(1)} %get-tuple-element.75), channel_id=1, source_target_pairs={{0,2},{1,5},{2,0},{3,7},{4,6},{5,1},{6,4},{7,3},{8,10},{9,13},{10,... | collective-permute-start | bytes 393224 | tf_op jit(solution)/shard_map/ppermute | solution.py:565
  27.4 6.2 %collective-permute-start.10 = (bf16[64,1024]{1,0:T(8,128)(2,1)S(1)}, bf16[64,1024]{1,0:T(8,128)(2,1)S(1)}, u32[]{:S(2)}, u32[]{:S(2)}) collective-permute-start(bf16[64,1024]{1,0:T(8,128)(2,1)S(1)} %get-tuple-element.77), channel_id=1, source_target_pairs={{0,2},{1,5},{2,0},{3,7},{4,6},{5,1},{6,4},{7,3},{8,10},{9,13},{10,... | collective-permute-start | bytes 393224 | tf_op jit(solution)/shard_map/ppermute | solution.py:565
  29.2 5.8 %collective-permute-start.4 = (bf16[64,1024]{1,0:T(8,128)(2,1)S(1)}, bf16[64,1024]{1,0:T(8,128)(2,1)S(1)}, u32[]{:S(2)}, u32[]{:S(2)}) collective-permute-start(bf16[64,1024]{1,0:T(8,128)(2,1)S(1)} %get-tuple-element.79), channel_id=1, source_target_pairs={{0,2},{1,5},{2,0},{3,7},{4,6},{5,1},{6,4},{7,3},{8,10},{9,13},{10,... | collective-permute-start | bytes 393224 | tf_op jit(solution)/shard_map/ppermute | solution.py:565
  29.8 6.6 %collective-permute-start.22 = (bf16[72,1024]{1,0:T(8,128)(2,1)S(1)}, bf16[72,1024]{1,0:T(8,128)(2,1)S(1)}, u32[]{:S(2)}, u32[]{:S(2)}) collective-permute-start(bf16[72,1024]{1,0:T(8,128)(2,1)S(1)} %pad_maximum_fusion.5), channel_id=1, source_target_pairs={{0,2},{1,5},{2,0},{3,7},{4,6},{5,1},{6,4},{7,3},{8,10},{9,13},{10,... | collective-permute-start | bytes 442376 | tf_op jit(solution)/shard_map/ppermute | solution.py:565
  32.0 6.1 %collective-permute-start.17 = (bf16[32,1024]{1,0:T(8,128)(2,1)S(1)}, bf16[32,1024]{1,0:T(8,128)(2,1)S(1)}, u32[]{:S(2)}, u32[]{:S(2)}) collective-permute-start(bf16[32,1024]{1,0:T(8,128)(2,1)S(1)} %select_convert_fusion.10), channel_id=1, source_target_pairs={{0,4},{1,9},{2,6},{3,11},{4,0},{5,13},{6,2},{7,15},{8,12},{9,1},{1... | collective-permute-start | bytes 196616 | tf_op jit(solution)/shard_map/ppermute | solution.py:565
  33.7 7.1 %collective-permute-start.11 = (bf16[32,1024]{1,0:T(8,128)(2,1)S(1)}, bf16[32,1024]{1,0:T(8,128)(2,1)S(1)}, u32[]{:S(2)}, u32[]{:S(2)}) collective-permute-start(bf16[32,1024]{1,0:T(8,128)(2,1)S(1)} %select_convert_fusion.12), channel_id=1, source_target_pairs={{0,4},{1,9},{2,6},{3,11},{4,0},{5,13},{6,2},{7,15},{8,12},{9,1},{1... | collective-permute-start | bytes 196616 | tf_op jit(solution)/shard_map/ppermute | solution.py:565
  35.1 6.3 %collective-permute-start.5 = (bf16[32,1024]{1,0:T(8,128)(2,1)S(1)}, bf16[32,1024]{1,0:T(8,128)(2,1)S(1)}, u32[]{:S(2)}, u32[]{:S(2)}) collective-permute-start(bf16[32,1024]{1,0:T(8,128)(2,1)S(1)} %select_convert_fusion.14), channel_id=1, source_target_pairs={{0,4},{1,9},{2,6},{3,11},{4,0},{5,13},{6,2},{7,15},{8,12},{9,1},{1... | collective-permute-start | bytes 196616 | tf_op jit(solution)/shard_map/ppermute | solution.py:565
  36.5 7.4 %collective-permute-start.23 = (bf16[40,1024]{1,0:T(8,128)(2,1)S(1)}, bf16[40,1024]{1,0:T(8,128)(2,1)S(1)}, u32[]{:S(2)}, u32[]{:S(2)}) collective-permute-start(bf16[40,1024]{1,0:T(8,128)(2,1)S(1)} %pad_maximum_fusion.10), channel_id=1, source_target_pairs={{0,4},{1,9},{2,6},{3,11},{4,0},{5,13},{6,2},{7,15},{8,12},{9,1},{1... | collective-permute-start | bytes 245768 | tf_op jit(solution)/shard_map/ppermute | solution.py:565
  38.1 6.5 %collective-permute-start.18 = (bf16[32,1024]{1,0:T(8,128)(2,1)S(1)}, bf16[32,1024]{1,0:T(8,128)(2,1)S(1)}, u32[]{:S(2)}, u32[]{:S(2)}) collective-permute-start(bf16[32,1024]{1,0:T(8,128)(2,1)S(1)} %add_convert_fusion.3), channel_id=1, source_target_pairs={{0,8},{1,3},{2,10},{3,1},{4,12},{5,7},{6,14},{7,5},{8,0},{9,11},{1... | collective-permute-start | bytes 196616 | tf_op jit(solution)/shard_map/ppermute | solution.py:565
  40.8 6.0 %collective-permute-start.12 = (bf16[32,1024]{1,0:T(8,128)(2,1)S(1)}, bf16[32,1024]{1,0:T(8,128)(2,1)S(1)}, u32[]{:S(2)}, u32[]{:S(2)}) collective-permute-start(bf16[32,1024]{1,0:T(8,128)(2,1)S(1)} %add_convert_fusion.5), channel_id=1, source_target_pairs={{0,8},{1,3},{2,10},{3,1},{4,12},{5,7},{6,14},{7,5},{8,0},{9,11},{1... | collective-permute-start | bytes 196616 | tf_op jit(solution)/shard_map/ppermute | solution.py:565
  41.4 11.2 %collective-permute-start.6 = (bf16[32,1024]{1,0:T(8,128)(2,1)S(1)}, bf16[32,1024]{1,0:T(8,128)(2,1)S(1)}, u32[]{:S(2)}, u32[]{:S(2)}) collective-permute-start(bf16[32,1024]{1,0:T(8,128)(2,1)S(1)} %add_convert_fusion.7), channel_id=1, source_target_pairs={{0,8},{1,3},{2,10},{3,1},{4,12},{5,7},{6,14},{7,5},{8,0},{9,11},{1... | collective-permute-start | bytes 196616 | tf_op jit(solution)/shard_map/ppermute | solution.py:565
  44.0 10.4 %collective-permute-start.24 = (bf16[40,1024]{1,0:T(8,128)(2,1)S(1)}, bf16[40,1024]{1,0:T(8,128)(2,1)S(1)}, u32[]{:S(2)}, u32[]{:S(2)}) collective-permute-start(bf16[40,1024]{1,0:T(8,128)(2,1)S(1)} %pad_maximum_fusion.11), channel_id=1, source_target_pairs={{0,8},{1,3},{2,10},{3,1},{4,12},{5,7},{6,14},{7,5},{8,0},{9,11},{1... | collective-permute-start | bytes 245768 | tf_op jit(solution)/shard_map/ppermute | solution.py:565
  44.6 10.2 %collective-permute-start.19 = (bf16[32,1024]{1,0:T(8,128)(2,1)S(1)}, bf16[32,1024]{1,0:T(8,128)(2,1)S(1)}, u32[]{:S(2)}, u32[]{:S(2)}) collective-permute-start(bf16[32,1024]{1,0:T(8,128)(2,1)S(1)} %add_convert_fusion.2), channel_id=1, source_target_pairs={{0,4},{1,9},{2,6},{3,11},{4,0},{5,13},{6,2},{7,15},{8,12},{9,1},{1... | collective-permute-start | bytes 196616 | tf_op jit(solution)/shard_map/ppermute | solution.py:565
  46.8 8.3 %collective-permute-start.13 = (bf16[32,1024]{1,0:T(8,128)(2,1)S(1)}, bf16[32,1024]{1,0:T(8,128)(2,1)S(1)}, u32[]{:S(2)}, u32[]{:S(2)}) collective-permute-start(bf16[32,1024]{1,0:T(8,128)(2,1)S(1)} %add_convert_fusion.4), channel_id=1, source_target_pairs={{0,4},{1,9},{2,6},{3,11},{4,0},{5,13},{6,2},{7,15},{8,12},{9,1},{1... | collective-permute-start | bytes 196616 | tf_op jit(solution)/shard_map/ppermute | solution.py:565
  52.6 5.0 %collective-permute-start.7 = (bf16[32,1024]{1,0:T(8,128)(2,1)S(1)}, bf16[32,1024]{1,0:T(8,128)(2,1)S(1)}, u32[]{:S(2)}, u32[]{:S(2)}) collective-permute-start(bf16[32,1024]{1,0:T(8,128)(2,1)S(1)} %add_convert_fusion.6), channel_id=1, source_target_pairs={{0,4},{1,9},{2,6},{3,11},{4,0},{5,13},{6,2},{7,15},{8,12},{9,1},{1... | collective-permute-start | bytes 196616 | tf_op jit(solution)/shard_map/ppermute | solution.py:565
  54.4 5.0 %collective-permute-start.25 = (bf16[32,1024]{1,0:T(8,128)(2,1)S(1)}, bf16[32,1024]{1,0:T(8,128)(2,1)S(1)}, u32[]{:S(2)}, u32[]{:S(2)}) collective-permute-start(bf16[32,1024]{1,0:T(8,128)(2,1)S(1)} %add_convert_fusion), channel_id=1, source_target_pairs={{0,4},{1,9},{2,6},{3,11},{4,0},{5,13},{6,2},{7,15},{8,12},{9,1},{1... | collective-permute-start | bytes 196616 | tf_op jit(solution)/shard_map/ppermute | solution.py:565
  54.8 5.2 %collective-permute-start.20 = (bf16[64,1024]{1,0:T(8,128)(2,1)S(1)}, bf16[64,1024]{1,0:T(8,128)(2,1)S(1)}, u32[]{:S(2)}, u32[]{:S(2)}) collective-permute-start(bf16[64,1024]{1,0:T(8,128)(2,1)S(1)} %pad_maximum_fusion.8), channel_id=1, source_target_pairs={{0,2},{1,5},{2,0},{3,7},{4,6},{5,1},{6,4},{7,3},{8,10},{9,13},{10,... | collective-permute-start | bytes 393224 | tf_op jit(solution)/shard_map/ppermute | solution.py:565
  55.2 6.1 %collective-permute-start.14 = (bf16[64,1024]{1,0:T(8,128)(2,1)S(1)}, bf16[64,1024]{1,0:T(8,128)(2,1)S(1)}, u32[]{:S(2)}, u32[]{:S(2)}) collective-permute-start(bf16[64,1024]{1,0:T(8,128)(2,1)S(1)} %pad_maximum_fusion.7), channel_id=1, source_target_pairs={{0,2},{1,5},{2,0},{3,7},{4,6},{5,1},{6,4},{7,3},{8,10},{9,13},{10,... | collective-permute-start | bytes 393224 | tf_op jit(solution)/shard_map/ppermute | solution.py:565
  57.7 5.0 %collective-permute-start.8 = (bf16[64,1024]{1,0:T(8,128)(2,1)S(1)}, bf16[64,1024]{1,0:T(8,128)(2,1)S(1)}, u32[]{:S(2)}, u32[]{:S(2)}) collective-permute-start(bf16[64,1024]{1,0:T(8,128)(2,1)S(1)} %pad_maximum_fusion.6), channel_id=1, source_target_pairs={{0,2},{1,5},{2,0},{3,7},{4,6},{5,1},{6,4},{7,3},{8,10},{9,13},{10,... | collective-permute-start | bytes 393224 | tf_op jit(solution)/shard_map/ppermute | solution.py:565
  59.4 5.0 %collective-permute-start.26 = (bf16[64,1024]{1,0:T(8,128)(2,1)S(1)}, bf16[64,1024]{1,0:T(8,128)(2,1)S(1)}, u32[]{:S(2)}, u32[]{:S(2)}) collective-permute-start(bf16[64,1024]{1,0:T(8,128)(2,1)S(1)} %pad_maximum_fusion.9), channel_id=1, source_target_pairs={{0,2},{1,5},{2,0},{3,7},{4,6},{5,1},{6,4},{7,3},{8,10},{9,13},{10,... | collective-permute-start | bytes 393224 | tf_op jit(solution)/shard_map/ppermute | solution.py:565
  60.2 5.1 %collective-permute-start.29 = (bf16[128,1024]{1,0:T(8,128)(2,1)S(1)}, bf16[128,1024]{1,0:T(8,128)(2,1)S(1)}, u32[]{:S(2)}, u32[]{:S(2)}) collective-permute-start(bf16[128,1024]{1,0:T(8,128)(2,1)S(1)} %pad_maximum_fusion.3.refs_2_), channel_id=1, source_target_pairs={{0,1},{1,0},{2,3},{3,2},{4,5},{5,4},{6,7},{7,6},{8,9},{9,8},{10,11... | collective-permute-start | bytes 786440 | tf_op jit(solution)/shard_map/ppermute | solution.py:565
  64.6 3.9 %collective-permute-start.30 = (bf16[136,1024]{1,0:T(8,128)(2,1)S(1)}, bf16[136,1024]{1,0:T(8,128)(2,1)S(1)}, u32[]{:S(2)}, u32[]{:S(2)}) collective-permute-start(bf16[136,1024]{1,0:T(8,128)(2,1)S(1)} %pad_maximum_fusion), channel_id=1, source_target_pairs={{0,1},{1,0},{2,3},{3,2},{4,5},{5,4},{6,7},{7,6},{8,9},{9,8},{10,11... | collective-permute-start | bytes 835592 | tf_op jit(solution)/shard_map/ppermute | solution.py:565
  (8 other events, 30.2 us)

commit v7 on v6

--- a/solution.py
+++ b/solution.py
@@ -643,8 +643,7 @@
     last = chunks - 1
     own = [(w, 0, k) for k, w in enumerate(mine)]
     other = [(w, 1, k) for k, w in enumerate(arrived)]
-    grad_first = written(None, own + other[:last], rows, total)
-    grad_first, grad_second = written(grad_first, other[last:], rows, total, own_extra)
+    grad_first, grad_second = written(None, own + other, rows, total, own_extra)
     return grad_first, grad_second.reshape(total[1:])
 
 

time: 70.2 us -> 69.5 us (0.990)
    pallas_call x2 -> x1, Pallas kernels: 3.35 us -> 2.7 us  [written(): pl.pallas_call(kernel, out_shape=tuple(outs), in_specs=[HBM] * aliased +...]
  transfers between devices with their start and end apart: 31 -> 31, of which waited for: 13 -> 13; matrix products, arithmetic and copies ran while one was open for 2% -> 2% of each run, Pallas kernels for 15% -> 12%
where the time goes in v7:
time: 69.5 us; the launch traced here: 69.3 us
  starting transfers between devices  27.5 us (40%)
  waiting for transfers between devices  19.7 us (28%)
  Pallas kernels  18.5 us (27%)
  between operations  1.67 us (2%)
  other arithmetic  1.18 us (2%)
  local copies, waits for them, and re-layouts  0.73 us (1%)
    ppermute x28, starting transfers between devices, swap(): return lax.ppermute(value, axes, pairs)  24 us
    pallas_call x6, Pallas kernels, call(): pl.pallas_call(loading(kernel, len(loaded), len(given), len(out_shape), w...  15.8 us
    ppermute x28, waiting for transfers between devices, swap(): return lax.ppermute(value, axes, pairs)  15.4 us
    ppermute x1, waiting for transfers between devices, body(): incoming = lax.ppermute(chip_state, 'tm', onward)  3.11 us
    pallas_call x1, Pallas kernels, written(): pl.pallas_call(kernel, out_shape=tuple(outs), in_specs=[HBM] * aliased +...  2.7 us
    ppermute x1, starting transfers between devices, body(): other = lax.ppermute(pay, 'tm', [(i, i ^ 1) for i in range(n_tm)])  2.66 us
  transfers between devices with their start and end apart: 31, of which 13 were waited for; matrix products, arithmetic and copies ran while one was open for 2% of the time, Pallas kernels for 12%

profile of v7, /device:TPU:0, one launch (start us, length us, event | category | flops | bytes accessed | tf_op | source)
XLA Modules:
  0.0 69.3 jit_solution(3105945706350114587)
XLA Ops:
  1.8 3.4 %shard_map.192 = (bf16[256,1280]{1,0:T(8,128)(2,1)S(1)}, f32[256,16]{1,0:T(8,128)S(1)}, f32[16,256]{1,0:T(8,128)S(1)}, f32[16,256]{1,0:T(8,128)S(1)}, f32[16,16]...) custom-call(bf16[256,512]{1,0:T(8,128)(2,1)} %bitcast.12, ...), custom_call_target="tpu_custom_call" | custom-call | flops 335544320 | bytes 2621440 | tf_op jit(solution)/shard_map/pallas_call | solution.py:380
  5.9 2.7 %collective-permute-start.1 = (bf16[144,1024]{1,0:T(8,128)(2,1)S(1)}, bf16[144,1024]{1,0:T(8,128)(2,1)S(1)}, u32[]{:S(2)}, u32[]{:S(2)}) collective-permute-start(bf16[144,1024]{1,0:T(8,128)(2,1)S(1)} %get-tuple-element.46.refs_0_), channel_id=1, source_target_pairs={{0,1},{1,0},{2,3},{3,2},{4,5},{5,4},{6,7},{7,6},{8,9},{9,8},{10,11... | collective-permute-start | bytes 884744 | tf_op jit(solution)/shard_map/ppermute | solution.py:474
  8.6 1.2 %collective-permute-done.1.refs_1_.refs_7_ = bf16[144,1024]{1,0:T(8,128)(2,1)S(1)} collective-permute-done((bf16[144,1024]{1,0:T(8,128)(2,1)S(1)}, bf16[144,1024]{1,0:T(8,128)(2,1)S(1)}, u32[]{:S(2)}, u32[]{:S(2)}) %collective-permute-start.1) | collective-permute-done | bytes 294944 | tf_op jit(solution)/shard_map/ppermute | solution.py:474
  11.4 4.5 %shard_map.195 = (f32[256,1024]{1,0:T(8,128)S(1)}, f32[256,1024]{1,0:T(8,128)S(1)}, f32[512,1024]{1,0:T(8,128)S(1)}, bf16[512,256]{1,0:T(8,128)(2,1)S(1)}, bf16[...) custom-call(bf16[256,512]{1,0:T(8,128)(2,1)} %bitcast.13, bf16[512,1024]{1,0:T(8,128)(2,1)} %refs_1_.2, ...), custom_call_target="tpu_custom_call" | custom-call | flops 1073741824 | bytes 16777216 | tf_op jit(solution)/shard_map/pallas_call | solution.py:380
  16.0 3.1 %collective-permute-done.2.refs_6_ = bf16[128,1024]{1,0:T(8,128)(2,1)S(1)} collective-permute-done((bf16[128,1024]{1,0:T(8,128)(2,1)S(1)}, bf16[128,1024]{1,0:T(8,128)(2,1)S(1)}, u32[]{:S(2)}, u32[]{:S(2)}) %collective-permute-start.2) | collective-permute-done | bytes 262176 | tf_op jit(solution)/shard_map/ppermute | solution.py:486
  19.1 5.9 %shard_map.196 = (bf16[256,512]{1,0:T(8,128)(2,1)}, f32[1,512]{1,0:T(1,128)}, bf16[512,1024]{1,0:T(8,128)(2,1)S(1)}, bf16[512,512]{1,0:T(8,128)(2,1)S(1)}, bf16[...) custom-call(f32[1,1024]{1,0:T(1,128)} %bitcast.17, ...), custom_call_target="tpu_custom_call" | custom-call | flops 1073741824 | bytes 4194304 | tf_op jit(solution)/shard_map/pallas_call | solution.py:380
  27.4 1.7 %collective-permute-start.10 = (bf16[64,1024]{1,0:T(8,128)(2,1)S(1)}, bf16[64,1024]{1,0:T(8,128)(2,1)S(1)}, u32[]{:S(2)}, u32[]{:S(2)}) collective-permute-start(bf16[64,1024]{1,0:T(8,128)(2,1)S(1)} %get-tuple-element.77), channel_id=1, source_target_pairs={{0,2},{1,5},{2,0},{3,7},{4,6},{5,1},{6,4},{7,3},{8,10},{9,13},{10,... | collective-permute-start | bytes 393224 | tf_op jit(solution)/shard_map/ppermute | solution.py:565
  29.8 1.7 %collective-permute-start.22 = (bf16[72,1024]{1,0:T(8,128)(2,1)S(1)}, bf16[72,1024]{1,0:T(8,128)(2,1)S(1)}, u32[]{:S(2)}, u32[]{:S(2)}) collective-permute-start(bf16[72,1024]{1,0:T(8,128)(2,1)S(1)} %pad_maximum_fusion.5), channel_id=1, source_target_pairs={{0,2},{1,5},{2,0},{3,7},{4,6},{5,1},{6,4},{7,3},{8,10},{9,13},{10,... | collective-permute-start | bytes 442376 | tf_op jit(solution)/shard_map/ppermute | solution.py:565
  32.0 1.6 %collective-permute-start.17 = (bf16[32,1024]{1,0:T(8,128)(2,1)S(1)}, bf16[32,1024]{1,0:T(8,128)(2,1)S(1)}, u32[]{:S(2)}, u32[]{:S(2)}) collective-permute-start(bf16[32,1024]{1,0:T(8,128)(2,1)S(1)} %select_convert_fusion.10), channel_id=1, source_target_pairs={{0,4},{1,9},{2,6},{3,11},{4,0},{5,13},{6,2},{7,15},{8,12},{9,1},{1... | collective-permute-start | bytes 196616 | tf_op jit(solution)/shard_map/ppermute | solution.py:565
  33.7 1.4 %collective-permute-start.11 = (bf16[32,1024]{1,0:T(8,128)(2,1)S(1)}, bf16[32,1024]{1,0:T(8,128)(2,1)S(1)}, u32[]{:S(2)}, u32[]{:S(2)}) collective-permute-start(bf16[32,1024]{1,0:T(8,128)(2,1)S(1)} %select_convert_fusion.12), channel_id=1, source_target_pairs={{0,4},{1,9},{2,6},{3,11},{4,0},{5,13},{6,2},{7,15},{8,12},{9,1},{1... | collective-permute-start | bytes 196616 | tf_op jit(solution)/shard_map/ppermute | solution.py:565
  35.1 1.4 %collective-permute-start.5 = (bf16[32,1024]{1,0:T(8,128)(2,1)S(1)}, bf16[32,1024]{1,0:T(8,128)(2,1)S(1)}, u32[]{:S(2)}, u32[]{:S(2)}) collective-permute-start(bf16[32,1024]{1,0:T(8,128)(2,1)S(1)} %select_convert_fusion.14), channel_id=1, source_target_pairs={{0,4},{1,9},{2,6},{3,11},{4,0},{5,13},{6,2},{7,15},{8,12},{9,1},{1... | collective-permute-start | bytes 196616 | tf_op jit(solution)/shard_map/ppermute | solution.py:565
  36.5 1.5 %collective-permute-start.23 = (bf16[40,1024]{1,0:T(8,128)(2,1)S(1)}, bf16[40,1024]{1,0:T(8,128)(2,1)S(1)}, u32[]{:S(2)}, u32[]{:S(2)}) collective-permute-start(bf16[40,1024]{1,0:T(8,128)(2,1)S(1)} %pad_maximum_fusion.10), channel_id=1, source_target_pairs={{0,4},{1,9},{2,6},{3,11},{4,0},{5,13},{6,2},{7,15},{8,12},{9,1},{1... | collective-permute-start | bytes 245768 | tf_op jit(solution)/shard_map/ppermute | solution.py:565
  38.1 2.6 %collective-permute-start.18 = (bf16[32,1024]{1,0:T(8,128)(2,1)S(1)}, bf16[32,1024]{1,0:T(8,128)(2,1)S(1)}, u32[]{:S(2)}, u32[]{:S(2)}) collective-permute-start(bf16[32,1024]{1,0:T(8,128)(2,1)S(1)} %add_convert_fusion.3), channel_id=1, source_target_pairs={{0,8},{1,3},{2,10},{3,1},{4,12},{5,7},{6,14},{7,5},{8,0},{9,11},{1... | collective-permute-start | bytes 196616 | tf_op jit(solution)/shard_map/ppermute | solution.py:565
  41.4 2.5 %collective-permute-start.6 = (bf16[32,1024]{1,0:T(8,128)(2,1)S(1)}, bf16[32,1024]{1,0:T(8,128)(2,1)S(1)}, u32[]{:S(2)}, u32[]{:S(2)}) collective-permute-start(bf16[32,1024]{1,0:T(8,128)(2,1)S(1)} %add_convert_fusion.7), channel_id=1, source_target_pairs={{0,8},{1,3},{2,10},{3,1},{4,12},{5,7},{6,14},{7,5},{8,0},{9,11},{1... | collective-permute-start | bytes 196616 | tf_op jit(solution)/shard_map/ppermute | solution.py:565
  44.6 1.9 %collective-permute-start.19 = (bf16[32,1024]{1,0:T(8,128)(2,1)S(1)}, bf16[32,1024]{1,0:T(8,128)(2,1)S(1)}, u32[]{:S(2)}, u32[]{:S(2)}) collective-permute-start(bf16[32,1024]{1,0:T(8,128)(2,1)S(1)} %add_convert_fusion.2), channel_id=1, source_target_pairs={{0,4},{1,9},{2,6},{3,11},{4,0},{5,13},{6,2},{7,15},{8,12},{9,1},{1... | collective-permute-start | bytes 196616 | tf_op jit(solution)/shard_map/ppermute | solution.py:565
  47.3 5.3 %collective-permute-done.6 = bf16[32,1024]{1,0:T(8,128)(2,1)S(1)} collective-permute-done((bf16[32,1024]{1,0:T(8,128)(2,1)S(1)}, bf16[32,1024]{1,0:T(8,128)(2,1)S(1)}, u32[]{:S(2)}, u32[]{:S(2)}) %collective-permute-start.6) | collective-permute-done | bytes 65568 | tf_op jit(solution)/shard_map/ppermute | solution.py:565
  52.7 1.7 %collective-permute-done.24 = bf16[40,1024]{1,0:T(8,128)(2,1)S(1)} collective-permute-done((bf16[40,1024]{1,0:T(8,128)(2,1)S(1)}, bf16[40,1024]{1,0:T(8,128)(2,1)S(1)}, u32[]{:S(2)}, u32[]{:S(2)}) %collective-permute-start.24) | collective-permute-done | bytes 81952 | tf_op jit(solution)/shard_map/ppermute | solution.py:565
  55.2 1.9 %collective-permute-start.14 = (bf16[64,1024]{1,0:T(8,128)(2,1)S(1)}, bf16[64,1024]{1,0:T(8,128)(2,1)S(1)}, u32[]{:S(2)}, u32[]{:S(2)}) collective-permute-start(bf16[64,1024]{1,0:T(8,128)(2,1)S(1)} %pad_maximum_fusion.7), channel_id=1, source_target_pairs={{0,2},{1,5},{2,0},{3,7},{4,6},{5,1},{6,4},{7,3},{8,10},{9,13},{10,... | collective-permute-start | bytes 393224 | tf_op jit(solution)/shard_map/ppermute | solution.py:565
  57.8 1.6 %collective-permute-done.25 = bf16[32,1024]{1,0:T(8,128)(2,1)S(1)} collective-permute-done((bf16[32,1024]{1,0:T(8,128)(2,1)S(1)}, bf16[32,1024]{1,0:T(8,128)(2,1)S(1)}, u32[]{:S(2)}, u32[]{:S(2)}) %collective-permute-start.25) | collective-permute-done | bytes 65568 | tf_op jit(solution)/shard_map/ppermute | solution.py:565
  60.2 1.0 %collective-permute-done.14 = bf16[64,1024]{1,0:T(8,128)(2,1)S(1)} collective-permute-done((bf16[64,1024]{1,0:T(8,128)(2,1)S(1)}, bf16[64,1024]{1,0:T(8,128)(2,1)S(1)}, u32[]{:S(2)}, u32[]{:S(2)}) %collective-permute-start.14) | collective-permute-done | bytes 131104 | tf_op jit(solution)/shard_map/ppermute | solution.py:565
  61.4 1.3 %collective-permute-done.8 = bf16[64,1024]{1,0:T(8,128)(2,1)S(1)} collective-permute-done((bf16[64,1024]{1,0:T(8,128)(2,1)S(1)}, bf16[64,1024]{1,0:T(8,128)(2,1)S(1)}, u32[]{:S(2)}, u32[]{:S(2)}) %collective-permute-start.8) | collective-permute-done | bytes 131104 | tf_op jit(solution)/shard_map/ppermute | solution.py:565
  62.8 1.7 %collective-permute-done.26 = bf16[64,1024]{1,0:T(8,128)(2,1)S(1)} collective-permute-done((bf16[64,1024]{1,0:T(8,128)(2,1)S(1)}, bf16[64,1024]{1,0:T(8,128)(2,1)S(1)}, u32[]{:S(2)}, u32[]{:S(2)}) %collective-permute-start.26) | collective-permute-done | bytes 131104 | tf_op jit(solution)/shard_map/ppermute | solution.py:565
  65.3 1.3 %collective-permute-done.27.refs_4_ = bf16[128,1024]{1,0:T(8,128)(2,1)S(1)} collective-permute-done((bf16[128,1024]{1,0:T(8,128)(2,1)S(1)}, bf16[128,1024]{1,0:T(8,128)(2,1)S(1)}, u32[]{:S(2)}, u32[]{:S(2)}) %collective-permute-start.27) | collective-permute-done | bytes 262176 | tf_op jit(solution)/shard_map/ppermute | solution.py:565
  66.6 2.7 %shard_map.198 = (f32[1024,1024]{1,0:T(8,128)}, f32[1,1024]{1,0:T(1,128)}) custom-call(bf16[128,1024]{1,0:T(8,128)(2,1)S(1)} %pad_maximum_fusion.1.refs_0_, bf16[128,1024]{1,0:T(8,128)(2,1)S(1)} %pad_maximum_fusion.2.refs_1_, bf16[128,1024]{1,0:T(8,128)(2,1)S(1)} %pad_maximum_fusion.3.refs_2_, bf16[128,1024]{1,0:T(8,128)(2,1)S(1)} %pad_maximum_fusion.4.refs_3_, ...), custom_call_target="tpu_custom_call" | custom-call | flops 1048576 | bytes 6291456 | tf_op jit(solution)/shard_map/pallas_call | solution.py:689
  (88 shorter events, 12.1 us)
Async XLA Ops:
  10.4 8.7 %collective-permute-start.2 = (bf16[128,1024]{1,0:T(8,128)(2,1)S(1)}, bf16[128,1024]{1,0:T(8,128)(2,1)S(1)}, u32[]{:S(2)}, u32[]{:S(2)}) collective-permute-start(bf16[128,1024]{1,0:T(8,128)(2,1)S(1)} %get-tuple-element.47), channel_id=1, source_target_pairs={{0,2},{1,3},{2,0},{3,1},{4,6},{5,7},{6,4},{7,5},{8,10},{9,11},{10,... | collective-permute-start | bytes 786440 | tf_op jit(solution)/shard_map/ppermute | solution.py:486
  25.1 4.6 %collective-permute-start.21 = (bf16[136,1024]{1,0:T(8,128)(2,1)S(1)}, bf16[136,1024]{1,0:T(8,128)(2,1)S(1)}, u32[]{:S(2)}, u32[]{:S(2)}) collective-permute-start(bf16[136,1024]{1,0:T(8,128)(2,1)S(1)} %get-tuple-element.62.refs_3_), channel_id=1, source_target_pairs={{0,1},{1,0},{2,3},{3,2},{4,5},{5,4},{6,7},{7,6},{8,9},{9,8},{10,11... | collective-permute-start | bytes 835592 | tf_op jit(solution)/shard_map/ppermute | solution.py:565
  26.9 5.0 %collective-permute-start.16 = (bf16[64,1024]{1,0:T(8,128)(2,1)S(1)}, bf16[64,1024]{1,0:T(8,128)(2,1)S(1)}, u32[]{:S(2)}, u32[]{:S(2)}) collective-permute-start(bf16[64,1024]{1,0:T(8,128)(2,1)S(1)} %get-tuple-element.75), channel_id=1, source_target_pairs={{0,2},{1,5},{2,0},{3,7},{4,6},{5,1},{6,4},{7,3},{8,10},{9,13},{10,... | collective-permute-start | bytes 393224 | tf_op jit(solution)/shard_map/ppermute | solution.py:565
  27.4 6.2 %collective-permute-start.10 = (bf16[64,1024]{1,0:T(8,128)(2,1)S(1)}, bf16[64,1024]{1,0:T(8,128)(2,1)S(1)}, u32[]{:S(2)}, u32[]{:S(2)}) collective-permute-start(bf16[64,1024]{1,0:T(8,128)(2,1)S(1)} %get-tuple-element.77), channel_id=1, source_target_pairs={{0,2},{1,5},{2,0},{3,7},{4,6},{5,1},{6,4},{7,3},{8,10},{9,13},{10,... | collective-permute-start | bytes 393224 | tf_op jit(solution)/shard_map/ppermute | solution.py:565
  29.2 5.8 %collective-permute-start.4 = (bf16[64,1024]{1,0:T(8,128)(2,1)S(1)}, bf16[64,1024]{1,0:T(8,128)(2,1)S(1)}, u32[]{:S(2)}, u32[]{:S(2)}) collective-permute-start(bf16[64,1024]{1,0:T(8,128)(2,1)S(1)} %get-tuple-element.79), channel_id=1, source_target_pairs={{0,2},{1,5},{2,0},{3,7},{4,6},{5,1},{6,4},{7,3},{8,10},{9,13},{10,... | collective-permute-start | bytes 393224 | tf_op jit(solution)/shard_map/ppermute | solution.py:565
  29.8 6.6 %collective-permute-start.22 = (bf16[72,1024]{1,0:T(8,128)(2,1)S(1)}, bf16[72,1024]{1,0:T(8,128)(2,1)S(1)}, u32[]{:S(2)}, u32[]{:S(2)}) collective-permute-start(bf16[72,1024]{1,0:T(8,128)(2,1)S(1)} %pad_maximum_fusion.5), channel_id=1, source_target_pairs={{0,2},{1,5},{2,0},{3,7},{4,6},{5,1},{6,4},{7,3},{8,10},{9,13},{10,... | collective-permute-start | bytes 442376 | tf_op jit(solution)/shard_map/ppermute | solution.py:565
  32.0 6.1 %collective-permute-start.17 = (bf16[32,1024]{1,0:T(8,128)(2,1)S(1)}, bf16[32,1024]{1,0:T(8,128)(2,1)S(1)}, u32[]{:S(2)}, u32[]{:S(2)}) collective-permute-start(bf16[32,1024]{1,0:T(8,128)(2,1)S(1)} %select_convert_fusion.10), channel_id=1, source_target_pairs={{0,4},{1,9},{2,6},{3,11},{4,0},{5,13},{6,2},{7,15},{8,12},{9,1},{1... | collective-permute-start | bytes 196616 | tf_op jit(solution)/shard_map/ppermute | solution.py:565
  33.7 7.1 %collective-permute-start.11 = (bf16[32,1024]{1,0:T(8,128)(2,1)S(1)}, bf16[32,1024]{1,0:T(8,128)(2,1)S(1)}, u32[]{:S(2)}, u32[]{:S(2)}) collective-permute-start(bf16[32,1024]{1,0:T(8,128)(2,1)S(1)} %select_convert_fusion.12), channel_id=1, source_target_pairs={{0,4},{1,9},{2,6},{3,11},{4,0},{5,13},{6,2},{7,15},{8,12},{9,1},{1... | collective-permute-start | bytes 196616 | tf_op jit(solution)/shard_map/ppermute | solution.py:565
  35.1 6.3 %collective-permute-start.5 = (bf16[32,1024]{1,0:T(8,128)(2,1)S(1)}, bf16[32,1024]{1,0:T(8,128)(2,1)S(1)}, u32[]{:S(2)}, u32[]{:S(2)}) collective-permute-start(bf16[32,1024]{1,0:T(8,128)(2,1)S(1)} %select_convert_fusion.14), channel_id=1, source_target_pairs={{0,4},{1,9},{2,6},{3,11},{4,0},{5,13},{6,2},{7,15},{8,12},{9,1},{1... | collective-permute-start | bytes 196616 | tf_op jit(solution)/shard_map/ppermute | solution.py:565
  36.5 7.4 %collective-permute-start.23 = (bf16[40,1024]{1,0:T(8,128)(2,1)S(1)}, bf16[40,1024]{1,0:T(8,128)(2,1)S(1)}, u32[]{:S(2)}, u32[]{:S(2)}) collective-permute-start(bf16[40,1024]{1,0:T(8,128)(2,1)S(1)} %pad_maximum_fusion.10), channel_id=1, source_target_pairs={{0,4},{1,9},{2,6},{3,11},{4,0},{5,13},{6,2},{7,15},{8,12},{9,1},{1... | collective-permute-start | bytes 245768 | tf_op jit(solution)/shard_map/ppermute | solution.py:565
  38.1 6.5 %collective-permute-start.18 = (bf16[32,1024]{1,0:T(8,128)(2,1)S(1)}, bf16[32,1024]{1,0:T(8,128)(2,1)S(1)}, u32[]{:S(2)}, u32[]{:S(2)}) collective-permute-start(bf16[32,1024]{1,0:T(8,128)(2,1)S(1)} %add_convert_fusion.3), channel_id=1, source_target_pairs={{0,8},{1,3},{2,10},{3,1},{4,12},{5,7},{6,14},{7,5},{8,0},{9,11},{1... | collective-permute-start | bytes 196616 | tf_op jit(solution)/shard_map/ppermute | solution.py:565
  40.8 6.0 %collective-permute-start.12 = (bf16[32,1024]{1,0:T(8,128)(2,1)S(1)}, bf16[32,1024]{1,0:T(8,128)(2,1)S(1)}, u32[]{:S(2)}, u32[]{:S(2)}) collective-permute-start(bf16[32,1024]{1,0:T(8,128)(2,1)S(1)} %add_convert_fusion.5), channel_id=1, source_target_pairs={{0,8},{1,3},{2,10},{3,1},{4,12},{5,7},{6,14},{7,5},{8,0},{9,11},{1... | collective-permute-start | bytes 196616 | tf_op jit(solution)/shard_map/ppermute | solution.py:565
  41.4 11.2 %collective-permute-start.6 = (bf16[32,1024]{1,0:T(8,128)(2,1)S(1)}, bf16[32,1024]{1,0:T(8,128)(2,1)S(1)}, u32[]{:S(2)}, u32[]{:S(2)}) collective-permute-start(bf16[32,1024]{1,0:T(8,128)(2,1)S(1)} %add_convert_fusion.7), channel_id=1, source_target_pairs={{0,8},{1,3},{2,10},{3,1},{4,12},{5,7},{6,14},{7,5},{8,0},{9,11},{1... | collective-permute-start | bytes 196616 | tf_op jit(solution)/shard_map/ppermute | solution.py:565
  44.0 10.4 %collective-permute-start.24 = (bf16[40,1024]{1,0:T(8,128)(2,1)S(1)}, bf16[40,1024]{1,0:T(8,128)(2,1)S(1)}, u32[]{:S(2)}, u32[]{:S(2)}) collective-permute-start(bf16[40,1024]{1,0:T(8,128)(2,1)S(1)} %pad_maximum_fusion.11), channel_id=1, source_target_pairs={{0,8},{1,3},{2,10},{3,1},{4,12},{5,7},{6,14},{7,5},{8,0},{9,11},{1... | collective-permute-start | bytes 245768 | tf_op jit(solution)/shard_map/ppermute | solution.py:565
  44.6 10.2 %collective-permute-start.19 = (bf16[32,1024]{1,0:T(8,128)(2,1)S(1)}, bf16[32,1024]{1,0:T(8,128)(2,1)S(1)}, u32[]{:S(2)}, u32[]{:S(2)}) collective-permute-start(bf16[32,1024]{1,0:T(8,128)(2,1)S(1)} %add_convert_fusion.2), channel_id=1, source_target_pairs={{0,4},{1,9},{2,6},{3,11},{4,0},{5,13},{6,2},{7,15},{8,12},{9,1},{1... | collective-permute-start | bytes 196616 | tf_op jit(solution)/shard_map/ppermute | solution.py:565
  46.8 8.3 %collective-permute-start.13 = (bf16[32,1024]{1,0:T(8,128)(2,1)S(1)}, bf16[32,1024]{1,0:T(8,128)(2,1)S(1)}, u32[]{:S(2)}, u32[]{:S(2)}) collective-permute-start(bf16[32,1024]{1,0:T(8,128)(2,1)S(1)} %add_convert_fusion.4), channel_id=1, source_target_pairs={{0,4},{1,9},{2,6},{3,11},{4,0},{5,13},{6,2},{7,15},{8,12},{9,1},{1... | collective-permute-start | bytes 196616 | tf_op jit(solution)/shard_map/ppermute | solution.py:565
  52.6 5.0 %collective-permute-start.7 = (bf16[32,1024]{1,0:T(8,128)(2,1)S(1)}, bf16[32,1024]{1,0:T(8,128)(2,1)S(1)}, u32[]{:S(2)}, u32[]{:S(2)}) collective-permute-start(bf16[32,1024]{1,0:T(8,128)(2,1)S(1)} %add_convert_fusion.6), channel_id=1, source_target_pairs={{0,4},{1,9},{2,6},{3,11},{4,0},{5,13},{6,2},{7,15},{8,12},{9,1},{1... | collective-permute-start | bytes 196616 | tf_op jit(solution)/shard_map/ppermute | solution.py:565
  54.4 5.0 %collective-permute-start.25 = (bf16[32,1024]{1,0:T(8,128)(2,1)S(1)}, bf16[32,1024]{1,0:T(8,128)(2,1)S(1)}, u32[]{:S(2)}, u32[]{:S(2)}) collective-permute-start(bf16[32,1024]{1,0:T(8,128)(2,1)S(1)} %add_convert_fusion), channel_id=1, source_target_pairs={{0,4},{1,9},{2,6},{3,11},{4,0},{5,13},{6,2},{7,15},{8,12},{9,1},{1... | collective-permute-start | bytes 196616 | tf_op jit(solution)/shard_map/ppermute | solution.py:565
  54.8 5.2 %collective-permute-start.20 = (bf16[64,1024]{1,0:T(8,128)(2,1)S(1)}, bf16[64,1024]{1,0:T(8,128)(2,1)S(1)}, u32[]{:S(2)}, u32[]{:S(2)}) collective-permute-start(bf16[64,1024]{1,0:T(8,128)(2,1)S(1)} %pad_maximum_fusion.8), channel_id=1, source_target_pairs={{0,2},{1,5},{2,0},{3,7},{4,6},{5,1},{6,4},{7,3},{8,10},{9,13},{10,... | collective-permute-start | bytes 393224 | tf_op jit(solution)/shard_map/ppermute | solution.py:565
  55.2 6.1 %collective-permute-start.14 = (bf16[64,1024]{1,0:T(8,128)(2,1)S(1)}, bf16[64,1024]{1,0:T(8,128)(2,1)S(1)}, u32[]{:S(2)}, u32[]{:S(2)}) collective-permute-start(bf16[64,1024]{1,0:T(8,128)(2,1)S(1)} %pad_maximum_fusion.7), channel_id=1, source_target_pairs={{0,2},{1,5},{2,0},{3,7},{4,6},{5,1},{6,4},{7,3},{8,10},{9,13},{10,... | collective-permute-start | bytes 393224 | tf_op jit(solution)/shard_map/ppermute | solution.py:565
  57.7 5.0 %collective-permute-start.8 = (bf16[64,1024]{1,0:T(8,128)(2,1)S(1)}, bf16[64,1024]{1,0:T(8,128)(2,1)S(1)}, u32[]{:S(2)}, u32[]{:S(2)}) collective-permute-start(bf16[64,1024]{1,0:T(8,128)(2,1)S(1)} %pad_maximum_fusion.6), channel_id=1, source_target_pairs={{0,2},{1,5},{2,0},{3,7},{4,6},{5,1},{6,4},{7,3},{8,10},{9,13},{10,... | collective-permute-start | bytes 393224 | tf_op jit(solution)/shard_map/ppermute | solution.py:565
  59.4 5.0 %collective-permute-start.26 = (bf16[64,1024]{1,0:T(8,128)(2,1)S(1)}, bf16[64,1024]{1,0:T(8,128)(2,1)S(1)}, u32[]{:S(2)}, u32[]{:S(2)}) collective-permute-start(bf16[64,1024]{1,0:T(8,128)(2,1)S(1)} %pad_maximum_fusion.9), channel_id=1, source_target_pairs={{0,2},{1,5},{2,0},{3,7},{4,6},{5,1},{6,4},{7,3},{8,10},{9,13},{10,... | collective-permute-start | bytes 393224 | tf_op jit(solution)/shard_map/ppermute | solution.py:565
  60.2 5.1 %collective-permute-start.29 = (bf16[128,1024]{1,0:T(8,128)(2,1)S(1)}, bf16[128,1024]{1,0:T(8,128)(2,1)S(1)}, u32[]{:S(2)}, u32[]{:S(2)}) collective-permute-start(bf16[128,1024]{1,0:T(8,128)(2,1)S(1)} %pad_maximum_fusion.3.refs_2_), channel_id=1, source_target_pairs={{0,1},{1,0},{2,3},{3,2},{4,5},{5,4},{6,7},{7,6},{8,9},{9,8},{10,11... | collective-permute-start | bytes 786440 | tf_op jit(solution)/shard_map/ppermute | solution.py:565
  61.4 3.9 %collective-permute-start.28 = (bf16[128,1024]{1,0:T(8,128)(2,1)S(1)}, bf16[128,1024]{1,0:T(8,128)(2,1)S(1)}, u32[]{:S(2)}, u32[]{:S(2)}) collective-permute-start(bf16[128,1024]{1,0:T(8,128)(2,1)S(1)} %pad_maximum_fusion.2.refs_1_), channel_id=1, source_target_pairs={{0,1},{1,0},{2,3},{3,2},{4,5},{5,4},{6,7},{7,6},{8,9},{9,8},{10,11... | collective-permute-start | bytes 786440 | tf_op jit(solution)/shard_map/ppermute | solution.py:565
  (8 other events, 28.3 us)

commit v8 on v7

--- a/solution.py
+++ b/solution.py
@@ -6,6 +6,7 @@
 from jax.experimental import pallas as pl
 from jax.experimental.pallas import tpu as pltpu
 from jax.sharding import PartitionSpec as P
+
 
 F32 = jnp.float32
 BF16 = jnp.bfloat16
@@ -136,12 +137,20 @@
 
 
 def chip_kernel(take, mine, other, out, gain_out):
-    state = out.shape[0]
+    state, half = out.shape
     odd = lax.rem(lax.axis_index("tm"), 2) == 1
-    m = mine[:state, :].astype(F32)
-    o = other[:state, :].astype(F32)
-    gm = gain_row(mine, state)
-    go = gain_row(other, state)
+
+    def part(ref, rows):
+        return jnp.where(odd, ref[rows, half:].astype(F32), ref[rows, :half].astype(F32))
+
+    def gain_of(ref):
+        tail = part(ref, slice(state, state + ALIGN))
+        return tail[0:1, :] + tail[1:2, :]
+
+    m = part(mine, slice(0, state))
+    o = part(other, slice(0, state))
+    gm = gain_of(mine)
+    go = gain_of(other)
     out[...] = jnp.where(odd, o * gm + m, m * go + o).astype(BF16)
     gain_out[...] = jnp.broadcast_to(gm * go, gain_out.shape)
 
@@ -216,6 +225,7 @@
     take,
     count,
     incoming,
+    incoming_other,
     other,
     xbc,
     own,
@@ -237,7 +247,11 @@
     slots = pre.shape[0]
     tm = lax.axis_index("tm")
     odd = lax.rem(tm, 2) == 1
-    arrived = jnp.where(tm < 2, 0.0, incoming[...].astype(F32))
+    half_a, half_b = incoming[...].astype(F32), incoming_other[...].astype(F32)
+    arrived = jnp.concatenate(
+        [jnp.where(odd, half_b, half_a), jnp.where(odd, half_a, half_b)], axis=1
+    )
+    arrived = jnp.where(tm < 2, 0.0, arrived)
     enter = jnp.where(
         odd, arrived * gain_row(other, state) + other[:state, :].astype(F32), arrived
     )
@@ -476,7 +490,7 @@
         chip_kernel,
         (),
         (pay, other),
-        (shape((state, inner), BF16), shape((8, inner), F32)),
+        (shape((state, inner // 2), BF16), shape((8, inner // 2), F32)),
         [],
         state * inner,
         6 * state * inner,
@@ -488,6 +502,7 @@
         incoming = jnp.where(tm < 2, 0.0, incoming.astype(F32))
         passed = chip_gain[0:1] * incoming + chip_state.astype(F32)
         incoming = lax.ppermute(passed.astype(BF16), "tm", onward)
+    incoming_other = lax.ppermute(incoming, "tm", [(i, i ^ 1) for i in range(n_tm)])
     own, across, pre, hot, hot_t, item_t = call(
         functools.partial(within_kernel, heads),
         (hist, z_weight, item, first_weight, label_pos),
@@ -516,7 +531,7 @@
             second_weight.reshape(hidden // LANES, LANES),
             label_value,
         ),
-        (label_count, incoming, other, xbc, own, across, pre, hot, hot_t, item_t),
+        (label_count, incoming, incoming_other, other, xbc, own, across, pre, hot, hot_t, item_t),
         (
             shape((length, width), BF16),
             shape((1, slots), F32),
@@ -640,7 +655,6 @@
     own_extra = wholes[-1][1]
     mine = [whole for whole, _ in wholes]
     total = (2 * rows,) + mine[0].shape[1:]
-    last = chunks - 1
     own = [(w, 0, k) for k, w in enumerate(mine)]
     other = [(w, 1, k) for k, w in enumerate(arrived)]
     grad_first, grad_second = written(None, own + other, rows, total, own_extra)
@@ -722,4 +736,5 @@
         P(),
     )
     out_specs = (P(("grp", "user"), "tm", None), P(("grp", "user"), "tm"), P("grp", None), P("grp"))
+
     return jax.shard_map(body, mesh=mesh, in_specs=in_specs, out_specs=out_specs, check_vma=False)

time: 69.5 us -> 71.8 us (1.033)
  starting transfers between devices: 27.5 us -> 29.3 us
    ppermute x1, waiting for transfers between devices: 3.11 us -> 5.52 us  [body(): incoming = lax.ppermute(chip_state, 'tm', onward)]
    ppermute x28, waiting for transfers between devices: 15.4 us -> 13.4 us  [swap(): return lax.ppermute(value, axes, pairs)]
    ppermute x28, starting transfers between devices: 24 us -> 25.8 us  [swap(): return lax.ppermute(value, axes, pairs)]
  transfers between devices with their start and end apart: 31 -> 32, of which waited for: 13 -> 13; matrix products, arithmetic and copies ran while one was open for 2% -> 2% of each run, Pallas kernels for 12% -> 12%
where the time goes in v8:
time: 71.8 us; the launch traced here: 71.5 us
  starting transfers between devices  29.3 us (41%)
  waiting for transfers between devices  20.1 us (28%)
  Pallas kernels  18.5 us (26%)
  between operations  1.65 us (2%)
  other arithmetic  1.18 us (2%)
  local copies, waits for them, and re-layouts  0.73 us (1%)
    ppermute x28, starting transfers between devices, swap(): return lax.ppermute(value, axes, pairs)  25.8 us
    pallas_call x6, Pallas kernels, call(): pl.pallas_call(loading(kernel, len(loaded), len(given), len(out_shape), w...  15.9 us
    ppermute x28, waiting for transfers between devices, swap(): return lax.ppermute(value, axes, pairs)  13.4 us
    ppermute x1, waiting for transfers between devices, body(): incoming = lax.ppermute(chip_state, 'tm', onward)  5.52 us
    pallas_call x1, Pallas kernels, written(): pl.pallas_call(kernel, out_shape=tuple(outs), in_specs=[HBM] * aliased +...  2.7 us
    ppermute x1, starting transfers between devices, body(): other = lax.ppermute(pay, 'tm', [(i, i ^ 1) for i in range(n_tm)])  2.66 us
  transfers between devices with their start and end apart: 32, of which 13 were waited for; matrix products, arithmetic and copies ran while one was open for 2% of the time, Pallas kernels for 12%

profile of v8, /device:TPU:0, one launch (start us, length us, event | category | flops | bytes accessed | tf_op | source)
XLA Modules:
  0.0 71.5 jit_solution(6549177694953746665)
XLA Ops:
  1.8 3.4 %shard_map.192 = (bf16[256,1280]{1,0:T(8,128)(2,1)S(1)}, f32[256,16]{1,0:T(8,128)S(1)}, f32[16,256]{1,0:T(8,128)S(1)}, f32[16,256]{1,0:T(8,128)S(1)}, f32[16,16]...) custom-call(bf16[256,512]{1,0:T(8,128)(2,1)} %bitcast.12, ...), custom_call_target="tpu_custom_call" | custom-call | flops 335544320 | bytes 2621440 | tf_op jit(solution)/shard_map/pallas_call | solution.py:394
  5.9 2.7 %collective-permute-start.1 = (bf16[144,1024]{1,0:T(8,128)(2,1)S(1)}, bf16[144,1024]{1,0:T(8,128)(2,1)S(1)}, u32[]{:S(2)}, u32[]{:S(2)}) collective-permute-start(bf16[144,1024]{1,0:T(8,128)(2,1)S(1)} %get-tuple-element.46.refs_0_), channel_id=1, source_target_pairs={{0,1},{1,0},{2,3},{3,2},{4,5},{5,4},{6,7},{7,6},{8,9},{9,8},{10,11... | collective-permute-start | bytes 884744 | tf_op jit(solution)/shard_map/ppermute | solution.py:488
  8.6 1.2 %collective-permute-done.1.refs_1_.refs_8_ = bf16[144,1024]{1,0:T(8,128)(2,1)S(1)} collective-permute-done((bf16[144,1024]{1,0:T(8,128)(2,1)S(1)}, bf16[144,1024]{1,0:T(8,128)(2,1)S(1)}, u32[]{:S(2)}, u32[]{:S(2)}) %collective-permute-start.1) | collective-permute-done | bytes 294944 | tf_op jit(solution)/shard_map/ppermute | solution.py:488
  10.7 5.5 %collective-permute-done.2.refs_6_ = bf16[128,512]{1,0:T(8,128)(2,1)S(1)} collective-permute-done((bf16[128,512]{1,0:T(8,128)(2,1)S(1)}, bf16[128,512]{1,0:T(8,128)(2,1)S(1)}, u32[]{:S(2)}, u32[]{:S(2)}) %collective-permute-start.2) | collective-permute-done | bytes 131104 | tf_op jit(solution)/shard_map/ppermute | solution.py:500
  16.9 4.5 %shard_map.195 = (f32[256,1024]{1,0:T(8,128)S(1)}, f32[256,1024]{1,0:T(8,128)S(1)}, f32[512,1024]{1,0:T(8,128)S(1)}, bf16[512,256]{1,0:T(8,128)(2,1)S(1)}, bf16[...) custom-call(bf16[256,512]{1,0:T(8,128)(2,1)} %bitcast.13, bf16[512,1024]{1,0:T(8,128)(2,1)} %refs_1_.2, ...), custom_call_target="tpu_custom_call" | custom-call | flops 1073741824 | bytes 16777216 | tf_op jit(solution)/shard_map/pallas_call | solution.py:394
  21.5 5.9 %shard_map.196 = (bf16[256,512]{1,0:T(8,128)(2,1)}, f32[1,512]{1,0:T(1,128)}, bf16[512,1024]{1,0:T(8,128)(2,1)S(1)}, bf16[512,512]{1,0:T(8,128)(2,1)S(1)}, bf16[...) custom-call(f32[1,1024]{1,0:T(1,128)} %bitcast.17, ...), custom_call_target="tpu_custom_call" | custom-call | flops 1073741824 | bytes 4194304 | tf_op jit(solution)/shard_map/pallas_call | solution.py:394
  30.0 1.7 %collective-permute-start.11 = (bf16[64,1024]{1,0:T(8,128)(2,1)S(1)}, bf16[64,1024]{1,0:T(8,128)(2,1)S(1)}, u32[]{:S(2)}, u32[]{:S(2)}) collective-permute-start(bf16[64,1024]{1,0:T(8,128)(2,1)S(1)} %get-tuple-element.77), channel_id=1, source_target_pairs={{0,2},{1,5},{2,0},{3,7},{4,6},{5,1},{6,4},{7,3},{8,10},{9,13},{10,... | collective-permute-start | bytes 393224 | tf_op jit(solution)/shard_map/ppermute | solution.py:580
  32.4 1.7 %collective-permute-start.23 = (bf16[72,1024]{1,0:T(8,128)(2,1)S(1)}, bf16[72,1024]{1,0:T(8,128)(2,1)S(1)}, u32[]{:S(2)}, u32[]{:S(2)}) collective-permute-start(bf16[72,1024]{1,0:T(8,128)(2,1)S(1)} %pad_maximum_fusion.5), channel_id=1, source_target_pairs={{0,2},{1,5},{2,0},{3,7},{4,6},{5,1},{6,4},{7,3},{8,10},{9,13},{10,... | collective-permute-start | bytes 442376 | tf_op jit(solution)/shard_map/ppermute | solution.py:580
  34.5 1.6 %collective-permute-start.18 = (bf16[32,1024]{1,0:T(8,128)(2,1)S(1)}, bf16[32,1024]{1,0:T(8,128)(2,1)S(1)}, u32[]{:S(2)}, u32[]{:S(2)}) collective-permute-start(bf16[32,1024]{1,0:T(8,128)(2,1)S(1)} %select_convert_fusion.10), channel_id=1, source_target_pairs={{0,4},{1,9},{2,6},{3,11},{4,0},{5,13},{6,2},{7,15},{8,12},{9,1},{1... | collective-permute-start | bytes 196616 | tf_op jit(solution)/shard_map/ppermute | solution.py:580
  36.2 1.4 %collective-permute-start.12 = (bf16[32,1024]{1,0:T(8,128)(2,1)S(1)}, bf16[32,1024]{1,0:T(8,128)(2,1)S(1)}, u32[]{:S(2)}, u32[]{:S(2)}) collective-permute-start(bf16[32,1024]{1,0:T(8,128)(2,1)S(1)} %select_convert_fusion.12), channel_id=1, source_target_pairs={{0,4},{1,9},{2,6},{3,11},{4,0},{5,13},{6,2},{7,15},{8,12},{9,1},{1... | collective-permute-start | bytes 196616 | tf_op jit(solution)/shard_map/ppermute | solution.py:580
  37.6 1.4 %collective-permute-start.6 = (bf16[32,1024]{1,0:T(8,128)(2,1)S(1)}, bf16[32,1024]{1,0:T(8,128)(2,1)S(1)}, u32[]{:S(2)}, u32[]{:S(2)}) collective-permute-start(bf16[32,1024]{1,0:T(8,128)(2,1)S(1)} %select_convert_fusion.14), channel_id=1, source_target_pairs={{0,4},{1,9},{2,6},{3,11},{4,0},{5,13},{6,2},{7,15},{8,12},{9,1},{1... | collective-permute-start | bytes 196616 | tf_op jit(solution)/shard_map/ppermute | solution.py:580
  39.0 1.5 %collective-permute-start.24 = (bf16[40,1024]{1,0:T(8,128)(2,1)S(1)}, bf16[40,1024]{1,0:T(8,128)(2,1)S(1)}, u32[]{:S(2)}, u32[]{:S(2)}) collective-permute-start(bf16[40,1024]{1,0:T(8,128)(2,1)S(1)} %pad_maximum_fusion.10), channel_id=1, source_target_pairs={{0,4},{1,9},{2,6},{3,11},{4,0},{5,13},{6,2},{7,15},{8,12},{9,1},{1... | collective-permute-start | bytes 245768 | tf_op jit(solution)/shard_map/ppermute | solution.py:580
  40.6 2.6 %collective-permute-start.19 = (bf16[32,1024]{1,0:T(8,128)(2,1)S(1)}, bf16[32,1024]{1,0:T(8,128)(2,1)S(1)}, u32[]{:S(2)}, u32[]{:S(2)}) collective-permute-start(bf16[32,1024]{1,0:T(8,128)(2,1)S(1)} %add_convert_fusion.3), channel_id=1, source_target_pairs={{0,8},{1,3},{2,10},{3,1},{4,12},{5,7},{6,14},{7,5},{8,0},{9,11},{1... | collective-permute-start | bytes 196616 | tf_op jit(solution)/shard_map/ppermute | solution.py:580
  44.0 2.5 %collective-permute-start.7 = (bf16[32,1024]{1,0:T(8,128)(2,1)S(1)}, bf16[32,1024]{1,0:T(8,128)(2,1)S(1)}, u32[]{:S(2)}, u32[]{:S(2)}) collective-permute-start(bf16[32,1024]{1,0:T(8,128)(2,1)S(1)} %add_convert_fusion.7), channel_id=1, source_target_pairs={{0,8},{1,3},{2,10},{3,1},{4,12},{5,7},{6,14},{7,5},{8,0},{9,11},{1... | collective-permute-start | bytes 196616 | tf_op jit(solution)/shard_map/ppermute | solution.py:580
  47.3 2.0 %collective-permute-start.20 = (bf16[32,1024]{1,0:T(8,128)(2,1)S(1)}, bf16[32,1024]{1,0:T(8,128)(2,1)S(1)}, u32[]{:S(2)}, u32[]{:S(2)}) collective-permute-start(bf16[32,1024]{1,0:T(8,128)(2,1)S(1)} %add_convert_fusion.2), channel_id=1, source_target_pairs={{0,4},{1,9},{2,6},{3,11},{4,0},{5,13},{6,2},{7,15},{8,12},{9,1},{1... | collective-permute-start | bytes 196616 | tf_op jit(solution)/shard_map/ppermute | solution.py:580
  50.1 3.4 %collective-permute-done.7 = bf16[32,1024]{1,0:T(8,128)(2,1)S(1)} collective-permute-done((bf16[32,1024]{1,0:T(8,128)(2,1)S(1)}, bf16[32,1024]{1,0:T(8,128)(2,1)S(1)}, u32[]{:S(2)}, u32[]{:S(2)}) %collective-permute-start.7) | collective-permute-done | bytes 65568 | tf_op jit(solution)/shard_map/ppermute | solution.py:580
  54.1 2.4 %collective-permute-done.25 = bf16[40,1024]{1,0:T(8,128)(2,1)S(1)} collective-permute-done((bf16[40,1024]{1,0:T(8,128)(2,1)S(1)}, bf16[40,1024]{1,0:T(8,128)(2,1)S(1)}, u32[]{:S(2)}, u32[]{:S(2)}) %collective-permute-start.25) | collective-permute-done | bytes 81952 | tf_op jit(solution)/shard_map/ppermute | solution.py:580
  56.7 1.1 %collective-permute-start.21 = (bf16[64,1024]{1,0:T(8,128)(2,1)S(1)}, bf16[64,1024]{1,0:T(8,128)(2,1)S(1)}, u32[]{:S(2)}, u32[]{:S(2)}) collective-permute-start(bf16[64,1024]{1,0:T(8,128)(2,1)S(1)} %pad_maximum_fusion.8), channel_id=1, source_target_pairs={{0,2},{1,5},{2,0},{3,7},{4,6},{5,1},{6,4},{7,3},{8,10},{9,13},{10,... | collective-permute-start | bytes 393224 | tf_op jit(solution)/shard_map/ppermute | solution.py:580
  57.8 1.1 %collective-permute-start.15 = (bf16[64,1024]{1,0:T(8,128)(2,1)S(1)}, bf16[64,1024]{1,0:T(8,128)(2,1)S(1)}, u32[]{:S(2)}, u32[]{:S(2)}) collective-permute-start(bf16[64,1024]{1,0:T(8,128)(2,1)S(1)} %pad_maximum_fusion.7), channel_id=1, source_target_pairs={{0,2},{1,5},{2,0},{3,7},{4,6},{5,1},{6,4},{7,3},{8,10},{9,13},{10,... | collective-permute-start | bytes 393224 | tf_op jit(solution)/shard_map/ppermute | solution.py:580
  60.0 1.6 %collective-permute-done.26 = bf16[32,1024]{1,0:T(8,128)(2,1)S(1)} collective-permute-done((bf16[32,1024]{1,0:T(8,128)(2,1)S(1)}, bf16[32,1024]{1,0:T(8,128)(2,1)S(1)}, u32[]{:S(2)}, u32[]{:S(2)}) %collective-permute-start.26) | collective-permute-done | bytes 65568 | tf_op jit(solution)/shard_map/ppermute | solution.py:580
  61.7 1.1 %collective-permute-start.27 = (bf16[64,1024]{1,0:T(8,128)(2,1)S(1)}, bf16[64,1024]{1,0:T(8,128)(2,1)S(1)}, u32[]{:S(2)}, u32[]{:S(2)}) collective-permute-start(bf16[64,1024]{1,0:T(8,128)(2,1)S(1)} %pad_maximum_fusion.9), channel_id=1, source_target_pairs={{0,2},{1,5},{2,0},{3,7},{4,6},{5,1},{6,4},{7,3},{8,10},{9,13},{10,... | collective-permute-start | bytes 393224 | tf_op jit(solution)/shard_map/ppermute | solution.py:580
  64.6 2.1 %collective-permute-done.27 = bf16[64,1024]{1,0:T(8,128)(2,1)S(1)} collective-permute-done((bf16[64,1024]{1,0:T(8,128)(2,1)S(1)}, bf16[64,1024]{1,0:T(8,128)(2,1)S(1)}, u32[]{:S(2)}, u32[]{:S(2)}) %collective-permute-start.27) | collective-permute-done | bytes 131104 | tf_op jit(solution)/shard_map/ppermute | solution.py:580
  67.5 1.3 %collective-permute-done.28.refs_4_ = bf16[128,1024]{1,0:T(8,128)(2,1)S(1)} collective-permute-done((bf16[128,1024]{1,0:T(8,128)(2,1)S(1)}, bf16[128,1024]{1,0:T(8,128)(2,1)S(1)}, u32[]{:S(2)}, u32[]{:S(2)}) %collective-permute-start.28) | collective-permute-done | bytes 262176 | tf_op jit(solution)/shard_map/ppermute | solution.py:580
  68.8 2.7 %shard_map.198 = (f32[1024,1024]{1,0:T(8,128)}, f32[1,1024]{1,0:T(1,128)}) custom-call(bf16[128,1024]{1,0:T(8,128)(2,1)S(1)} %pad_maximum_fusion.1.refs_0_, bf16[128,1024]{1,0:T(8,128)(2,1)S(1)} %pad_maximum_fusion.2.refs_1_, bf16[128,1024]{1,0:T(8,128)(2,1)S(1)} %pad_maximum_fusion.3.refs_2_, bf16[128,1024]{1,0:T(8,128)(2,1)S(1)} %pad_maximum_fusion.4.refs_3_, ...), custom_call_target="tpu_custom_call" | custom-call | flops 1048576 | bytes 6291456 | tf_op jit(solution)/shard_map/pallas_call | solution.py:703
  (90 shorter events, 13.5 us)
Async XLA Ops:
  10.4 5.8 %collective-permute-start.2 = (bf16[128,512]{1,0:T(8,128)(2,1)S(1)}, bf16[128,512]{1,0:T(8,128)(2,1)S(1)}, u32[]{:S(2)}, u32[]{:S(2)}) collective-permute-start(bf16[128,512]{1,0:T(8,128)(2,1)S(1)} %get-tuple-element.47), channel_id=1, source_target_pairs={{0,2},{1,3},{2,0},{3,1},{4,6},{5,7},{6,4},{7,5},{8,10},{9,11},{10,... | collective-permute-start | bytes 393224 | tf_op jit(solution)/shard_map/ppermute | solution.py:500
  16.3 5.2 %collective-permute-start.3 = (bf16[128,512]{1,0:T(8,128)(2,1)S(1)}, bf16[128,512]{1,0:T(8,128)(2,1)S(1)}, u32[]{:S(2)}, u32[]{:S(2)}) collective-permute-start(bf16[128,512]{1,0:T(8,128)(2,1)S(1)} %collective-permute-done.2.refs_6_), channel_id=1, source_target_pairs={{0,1},{1,0},{2,3},{3,2},{4,5},{5,4},{6,7},{7,6},{8,9},{9,8},{10,11... | collective-permute-start | bytes 393224 | tf_op jit(solution)/shard_map/ppermute | solution.py:505
  28.0 4.3 %collective-permute-start.22 = (bf16[136,1024]{1,0:T(8,128)(2,1)S(1)}, bf16[136,1024]{1,0:T(8,128)(2,1)S(1)}, u32[]{:S(2)}, u32[]{:S(2)}) collective-permute-start(bf16[136,1024]{1,0:T(8,128)(2,1)S(1)} %get-tuple-element.62.refs_3_), channel_id=1, source_target_pairs={{0,1},{1,0},{2,3},{3,2},{4,5},{5,4},{6,7},{7,6},{8,9},{9,8},{10,11... | collective-permute-start | bytes 835592 | tf_op jit(solution)/shard_map/ppermute | solution.py:580
  29.4 5.0 %collective-permute-start.17 = (bf16[64,1024]{1,0:T(8,128)(2,1)S(1)}, bf16[64,1024]{1,0:T(8,128)(2,1)S(1)}, u32[]{:S(2)}, u32[]{:S(2)}) collective-permute-start(bf16[64,1024]{1,0:T(8,128)(2,1)S(1)} %get-tuple-element.75), channel_id=1, source_target_pairs={{0,2},{1,5},{2,0},{3,7},{4,6},{5,1},{6,4},{7,3},{8,10},{9,13},{10,... | collective-permute-start | bytes 393224 | tf_op jit(solution)/shard_map/ppermute | solution.py:580
  30.0 6.2 %collective-permute-start.11 = (bf16[64,1024]{1,0:T(8,128)(2,1)S(1)}, bf16[64,1024]{1,0:T(8,128)(2,1)S(1)}, u32[]{:S(2)}, u32[]{:S(2)}) collective-permute-start(bf16[64,1024]{1,0:T(8,128)(2,1)S(1)} %get-tuple-element.77), channel_id=1, source_target_pairs={{0,2},{1,5},{2,0},{3,7},{4,6},{5,1},{6,4},{7,3},{8,10},{9,13},{10,... | collective-permute-start | bytes 393224 | tf_op jit(solution)/shard_map/ppermute | solution.py:580
  31.8 5.8 %collective-permute-start.5 = (bf16[64,1024]{1,0:T(8,128)(2,1)S(1)}, bf16[64,1024]{1,0:T(8,128)(2,1)S(1)}, u32[]{:S(2)}, u32[]{:S(2)}) collective-permute-start(bf16[64,1024]{1,0:T(8,128)(2,1)S(1)} %get-tuple-element.79), channel_id=1, source_target_pairs={{0,2},{1,5},{2,0},{3,7},{4,6},{5,1},{6,4},{7,3},{8,10},{9,13},{10,... | collective-permute-start | bytes 393224 | tf_op jit(solution)/shard_map/ppermute | solution.py:580
  32.4 6.6 %collective-permute-start.23 = (bf16[72,1024]{1,0:T(8,128)(2,1)S(1)}, bf16[72,1024]{1,0:T(8,128)(2,1)S(1)}, u32[]{:S(2)}, u32[]{:S(2)}) collective-permute-start(bf16[72,1024]{1,0:T(8,128)(2,1)S(1)} %pad_maximum_fusion.5), channel_id=1, source_target_pairs={{0,2},{1,5},{2,0},{3,7},{4,6},{5,1},{6,4},{7,3},{8,10},{9,13},{10,... | collective-permute-start | bytes 442376 | tf_op jit(solution)/shard_map/ppermute | solution.py:580
  34.5 6.1 %collective-permute-start.18 = (bf16[32,1024]{1,0:T(8,128)(2,1)S(1)}, bf16[32,1024]{1,0:T(8,128)(2,1)S(1)}, u32[]{:S(2)}, u32[]{:S(2)}) collective-permute-start(bf16[32,1024]{1,0:T(8,128)(2,1)S(1)} %select_convert_fusion.10), channel_id=1, source_target_pairs={{0,4},{1,9},{2,6},{3,11},{4,0},{5,13},{6,2},{7,15},{8,12},{9,1},{1... | collective-permute-start | bytes 196616 | tf_op jit(solution)/shard_map/ppermute | solution.py:580
  36.2 7.1 %collective-permute-start.12 = (bf16[32,1024]{1,0:T(8,128)(2,1)S(1)}, bf16[32,1024]{1,0:T(8,128)(2,1)S(1)}, u32[]{:S(2)}, u32[]{:S(2)}) collective-permute-start(bf16[32,1024]{1,0:T(8,128)(2,1)S(1)} %select_convert_fusion.12), channel_id=1, source_target_pairs={{0,4},{1,9},{2,6},{3,11},{4,0},{5,13},{6,2},{7,15},{8,12},{9,1},{1... | collective-permute-start | bytes 196616 | tf_op jit(solution)/shard_map/ppermute | solution.py:580
  37.6 6.3 %collective-permute-start.6 = (bf16[32,1024]{1,0:T(8,128)(2,1)S(1)}, bf16[32,1024]{1,0:T(8,128)(2,1)S(1)}, u32[]{:S(2)}, u32[]{:S(2)}) collective-permute-start(bf16[32,1024]{1,0:T(8,128)(2,1)S(1)} %select_convert_fusion.14), channel_id=1, source_target_pairs={{0,4},{1,9},{2,6},{3,11},{4,0},{5,13},{6,2},{7,15},{8,12},{9,1},{1... | collective-permute-start | bytes 196616 | tf_op jit(solution)/shard_map/ppermute | solution.py:580
  39.0 7.4 %collective-permute-start.24 = (bf16[40,1024]{1,0:T(8,128)(2,1)S(1)}, bf16[40,1024]{1,0:T(8,128)(2,1)S(1)}, u32[]{:S(2)}, u32[]{:S(2)}) collective-permute-start(bf16[40,1024]{1,0:T(8,128)(2,1)S(1)} %pad_maximum_fusion.10), channel_id=1, source_target_pairs={{0,4},{1,9},{2,6},{3,11},{4,0},{5,13},{6,2},{7,15},{8,12},{9,1},{1... | collective-permute-start | bytes 245768 | tf_op jit(solution)/shard_map/ppermute | solution.py:580
  40.6 6.6 %collective-permute-start.19 = (bf16[32,1024]{1,0:T(8,128)(2,1)S(1)}, bf16[32,1024]{1,0:T(8,128)(2,1)S(1)}, u32[]{:S(2)}, u32[]{:S(2)}) collective-permute-start(bf16[32,1024]{1,0:T(8,128)(2,1)S(1)} %add_convert_fusion.3), channel_id=1, source_target_pairs={{0,8},{1,3},{2,10},{3,1},{4,12},{5,7},{6,14},{7,5},{8,0},{9,11},{1... | collective-permute-start | bytes 196616 | tf_op jit(solution)/shard_map/ppermute | solution.py:580
  43.3 6.0 %collective-permute-start.13 = (bf16[32,1024]{1,0:T(8,128)(2,1)S(1)}, bf16[32,1024]{1,0:T(8,128)(2,1)S(1)}, u32[]{:S(2)}, u32[]{:S(2)}) collective-permute-start(bf16[32,1024]{1,0:T(8,128)(2,1)S(1)} %add_convert_fusion.5), channel_id=1, source_target_pairs={{0,8},{1,3},{2,10},{3,1},{4,12},{5,7},{6,14},{7,5},{8,0},{9,11},{1... | collective-permute-start | bytes 196616 | tf_op jit(solution)/shard_map/ppermute | solution.py:580
  44.0 9.5 %collective-permute-start.7 = (bf16[32,1024]{1,0:T(8,128)(2,1)S(1)}, bf16[32,1024]{1,0:T(8,128)(2,1)S(1)}, u32[]{:S(2)}, u32[]{:S(2)}) collective-permute-start(bf16[32,1024]{1,0:T(8,128)(2,1)S(1)} %add_convert_fusion.7), channel_id=1, source_target_pairs={{0,8},{1,3},{2,10},{3,1},{4,12},{5,7},{6,14},{7,5},{8,0},{9,11},{1... | collective-permute-start | bytes 196616 | tf_op jit(solution)/shard_map/ppermute | solution.py:580
  46.5 10.1 %collective-permute-start.25 = (bf16[40,1024]{1,0:T(8,128)(2,1)S(1)}, bf16[40,1024]{1,0:T(8,128)(2,1)S(1)}, u32[]{:S(2)}, u32[]{:S(2)}) collective-permute-start(bf16[40,1024]{1,0:T(8,128)(2,1)S(1)} %pad_maximum_fusion.11), channel_id=1, source_target_pairs={{0,8},{1,3},{2,10},{3,1},{4,12},{5,7},{6,14},{7,5},{8,0},{9,11},{1... | collective-permute-start | bytes 245768 | tf_op jit(solution)/shard_map/ppermute | solution.py:580
  47.3 9.4 %collective-permute-start.20 = (bf16[32,1024]{1,0:T(8,128)(2,1)S(1)}, bf16[32,1024]{1,0:T(8,128)(2,1)S(1)}, u32[]{:S(2)}, u32[]{:S(2)}) collective-permute-start(bf16[32,1024]{1,0:T(8,128)(2,1)S(1)} %add_convert_fusion.2), channel_id=1, source_target_pairs={{0,4},{1,9},{2,6},{3,11},{4,0},{5,13},{6,2},{7,15},{8,12},{9,1},{1... | collective-permute-start | bytes 196616 | tf_op jit(solution)/shard_map/ppermute | solution.py:580
  49.4 8.4 %collective-permute-start.14 = (bf16[32,1024]{1,0:T(8,128)(2,1)S(1)}, bf16[32,1024]{1,0:T(8,128)(2,1)S(1)}, u32[]{:S(2)}, u32[]{:S(2)}) collective-permute-start(bf16[32,1024]{1,0:T(8,128)(2,1)S(1)} %add_convert_fusion.4), channel_id=1, source_target_pairs={{0,4},{1,9},{2,6},{3,11},{4,0},{5,13},{6,2},{7,15},{8,12},{9,1},{1... | collective-permute-start | bytes 196616 | tf_op jit(solution)/shard_map/ppermute | solution.py:580
  53.5 5.9 %collective-permute-start.8 = (bf16[32,1024]{1,0:T(8,128)(2,1)S(1)}, bf16[32,1024]{1,0:T(8,128)(2,1)S(1)}, u32[]{:S(2)}, u32[]{:S(2)}) collective-permute-start(bf16[32,1024]{1,0:T(8,128)(2,1)S(1)} %add_convert_fusion.6), channel_id=1, source_target_pairs={{0,4},{1,9},{2,6},{3,11},{4,0},{5,13},{6,2},{7,15},{8,12},{9,1},{1... | collective-permute-start | bytes 196616 | tf_op jit(solution)/shard_map/ppermute | solution.py:580
  56.6 5.0 %collective-permute-start.26 = (bf16[32,1024]{1,0:T(8,128)(2,1)S(1)}, bf16[32,1024]{1,0:T(8,128)(2,1)S(1)}, u32[]{:S(2)}, u32[]{:S(2)}) collective-permute-start(bf16[32,1024]{1,0:T(8,128)(2,1)S(1)} %add_convert_fusion), channel_id=1, source_target_pairs={{0,4},{1,9},{2,6},{3,11},{4,0},{5,13},{6,2},{7,15},{8,12},{9,1},{1... | collective-permute-start | bytes 196616 | tf_op jit(solution)/shard_map/ppermute | solution.py:580
  56.7 6.0 %collective-permute-start.21 = (bf16[64,1024]{1,0:T(8,128)(2,1)S(1)}, bf16[64,1024]{1,0:T(8,128)(2,1)S(1)}, u32[]{:S(2)}, u32[]{:S(2)}) collective-permute-start(bf16[64,1024]{1,0:T(8,128)(2,1)S(1)} %pad_maximum_fusion.8), channel_id=1, source_target_pairs={{0,2},{1,5},{2,0},{3,7},{4,6},{5,1},{6,4},{7,3},{8,10},{9,13},{10,... | collective-permute-start | bytes 393224 | tf_op jit(solution)/shard_map/ppermute | solution.py:580
  57.8 5.3 %collective-permute-start.15 = (bf16[64,1024]{1,0:T(8,128)(2,1)S(1)}, bf16[64,1024]{1,0:T(8,128)(2,1)S(1)}, u32[]{:S(2)}, u32[]{:S(2)}) collective-permute-start(bf16[64,1024]{1,0:T(8,128)(2,1)S(1)} %pad_maximum_fusion.7), channel_id=1, source_target_pairs={{0,2},{1,5},{2,0},{3,7},{4,6},{5,1},{6,4},{7,3},{8,10},{9,13},{10,... | collective-permute-start | bytes 393224 | tf_op jit(solution)/shard_map/ppermute | solution.py:580
  59.5 5.1 %collective-permute-start.9 = (bf16[64,1024]{1,0:T(8,128)(2,1)S(1)}, bf16[64,1024]{1,0:T(8,128)(2,1)S(1)}, u32[]{:S(2)}, u32[]{:S(2)}) collective-permute-start(bf16[64,1024]{1,0:T(8,128)(2,1)S(1)} %pad_maximum_fusion.6), channel_id=1, source_target_pairs={{0,2},{1,5},{2,0},{3,7},{4,6},{5,1},{6,4},{7,3},{8,10},{9,13},{10,... | collective-permute-start | bytes 393224 | tf_op jit(solution)/shard_map/ppermute | solution.py:580
  61.7 5.0 %collective-permute-start.27 = (bf16[64,1024]{1,0:T(8,128)(2,1)S(1)}, bf16[64,1024]{1,0:T(8,128)(2,1)S(1)}, u32[]{:S(2)}, u32[]{:S(2)}) collective-permute-start(bf16[64,1024]{1,0:T(8,128)(2,1)S(1)} %pad_maximum_fusion.9), channel_id=1, source_target_pairs={{0,2},{1,5},{2,0},{3,7},{4,6},{5,1},{6,4},{7,3},{8,10},{9,13},{10,... | collective-permute-start | bytes 393224 | tf_op jit(solution)/shard_map/ppermute | solution.py:580
  62.8 4.7 %collective-permute-start.30 = (bf16[128,1024]{1,0:T(8,128)(2,1)S(1)}, bf16[128,1024]{1,0:T(8,128)(2,1)S(1)}, u32[]{:S(2)}, u32[]{:S(2)}) collective-permute-start(bf16[128,1024]{1,0:T(8,128)(2,1)S(1)} %pad_maximum_fusion.3.refs_2_), channel_id=1, source_target_pairs={{0,1},{1,0},{2,3},{3,2},{4,5},{5,4},{6,7},{7,6},{8,9},{9,8},{10,11... | collective-permute-start | bytes 786440 | tf_op jit(solution)/shard_map/ppermute | solution.py:580
  (9 other events, 37.9 us)

commit v9 on v8

--- a/solution.py
+++ b/solution.py
@@ -278,7 +278,7 @@
 
     hidden_width = pre.shape[1]
     step = 2 * LANES
-    logit = jnp.zeros((slots, LANES), F32)
+    logit8 = jnp.zeros((8, slots), F32)
     first, second = take(2), take(3)
     weights2 = second[...].astype(F32)
     for start in range(0, hidden_width, step):
@@ -290,13 +290,9 @@
         hid_s[:, cols] = hid
         k = start // LANES
         w2 = jnp.concatenate([weights2[k : k + 1], weights2[k + 1 : k + 2]], axis=1)
-        prod = hid.astype(F32) * w2
-        for k in range(0, step, LANES):
-            logit = logit + prod[:, k : k + LANES]
+        w8 = jnp.broadcast_to(w2, (8, step)).astype(BF16)
+        logit8 = logit8 + dot_nt(w8, hid)
         slope_s[:, cols] = w2 * (sig + silu * (1.0 - sig))
-    ones = jnp.ones((8, LANES), BF16)
-    p = split3(logit)
-    logit8 = dot_nt(ones, p[0]) + (dot_nt(ones, p[1]) + dot_nt(ones, p[2]))
     slot = lax.broadcasted_iota(jnp.int32, (8, slots), 1)
     live = jnp.where(slot < count[0, 0], 1.0, 0.0)
     logit_o[...] = (live * logit8)[0:1, :]
@@ -649,15 +645,16 @@
         wholes = after
     arrived = []
     for whole, extra in wholes:
-        arrived.append(
-            swap(whole if extra is None else jnp.concatenate([whole, extra], axis=0), across)
-        )
+        leave = whole if extra is None else jnp.concatenate([whole, extra], axis=0)
+        arrived.append(swap(leave, across))
     own_extra = wholes[-1][1]
     mine = [whole for whole, _ in wholes]
     total = (2 * rows,) + mine[0].shape[1:]
+    last = chunks - 1
     own = [(w, 0, k) for k, w in enumerate(mine)]
     other = [(w, 1, k) for k, w in enumerate(arrived)]
-    grad_first, grad_second = written(None, own + other, rows, total, own_extra)
+    grad_first = written(None, own[:last] + own[last:] + other[1:last], rows, total)
+    grad_first, grad_second = written(grad_first, [other[0], other[last]], rows, total, own_extra)
     return grad_first, grad_second.reshape(total[1:])
 
 

time: 71.8 us -> 71.3 us (level)
  waiting for transfers between devices: 20.1 us -> 18.8 us
  Pallas kernels: 18.5 us -> 19.4 us
    ppermute x28, waiting for transfers between devices: 13.4 us -> 12.1 us  [swap(): return lax.ppermute(value, axes, pairs)]
    pallas_call x1 -> x2, Pallas kernels: 2.7 us -> 3.36 us  [written(): pl.pallas_call(kernel, out_shape=tuple(outs), in_specs=[HBM] * aliased +...]
  transfers between devices with their start and end apart: 32 -> 32, of which waited for: 13 -> 12; matrix products, arithmetic and copies ran while one was open for 2% -> 2% of each run, Pallas kernels for 12% -> 15%
where the time goes in v9:
time: 71.3 us; the launch traced here: 71 us
  starting transfers between devices  29.3 us (41%)
  Pallas kernels  19.4 us (27%)
  waiting for transfers between devices  18.8 us (26%)
  between operations  1.68 us (2%)
  other arithmetic  1.18 us (2%)
  local copies, waits for them, and re-layouts  0.73 us (1%)
    ppermute x28, starting transfers between devices, swap(): return lax.ppermute(value, axes, pairs)  25.8 us
    pallas_call x6, Pallas kernels, call(): pl.pallas_call(loading(kernel, len(loaded), len(given), len(out_shape), w...  16 us
    ppermute x28, waiting for transfers between devices, swap(): return lax.ppermute(value, axes, pairs)  12.1 us
    ppermute x1, waiting for transfers between devices, body(): incoming = lax.ppermute(chip_state, 'tm', onward)  5.52 us
    pallas_call x2, Pallas kernels, written(): pl.pallas_call(kernel, out_shape=tuple(outs), in_specs=[HBM] * aliased +...  3.36 us
    ppermute x1, starting transfers between devices, body(): other = lax.ppermute(pay, 'tm', [(i, i ^ 1) for i in range(n_tm)])  2.66 us
  transfers between devices with their start and end apart: 32, of which 12 were waited for; matrix products, arithmetic and copies ran while one was open for 2% of the time, Pallas kernels for 15%

profile of v9, /device:TPU:0, one launch (start us, length us, event | category | flops | bytes accessed | tf_op | source)
XLA Modules:
  0.0 71.0 jit_solution(2721819201550729978)
XLA Ops:
  1.8 3.4 %shard_map.192 = (bf16[256,1280]{1,0:T(8,128)(2,1)S(1)}, f32[256,16]{1,0:T(8,128)S(1)}, f32[16,256]{1,0:T(8,128)S(1)}, f32[16,256]{1,0:T(8,128)S(1)}, f32[16,16]...) custom-call(bf16[256,512]{1,0:T(8,128)(2,1)} %bitcast.12, ...), custom_call_target="tpu_custom_call" | custom-call | flops 335544320 | bytes 2621440 | tf_op jit(solution)/shard_map/pallas_call | solution.py:390
  5.9 2.7 %collective-permute-start.1 = (bf16[144,1024]{1,0:T(8,128)(2,1)S(1)}, bf16[144,1024]{1,0:T(8,128)(2,1)S(1)}, u32[]{:S(2)}, u32[]{:S(2)}) collective-permute-start(bf16[144,1024]{1,0:T(8,128)(2,1)S(1)} %get-tuple-element.46.refs_0_), channel_id=1, source_target_pairs={{0,1},{1,0},{2,3},{3,2},{4,5},{5,4},{6,7},{7,6},{8,9},{9,8},{10,11... | collective-permute-start | bytes 884744 | tf_op jit(solution)/shard_map/ppermute | solution.py:484
  8.6 1.2 %collective-permute-done.1.refs_1_.refs_8_ = bf16[144,1024]{1,0:T(8,128)(2,1)S(1)} collective-permute-done((bf16[144,1024]{1,0:T(8,128)(2,1)S(1)}, bf16[144,1024]{1,0:T(8,128)(2,1)S(1)}, u32[]{:S(2)}, u32[]{:S(2)}) %collective-permute-start.1) | collective-permute-done | bytes 294944 | tf_op jit(solution)/shard_map/ppermute | solution.py:484
  10.7 5.5 %collective-permute-done.2.refs_6_ = bf16[128,512]{1,0:T(8,128)(2,1)S(1)} collective-permute-done((bf16[128,512]{1,0:T(8,128)(2,1)S(1)}, bf16[128,512]{1,0:T(8,128)(2,1)S(1)}, u32[]{:S(2)}, u32[]{:S(2)}) %collective-permute-start.2) | collective-permute-done | bytes 131104 | tf_op jit(solution)/shard_map/ppermute | solution.py:496
  16.9 4.5 %shard_map.195 = (f32[256,1024]{1,0:T(8,128)S(1)}, f32[256,1024]{1,0:T(8,128)S(1)}, f32[512,1024]{1,0:T(8,128)S(1)}, bf16[512,256]{1,0:T(8,128)(2,1)S(1)}, bf16[...) custom-call(bf16[256,512]{1,0:T(8,128)(2,1)} %bitcast.13, bf16[512,1024]{1,0:T(8,128)(2,1)} %refs_1_.2, ...), custom_call_target="tpu_custom_call" | custom-call | flops 1073741824 | bytes 16777216 | tf_op jit(solution)/shard_map/pallas_call | solution.py:390
  21.5 6.1 %shard_map.196 = (bf16[256,512]{1,0:T(8,128)(2,1)}, f32[1,512]{1,0:T(1,128)}, bf16[512,1024]{1,0:T(8,128)(2,1)S(1)}, bf16[512,512]{1,0:T(8,128)(2,1)S(1)}, bf16[...) custom-call(f32[1,1024]{1,0:T(1,128)} %bitcast.17, ...), custom_call_target="tpu_custom_call" | custom-call | flops 1073741824 | bytes 4194304 | tf_op jit(solution)/shard_map/pallas_call | solution.py:390
  30.1 1.7 %collective-permute-start.11 = (bf16[64,1024]{1,0:T(8,128)(2,1)S(1)}, bf16[64,1024]{1,0:T(8,128)(2,1)S(1)}, u32[]{:S(2)}, u32[]{:S(2)}) collective-permute-start(bf16[64,1024]{1,0:T(8,128)(2,1)S(1)} %get-tuple-element.77), channel_id=1, source_target_pairs={{0,2},{1,5},{2,0},{3,7},{4,6},{5,1},{6,4},{7,3},{8,10},{9,13},{10,... | collective-permute-start | bytes 393224 | tf_op jit(solution)/shard_map/ppermute | solution.py:576
  32.5 1.7 %collective-permute-start.23 = (bf16[72,1024]{1,0:T(8,128)(2,1)S(1)}, bf16[72,1024]{1,0:T(8,128)(2,1)S(1)}, u32[]{:S(2)}, u32[]{:S(2)}) collective-permute-start(bf16[72,1024]{1,0:T(8,128)(2,1)S(1)} %pad_maximum_fusion.5), channel_id=1, source_target_pairs={{0,2},{1,5},{2,0},{3,7},{4,6},{5,1},{6,4},{7,3},{8,10},{9,13},{10,... | collective-permute-start | bytes 442376 | tf_op jit(solution)/shard_map/ppermute | solution.py:576
  34.6 1.6 %collective-permute-start.18 = (bf16[32,1024]{1,0:T(8,128)(2,1)S(1)}, bf16[32,1024]{1,0:T(8,128)(2,1)S(1)}, u32[]{:S(2)}, u32[]{:S(2)}) collective-permute-start(bf16[32,1024]{1,0:T(8,128)(2,1)S(1)} %select_convert_fusion.10), channel_id=1, source_target_pairs={{0,4},{1,9},{2,6},{3,11},{4,0},{5,13},{6,2},{7,15},{8,12},{9,1},{1... | collective-permute-start | bytes 196616 | tf_op jit(solution)/shard_map/ppermute | solution.py:576
  36.3 1.4 %collective-permute-start.12 = (bf16[32,1024]{1,0:T(8,128)(2,1)S(1)}, bf16[32,1024]{1,0:T(8,128)(2,1)S(1)}, u32[]{:S(2)}, u32[]{:S(2)}) collective-permute-start(bf16[32,1024]{1,0:T(8,128)(2,1)S(1)} %select_convert_fusion.12), channel_id=1, source_target_pairs={{0,4},{1,9},{2,6},{3,11},{4,0},{5,13},{6,2},{7,15},{8,12},{9,1},{1... | collective-permute-start | bytes 196616 | tf_op jit(solution)/shard_map/ppermute | solution.py:576
  37.7 1.4 %collective-permute-start.6 = (bf16[32,1024]{1,0:T(8,128)(2,1)S(1)}, bf16[32,1024]{1,0:T(8,128)(2,1)S(1)}, u32[]{:S(2)}, u32[]{:S(2)}) collective-permute-start(bf16[32,1024]{1,0:T(8,128)(2,1)S(1)} %select_convert_fusion.14), channel_id=1, source_target_pairs={{0,4},{1,9},{2,6},{3,11},{4,0},{5,13},{6,2},{7,15},{8,12},{9,1},{1... | collective-permute-start | bytes 196616 | tf_op jit(solution)/shard_map/ppermute | solution.py:576
  39.2 1.5 %collective-permute-start.24 = (bf16[40,1024]{1,0:T(8,128)(2,1)S(1)}, bf16[40,1024]{1,0:T(8,128)(2,1)S(1)}, u32[]{:S(2)}, u32[]{:S(2)}) collective-permute-start(bf16[40,1024]{1,0:T(8,128)(2,1)S(1)} %pad_maximum_fusion.10), channel_id=1, source_target_pairs={{0,4},{1,9},{2,6},{3,11},{4,0},{5,13},{6,2},{7,15},{8,12},{9,1},{1... | collective-permute-start | bytes 245768 | tf_op jit(solution)/shard_map/ppermute | solution.py:576
  40.8 2.6 %collective-permute-start.19 = (bf16[32,1024]{1,0:T(8,128)(2,1)S(1)}, bf16[32,1024]{1,0:T(8,128)(2,1)S(1)}, u32[]{:S(2)}, u32[]{:S(2)}) collective-permute-start(bf16[32,1024]{1,0:T(8,128)(2,1)S(1)} %add_convert_fusion.3), channel_id=1, source_target_pairs={{0,8},{1,3},{2,10},{3,1},{4,12},{5,7},{6,14},{7,5},{8,0},{9,11},{1... | collective-permute-start | bytes 196616 | tf_op jit(solution)/shard_map/ppermute | solution.py:576
  44.1 2.5 %collective-permute-start.7 = (bf16[32,1024]{1,0:T(8,128)(2,1)S(1)}, bf16[32,1024]{1,0:T(8,128)(2,1)S(1)}, u32[]{:S(2)}, u32[]{:S(2)}) collective-permute-start(bf16[32,1024]{1,0:T(8,128)(2,1)S(1)} %add_convert_fusion.7), channel_id=1, source_target_pairs={{0,8},{1,3},{2,10},{3,1},{4,12},{5,7},{6,14},{7,5},{8,0},{9,11},{1... | collective-permute-start | bytes 196616 | tf_op jit(solution)/shard_map/ppermute | solution.py:576
  47.4 2.0 %collective-permute-start.20 = (bf16[32,1024]{1,0:T(8,128)(2,1)S(1)}, bf16[32,1024]{1,0:T(8,128)(2,1)S(1)}, u32[]{:S(2)}, u32[]{:S(2)}) collective-permute-start(bf16[32,1024]{1,0:T(8,128)(2,1)S(1)} %add_convert_fusion.2), channel_id=1, source_target_pairs={{0,4},{1,9},{2,6},{3,11},{4,0},{5,13},{6,2},{7,15},{8,12},{9,1},{1... | collective-permute-start | bytes 196616 | tf_op jit(solution)/shard_map/ppermute | solution.py:576
  50.3 3.4 %collective-permute-done.7 = bf16[32,1024]{1,0:T(8,128)(2,1)S(1)} collective-permute-done((bf16[32,1024]{1,0:T(8,128)(2,1)S(1)}, bf16[32,1024]{1,0:T(8,128)(2,1)S(1)}, u32[]{:S(2)}, u32[]{:S(2)}) %collective-permute-start.7) | collective-permute-done | bytes 65568 | tf_op jit(solution)/shard_map/ppermute | solution.py:576
  54.3 2.4 %collective-permute-done.25 = bf16[40,1024]{1,0:T(8,128)(2,1)S(1)} collective-permute-done((bf16[40,1024]{1,0:T(8,128)(2,1)S(1)}, bf16[40,1024]{1,0:T(8,128)(2,1)S(1)}, u32[]{:S(2)}, u32[]{:S(2)}) %collective-permute-start.25) | collective-permute-done | bytes 81952 | tf_op jit(solution)/shard_map/ppermute | solution.py:576
  56.9 1.0 %collective-permute-start.21 = (bf16[64,1024]{1,0:T(8,128)(2,1)S(1)}, bf16[64,1024]{1,0:T(8,128)(2,1)S(1)}, u32[]{:S(2)}, u32[]{:S(2)}) collective-permute-start(bf16[64,1024]{1,0:T(8,128)(2,1)S(1)} %pad_maximum_fusion.8), channel_id=1, source_target_pairs={{0,2},{1,5},{2,0},{3,7},{4,6},{5,1},{6,4},{7,3},{8,10},{9,13},{10,... | collective-permute-start | bytes 393224 | tf_op jit(solution)/shard_map/ppermute | solution.py:576
  58.0 1.1 %collective-permute-start.15 = (bf16[64,1024]{1,0:T(8,128)(2,1)S(1)}, bf16[64,1024]{1,0:T(8,128)(2,1)S(1)}, u32[]{:S(2)}, u32[]{:S(2)}) collective-permute-start(bf16[64,1024]{1,0:T(8,128)(2,1)S(1)} %pad_maximum_fusion.7), channel_id=1, source_target_pairs={{0,2},{1,5},{2,0},{3,7},{4,6},{5,1},{6,4},{7,3},{8,10},{9,13},{10,... | collective-permute-start | bytes 393224 | tf_op jit(solution)/shard_map/ppermute | solution.py:576
  60.2 1.6 %collective-permute-done.26 = bf16[32,1024]{1,0:T(8,128)(2,1)S(1)} collective-permute-done((bf16[32,1024]{1,0:T(8,128)(2,1)S(1)}, bf16[32,1024]{1,0:T(8,128)(2,1)S(1)}, u32[]{:S(2)}, u32[]{:S(2)}) %collective-permute-start.26) | collective-permute-done | bytes 65568 | tf_op jit(solution)/shard_map/ppermute | solution.py:576
  63.7 1.1 %collective-permute-done.9 = bf16[64,1024]{1,0:T(8,128)(2,1)S(1)} collective-permute-done((bf16[64,1024]{1,0:T(8,128)(2,1)S(1)}, bf16[64,1024]{1,0:T(8,128)(2,1)S(1)}, u32[]{:S(2)}, u32[]{:S(2)}) %collective-permute-start.9) | collective-permute-done | bytes 131104 | tf_op jit(solution)/shard_map/ppermute | solution.py:576
  64.8 2.1 %collective-permute-done.27 = bf16[64,1024]{1,0:T(8,128)(2,1)S(1)} collective-permute-done((bf16[64,1024]{1,0:T(8,128)(2,1)S(1)}, bf16[64,1024]{1,0:T(8,128)(2,1)S(1)}, u32[]{:S(2)}, u32[]{:S(2)}) %collective-permute-start.27) | collective-permute-done | bytes 131104 | tf_op jit(solution)/shard_map/ppermute | solution.py:576
  67.6 1.7 %shard_map.198.refs_0_ = f32[1024,1024]{1,0:T(8,128)} custom-call(bf16[128,1024]{1,0:T(8,128)(2,1)S(1)} %pad_maximum_fusion.1.refs_0_, bf16[128,1024]{1,0:T(8,128)(2,1)S(1)} %pad_maximum_fusion.2.refs_1_, bf16[128,1024]{1,0:T(8,128)(2,1)S(1)} %pad_maximum_fusion.3.refs_2_, bf16[128,1024]{1,0:T(8,128)(2,1)S(1)} %pad_maximum_fusion.4.refs_3_, ...), custom_call_target="tpu_custom_call" | custom-call | flops 786432 | bytes 4718592 | tf_op jit(solution)/shard_map/pallas_call | solution.py:700
  69.4 1.6 %shard_map.199 = (f32[1024,1024]{1,0:T(8,128)}, f32[1,1024]{1,0:T(1,128)}) custom-call(f32[1024,1024]{1,0:T(8,128)} %shard_map.198.refs_0_, bf16[128,1024]{1,0:T(8,128)(2,1)S(1)} %collective-permute-done.30.refs_1_, bf16[136,1024]{1,0:T(8,128)(2,1)S(1)} %collective-permute-done.31.refs_2_, ...), custom_call_target="tpu_custom_call", output_to_operand_aliasing={{0}: (0, {})} | custom-call | flops 262144 | bytes 1572864 | tf_op jit(solution)/shard_map/pallas_call | solution.py:700
  (91 shorter events, 13.5 us)
Async XLA Ops:
  10.4 5.8 %collective-permute-start.2 = (bf16[128,512]{1,0:T(8,128)(2,1)S(1)}, bf16[128,512]{1,0:T(8,128)(2,1)S(1)}, u32[]{:S(2)}, u32[]{:S(2)}) collective-permute-start(bf16[128,512]{1,0:T(8,128)(2,1)S(1)} %get-tuple-element.47), channel_id=1, source_target_pairs={{0,2},{1,3},{2,0},{3,1},{4,6},{5,7},{6,4},{7,5},{8,10},{9,11},{10,... | collective-permute-start | bytes 393224 | tf_op jit(solution)/shard_map/ppermute | solution.py:496
  16.3 5.2 %collective-permute-start.3 = (bf16[128,512]{1,0:T(8,128)(2,1)S(1)}, bf16[128,512]{1,0:T(8,128)(2,1)S(1)}, u32[]{:S(2)}, u32[]{:S(2)}) collective-permute-start(bf16[128,512]{1,0:T(8,128)(2,1)S(1)} %collective-permute-done.2.refs_6_), channel_id=1, source_target_pairs={{0,1},{1,0},{2,3},{3,2},{4,5},{5,4},{6,7},{7,6},{8,9},{9,8},{10,11... | collective-permute-start | bytes 393224 | tf_op jit(solution)/shard_map/ppermute | solution.py:501
  28.1 4.3 %collective-permute-start.22 = (bf16[136,1024]{1,0:T(8,128)(2,1)S(1)}, bf16[136,1024]{1,0:T(8,128)(2,1)S(1)}, u32[]{:S(2)}, u32[]{:S(2)}) collective-permute-start(bf16[136,1024]{1,0:T(8,128)(2,1)S(1)} %get-tuple-element.62.refs_3_), channel_id=1, source_target_pairs={{0,1},{1,0},{2,3},{3,2},{4,5},{5,4},{6,7},{7,6},{8,9},{9,8},{10,11... | collective-permute-start | bytes 835592 | tf_op jit(solution)/shard_map/ppermute | solution.py:576
  29.6 5.0 %collective-permute-start.17 = (bf16[64,1024]{1,0:T(8,128)(2,1)S(1)}, bf16[64,1024]{1,0:T(8,128)(2,1)S(1)}, u32[]{:S(2)}, u32[]{:S(2)}) collective-permute-start(bf16[64,1024]{1,0:T(8,128)(2,1)S(1)} %get-tuple-element.75), channel_id=1, source_target_pairs={{0,2},{1,5},{2,0},{3,7},{4,6},{5,1},{6,4},{7,3},{8,10},{9,13},{10,... | collective-permute-start | bytes 393224 | tf_op jit(solution)/shard_map/ppermute | solution.py:576
  30.1 6.2 %collective-permute-start.11 = (bf16[64,1024]{1,0:T(8,128)(2,1)S(1)}, bf16[64,1024]{1,0:T(8,128)(2,1)S(1)}, u32[]{:S(2)}, u32[]{:S(2)}) collective-permute-start(bf16[64,1024]{1,0:T(8,128)(2,1)S(1)} %get-tuple-element.77), channel_id=1, source_target_pairs={{0,2},{1,5},{2,0},{3,7},{4,6},{5,1},{6,4},{7,3},{8,10},{9,13},{10,... | collective-permute-start | bytes 393224 | tf_op jit(solution)/shard_map/ppermute | solution.py:576
  31.9 5.8 %collective-permute-start.5 = (bf16[64,1024]{1,0:T(8,128)(2,1)S(1)}, bf16[64,1024]{1,0:T(8,128)(2,1)S(1)}, u32[]{:S(2)}, u32[]{:S(2)}) collective-permute-start(bf16[64,1024]{1,0:T(8,128)(2,1)S(1)} %get-tuple-element.79), channel_id=1, source_target_pairs={{0,2},{1,5},{2,0},{3,7},{4,6},{5,1},{6,4},{7,3},{8,10},{9,13},{10,... | collective-permute-start | bytes 393224 | tf_op jit(solution)/shard_map/ppermute | solution.py:576
  32.5 6.6 %collective-permute-start.23 = (bf16[72,1024]{1,0:T(8,128)(2,1)S(1)}, bf16[72,1024]{1,0:T(8,128)(2,1)S(1)}, u32[]{:S(2)}, u32[]{:S(2)}) collective-permute-start(bf16[72,1024]{1,0:T(8,128)(2,1)S(1)} %pad_maximum_fusion.5), channel_id=1, source_target_pairs={{0,2},{1,5},{2,0},{3,7},{4,6},{5,1},{6,4},{7,3},{8,10},{9,13},{10,... | collective-permute-start | bytes 442376 | tf_op jit(solution)/shard_map/ppermute | solution.py:576
  34.6 6.1 %collective-permute-start.18 = (bf16[32,1024]{1,0:T(8,128)(2,1)S(1)}, bf16[32,1024]{1,0:T(8,128)(2,1)S(1)}, u32[]{:S(2)}, u32[]{:S(2)}) collective-permute-start(bf16[32,1024]{1,0:T(8,128)(2,1)S(1)} %select_convert_fusion.10), channel_id=1, source_target_pairs={{0,4},{1,9},{2,6},{3,11},{4,0},{5,13},{6,2},{7,15},{8,12},{9,1},{1... | collective-permute-start | bytes 196616 | tf_op jit(solution)/shard_map/ppermute | solution.py:576
  36.3 7.1 %collective-permute-start.12 = (bf16[32,1024]{1,0:T(8,128)(2,1)S(1)}, bf16[32,1024]{1,0:T(8,128)(2,1)S(1)}, u32[]{:S(2)}, u32[]{:S(2)}) collective-permute-start(bf16[32,1024]{1,0:T(8,128)(2,1)S(1)} %select_convert_fusion.12), channel_id=1, source_target_pairs={{0,4},{1,9},{2,6},{3,11},{4,0},{5,13},{6,2},{7,15},{8,12},{9,1},{1... | collective-permute-start | bytes 196616 | tf_op jit(solution)/shard_map/ppermute | solution.py:576
  37.7 6.3 %collective-permute-start.6 = (bf16[32,1024]{1,0:T(8,128)(2,1)S(1)}, bf16[32,1024]{1,0:T(8,128)(2,1)S(1)}, u32[]{:S(2)}, u32[]{:S(2)}) collective-permute-start(bf16[32,1024]{1,0:T(8,128)(2,1)S(1)} %select_convert_fusion.14), channel_id=1, source_target_pairs={{0,4},{1,9},{2,6},{3,11},{4,0},{5,13},{6,2},{7,15},{8,12},{9,1},{1... | collective-permute-start | bytes 196616 | tf_op jit(solution)/shard_map/ppermute | solution.py:576
  39.2 7.4 %collective-permute-start.24 = (bf16[40,1024]{1,0:T(8,128)(2,1)S(1)}, bf16[40,1024]{1,0:T(8,128)(2,1)S(1)}, u32[]{:S(2)}, u32[]{:S(2)}) collective-permute-start(bf16[40,1024]{1,0:T(8,128)(2,1)S(1)} %pad_maximum_fusion.10), channel_id=1, source_target_pairs={{0,4},{1,9},{2,6},{3,11},{4,0},{5,13},{6,2},{7,15},{8,12},{9,1},{1... | collective-permute-start | bytes 245768 | tf_op jit(solution)/shard_map/ppermute | solution.py:576
  40.8 6.6 %collective-permute-start.19 = (bf16[32,1024]{1,0:T(8,128)(2,1)S(1)}, bf16[32,1024]{1,0:T(8,128)(2,1)S(1)}, u32[]{:S(2)}, u32[]{:S(2)}) collective-permute-start(bf16[32,1024]{1,0:T(8,128)(2,1)S(1)} %add_convert_fusion.3), channel_id=1, source_target_pairs={{0,8},{1,3},{2,10},{3,1},{4,12},{5,7},{6,14},{7,5},{8,0},{9,11},{1... | collective-permute-start | bytes 196616 | tf_op jit(solution)/shard_map/ppermute | solution.py:576
  43.5 6.0 %collective-permute-start.13 = (bf16[32,1024]{1,0:T(8,128)(2,1)S(1)}, bf16[32,1024]{1,0:T(8,128)(2,1)S(1)}, u32[]{:S(2)}, u32[]{:S(2)}) collective-permute-start(bf16[32,1024]{1,0:T(8,128)(2,1)S(1)} %add_convert_fusion.5), channel_id=1, source_target_pairs={{0,8},{1,3},{2,10},{3,1},{4,12},{5,7},{6,14},{7,5},{8,0},{9,11},{1... | collective-permute-start | bytes 196616 | tf_op jit(solution)/shard_map/ppermute | solution.py:576
  44.1 9.5 %collective-permute-start.7 = (bf16[32,1024]{1,0:T(8,128)(2,1)S(1)}, bf16[32,1024]{1,0:T(8,128)(2,1)S(1)}, u32[]{:S(2)}, u32[]{:S(2)}) collective-permute-start(bf16[32,1024]{1,0:T(8,128)(2,1)S(1)} %add_convert_fusion.7), channel_id=1, source_target_pairs={{0,8},{1,3},{2,10},{3,1},{4,12},{5,7},{6,14},{7,5},{8,0},{9,11},{1... | collective-permute-start | bytes 196616 | tf_op jit(solution)/shard_map/ppermute | solution.py:576
  46.6 10.1 %collective-permute-start.25 = (bf16[40,1024]{1,0:T(8,128)(2,1)S(1)}, bf16[40,1024]{1,0:T(8,128)(2,1)S(1)}, u32[]{:S(2)}, u32[]{:S(2)}) collective-permute-start(bf16[40,1024]{1,0:T(8,128)(2,1)S(1)} %pad_maximum_fusion.11), channel_id=1, source_target_pairs={{0,8},{1,3},{2,10},{3,1},{4,12},{5,7},{6,14},{7,5},{8,0},{9,11},{1... | collective-permute-start | bytes 245768 | tf_op jit(solution)/shard_map/ppermute | solution.py:576
  47.4 9.4 %collective-permute-start.20 = (bf16[32,1024]{1,0:T(8,128)(2,1)S(1)}, bf16[32,1024]{1,0:T(8,128)(2,1)S(1)}, u32[]{:S(2)}, u32[]{:S(2)}) collective-permute-start(bf16[32,1024]{1,0:T(8,128)(2,1)S(1)} %add_convert_fusion.2), channel_id=1, source_target_pairs={{0,4},{1,9},{2,6},{3,11},{4,0},{5,13},{6,2},{7,15},{8,12},{9,1},{1... | collective-permute-start | bytes 196616 | tf_op jit(solution)/shard_map/ppermute | solution.py:576
  49.5 8.4 %collective-permute-start.14 = (bf16[32,1024]{1,0:T(8,128)(2,1)S(1)}, bf16[32,1024]{1,0:T(8,128)(2,1)S(1)}, u32[]{:S(2)}, u32[]{:S(2)}) collective-permute-start(bf16[32,1024]{1,0:T(8,128)(2,1)S(1)} %add_convert_fusion.4), channel_id=1, source_target_pairs={{0,4},{1,9},{2,6},{3,11},{4,0},{5,13},{6,2},{7,15},{8,12},{9,1},{1... | collective-permute-start | bytes 196616 | tf_op jit(solution)/shard_map/ppermute | solution.py:576
  53.7 5.9 %collective-permute-start.8 = (bf16[32,1024]{1,0:T(8,128)(2,1)S(1)}, bf16[32,1024]{1,0:T(8,128)(2,1)S(1)}, u32[]{:S(2)}, u32[]{:S(2)}) collective-permute-start(bf16[32,1024]{1,0:T(8,128)(2,1)S(1)} %add_convert_fusion.6), channel_id=1, source_target_pairs={{0,4},{1,9},{2,6},{3,11},{4,0},{5,13},{6,2},{7,15},{8,12},{9,1},{1... | collective-permute-start | bytes 196616 | tf_op jit(solution)/shard_map/ppermute | solution.py:576
  56.7 5.0 %collective-permute-start.26 = (bf16[32,1024]{1,0:T(8,128)(2,1)S(1)}, bf16[32,1024]{1,0:T(8,128)(2,1)S(1)}, u32[]{:S(2)}, u32[]{:S(2)}) collective-permute-start(bf16[32,1024]{1,0:T(8,128)(2,1)S(1)} %add_convert_fusion), channel_id=1, source_target_pairs={{0,4},{1,9},{2,6},{3,11},{4,0},{5,13},{6,2},{7,15},{8,12},{9,1},{1... | collective-permute-start | bytes 196616 | tf_op jit(solution)/shard_map/ppermute | solution.py:576
  56.9 6.0 %collective-permute-start.21 = (bf16[64,1024]{1,0:T(8,128)(2,1)S(1)}, bf16[64,1024]{1,0:T(8,128)(2,1)S(1)}, u32[]{:S(2)}, u32[]{:S(2)}) collective-permute-start(bf16[64,1024]{1,0:T(8,128)(2,1)S(1)} %pad_maximum_fusion.8), channel_id=1, source_target_pairs={{0,2},{1,5},{2,0},{3,7},{4,6},{5,1},{6,4},{7,3},{8,10},{9,13},{10,... | collective-permute-start | bytes 393224 | tf_op jit(solution)/shard_map/ppermute | solution.py:576
  58.0 5.3 %collective-permute-start.15 = (bf16[64,1024]{1,0:T(8,128)(2,1)S(1)}, bf16[64,1024]{1,0:T(8,128)(2,1)S(1)}, u32[]{:S(2)}, u32[]{:S(2)}) collective-permute-start(bf16[64,1024]{1,0:T(8,128)(2,1)S(1)} %pad_maximum_fusion.7), channel_id=1, source_target_pairs={{0,2},{1,5},{2,0},{3,7},{4,6},{5,1},{6,4},{7,3},{8,10},{9,13},{10,... | collective-permute-start | bytes 393224 | tf_op jit(solution)/shard_map/ppermute | solution.py:576
  59.6 5.1 %collective-permute-start.9 = (bf16[64,1024]{1,0:T(8,128)(2,1)S(1)}, bf16[64,1024]{1,0:T(8,128)(2,1)S(1)}, u32[]{:S(2)}, u32[]{:S(2)}) collective-permute-start(bf16[64,1024]{1,0:T(8,128)(2,1)S(1)} %pad_maximum_fusion.6), channel_id=1, source_target_pairs={{0,2},{1,5},{2,0},{3,7},{4,6},{5,1},{6,4},{7,3},{8,10},{9,13},{10,... | collective-permute-start | bytes 393224 | tf_op jit(solution)/shard_map/ppermute | solution.py:576
  61.8 5.0 %collective-permute-start.27 = (bf16[64,1024]{1,0:T(8,128)(2,1)S(1)}, bf16[64,1024]{1,0:T(8,128)(2,1)S(1)}, u32[]{:S(2)}, u32[]{:S(2)}) collective-permute-start(bf16[64,1024]{1,0:T(8,128)(2,1)S(1)} %pad_maximum_fusion.9), channel_id=1, source_target_pairs={{0,2},{1,5},{2,0},{3,7},{4,6},{5,1},{6,4},{7,3},{8,10},{9,13},{10,... | collective-permute-start | bytes 393224 | tf_op jit(solution)/shard_map/ppermute | solution.py:576
  62.9 4.7 %collective-permute-start.29 = (bf16[128,1024]{1,0:T(8,128)(2,1)S(1)}, bf16[128,1024]{1,0:T(8,128)(2,1)S(1)}, u32[]{:S(2)}, u32[]{:S(2)}) collective-permute-start(bf16[128,1024]{1,0:T(8,128)(2,1)S(1)} %pad_maximum_fusion.3.refs_2_), channel_id=1, source_target_pairs={{0,1},{1,0},{2,3},{3,2},{4,5},{5,4},{6,7},{7,6},{8,9},{9,8},{10,11... | collective-permute-start | bytes 786440 | tf_op jit(solution)/shard_map/ppermute | solution.py:576
  (9 other events, 38.8 us)

commit v10 on v8

--- a/solution.py
+++ b/solution.py
@@ -584,27 +584,31 @@
 
     chip_bits = [("tm", k) for k in range(bits_of(n_tm // 2))]
     user_bits = [("user", k) for k in range(bits_of(n_user))]
-    order_even = chip_bits + user_bits
-    order_odd = user_bits + chip_bits
-
-    def partner_of(level):
+    chip_first = chip_bits + user_bits
+    user_first = user_bits + chip_bits
+    mixed = (chip_first, user_first)
+    alike = (chip_first, chip_first)
+    orders = [mixed, mixed, alike, mixed]
+
+    def partner_of(level, chunk):
         def partner(u, t):
-            axis, k = (order_even if t % 2 == 0 else order_odd)[level]
+            axis, k = orders[chunk][t % 2][level]
             if axis == "tm":
                 return u * n_tm + (t ^ (2 << k))
             return (u ^ (1 << k)) * n_tm + t
 
         return partner
 
-    def bit_of(level):
+    def bit_of(level, chunk):
         def one(entry):
             axis, k = entry
             return (tm >> (k + 1)) & 1 if axis == "tm" else (user >> k) & 1
 
-        return jnp.where(odd == 0, one(order_even[level]), one(order_odd[level])) == 1
-
-    levels = len(order_even)
-    bits = [bit_of(level) for level in range(levels)]
+        even_one, odd_one = (one(order[level]) for order in orders[chunk])
+        return jnp.where(odd == 0, even_one, odd_one) == 1
+
+    levels = len(chip_first)
+    bits = [[bit_of(level, chunk) for chunk in range(chunks)] for level in range(levels)]
     size = rows // chunks
     state = []
     for leave, stay in zip(send, keep):
@@ -615,49 +619,50 @@
         state.append((stay[:size], got[:size], extra))
     for level in range(levels - 1):
         after = []
-        for a, b, extra in state:
+        for chunk, (a, b, extra) in enumerate(state):
             size = a.shape[0] // 2
             low = a[:size].astype(F32) + b[:size].astype(F32)
             high = a[size:].astype(F32) + b[size:].astype(F32)
-            leave = jnp.where(bits[level], low, high).astype(BF16)
-            stay = jnp.where(bits[level], high, low).astype(BF16)
+            leave = jnp.where(bits[level][chunk], low, high).astype(BF16)
+            stay = jnp.where(bits[level][chunk], high, low).astype(BF16)
             if extra is not None:
                 leave = jnp.concatenate([leave, extra], axis=0)
-            got = swap(leave, partner_of(level))
+            got = swap(leave, partner_of(level, chunk))
             if extra is not None:
                 extra = (extra.astype(F32) + got[size:].astype(F32)).astype(BF16)
             after.append((stay, got[:size], extra))
         state = after
     wholes = []
-    for a, b, extra in state:
+    for chunk, (a, b, extra) in enumerate(state):
         size = a.shape[0]
         whole = (a.astype(F32) + b.astype(F32)).astype(BF16)
         if levels:
             leave = whole if extra is None else jnp.concatenate([whole, extra], axis=0)
-            got = swap(leave, partner_of(levels - 1))
+            got = swap(leave, partner_of(levels - 1, chunk))
             whole = (whole.astype(F32) + got[:size].astype(F32)).astype(BF16)
             if extra is not None:
                 extra = (extra.astype(F32) + got[size:].astype(F32)).astype(BF16)
         wholes.append((whole, extra))
     for level in reversed(range(levels - 1)):
         after = []
-        for whole, extra in wholes:
-            got = swap(whole, partner_of(level))
-            first = jnp.where(bits[level], got, whole)
-            second = jnp.where(bits[level], whole, got)
+        for chunk, (whole, extra) in enumerate(wholes):
+            got = swap(whole, partner_of(level, chunk))
+            first = jnp.where(bits[level][chunk], got, whole)
+            second = jnp.where(bits[level][chunk], whole, got)
             after.append((jnp.concatenate([first, second], axis=0), extra))
         wholes = after
     arrived = []
     for whole, extra in wholes:
-        arrived.append(
-            swap(whole if extra is None else jnp.concatenate([whole, extra], axis=0), across)
-        )
+        leave = whole if extra is None else jnp.concatenate([whole, extra], axis=0)
+        arrived.append(swap(leave, across))
     own_extra = wholes[-1][1]
     mine = [whole for whole, _ in wholes]
     total = (2 * rows,) + mine[0].shape[1:]
+    last = chunks - 1
     own = [(w, 0, k) for k, w in enumerate(mine)]
     other = [(w, 1, k) for k, w in enumerate(arrived)]
-    grad_first, grad_second = written(None, own + other, rows, total, own_extra)
+    grad_first = written(None, own[:last] + own[last:] + other[1:last], rows, total)
+    grad_first, grad_second = written(grad_first, [other[0], other[last]], rows, total, own_extra)
     return grad_first, grad_second.reshape(total[1:])
 
 

time: 71.8 us -> 70.8 us (0.986)
  starting transfers between devices: 29.3 us -> 27 us
    ppermute x28, starting transfers between devices: 25.8 us -> 23.5 us  [swap(): return lax.ppermute(value, axes, pairs)]
    pallas_call x1 -> x2, Pallas kernels: 2.7 us -> 3.36 us  [written(): pl.pallas_call(kernel, out_shape=tuple(outs), in_specs=[HBM] * aliased +...]
  transfers between devices with their start and end apart: 32 -> 32, of which waited for: 13 -> 12; matrix products, arithmetic and copies ran while one was open for 2% -> 2% of each run, Pallas kernels for 12% -> 15%
where the time goes in v10:
time: 70.8 us; the launch traced here: 70.5 us
  starting transfers between devices  27 us (38%)
  waiting for transfers between devices  20.7 us (29%)
  Pallas kernels  19.2 us (27%)
  between operations  1.68 us (2%)
  other arithmetic  1.18 us (2%)
  local copies, waits for them, and re-layouts  0.73 us (1%)
    ppermute x28, starting transfers between devices, swap(): return lax.ppermute(value, axes, pairs)  23.5 us
    pallas_call x6, Pallas kernels, call(): pl.pallas_call(loading(kernel, len(loaded), len(given), len(out_shape), w...  15.9 us
    ppermute x28, waiting for transfers between devices, swap(): return lax.ppermute(value, axes, pairs)  14 us
    ppermute x1, waiting for transfers between devices, body(): incoming = lax.ppermute(chip_state, 'tm', onward)  5.52 us
    pallas_call x2, Pallas kernels, written(): pl.pallas_call(kernel, out_shape=tuple(outs), in_specs=[HBM] * aliased +...  3.36 us
    ppermute x1, starting transfers between devices, body(): other = lax.ppermute(pay, 'tm', [(i, i ^ 1) for i in range(n_tm)])  2.66 us
  transfers between devices with their start and end apart: 32, of which 12 were waited for; matrix products, arithmetic and copies ran while one was open for 2% of the time, Pallas kernels for 15%

profile of v10, /device:TPU:0, one launch (start us, length us, event | category | flops | bytes accessed | tf_op | source)
XLA Modules:
  0.0 70.5 jit_solution(15537059102801015045)
XLA Ops:
  1.8 3.4 %shard_map.192 = (bf16[256,1280]{1,0:T(8,128)(2,1)S(1)}, f32[256,16]{1,0:T(8,128)S(1)}, f32[16,256]{1,0:T(8,128)S(1)}, f32[16,256]{1,0:T(8,128)S(1)}, f32[16,16]...) custom-call(bf16[256,512]{1,0:T(8,128)(2,1)} %bitcast.12, ...), custom_call_target="tpu_custom_call" | custom-call | flops 335544320 | bytes 2621440 | tf_op jit(solution)/shard_map/pallas_call | solution.py:394
  5.9 2.7 %collective-permute-start.1 = (bf16[144,1024]{1,0:T(8,128)(2,1)S(1)}, bf16[144,1024]{1,0:T(8,128)(2,1)S(1)}, u32[]{:S(2)}, u32[]{:S(2)}) collective-permute-start(bf16[144,1024]{1,0:T(8,128)(2,1)S(1)} %get-tuple-element.46.refs_0_), channel_id=1, source_target_pairs={{0,1},{1,0},{2,3},{3,2},{4,5},{5,4},{6,7},{7,6},{8,9},{9,8},{10,11... | collective-permute-start | bytes 884744 | tf_op jit(solution)/shard_map/ppermute | solution.py:488
  8.6 1.2 %collective-permute-done.1.refs_1_.refs_8_ = bf16[144,1024]{1,0:T(8,128)(2,1)S(1)} collective-permute-done((bf16[144,1024]{1,0:T(8,128)(2,1)S(1)}, bf16[144,1024]{1,0:T(8,128)(2,1)S(1)}, u32[]{:S(2)}, u32[]{:S(2)}) %collective-permute-start.1) | collective-permute-done | bytes 294944 | tf_op jit(solution)/shard_map/ppermute | solution.py:488
  10.7 5.5 %collective-permute-done.2.refs_6_ = bf16[128,512]{1,0:T(8,128)(2,1)S(1)} collective-permute-done((bf16[128,512]{1,0:T(8,128)(2,1)S(1)}, bf16[128,512]{1,0:T(8,128)(2,1)S(1)}, u32[]{:S(2)}, u32[]{:S(2)}) %collective-permute-start.2) | collective-permute-done | bytes 131104 | tf_op jit(solution)/shard_map/ppermute | solution.py:500
  16.9 4.5 %shard_map.195 = (f32[256,1024]{1,0:T(8,128)S(1)}, f32[256,1024]{1,0:T(8,128)S(1)}, f32[512,1024]{1,0:T(8,128)S(1)}, bf16[512,256]{1,0:T(8,128)(2,1)S(1)}, bf16[...) custom-call(bf16[256,512]{1,0:T(8,128)(2,1)} %bitcast.13, bf16[512,1024]{1,0:T(8,128)(2,1)} %refs_1_.2, ...), custom_call_target="tpu_custom_call" | custom-call | flops 1073741824 | bytes 16777216 | tf_op jit(solution)/shard_map/pallas_call | solution.py:394
  21.5 5.9 %shard_map.196 = (bf16[256,512]{1,0:T(8,128)(2,1)}, f32[1,512]{1,0:T(1,128)}, bf16[512,1024]{1,0:T(8,128)(2,1)S(1)}, bf16[512,512]{1,0:T(8,128)(2,1)S(1)}, bf16[...) custom-call(f32[1,1024]{1,0:T(1,128)} %bitcast.17, ...), custom_call_target="tpu_custom_call" | custom-call | flops 1073741824 | bytes 4194304 | tf_op jit(solution)/shard_map/pallas_call | solution.py:394
  30.0 1.7 %collective-permute-start.11 = (bf16[64,1024]{1,0:T(8,128)(2,1)S(1)}, bf16[64,1024]{1,0:T(8,128)(2,1)S(1)}, u32[]{:S(2)}, u32[]{:S(2)}) collective-permute-start(bf16[64,1024]{1,0:T(8,128)(2,1)S(1)} %get-tuple-element.77), channel_id=1, source_target_pairs={{0,2},{1,5},{2,0},{3,7},{4,6},{5,1},{6,4},{7,3},{8,10},{9,13},{10,... | collective-permute-start | bytes 393224 | tf_op jit(solution)/shard_map/ppermute | solution.py:580
  32.4 1.7 %collective-permute-start.23 = (bf16[72,1024]{1,0:T(8,128)(2,1)S(1)}, bf16[72,1024]{1,0:T(8,128)(2,1)S(1)}, u32[]{:S(2)}, u32[]{:S(2)}) collective-permute-start(bf16[72,1024]{1,0:T(8,128)(2,1)S(1)} %pad_maximum_fusion.5), channel_id=1, source_target_pairs={{0,2},{1,5},{2,0},{3,7},{4,6},{5,1},{6,4},{7,3},{8,10},{9,13},{10,... | collective-permute-start | bytes 442376 | tf_op jit(solution)/shard_map/ppermute | solution.py:580
  34.1 1.3 %collective-permute-done.17 = bf16[64,1024]{1,0:T(8,128)(2,1)S(1)} collective-permute-done((bf16[64,1024]{1,0:T(8,128)(2,1)S(1)}, bf16[64,1024]{1,0:T(8,128)(2,1)S(1)}, u32[]{:S(2)}, u32[]{:S(2)}) %collective-permute-start.17) | collective-permute-done | bytes 131104 | tf_op jit(solution)/shard_map/ppermute | solution.py:580
  35.3 1.6 %collective-permute-start.18 = (bf16[32,1024]{1,0:T(8,128)(2,1)S(1)}, bf16[32,1024]{1,0:T(8,128)(2,1)S(1)}, u32[]{:S(2)}, u32[]{:S(2)}) collective-permute-start(bf16[32,1024]{1,0:T(8,128)(2,1)S(1)} %select_convert_fusion.10), channel_id=1, source_target_pairs={{0,4},{1,5},{2,6},{3,7},{4,0},{5,1},{6,2},{7,3},{8,12},{9,13},{10,... | collective-permute-start | bytes 196616 | tf_op jit(solution)/shard_map/ppermute | solution.py:580
  37.0 1.4 %collective-permute-start.12 = (bf16[32,1024]{1,0:T(8,128)(2,1)S(1)}, bf16[32,1024]{1,0:T(8,128)(2,1)S(1)}, u32[]{:S(2)}, u32[]{:S(2)}) collective-permute-start(bf16[32,1024]{1,0:T(8,128)(2,1)S(1)} %select_convert_fusion.12), channel_id=1, source_target_pairs={{0,4},{1,9},{2,6},{3,11},{4,0},{5,13},{6,2},{7,15},{8,12},{9,1},{1... | collective-permute-start | bytes 196616 | tf_op jit(solution)/shard_map/ppermute | solution.py:580
  38.4 1.4 %collective-permute-start.6 = (bf16[32,1024]{1,0:T(8,128)(2,1)S(1)}, bf16[32,1024]{1,0:T(8,128)(2,1)S(1)}, u32[]{:S(2)}, u32[]{:S(2)}) collective-permute-start(bf16[32,1024]{1,0:T(8,128)(2,1)S(1)} %select_convert_fusion.14), channel_id=1, source_target_pairs={{0,4},{1,9},{2,6},{3,11},{4,0},{5,13},{6,2},{7,15},{8,12},{9,1},{1... | collective-permute-start | bytes 196616 | tf_op jit(solution)/shard_map/ppermute | solution.py:580
  39.9 1.5 %collective-permute-start.24 = (bf16[40,1024]{1,0:T(8,128)(2,1)S(1)}, bf16[40,1024]{1,0:T(8,128)(2,1)S(1)}, u32[]{:S(2)}, u32[]{:S(2)}) collective-permute-start(bf16[40,1024]{1,0:T(8,128)(2,1)S(1)} %pad_maximum_fusion.10), channel_id=1, source_target_pairs={{0,4},{1,9},{2,6},{3,11},{4,0},{5,13},{6,2},{7,15},{8,12},{9,1},{1... | collective-permute-start | bytes 245768 | tf_op jit(solution)/shard_map/ppermute | solution.py:580
  41.5 2.6 %collective-permute-start.19 = (bf16[32,1024]{1,0:T(8,128)(2,1)S(1)}, bf16[32,1024]{1,0:T(8,128)(2,1)S(1)}, u32[]{:S(2)}, u32[]{:S(2)}) collective-permute-start(bf16[32,1024]{1,0:T(8,128)(2,1)S(1)} %add_convert_fusion.3), channel_id=1, source_target_pairs={{0,8},{1,9},{2,10},{3,11},{4,12},{5,13},{6,14},{7,15},{8,0},{9,1},... | collective-permute-start | bytes 196616 | tf_op jit(solution)/shard_map/ppermute | solution.py:580
  44.8 2.4 %collective-permute-start.7 = (bf16[32,1024]{1,0:T(8,128)(2,1)S(1)}, bf16[32,1024]{1,0:T(8,128)(2,1)S(1)}, u32[]{:S(2)}, u32[]{:S(2)}) collective-permute-start(bf16[32,1024]{1,0:T(8,128)(2,1)S(1)} %add_convert_fusion.7), channel_id=1, source_target_pairs={{0,8},{1,3},{2,10},{3,1},{4,12},{5,7},{6,14},{7,5},{8,0},{9,11},{1... | collective-permute-start | bytes 196616 | tf_op jit(solution)/shard_map/ppermute | solution.py:580
  48.1 1.2 %collective-permute-start.20 = (bf16[32,1024]{1,0:T(8,128)(2,1)S(1)}, bf16[32,1024]{1,0:T(8,128)(2,1)S(1)}, u32[]{:S(2)}, u32[]{:S(2)}) collective-permute-start(bf16[32,1024]{1,0:T(8,128)(2,1)S(1)} %add_convert_fusion.2), channel_id=1, source_target_pairs={{0,4},{1,5},{2,6},{3,7},{4,0},{5,1},{6,2},{7,3},{8,12},{9,13},{10,... | collective-permute-start | bytes 196616 | tf_op jit(solution)/shard_map/ppermute | solution.py:580
  50.3 1.3 %collective-permute-done.7 = bf16[32,1024]{1,0:T(8,128)(2,1)S(1)} collective-permute-done((bf16[32,1024]{1,0:T(8,128)(2,1)S(1)}, bf16[32,1024]{1,0:T(8,128)(2,1)S(1)}, u32[]{:S(2)}, u32[]{:S(2)}) %collective-permute-start.7) | collective-permute-done | bytes 65568 | tf_op jit(solution)/shard_map/ppermute | solution.py:580
  52.4 3.9 %collective-permute-done.25 = bf16[40,1024]{1,0:T(8,128)(2,1)S(1)} collective-permute-done((bf16[40,1024]{1,0:T(8,128)(2,1)S(1)}, bf16[40,1024]{1,0:T(8,128)(2,1)S(1)}, u32[]{:S(2)}, u32[]{:S(2)}) %collective-permute-start.25) | collective-permute-done | bytes 81952 | tf_op jit(solution)/shard_map/ppermute | solution.py:580
  56.9 1.7 %collective-permute-start.15 = (bf16[64,1024]{1,0:T(8,128)(2,1)S(1)}, bf16[64,1024]{1,0:T(8,128)(2,1)S(1)}, u32[]{:S(2)}, u32[]{:S(2)}) collective-permute-start(bf16[64,1024]{1,0:T(8,128)(2,1)S(1)} %pad_maximum_fusion.7), channel_id=1, source_target_pairs={{0,2},{1,5},{2,0},{3,7},{4,6},{5,1},{6,4},{7,3},{8,10},{9,13},{10,... | collective-permute-start | bytes 393224 | tf_op jit(solution)/shard_map/ppermute | solution.py:580
  59.1 2.2 %collective-permute-done.26 = bf16[32,1024]{1,0:T(8,128)(2,1)S(1)} collective-permute-done((bf16[32,1024]{1,0:T(8,128)(2,1)S(1)}, bf16[32,1024]{1,0:T(8,128)(2,1)S(1)}, u32[]{:S(2)}, u32[]{:S(2)}) %collective-permute-start.26) | collective-permute-done | bytes 65568 | tf_op jit(solution)/shard_map/ppermute | solution.py:580
  63.0 1.2 %collective-permute-done.9 = bf16[64,1024]{1,0:T(8,128)(2,1)S(1)} collective-permute-done((bf16[64,1024]{1,0:T(8,128)(2,1)S(1)}, bf16[64,1024]{1,0:T(8,128)(2,1)S(1)}, u32[]{:S(2)}, u32[]{:S(2)}) %collective-permute-start.9) | collective-permute-done | bytes 131104 | tf_op jit(solution)/shard_map/ppermute | solution.py:580
  64.3 2.1 %collective-permute-done.27 = bf16[64,1024]{1,0:T(8,128)(2,1)S(1)} collective-permute-done((bf16[64,1024]{1,0:T(8,128)(2,1)S(1)}, bf16[64,1024]{1,0:T(8,128)(2,1)S(1)}, u32[]{:S(2)}, u32[]{:S(2)}) %collective-permute-start.27) | collective-permute-done | bytes 131104 | tf_op jit(solution)/shard_map/ppermute | solution.py:580
  67.2 1.7 %shard_map.198.refs_0_ = f32[1024,1024]{1,0:T(8,128)} custom-call(bf16[128,1024]{1,0:T(8,128)(2,1)S(1)} %pad_maximum_fusion.1.refs_0_, bf16[128,1024]{1,0:T(8,128)(2,1)S(1)} %pad_maximum_fusion.2.refs_1_, bf16[128,1024]{1,0:T(8,128)(2,1)S(1)} %pad_maximum_fusion.3.refs_2_, bf16[128,1024]{1,0:T(8,128)(2,1)S(1)} %pad_maximum_fusion.4.refs_3_, ...), custom_call_target="tpu_custom_call" | custom-call | flops 786432 | bytes 4718592 | tf_op jit(solution)/shard_map/pallas_call | solution.py:708
  68.9 1.6 %shard_map.199 = (f32[1024,1024]{1,0:T(8,128)}, f32[1,1024]{1,0:T(1,128)}) custom-call(f32[1024,1024]{1,0:T(8,128)} %shard_map.198.refs_0_, bf16[128,1024]{1,0:T(8,128)(2,1)S(1)} %collective-permute-done.30.refs_1_, bf16[136,1024]{1,0:T(8,128)(2,1)S(1)} %collective-permute-done.31.refs_2_, ...), custom_call_target="tpu_custom_call", output_to_operand_aliasing={{0}: (0, {})} | custom-call | flops 262144 | bytes 1572864 | tf_op jit(solution)/shard_map/pallas_call | solution.py:708
  (91 shorter events, 13.1 us)
Async XLA Ops:
  10.4 5.8 %collective-permute-start.2 = (bf16[128,512]{1,0:T(8,128)(2,1)S(1)}, bf16[128,512]{1,0:T(8,128)(2,1)S(1)}, u32[]{:S(2)}, u32[]{:S(2)}) collective-permute-start(bf16[128,512]{1,0:T(8,128)(2,1)S(1)} %get-tuple-element.47), channel_id=1, source_target_pairs={{0,2},{1,3},{2,0},{3,1},{4,6},{5,7},{6,4},{7,5},{8,10},{9,11},{10,... | collective-permute-start | bytes 393224 | tf_op jit(solution)/shard_map/ppermute | solution.py:500
  16.3 5.2 %collective-permute-start.3 = (bf16[128,512]{1,0:T(8,128)(2,1)S(1)}, bf16[128,512]{1,0:T(8,128)(2,1)S(1)}, u32[]{:S(2)}, u32[]{:S(2)}) collective-permute-start(bf16[128,512]{1,0:T(8,128)(2,1)S(1)} %collective-permute-done.2.refs_6_), channel_id=1, source_target_pairs={{0,1},{1,0},{2,3},{3,2},{4,5},{5,4},{6,7},{7,6},{8,9},{9,8},{10,11... | collective-permute-start | bytes 393224 | tf_op jit(solution)/shard_map/ppermute | solution.py:505
  28.0 4.3 %collective-permute-start.22 = (bf16[136,1024]{1,0:T(8,128)(2,1)S(1)}, bf16[136,1024]{1,0:T(8,128)(2,1)S(1)}, u32[]{:S(2)}, u32[]{:S(2)}) collective-permute-start(bf16[136,1024]{1,0:T(8,128)(2,1)S(1)} %get-tuple-element.62.refs_3_), channel_id=1, source_target_pairs={{0,1},{1,0},{2,3},{3,2},{4,5},{5,4},{6,7},{7,6},{8,9},{9,8},{10,11... | collective-permute-start | bytes 835592 | tf_op jit(solution)/shard_map/ppermute | solution.py:580
  29.4 5.9 %collective-permute-start.17 = (bf16[64,1024]{1,0:T(8,128)(2,1)S(1)}, bf16[64,1024]{1,0:T(8,128)(2,1)S(1)}, u32[]{:S(2)}, u32[]{:S(2)}) collective-permute-start(bf16[64,1024]{1,0:T(8,128)(2,1)S(1)} %get-tuple-element.75), channel_id=1, source_target_pairs={{0,2},{1,3},{2,0},{3,1},{4,6},{5,7},{6,4},{7,5},{8,10},{9,11},{10,... | collective-permute-start | bytes 393224 | tf_op jit(solution)/shard_map/ppermute | solution.py:580
  30.0 7.0 %collective-permute-start.11 = (bf16[64,1024]{1,0:T(8,128)(2,1)S(1)}, bf16[64,1024]{1,0:T(8,128)(2,1)S(1)}, u32[]{:S(2)}, u32[]{:S(2)}) collective-permute-start(bf16[64,1024]{1,0:T(8,128)(2,1)S(1)} %get-tuple-element.77), channel_id=1, source_target_pairs={{0,2},{1,5},{2,0},{3,7},{4,6},{5,1},{6,4},{7,3},{8,10},{9,13},{10,... | collective-permute-start | bytes 393224 | tf_op jit(solution)/shard_map/ppermute | solution.py:580
  31.8 6.6 %collective-permute-start.5 = (bf16[64,1024]{1,0:T(8,128)(2,1)S(1)}, bf16[64,1024]{1,0:T(8,128)(2,1)S(1)}, u32[]{:S(2)}, u32[]{:S(2)}) collective-permute-start(bf16[64,1024]{1,0:T(8,128)(2,1)S(1)} %get-tuple-element.79), channel_id=1, source_target_pairs={{0,2},{1,5},{2,0},{3,7},{4,6},{5,1},{6,4},{7,3},{8,10},{9,13},{10,... | collective-permute-start | bytes 393224 | tf_op jit(solution)/shard_map/ppermute | solution.py:580
  32.4 7.4 %collective-permute-start.23 = (bf16[72,1024]{1,0:T(8,128)(2,1)S(1)}, bf16[72,1024]{1,0:T(8,128)(2,1)S(1)}, u32[]{:S(2)}, u32[]{:S(2)}) collective-permute-start(bf16[72,1024]{1,0:T(8,128)(2,1)S(1)} %pad_maximum_fusion.5), channel_id=1, source_target_pairs={{0,2},{1,5},{2,0},{3,7},{4,6},{5,1},{6,4},{7,3},{8,10},{9,13},{10,... | collective-permute-start | bytes 442376 | tf_op jit(solution)/shard_map/ppermute | solution.py:580
  35.3 6.1 %collective-permute-start.18 = (bf16[32,1024]{1,0:T(8,128)(2,1)S(1)}, bf16[32,1024]{1,0:T(8,128)(2,1)S(1)}, u32[]{:S(2)}, u32[]{:S(2)}) collective-permute-start(bf16[32,1024]{1,0:T(8,128)(2,1)S(1)} %select_convert_fusion.10), channel_id=1, source_target_pairs={{0,4},{1,5},{2,6},{3,7},{4,0},{5,1},{6,2},{7,3},{8,12},{9,13},{10,... | collective-permute-start | bytes 196616 | tf_op jit(solution)/shard_map/ppermute | solution.py:580
  37.0 7.1 %collective-permute-start.12 = (bf16[32,1024]{1,0:T(8,128)(2,1)S(1)}, bf16[32,1024]{1,0:T(8,128)(2,1)S(1)}, u32[]{:S(2)}, u32[]{:S(2)}) collective-permute-start(bf16[32,1024]{1,0:T(8,128)(2,1)S(1)} %select_convert_fusion.12), channel_id=1, source_target_pairs={{0,4},{1,9},{2,6},{3,11},{4,0},{5,13},{6,2},{7,15},{8,12},{9,1},{1... | collective-permute-start | bytes 196616 | tf_op jit(solution)/shard_map/ppermute | solution.py:580
  38.4 6.3 %collective-permute-start.6 = (bf16[32,1024]{1,0:T(8,128)(2,1)S(1)}, bf16[32,1024]{1,0:T(8,128)(2,1)S(1)}, u32[]{:S(2)}, u32[]{:S(2)}) collective-permute-start(bf16[32,1024]{1,0:T(8,128)(2,1)S(1)} %select_convert_fusion.14), channel_id=1, source_target_pairs={{0,4},{1,9},{2,6},{3,11},{4,0},{5,13},{6,2},{7,15},{8,12},{9,1},{1... | collective-permute-start | bytes 196616 | tf_op jit(solution)/shard_map/ppermute | solution.py:580
  39.9 7.4 %collective-permute-start.24 = (bf16[40,1024]{1,0:T(8,128)(2,1)S(1)}, bf16[40,1024]{1,0:T(8,128)(2,1)S(1)}, u32[]{:S(2)}, u32[]{:S(2)}) collective-permute-start(bf16[40,1024]{1,0:T(8,128)(2,1)S(1)} %pad_maximum_fusion.10), channel_id=1, source_target_pairs={{0,4},{1,9},{2,6},{3,11},{4,0},{5,13},{6,2},{7,15},{8,12},{9,1},{1... | collective-permute-start | bytes 245768 | tf_op jit(solution)/shard_map/ppermute | solution.py:580
  41.5 6.7 %collective-permute-start.19 = (bf16[32,1024]{1,0:T(8,128)(2,1)S(1)}, bf16[32,1024]{1,0:T(8,128)(2,1)S(1)}, u32[]{:S(2)}, u32[]{:S(2)}) collective-permute-start(bf16[32,1024]{1,0:T(8,128)(2,1)S(1)} %add_convert_fusion.3), channel_id=1, source_target_pairs={{0,8},{1,9},{2,10},{3,11},{4,12},{5,13},{6,14},{7,15},{8,0},{9,1},... | collective-permute-start | bytes 196616 | tf_op jit(solution)/shard_map/ppermute | solution.py:580
  44.2 6.0 %collective-permute-start.13 = (bf16[32,1024]{1,0:T(8,128)(2,1)S(1)}, bf16[32,1024]{1,0:T(8,128)(2,1)S(1)}, u32[]{:S(2)}, u32[]{:S(2)}) collective-permute-start(bf16[32,1024]{1,0:T(8,128)(2,1)S(1)} %add_convert_fusion.5), channel_id=1, source_target_pairs={{0,8},{1,3},{2,10},{3,1},{4,12},{5,7},{6,14},{7,5},{8,0},{9,11},{1... | collective-permute-start | bytes 196616 | tf_op jit(solution)/shard_map/ppermute | solution.py:580
  44.8 6.8 %collective-permute-start.7 = (bf16[32,1024]{1,0:T(8,128)(2,1)S(1)}, bf16[32,1024]{1,0:T(8,128)(2,1)S(1)}, u32[]{:S(2)}, u32[]{:S(2)}) collective-permute-start(bf16[32,1024]{1,0:T(8,128)(2,1)S(1)} %add_convert_fusion.7), channel_id=1, source_target_pairs={{0,8},{1,3},{2,10},{3,1},{4,12},{5,7},{6,14},{7,5},{8,0},{9,11},{1... | collective-permute-start | bytes 196616 | tf_op jit(solution)/shard_map/ppermute | solution.py:580
  47.3 8.9 %collective-permute-start.25 = (bf16[40,1024]{1,0:T(8,128)(2,1)S(1)}, bf16[40,1024]{1,0:T(8,128)(2,1)S(1)}, u32[]{:S(2)}, u32[]{:S(2)}) collective-permute-start(bf16[40,1024]{1,0:T(8,128)(2,1)S(1)} %pad_maximum_fusion.11), channel_id=1, source_target_pairs={{0,8},{1,3},{2,10},{3,1},{4,12},{5,7},{6,14},{7,5},{8,0},{9,11},{1... | collective-permute-start | bytes 245768 | tf_op jit(solution)/shard_map/ppermute | solution.py:580
  48.1 8.2 %collective-permute-start.20 = (bf16[32,1024]{1,0:T(8,128)(2,1)S(1)}, bf16[32,1024]{1,0:T(8,128)(2,1)S(1)}, u32[]{:S(2)}, u32[]{:S(2)}) collective-permute-start(bf16[32,1024]{1,0:T(8,128)(2,1)S(1)} %add_convert_fusion.2), channel_id=1, source_target_pairs={{0,4},{1,5},{2,6},{3,7},{4,0},{5,1},{6,2},{7,3},{8,12},{9,13},{10,... | collective-permute-start | bytes 196616 | tf_op jit(solution)/shard_map/ppermute | solution.py:580
  50.2 6.7 %collective-permute-start.14 = (bf16[32,1024]{1,0:T(8,128)(2,1)S(1)}, bf16[32,1024]{1,0:T(8,128)(2,1)S(1)}, u32[]{:S(2)}, u32[]{:S(2)}) collective-permute-start(bf16[32,1024]{1,0:T(8,128)(2,1)S(1)} %add_convert_fusion.4), channel_id=1, source_target_pairs={{0,4},{1,9},{2,6},{3,11},{4,0},{5,13},{6,2},{7,15},{8,12},{9,1},{1... | collective-permute-start | bytes 196616 | tf_op jit(solution)/shard_map/ppermute | solution.py:580
  51.6 7.0 %collective-permute-start.8 = (bf16[32,1024]{1,0:T(8,128)(2,1)S(1)}, bf16[32,1024]{1,0:T(8,128)(2,1)S(1)}, u32[]{:S(2)}, u32[]{:S(2)}) collective-permute-start(bf16[32,1024]{1,0:T(8,128)(2,1)S(1)} %add_convert_fusion.6), channel_id=1, source_target_pairs={{0,4},{1,9},{2,6},{3,11},{4,0},{5,13},{6,2},{7,15},{8,12},{9,1},{1... | collective-permute-start | bytes 196616 | tf_op jit(solution)/shard_map/ppermute | solution.py:580
  56.3 5.0 %collective-permute-start.26 = (bf16[32,1024]{1,0:T(8,128)(2,1)S(1)}, bf16[32,1024]{1,0:T(8,128)(2,1)S(1)}, u32[]{:S(2)}, u32[]{:S(2)}) collective-permute-start(bf16[32,1024]{1,0:T(8,128)(2,1)S(1)} %add_convert_fusion), channel_id=1, source_target_pairs={{0,4},{1,9},{2,6},{3,11},{4,0},{5,13},{6,2},{7,15},{8,12},{9,1},{1... | collective-permute-start | bytes 196616 | tf_op jit(solution)/shard_map/ppermute | solution.py:580
  56.4 5.4 %collective-permute-start.21 = (bf16[64,1024]{1,0:T(8,128)(2,1)S(1)}, bf16[64,1024]{1,0:T(8,128)(2,1)S(1)}, u32[]{:S(2)}, u32[]{:S(2)}) collective-permute-start(bf16[64,1024]{1,0:T(8,128)(2,1)S(1)} %pad_maximum_fusion.8), channel_id=1, source_target_pairs={{0,2},{1,3},{2,0},{3,1},{4,6},{5,7},{6,4},{7,5},{8,10},{9,11},{10,... | collective-permute-start | bytes 393224 | tf_op jit(solution)/shard_map/ppermute | solution.py:580
  56.9 5.9 %collective-permute-start.15 = (bf16[64,1024]{1,0:T(8,128)(2,1)S(1)}, bf16[64,1024]{1,0:T(8,128)(2,1)S(1)}, u32[]{:S(2)}, u32[]{:S(2)}) collective-permute-start(bf16[64,1024]{1,0:T(8,128)(2,1)S(1)} %pad_maximum_fusion.7), channel_id=1, source_target_pairs={{0,2},{1,5},{2,0},{3,7},{4,6},{5,1},{6,4},{7,3},{8,10},{9,13},{10,... | collective-permute-start | bytes 393224 | tf_op jit(solution)/shard_map/ppermute | solution.py:580
  58.6 5.6 %collective-permute-start.9 = (bf16[64,1024]{1,0:T(8,128)(2,1)S(1)}, bf16[64,1024]{1,0:T(8,128)(2,1)S(1)}, u32[]{:S(2)}, u32[]{:S(2)}) collective-permute-start(bf16[64,1024]{1,0:T(8,128)(2,1)S(1)} %pad_maximum_fusion.6), channel_id=1, source_target_pairs={{0,2},{1,5},{2,0},{3,7},{4,6},{5,1},{6,4},{7,3},{8,10},{9,13},{10,... | collective-permute-start | bytes 393224 | tf_op jit(solution)/shard_map/ppermute | solution.py:580
  61.3 5.0 %collective-permute-start.27 = (bf16[64,1024]{1,0:T(8,128)(2,1)S(1)}, bf16[64,1024]{1,0:T(8,128)(2,1)S(1)}, u32[]{:S(2)}, u32[]{:S(2)}) collective-permute-start(bf16[64,1024]{1,0:T(8,128)(2,1)S(1)} %pad_maximum_fusion.9), channel_id=1, source_target_pairs={{0,2},{1,5},{2,0},{3,7},{4,6},{5,1},{6,4},{7,3},{8,10},{9,13},{10,... | collective-permute-start | bytes 393224 | tf_op jit(solution)/shard_map/ppermute | solution.py:580
  61.9 5.3 %collective-permute-start.29 = (bf16[128,1024]{1,0:T(8,128)(2,1)S(1)}, bf16[128,1024]{1,0:T(8,128)(2,1)S(1)}, u32[]{:S(2)}, u32[]{:S(2)}) collective-permute-start(bf16[128,1024]{1,0:T(8,128)(2,1)S(1)} %pad_maximum_fusion.3.refs_2_), channel_id=1, source_target_pairs={{0,1},{1,0},{2,3},{3,2},{4,5},{5,4},{6,7},{7,6},{8,9},{9,8},{10,11... | collective-permute-start | bytes 786440 | tf_op jit(solution)/shard_map/ppermute | solution.py:580
  (9 other events, 38.8 us)
